TPU v7x, 32 devices: a whole 2x2x4 slice. The times are simulated.
32 devices in a mesh: groups: 2 (over y), tm: 4 (over z), height: 2 (over x), chan: 2 (over core).
Axes of the slice: x: 2, y: 2, z: 4, core: 2. Of those that a mesh axis runs over, the one named last changes fastest.
Arguments:
- clip_video: bfloat16 [64, 32, 16, 256], P(('groups', 'tm'), 'height', None, 'chan'), parts along dimension 0, may hold values from -60 to 60
- norm_gain: float32 [256], P('chan'), may hold values from 0.25 to 1.75
- norm_bias: float32 [256], P('chan'), may hold values from -3 to 3
- conv_weight: bfloat16 [3, 3, 3, 256, 256], replicated, may hold values from -0.078125 to 0.078125
- clip_lengths: int32 [16], P('groups'), parts along dimension 0, may hold values from 1 to 24, 32 in all
- packed_frame: int32 [64], P(('groups', 'tm')), parts along dimension 0, may hold values from 0 to 31, as said below
- packed_grad: bfloat16 [64, 32, 16, 256], P(('groups', 'tm'), 'height', None, 'chan'), parts along dimension 0, may hold values from -6 to 6
Outputs:
- block_out: bfloat16 [64, 32, 16, 256], P(('groups', 'tm'), 'height', None, 'chan'), parts along dimension 0
- video_grad: bfloat16 [64, 32, 16, 256], P(('groups', 'tm'), 'height', None, 'chan'), parts along dimension 0
- weight_grad: float32 [6, 3, 3, 256, 256], P('groups', None, None, ('tm', 'height'), 'chan'), parts along dimension 0
- gain_grad: float32 [512], P(('groups', 'chan')), parts along dimension 0
- bias_grad: float32 [512], P(('groups', 'chan')), parts along dimension 0
There are 2 independent parts, one for each index of `groups`. A program takes and returns all parts, laid end to end along the dimension named above; an argument that names none is the same for every part. Nothing has to cross between parts.
Inputs may be any that keep to these rules, and one draw needn't show every extreme that they name: `packed_frame`: A permutation of the 32 frames. Each aligned block of 8 packed slots holds frames of exactly 4 time slabs of 8 frames, the same count 2 from each of them, and no frame of the other slabs. `clip_lengths`: the lengths sum to 32; the longest clip has exactly 24 frames.
All inputs are finite; a program needn't handle non-finite values.
Results may differ from a plain program's by a relative error of at most 0.0017.
Values may be sent and summed in bfloat16 or wider, within the bound.
No kernel may reach another device: no remote copies, remote signals or barrier semaphores. Data moves between devices by JAX's collectives and lax.ppermute only.
A program may use at most 128 MiB of HBM per device.

v0:
```python
import functools
import jax
import jax.numpy as jnp
from jax import lax
from jax.experimental import pallas as pl
from jax.experimental.pallas import tpu as pltpu
from jax.sharding import PartitionSpec as P

GROUPS = 32
NCLIPS = 8
F32 = jnp.float32
BF16 = jnp.bfloat16
HIGHEST = lax.Precision.HIGHEST
VM = pl.BlockSpec(memory_space=pltpu.VMEM)
SM = pl.BlockSpec(memory_space=pltpu.SMEM)


def call(body, out_shape, in_specs, scratch=(), flops=0, nbytes=0, name=None):
    return pl.pallas_call(
        body,
        out_shape=out_shape,
        in_specs=in_specs,
        out_specs=jax.tree.map(lambda _: VM, out_shape),
        scratch_shapes=list(scratch),
        compiler_params=pltpu.CompilerParams(vmem_limit_bytes=56 * 2**20),
        cost_estimate=pl.CostEstimate(flops=flops, bytes_accessed=nbytes, transcendentals=0),
        name=name,
    )


def fdot(a, b):
    return jnp.dot(a, b, precision=HIGHEST, preferred_element_type=F32)


def bdot(a, b):
    return jnp.dot(a, b, preferred_element_type=F32)


def ring(peers, by):
    return [(i, (i + by) % peers) for i in range(peers)]


def sibling(value):
    return lax.ppermute(value, "chan", ring(2, 1))


def sigmoid(v):
    return 1.0 / (1.0 + jnp.exp(-v))


def pack_body(peers, cap, pos, frames, grad, *outs):
    slots = frames.shape[0]
    slab_frames = slots
    tm = pos[0]
    number = [frames[i] for i in range(slots)]
    step = [lax.rem(n // slab_frames - tm + peers, peers) for n in number]
    rank = []
    for i in range(slots):
        r = jnp.int32(0)
        for j in range(i):
            r = r + jnp.where(step[j] == step[i], 1, 0)
        rank.append(r)
    rows = grad.shape[1]
    for k in range(peers):
        for j in range(cap):
            index = jnp.int32(0)
            local = jnp.int32(-1)
            for i in range(slots):
                hit = jnp.logical_and(step[i] == k, rank[i] == j)
                index = jnp.where(hit, i, index)
                local = jnp.where(hit, lax.rem(number[i], slab_frames), local)
            outs[k][j, :rows] = grad[index]
            outs[k][j, rows:] = jnp.full((1,) + grad.shape[2:], local.astype(F32), F32).astype(BF16)


def stat_body(video, gain, bias, average, out):
    frames, rows, cols, chans = video.shape
    cells = rows * cols
    sums = [
        jnp.sum(video[t].astype(F32).reshape(cells, chans), axis=0, keepdims=True)
        for t in range(frames)
    ]
    mean = fdot(jnp.concatenate(sums, axis=0) * (1.0 / cells), average[...])
    squares = []
    for t in range(frames):
        apart = video[t].astype(F32).reshape(cells, chans) - mean[t : t + 1]
        squares.append(jnp.sum(apart * apart, axis=0, keepdims=True))
    var = fdot(jnp.concatenate(squares, axis=0) * (1.0 / cells), average[...])
    rest = jnp.concatenate(
        [gain[...], bias[...], jnp.zeros((6, chans), F32)], axis=0
    )
    whole = jnp.concatenate([mean, var, rest], axis=0)
    for i in range(out.shape[0]):
        out[i] = whole


def table_body(got, same, picked, out):
    peers, bands = got.shape[:2]
    frames = (got.shape[3] - 8) // 2
    for c in range(2):
        mean = [
            jnp.concatenate([got[t, h, c, :frames] for t in range(peers)], axis=0)
            for h in range(bands)
        ]
        var = [
            jnp.concatenate([got[t, h, c, frames : 2 * frames] for t in range(peers)], axis=0)
            for h in range(bands)
        ]
        average = sum(mean[1:], mean[0]) * (1.0 / bands)
        clip_mean = fdot(same[...], average)
        spread = jnp.zeros_like(average)
        for h in range(bands):
            apart = mean[h] - clip_mean
            spread = spread + (var[h] + apart * apart)
        out[c, :16] = fdot(picked[...], average)
        out[c, 16:32] = lax.rsqrt(fdot(picked[...], spread * (1.0 / bands)) + 1e-06)
        out[c, 32:] = got[0, 0, c, 2 * frames :]


def shifts(value):
    length = value.shape[0]
    column = lax.rem(lax.broadcasted_iota(jnp.int32, value.shape, 0), 16)
    before = jnp.where(column == 0, 0.0, pltpu.roll(value, 1, 0))
    after = jnp.where(column == 15, 0.0, pltpu.roll(value, length - 1, 0))
    return before, after


def weight_body(peers, bands, cap, block, *refs):
    refs = list(refs)
    pos, source, table, pick_own, pick_sib = [refs.pop(0) for _ in range(5)]
    take = lambda n: [refs.pop(0) for _ in range(n)]
    own, sib, prev_own, prev_sib = take(bands), take(bands), take(bands), take(bands)
    ups = [take(peers) for _ in range(bands)]
    outs = take(peers)
    active, upright = refs
    frames, rows, cols, chans = own[0].shape
    cells = rows * cols
    width = peers * block
    c = pos[1]
    h = pos[2]
    band = [lax.rem(h - m + bands, bands) for m in range(bands)]
    lookup = fdot(table[c], pick_own[...].astype(F32)) + fdot(
        table[1 - c], pick_sib[...].astype(F32)
    )
    mean, inv = lookup[:16], lookup[16:32]
    scale = inv * lookup[32:33]
    bias = lookup[33:34]
    active[:, 0] = jnp.zeros((active.shape[0], cols, 3 * width), BF16)
    active[:, bands * rows + 1] = jnp.zeros((active.shape[0], cols, 3 * width), BF16)
    for f in range(frames + 2):
        for m in range(bands):
            if f < 2:
                a, b = prev_own[m][f], prev_sib[m][f]
            else:
                a, b = own[m][f - 2], sib[m][f - 2]
            x = bdot(a.reshape(cells, chans), pick_own[...]) + bdot(
                b.reshape(cells, chans), pick_sib[...]
            )
            v = (x - mean[f : f + 1]) * scale[f : f + 1] + bias
            v = v * sigmoid(v)
            before, after = shifts(v)
            at = pl.ds(band[m] * rows + 1, rows)
            active[f, at, :, :width] = before.astype(BF16).reshape(rows, cols, width)
            active[f, at, :, width : 2 * width] = v.astype(BF16).reshape(rows, cols, width)
            active[f, at, :, 2 * width :] = after.astype(BF16).reshape(rows, cols, width)
    for k in range(peers):
        for j in range(cap):
            local = jnp.max(ups[0][k][j, rows].astype(F32)).astype(jnp.int32)

            @pl.when(local >= 0)
            def _():
                for m in range(bands):
                    u = ups[m][k][j, :rows].reshape(cells, chans)
                    upright[local, m] = u.T

    def tap(i, carry):
        a = i // 3
        b = lax.rem(i, 3)
        total = jnp.zeros((chans, 3 * width), F32)
        for t in range(frames):
            s = source[t * 3 + a]
            for m in range(bands):
                patch = active[s, pl.ds(band[m] * rows + b, rows)].reshape(cells, 3 * width)
                total = total + bdot(upright[t, m], patch)
        for col in range(3):
            piece = total[:, col * width : (col + 1) * width].T
            for k in range(peers):
                outs[k][i * 3 + col] = piece[k * block : (k + 1) * block].astype(outs[k].dtype)
        return carry

    lax.fori_loop(0, 9, tap, 0)


def forward_body(bands, *refs):
    pos, source, table, weight, own, sib, prev_own, prev_sib, up_own, up_sib, dn_own, dn_sib = refs[:12]
    out, active = refs[12:]
    frames, rows, cols, chans = own.shape
    cells = rows * cols
    c = pos[1]
    h = pos[2]
    line = lax.broadcasted_iota(jnp.int32, (cells + 2 * cols, chans), 0)
    inside = jnp.logical_and(
        jnp.logical_or(line >= cols, h > 0),
        jnp.logical_or(line < cells + cols, h < bands - 1),
    )

    def one(f, current_own, current_sib, edges):
        parts = []
        for value, (top, bottom) in ((current_own, edges[0]), (current_sib, edges[1])):
            parts.append(
                jnp.concatenate(
                    [top, value.reshape(cells, chans), bottom], axis=0
                ).astype(F32)
            )
        halves = [jnp.where(c == 0, parts[0], parts[1]), jnp.where(c == 0, parts[1], parts[0])]
        for side in range(2):
            mean = table[side, pl.ds(f, 1)]
            scale = table[side, pl.ds(16 + f, 1)] * table[side, 32:33]
            v = (halves[side] - mean) * scale + table[side, 33:34]
            v = jnp.where(inside, v * sigmoid(v), 0.0)
            before, after = shifts(v)
            for n, w in enumerate((before, v, after)):
                at = n * 2 * chans + side * chans
                active[f, :, :, at : at + chans] = w.astype(BF16).reshape(rows + 2, cols, chans)

    for f in range(2):
        one(
            f,
            prev_own[f],
            prev_sib[f],
            (
                (up_own[frames + f], dn_own[frames + f]),
                (up_sib[frames + f], dn_sib[frames + f]),
            ),
        )

    def body(t, carry):
        one(
            t + 2,
            own[t],
            sib[t],
            ((up_own[t], dn_own[t]), (up_sib[t], dn_sib[t])),
        )
        return carry

    lax.fori_loop(0, frames, body, 0)

    def frame(t, carry):
        total = own[t].reshape(cells, chans).astype(F32)
        mixed = jnp.zeros((cells, chans), F32)
        for a in range(3):
            s = source[t * 3 + a]
            for b in range(3):
                patch = active[s, b : b + rows].reshape(cells, 6 * chans)
                mixed = mixed + bdot(patch, weight[a * 3 + b])
        out[t] = (total + mixed).astype(BF16).reshape(rows, cols, chans)
        return carry

    lax.fori_loop(0, frames, frame, 0)


def order_body(peers, bands, cap, pos, *refs):
    own, above, below = refs[:peers], refs[peers : 2 * peers], refs[2 * peers : 3 * peers]
    out, first = refs[3 * peers :]
    rows = own[0].shape[1] - 1
    h = pos[2]
    for k in range(peers):
        for j in range(cap):
            local = jnp.max(own[k][j, rows].astype(F32)).astype(jnp.int32)

            @pl.when(local >= 0)
            def _():
                out[local, 1 : rows + 1] = own[k][j, :rows]
                top = above[k][j, rows - 1].astype(F32)
                bottom = below[k][j, 0].astype(F32)
                out[local, 0] = jnp.where(h > 0, top, 0.0).astype(BF16)
                out[local, rows + 1] = jnp.where(h < bands - 1, bottom, 0.0).astype(BF16)

    first[...] = out[:2]


def backward_body(pos, target, table, member, weight, video, own, sib, next_own, next_sib, out, sums, spatial, total):
    frames, rows, cols, chans = video.shape
    cells = rows * cols
    c = pos[1]

    def fill(f, a, b):
        a = a.reshape(cells + 2 * cols, chans).astype(F32)
        b = b.reshape(cells + 2 * cols, chans).astype(F32)
        for side, v in enumerate((jnp.where(c == 0, a, b), jnp.where(c == 0, b, a))):
            before, after = shifts(v)
            for n, w in enumerate((after, v, before)):
                at = n * 2 * chans + side * chans
                spatial[f, :, :, at : at + chans] = w.astype(BF16).reshape(rows + 2, cols, chans)

    def body(t, carry):
        fill(t, own[t], sib[t])
        total[t] = jnp.zeros((cells, chans), F32)
        return carry

    lax.fori_loop(0, frames, body, 0)
    for f in range(2):
        fill(frames + f, next_own[f], next_sib[f])

    def frame(t, carry):
        for a in range(3):
            s = target[t * 3 + a]

            @pl.when(jnp.logical_and(s >= 0, s < frames))
            def _():
                grad = jnp.zeros((cells, chans), F32)
                for b in range(3):
                    patch = spatial[t, 2 - b : 2 - b + rows].reshape(cells, 6 * chans)
                    grad = grad + bdot(patch, weight[a * 3 + b])
                total[s] += grad

        return carry

    lax.fori_loop(0, frames + 2, frame, 0)
    firsts, seconds = [], []
    for t in range(frames):
        x = video[t].reshape(cells, chans).astype(F32)
        hat = (x - table[c, t + 2 : t + 3]) * table[c, t + 18 : t + 19]
        v = hat * table[c, 32:33] + table[c, 33:34]
        s = sigmoid(v)
        grad = total[t] * s * (1.0 + v * (1.0 - s))
        out[t] = grad
        firsts.append(jnp.sum(grad, axis=0, keepdims=True))
        seconds.append(jnp.sum(grad * hat, axis=0, keepdims=True))
    whole = jnp.concatenate(
        [
            fdot(member[...], jnp.concatenate(firsts, axis=0)),
            fdot(member[...], jnp.concatenate(seconds, axis=0)),
        ],
        axis=0,
    )
    for i in range(sums.shape[0]):
        sums[i] = whole


def finish_body(pos, table, group, spread, got, video, grad, up, out, small):
    frames, rows, cols, chans = video.shape
    cells = rows * cols
    c = pos[1]
    whole = jnp.sum(got[...], axis=0)
    gain = table[c, 32:33]
    small[0:1] = jnp.sum(whole[NCLIPS:], axis=0, keepdims=True)
    small[1:2] = jnp.sum(whole[:NCLIPS], axis=0, keepdims=True)
    small[2:] = jnp.zeros((6, chans), F32)
    first = fdot(spread[...], fdot(whole[:NCLIPS] * gain, group[...]))
    second = fdot(spread[...], fdot(whole[NCLIPS:] * gain, group[...]))
    for t in range(frames):
        inv = table[c, t + 18 : t + 19]
        x = video[t].reshape(cells, chans).astype(F32)
        hat = (x - table[c, t + 2 : t + 3]) * inv
        part = inv * (grad[t] * gain - first[t : t + 1] - hat * second[t : t + 1])
        u = up[t, 1 : rows + 1].reshape(cells, chans).astype(F32)
        out[t] = (u + part).astype(BF16).reshape(rows, cols, chans)


def per_device(
    clip_video, norm_gain, norm_bias, conv_weight, clip_lengths, packed_frame, packed_grad
):
    frames, rows, cols, chans = clip_video.shape
    full = conv_weight.shape[3]
    peers = lax.axis_size("tm")
    bands = lax.axis_size("height")
    tm = lax.axis_index("tm")
    h = lax.axis_index("height")
    c = lax.axis_index("chan")
    group_size = full // GROUPS
    cap = max(1, frames // peers)
    block = full // (peers * bands)
    width = peers * block
    cells = rows * cols
    everyone = ("tm", "height", "chan")
    i32 = jnp.int32
    sds = jax.ShapeDtypeStruct
    pos = jnp.stack([tm, c, h]).astype(i32)

    piece = sds((cap, rows + 1, cols, chans), BF16)
    pieces = call(
        functools.partial(pack_body, peers, cap), [piece] * peers, [SM, SM, VM],
        nbytes=2**20, name="pack",
    )(pos, packed_frame, packed_grad)
    ups = [[pieces[0]] + [lax.ppermute(pieces[k], "tm", ring(peers, k)) for k in range(1, peers)]]

    last = clip_video[frames - 2 :]
    own = [clip_video]
    prev_own = []
    for m in range(bands):
        if m > 0:
            own.append(lax.ppermute(clip_video, "height", ring(bands, m)))
        pairs = [
            (t * bands + b, (t + 1) * bands + (b + m) % bands)
            for t in range(peers - 1)
            for b in range(bands)
        ]
        prev_own.append(lax.ppermute(last, ("tm", "height"), pairs))
    sib = [sibling(v) for v in own]
    prev_sib = [sibling(v) for v in prev_own]
    for m in range(1, bands):
        ups.append([lax.ppermute(v, "height", ring(bands, m)) for v in ups[0]])

    lane = jnp.arange(chans, dtype=i32)
    group = (lane[:, None] // group_size == lane[None, :] // group_size).astype(F32)
    devices = peers * bands * 2
    stats = call(
        stat_body, sds((devices, 2 * frames + 8, chans), F32), [VM, VM, VM, VM],
        nbytes=2**20, name="stat",
    )(clip_video, norm_gain[None], norm_bias[None], group * (1.0 / group_size))
    got = lax.all_to_all(stats, everyone, 0, 0)
    got = got.reshape(peers, bands, 2, 2 * frames + 8, chans)

    clip = jnp.arange(NCLIPS, dtype=i32)
    ends = jnp.sum(jnp.where(clip[None, :] <= clip[:, None], clip_lengths[None, :], 0), axis=1)

    def start_of(frame):
        passed = ends[None, :] <= frame[:, None]
        return jnp.sum(jnp.where(passed, clip_lengths[None, :], 0), axis=1)

    def member_of(frame):
        passed = ends[None, :] <= frame[:, None]
        return jnp.sum(passed.astype(i32), axis=1)

    first_frame = tm * frames
    near = first_frame - 2 + jnp.arange(frames + 8, dtype=i32)
    near = jnp.clip(near, 0, peers * frames - 1)
    every = jnp.arange(peers * frames, dtype=i32)

    def one_hot(index):
        return (index[:, None] == clip[None, :]).astype(F32)

    every_member = one_hot(member_of(every))
    near_member = one_hot(member_of(near))
    over = every_member / clip_lengths.astype(F32)[None, :]
    same = jnp.dot(every_member, over.T, precision=HIGHEST)
    picked = jnp.dot(near_member, over.T, precision=HIGHEST)
    table = call(
        table_body, sds((2, 40, chans), F32), [VM, VM, VM], nbytes=2**18, name="table"
    )(got, same, picked)
    tap = jnp.arange(3, dtype=i32)
    ahead = first_frame + jnp.arange(frames + 2, dtype=i32)
    reach = jnp.maximum(ahead[:, None] - 2 + tap[None, :], start_of(ahead)[:, None])
    source = (reach[:frames] - (first_frame - 2)).reshape(-1)
    target = (reach - first_frame).reshape(-1)

    wanted = jnp.arange(width, dtype=i32)
    holder = lax.rem(tm + wanted // block, peers)
    wanted = (holder * bands + h) * block + lax.rem(wanted, block)
    pick_own = (c * chans + lane[:, None] == wanted[None, :]).astype(BF16)
    pick_sib = ((1 - c) * chans + lane[:, None] == wanted[None, :]).astype(BF16)
    grads = call(
        functools.partial(weight_body, peers, bands, cap, block),
        [sds((27, block, chans), F32)] + [sds((27, block, chans), BF16)] * (peers - 1),
        [SM, SM] + [VM] * (3 + 4 * bands + peers * bands),
        [
            pltpu.VMEM((frames + 2, bands * rows + 2, cols, 3 * width), BF16),
            pltpu.VMEM((frames, bands, chans, cells), BF16),
        ],
        flops=8 * 10**9, nbytes=6 * 2**20, name="weight",
    )(
        pos, source, table, pick_own, pick_sib, *own, *sib, *prev_own, *prev_sib,
        *[v for band in ups for v in band],
    )
    weight_grad = grads[0]
    for k in range(1, peers):
        weight_grad = weight_grad + lax.ppermute(grads[k], "tm", ring(peers, k)).astype(F32)
    weight_grad = weight_grad.reshape(3, 3, 3, block, chans)

    def edge(values, row):
        return jnp.concatenate([v[:, row] for v in values], axis=0)

    far = bands - 1
    weight_out = lax.dynamic_slice_in_dim(conv_weight, c * chans, chans, 4)
    weight_out = weight_out.reshape(9, 3 * full, chans)
    block_out = call(
        functools.partial(forward_body, bands),
        sds(clip_video.shape, BF16),
        [SM, SM] + [VM] * 10,
        [pltpu.VMEM((frames + 2, rows + 2, cols, 6 * chans), BF16)],
        flops=8 * 10**9, nbytes=6 * 2**20, name="forward",
    )(
        pos, source, table, weight_out, own[0], sib[0], prev_own[0], prev_sib[0],
        edge([own[1], prev_own[1]], rows - 1), edge([sib[1], prev_sib[1]], rows - 1),
        edge([own[far], prev_own[far]], 0), edge([sib[far], prev_sib[far]], 0),
    )

    up, up_first = call(
        functools.partial(order_body, peers, bands, cap),
        [sds((frames, rows + 2, cols, chans), BF16), sds((2, rows + 2, cols, chans), BF16)],
        [SM] + [VM] * (3 * peers),
        nbytes=2 * 2**20, name="order",
    )(pos, *ups[0], *ups[1], *ups[far])
    up_sib = sibling(up)
    next_own = lax.ppermute(up_first, "tm", [(t + 1, t) for t in range(peers - 1)])
    next_sib = sibling(next_own)
    weight_back = lax.dynamic_slice_in_dim(conv_weight, c * chans, chans, 3)
    weight_back = jnp.transpose(weight_back, (0, 1, 2, 4, 3)).reshape(9, 3 * full, chans)
    slab_member = near_member[2 : frames + 2]
    parts = peers * bands
    scaled, sums = call(
        backward_body,
        [sds((frames, cells, chans), F32), sds((parts, 2 * NCLIPS, chans), F32)],
        [SM, SM] + [VM] * 8,
        [
            pltpu.VMEM((frames + 2, rows + 2, cols, 6 * chans), BF16),
            pltpu.VMEM((frames, cells, chans), F32),
        ],
        flops=8 * 10**9, nbytes=6 * 2**20, name="backward",
    )(pos, target, table, slab_member.T, weight_back, clip_video, up, up_sib, next_own, next_sib)
    totals = lax.all_to_all(sums, ("tm", "height"), 0, 0)
    counts = clip_lengths.astype(F32) * (rows * bands * cols * group_size)
    video_grad, small = call(
        finish_body,
        [sds(clip_video.shape, BF16), sds((8, chans), F32)],
        [SM] + [VM] * 7,
        nbytes=3 * 2**20, name="finish",
    )(pos, table, group, slab_member / counts[None, :], totals, clip_video, scaled, up)
    return (block_out, video_grad, weight_grad, small[0], small[1])


def solution(mesh):
    placed = (
        P(("groups", "tm"), "height", None, "chan"),
        P("chan"),
        P("chan"),
        P(),
        P("groups"),
        P(("groups", "tm")),
        P(("groups", "tm"), "height", None, "chan"),
    )
    return jax.shard_map(
        per_device,
        mesh=mesh,
        in_specs=placed,
        out_specs=(
            P(("groups", "tm"), "height", None, "chan"),
            P(("groups", "tm"), "height", None, "chan"),
            P("groups", None, None, ("tm", "height"), "chan"),
            P(("groups", "chan")),
            P(("groups", "chan")),
        ),
        check_vma=False,
    )
```

profile of v0, /device:TPU:15, one launch (start us, length us, event | category | flops | bytes accessed | tf_op | source)
XLA Modules:
  0.0 138.4 jit_solution(18039165393935917262)
XLA Ops:
  1.4 2.6 %stat.1 = f32[16,24,128]{2,1,0:T(8,128)} custom-call(bf16[8,16,16,128]{3,2,1,0:T(8,128)(2,1)} %refs_5_.1, f32[1,128]{1,0:T(1,128)} %bitcast.36, f32[1,128]{1,0:T(1,128)} %bitcast.37, f32[128,128]{1,0:T(8,128)} %compare_select_fusion.average), custom_call_target="tpu_custom_call" | custom-call | bytes 1048576 | tf_op jit(solution)/shard_map/stat/pallas_call | solution.py:408
  3.9 6.6 %all-to-all-start = ((f32[16,24,128]{2,1,0:T(8,128)}), f32[16,24,128]{2,1,0:T(8,128)}, u32[]{:S(2)}, u32[]{:S(2)}) async-start(f32[16,24,128]{2,1,0:T(8,128)} %stat.1), calls=%async_computation | async-start | bytes 393216 | tf_op jit(solution)/shard_map/all_to_all | solution.py:412
  10.5 1.6 %slice.43 = bf16[2,16,16,128]{3,2,1,0:T(8,128)(2,1)} slice(bf16[8,16,16,128]{3,2,1,0:T(8,128)(2,1)} %refs_5_.1), slice={[6:8], [0:16], [0:16], [0:128]} | slice | bytes 262144 | tf_op jit(solution)/shard_map/slice | solution.py:388
  12.1 3.1 %collective-permute-start.4 = (bf16[2,16,16,128]{3,2,1,0:T(8,128)(2,1)}, bf16[2,16,16,128]{3,2,1,0:T(8,128)(2,1)}, u32[]{:S(2)}, u32[]{:S(2)}) collective-permute-start(bf16[2,16,16,128]{3,2,1,0:T(8,128)(2,1)} %slice.43), channel_id=1, source_target_pairs={{0,6},{2,4},{4,10},{6,8},{8,14},{10,12},{1,7},{3,5},{5,11},{7,9},{... | collective-permute-start | bytes 393224 | tf_op jit(solution)/shard_map/ppermute | solution.py:399
  15.7 2.0 %pack.1 = (bf16[2,17,16,128]{3,2,1,0:T(8,128)(2,1)}, bf16[2,17,16,128]{3,2,1,0:T(8,128)(2,1)}, bf16[2,17,16,128]{3,2,1,0:T(8,128)(2,1)}, bf16[2,17,16,128]{3,2,1,0:T(8,128)(2,1)}) custom-call(s32[3]{0:T(128)} %pad_add_fusion.refs_0_.pos, s32[8]{0:T(128)} %frames.1, bf16[8,16,16,128]{3,2,1,0:T(8,128)(2,1)} %grad.1), custom_call_target="tpu_custom_call" | custom-call | bytes 1048576 | tf_op jit(solution)/shard_map/pack/pallas_call | solution.py:382
  19.0 1.8 %collective-permute-start.8 = (bf16[2,17,16,128]{3,2,1,0:T(8,128)(2,1)}, bf16[2,17,16,128]{3,2,1,0:T(8,128)(2,1)}, u32[]{:S(2)}, u32[]{:S(2)}) collective-permute-start(bf16[2,17,16,128]{3,2,1,0:T(8,128)(2,1)} %get-tuple-element.21), channel_id=1, source_target_pairs={{0,8},{4,12},{8,0},{12,4},{1,9},{5,13},{9,1},{13,5},{2,10},{6,14},... | collective-permute-start | bytes 417800 | tf_op jit(solution)/shard_map/ppermute | solution.py:386
  34.7 1.4 %dynamic-slice_bitcast_fusion = bf16[3,3,3,256,128]{3,4,2,1,0:T(8,128)(2,1)} fusion(bf16[3,3,3,256,256]{4,3,2,1,0:T(8,128)(2,1)S(1)} %copy-done, s32[]{:T(128)S(6)} %select_n.44), kind=kLoop, calls=%fused_computation | loop fusion | bytes 3538948 | tf_op jit(solution)/shard_map/transpose | solution.py:499
  36.1 3.1 %collective-permute-start.1 = (bf16[2,16,16,128]{3,2,1,0:T(8,128)(2,1)}, bf16[2,16,16,128]{3,2,1,0:T(8,128)(2,1)}, u32[]{:S(2)}, u32[]{:S(2)}) collective-permute-start(bf16[2,16,16,128]{3,2,1,0:T(8,128)(2,1)} %slice.43), channel_id=1, source_target_pairs={{0,4},{2,6},{4,8},{6,10},{8,12},{10,14},{1,5},{3,7},{5,9},{7,11},{... | collective-permute-start | bytes 393224 | tf_op jit(solution)/shard_map/ppermute | solution.py:399
  40.5 2.0 %collective-permute-done.13.refs_7_.refs_11_.refs_20_ = bf16[2,17,16,128]{3,2,1,0:T(8,128)(2,1)S(1)} collective-permute-done((bf16[2,17,16,128]{3,2,1,0:T(8,128)(2,1)}, bf16[2,17,16,128]{3,2,1,0:T(8,128)(2,1)S(1)}, u32[]{:S(2)}, u32[]{:S(2)}) %collective-permute-start.13) | collective-permute-done | bytes 139296 | tf_op jit(solution)/shard_map/ppermute | solution.py:403
  43.2 3.4 %order.1 = (bf16[8,18,16,128]{3,2,1,0:T(8,128)(2,1)}, bf16[2,18,16,128]{3,2,1,0:T(8,128)(2,1)}) custom-call(s32[3]{0:T(128)} %pad_add_fusion.refs_0_.pos, bf16[2,17,16,128]{3,2,1,0:T(8,128)(2,1)} %get-tuple-element.19.refs_0_.refs_13_, bf16[2,17,16,128]{3,2,1,0:T(8,128)(2,1)} %collective-permute-done.7.refs_1_.refs_14_, ...), custom_call_target="tpu_custom_call" | custom-call | bytes 2097152 | tf_op jit(solution)/shard_map/order/pallas_call | solution.py:489
  46.6 4.4 %collective-permute-start.14 = (bf16[8,18,16,128]{3,2,1,0:T(8,128)(2,1)}, bf16[8,18,16,128]{3,2,1,0:T(8,128)(2,1)}, u32[]{:S(2)}, u32[]{:S(2)}) collective-permute-start(bf16[8,18,16,128]{3,2,1,0:T(8,128)(2,1)} %get-tuple-element.23.own.up), channel_id=1, source_target_pairs={{0,1},{1,0},{2,3},{3,2},{4,5},{5,4},{6,7},{7,6},{8,9},{9,8},{10,11... | collective-permute-start | bytes 1769480 | tf_op jit(solution)/shard_map/ppermute | solution.py:44
  51.0 1.6 %constant_dynamic-slice_fusion = bf16[3,3,3,256,128]{4,3,2,1,0:T(8,128)(2,1)} fusion(bf16[3,3,3,256,256]{4,3,2,1,0:T(8,128)(2,1)S(1)} %copy-done, s32[]{:T(128)S(6)} %select_n.44), kind=kLoop, calls=%fused_computation.59 | loop fusion | bytes 3538948 | tf_op jit(solution)/shard_map/dynamic_slice | solution.py:475
  54.4 3.8 %copy.16 = bf16[3,3,3,256,128]{4,3,2,1,0:T(8,128)(2,1)} copy(bf16[3,3,3,256,128]{3,4,2,1,0:T(8,128)(2,1)} %dynamic-slice_bitcast_fusion) | data formatting | bytes 3538944 | tf_op jit(solution)/shard_map/transpose | solution.py:499
  58.3 3.9 %collective-permute-start.15 = (bf16[2,18,16,128]{3,2,1,0:T(8,128)(2,1)}, bf16[2,18,16,128]{3,2,1,0:T(8,128)(2,1)}, u32[]{:S(2)}, u32[]{:S(2)}) collective-permute-start(bf16[2,18,16,128]{3,2,1,0:T(8,128)(2,1)} %get-tuple-element.24), channel_id=1, source_target_pairs={{4,0},{8,4},{12,8},{5,1},{9,5},{13,9},{6,2},{10,6},{14,10},{7,3},{... | collective-permute-start | bytes 442376 | tf_op jit(solution)/shard_map/ppermute | solution.py:496
  64.4 1.6 %collective-permute-done.15.next_own = bf16[2,18,16,128]{3,2,1,0:T(8,128)(2,1)} collective-permute-done((bf16[2,18,16,128]{3,2,1,0:T(8,128)(2,1)}, bf16[2,18,16,128]{3,2,1,0:T(8,128)(2,1)}, u32[]{:S(2)}, u32[]{:S(2)}) %collective-permute-start.15) | collective-permute-done | bytes 147488 | tf_op jit(solution)/shard_map/ppermute | solution.py:496
  67.0 1.9 %table.1.refs_2_ = f32[2,40,128]{2,1,0:T(8,128)} custom-call(f32[4,2,2,24,128]{4,3,2,1,0:T(8,128)} %bitcast.5.got, f32[32,32]{1,0:T(8,128)} %fusion.same, f32[16,32]{1,0:T(8,128)} %fusion.1.picked), custom_call_target="tpu_custom_call" | custom-call | bytes 262144 | tf_op jit(solution)/shard_map/table/pallas_call | solution.py:439
  69.0 16.2 %backward.1 = (f32[8,256,128]{2,1,0:T(8,128)}, f32[8,16,128]{2,1,0:T(8,128)}) custom-call(s32[3]{0:T(128)} %pad_add_fusion.refs_0_.pos, s32[30]{0:T(128)} %sub.51.target, f32[2,40,128]{2,1,0:T(8,128)} %table.1.refs_2_, f32[8,8]{1,0:T(8,128)} %copy.17.member, bf16[9,768,128]{2,1,0:T(8,128)(2,1)} %bitcast.33, bf16[8,16,16,128]{3,2,1,0:T(8,128)(2,1)} %refs_5_.1, ...), custom_call_target="tpu_custom_call" | custom-call | flops 8000000000 | bytes 6291456 | tf_op jit(solution)/shard_map/backward/pallas_call | solution.py:502
  85.2 7.0 %all-to-all-start.1 = ((f32[8,16,128]{2,1,0:T(8,128)}), f32[8,16,128]{2,1,0:T(8,128)}, u32[]{:S(2)}, u32[]{:S(2)}) async-start(f32[8,16,128]{2,1,0:T(8,128)} %get-tuple-element.25), calls=%async_computation.1 | async-start | bytes 131072 | tf_op jit(solution)/shard_map/all_to_all | solution.py:512
  94.3 1.8 %all-to-all-done.1.got = f32[8,16,128]{2,1,0:T(8,128)} async-done(((f32[8,16,128]{2,1,0:T(8,128)}), f32[8,16,128]{2,1,0:T(8,128)}, u32[]{:S(2)}, u32[]{:S(2)}) %all-to-all-start.1) | async-done | bytes 65568 | tf_op jit(solution)/shard_map/all_to_all | solution.py:512
  96.1 3.3 %finish.1 = (bf16[8,16,16,128]{3,2,1,0:T(8,128)(2,1)}, f32[8,128]{1,0:T(8,128)}) custom-call(s32[3]{0:T(128)} %pad_add_fusion.refs_0_.pos, f32[2,40,128]{2,1,0:T(8,128)} %table.1.refs_2_, f32[128,128]{1,0:T(8,128)} %compare_convert_fusion.group, f32[8,8]{1,0:T(8,128)} %convert_divide_fusion.3.spread, f32[8,16,128]{2,1,0:T(8,128)} %all-to-all-done.1.got, ...), custom_call_target="tpu_custom_call" | custom-call | bytes 3145728 | tf_op jit(solution)/shard_map/finish/pallas_call | solution.py:514
  100.7 14.2 %weight.1 = (f32[27,32,128]{2,1,0:T(8,128)}, bf16[27,32,128]{2,1,0:T(8,128)(2,1)}, bf16[27,32,128]{2,1,0:T(8,128)(2,1)}, bf16[27,32,128]{2,1,0:T(8,128)(2,1)}) custom-call(s32[3]{0:T(128)} %pad_add_fusion.refs_0_.pos, s32[24]{0:T(128)} %reshape.159.refs_1_, f32[2,40,128]{2,1,0:T(8,128)} %table.1.refs_2_, bf16[128,128]{1,0:T(8,128)(2,1)} %get-tuple-element.46.refs_3_, ...), custom_call_target="tpu_custom_call" | custom-call | flops 8000000000 | bytes 6291456 | tf_op jit(solution)/shard_map/weight/pallas_call | solution.py:453
  115.1 2.8 %collective-permute-start.18 = (bf16[27,32,128]{2,1,0:T(8,128)(2,1)}, bf16[27,32,128]{2,1,0:T(8,128)(2,1)S(1)}, u32[]{:S(2)}, u32[]{:S(2)}) collective-permute-start(bf16[27,32,128]{2,1,0:T(8,128)(2,1)} %get-tuple-element.30), channel_id=1, source_target_pairs={{0,8},{4,12},{8,0},{12,4},{1,9},{5,13},{9,1},{13,5},{2,10},{6,14},... | collective-permute-start | bytes 663560 | tf_op jit(solution)/shard_map/ppermute | solution.py:468
  119.3 13.4 %forward.1 = bf16[8,16,16,128]{3,2,1,0:T(8,128)(2,1)} custom-call(s32[3]{0:T(128)} %pad_add_fusion.refs_0_.pos, s32[24]{0:T(128)} %reshape.159.refs_1_, f32[2,40,128]{2,1,0:T(8,128)} %table.1.refs_2_, bf16[9,768,128]{2,1,0:T(8,128)(2,1)} %bitcast.34, bf16[8,16,16,128]{3,2,1,0:T(8,128)(2,1)} %refs_5_.1, ...), custom_call_target="tpu_custom_call" | custom-call | flops 8000000000 | bytes 6291456 | tf_op jit(solution)/shard_map/forward/pallas_call | solution.py:477
  133.0 4.4 %collective-permute-done.19 = bf16[27,32,128]{2,1,0:T(8,128)(2,1)S(1)} collective-permute-done((bf16[27,32,128]{2,1,0:T(8,128)(2,1)}, bf16[27,32,128]{2,1,0:T(8,128)(2,1)S(1)}, u32[]{:S(2)}, u32[]{:S(2)}) %collective-permute-start.19) | collective-permute-done | bytes 221216 | tf_op jit(solution)/shard_map/ppermute | solution.py:468
  (83 shorter events, 29.7 us)
Async XLA Ops:
  0.6 34.0 %copy-start = (bf16[3,3,3,256,256]{4,3,2,1,0:T(8,128)(2,1)S(1)}, bf16[3,3,3,256,256]{4,3,2,1,0:T(8,128)(2,1)}, u32[]{:S(2)}) copy-start(bf16[3,3,3,256,256]{4,3,2,1,0:T(8,128)(2,1)} %param.10) | copy-start | bytes 10616836
  0.6 21.3 %copy-start.7 = (s32[8]{0:T(128)S(1)}, s32[8]{0:T(128)}, u32[]{:S(2)}) copy-start(s32[8]{0:T(128)} %param.11) | copy-start | bytes 100
  3.9 63.1 %all-to-all-start = ((f32[16,24,128]{2,1,0:T(8,128)}), f32[16,24,128]{2,1,0:T(8,128)}, u32[]{:S(2)}, u32[]{:S(2)}) async-start(f32[16,24,128]{2,1,0:T(8,128)} %stat.1), calls=%async_computation | async-start | bytes 393216 | tf_op jit(solution)/shard_map/all_to_all | solution.py:412
  12.1 46.2 %collective-permute-start.4 = (bf16[2,16,16,128]{3,2,1,0:T(8,128)(2,1)}, bf16[2,16,16,128]{3,2,1,0:T(8,128)(2,1)}, u32[]{:S(2)}, u32[]{:S(2)}) collective-permute-start(bf16[2,16,16,128]{3,2,1,0:T(8,128)(2,1)} %slice.43), channel_id=1, source_target_pairs={{0,6},{2,4},{4,10},{6,8},{8,14},{10,12},{1,7},{3,5},{5,11},{7,9},{... | collective-permute-start | bytes 393224 | tf_op jit(solution)/shard_map/ppermute | solution.py:399
  17.8 14.9 %collective-permute-start.7 = (bf16[2,17,16,128]{3,2,1,0:T(8,128)(2,1)}, bf16[2,17,16,128]{3,2,1,0:T(8,128)(2,1)}, u32[]{:S(2)}, u32[]{:S(2)}) collective-permute-start(bf16[2,17,16,128]{3,2,1,0:T(8,128)(2,1)} %get-tuple-element.20), channel_id=1, source_target_pairs={{0,4},{4,8},{8,12},{12,0},{1,5},{5,9},{9,13},{13,1},{2,6},{6,10},{... | collective-permute-start | bytes 417800 | tf_op jit(solution)/shard_map/ppermute | solution.py:386
  19.0 14.0 %collective-permute-start.8 = (bf16[2,17,16,128]{3,2,1,0:T(8,128)(2,1)}, bf16[2,17,16,128]{3,2,1,0:T(8,128)(2,1)}, u32[]{:S(2)}, u32[]{:S(2)}) collective-permute-start(bf16[2,17,16,128]{3,2,1,0:T(8,128)(2,1)} %get-tuple-element.21), channel_id=1, source_target_pairs={{0,8},{4,12},{8,0},{12,4},{1,9},{5,13},{9,1},{13,5},{2,10},{6,14},... | collective-permute-start | bytes 417800 | tf_op jit(solution)/shard_map/ppermute | solution.py:386
  20.8 13.3 %collective-permute-start.9 = (bf16[2,17,16,128]{3,2,1,0:T(8,128)(2,1)}, bf16[2,17,16,128]{3,2,1,0:T(8,128)(2,1)}, u32[]{:S(2)}, u32[]{:S(2)}) collective-permute-start(bf16[2,17,16,128]{3,2,1,0:T(8,128)(2,1)} %get-tuple-element.22), channel_id=1, source_target_pairs={{0,12},{4,0},{8,4},{12,8},{1,13},{5,1},{9,5},{13,9},{2,14},{6,2},{... | collective-permute-start | bytes 417800 | tf_op jit(solution)/shard_map/ppermute | solution.py:386
  20.8 15.3 %collective-permute-start.10 = (bf16[2,17,16,128]{3,2,1,0:T(8,128)(2,1)}, bf16[2,17,16,128]{3,2,1,0:T(8,128)(2,1)}, u32[]{:S(2)}, u32[]{:S(2)}) collective-permute-start(bf16[2,17,16,128]{3,2,1,0:T(8,128)(2,1)} %get-tuple-element.19.refs_0_.refs_13_), channel_id=1, source_target_pairs={{0,2},{2,0},{1,3},{3,1},{4,6},{6,4},{5,7},{7,5},{8,10},{10,8},{9,1... | collective-permute-start | bytes 417800 | tf_op jit(solution)/shard_map/ppermute | solution.py:403
  32.6 6.6 %collective-permute-start.11 = (bf16[2,17,16,128]{3,2,1,0:T(8,128)(2,1)}, bf16[2,17,16,128]{3,2,1,0:T(8,128)(2,1)S(1)}, u32[]{:S(2)}, u32[]{:S(2)}) collective-permute-start(bf16[2,17,16,128]{3,2,1,0:T(8,128)(2,1)} %collective-permute-done.7.refs_1_.refs_14_), channel_id=1, source_target_pairs={{0,2},{2,0},{1,3},{3,1},{4,6},{6,4},{5,7},{7,5},{8,10},{10,8},{9,1... | collective-permute-start | bytes 417800 | tf_op jit(solution)/shard_map/ppermute | solution.py:403
  32.9 7.6 %collective-permute-start.12 = (bf16[2,17,16,128]{3,2,1,0:T(8,128)(2,1)}, bf16[2,17,16,128]{3,2,1,0:T(8,128)(2,1)S(1)}, u32[]{:S(2)}, u32[]{:S(2)}) collective-permute-start(bf16[2,17,16,128]{3,2,1,0:T(8,128)(2,1)} %collective-permute-done.8.refs_2_.refs_15_), channel_id=1, source_target_pairs={{0,2},{2,0},{1,3},{3,1},{4,6},{6,4},{5,7},{7,5},{8,10},{10,8},{9,1... | collective-permute-start | bytes 417800 | tf_op jit(solution)/shard_map/ppermute | solution.py:403
  34.1 8.4 %collective-permute-start.13 = (bf16[2,17,16,128]{3,2,1,0:T(8,128)(2,1)}, bf16[2,17,16,128]{3,2,1,0:T(8,128)(2,1)S(1)}, u32[]{:S(2)}, u32[]{:S(2)}) collective-permute-start(bf16[2,17,16,128]{3,2,1,0:T(8,128)(2,1)} %collective-permute-done.9.refs_3_.refs_16_), channel_id=1, source_target_pairs={{0,2},{2,0},{1,3},{3,1},{4,6},{6,4},{5,7},{7,5},{8,10},{10,8},{9,1... | collective-permute-start | bytes 417800 | tf_op jit(solution)/shard_map/ppermute | solution.py:403
  36.1 27.4 %collective-permute-start.1 = (bf16[2,16,16,128]{3,2,1,0:T(8,128)(2,1)}, bf16[2,16,16,128]{3,2,1,0:T(8,128)(2,1)}, u32[]{:S(2)}, u32[]{:S(2)}) collective-permute-start(bf16[2,16,16,128]{3,2,1,0:T(8,128)(2,1)} %slice.43), channel_id=1, source_target_pairs={{0,4},{2,6},{4,8},{6,10},{8,12},{10,14},{1,5},{3,7},{5,9},{7,11},{... | collective-permute-start | bytes 393224 | tf_op jit(solution)/shard_map/ppermute | solution.py:399
  39.2 29.7 %collective-permute-start.3 = (bf16[8,16,16,128]{3,2,1,0:T(8,128)(2,1)}, bf16[8,16,16,128]{3,2,1,0:T(8,128)(2,1)}, u32[]{:S(2)}, u32[]{:S(2)}) collective-permute-start(bf16[8,16,16,128]{3,2,1,0:T(8,128)(2,1)} %refs_5_.1), channel_id=1, source_target_pairs={{0,2},{2,0},{1,3},{3,1},{4,6},{6,4},{5,7},{7,5},{8,10},{10,8},{9,1... | collective-permute-start | bytes 1572872 | tf_op jit(solution)/shard_map/ppermute | solution.py:393
  46.6 22.4 %collective-permute-start.14 = (bf16[8,18,16,128]{3,2,1,0:T(8,128)(2,1)}, bf16[8,18,16,128]{3,2,1,0:T(8,128)(2,1)}, u32[]{:S(2)}, u32[]{:S(2)}) collective-permute-start(bf16[8,18,16,128]{3,2,1,0:T(8,128)(2,1)} %get-tuple-element.23.own.up), channel_id=1, source_target_pairs={{0,1},{1,0},{2,3},{3,2},{4,5},{5,4},{6,7},{7,6},{8,9},{9,8},{10,11... | collective-permute-start | bytes 1769480 | tf_op jit(solution)/shard_map/ppermute | solution.py:44
  58.3 6.1 %collective-permute-start.6 = (bf16[2,16,16,128]{3,2,1,0:T(8,128)(2,1)}, bf16[2,16,16,128]{3,2,1,0:T(8,128)(2,1)S(1)}, u32[]{:S(2)}, u32[]{:S(2)}) collective-permute-start(bf16[2,16,16,128]{3,2,1,0:T(8,128)(2,1)} %collective-permute-done.4.refs_10_), channel_id=1, source_target_pairs={{0,1},{1,0},{2,3},{3,2},{4,5},{5,4},{6,7},{7,6},{8,9},{9,8},{10,11... | collective-permute-start | bytes 393224 | tf_op jit(solution)/shard_map/ppermute | solution.py:44
  58.3 7.7 %collective-permute-start.15 = (bf16[2,18,16,128]{3,2,1,0:T(8,128)(2,1)}, bf16[2,18,16,128]{3,2,1,0:T(8,128)(2,1)}, u32[]{:S(2)}, u32[]{:S(2)}) collective-permute-start(bf16[2,18,16,128]{3,2,1,0:T(8,128)(2,1)} %get-tuple-element.24), channel_id=1, source_target_pairs={{4,0},{8,4},{12,8},{5,1},{9,5},{13,9},{6,2},{10,6},{14,10},{7,3},{... | collective-permute-start | bytes 442376 | tf_op jit(solution)/shard_map/ppermute | solution.py:496
  63.5 37.2 %collective-permute-start = (bf16[8,16,16,128]{3,2,1,0:T(8,128)(2,1)}, bf16[8,16,16,128]{3,2,1,0:T(8,128)(2,1)}, u32[]{:S(2)}, u32[]{:S(2)}) collective-permute-start(bf16[8,16,16,128]{3,2,1,0:T(8,128)(2,1)} %refs_5_.1), channel_id=1, source_target_pairs={{0,1},{1,0},{2,3},{3,2},{4,5},{5,4},{6,7},{7,6},{8,9},{9,8},{10,11... | collective-permute-start | bytes 1572872 | tf_op jit(solution)/shard_map/ppermute | solution.py:44
  64.3 36.4 %collective-permute-start.2 = (bf16[2,16,16,128]{3,2,1,0:T(8,128)(2,1)}, bf16[2,16,16,128]{3,2,1,0:T(8,128)(2,1)}, u32[]{:S(2)}, u32[]{:S(2)}) collective-permute-start(bf16[2,16,16,128]{3,2,1,0:T(8,128)(2,1)} %collective-permute-done.1.refs_6_.refs_9_), channel_id=1, source_target_pairs={{0,1},{1,0},{2,3},{3,2},{4,5},{5,4},{6,7},{7,6},{8,9},{9,8},{10,11... | collective-permute-start | bytes 393224 | tf_op jit(solution)/shard_map/ppermute | solution.py:44
  66.0 3.0 %collective-permute-start.16 = (bf16[2,18,16,128]{3,2,1,0:T(8,128)(2,1)}, bf16[2,18,16,128]{3,2,1,0:T(8,128)(2,1)}, u32[]{:S(2)}, u32[]{:S(2)}) collective-permute-start(bf16[2,18,16,128]{3,2,1,0:T(8,128)(2,1)} %collective-permute-done.15.next_own), channel_id=1, source_target_pairs={{0,1},{1,0},{2,3},{3,2},{4,5},{5,4},{6,7},{7,6},{8,9},{9,8},{10,11... | collective-permute-start | bytes 442376 | tf_op jit(solution)/shard_map/ppermute | solution.py:44
  69.0 31.7 %collective-permute-start.5 = (bf16[8,16,16,128]{3,2,1,0:T(8,128)(2,1)}, bf16[8,16,16,128]{3,2,1,0:T(8,128)(2,1)}, u32[]{:S(2)}, u32[]{:S(2)}) collective-permute-start(bf16[8,16,16,128]{3,2,1,0:T(8,128)(2,1)} %collective-permute-done.3.refs_6_), channel_id=1, source_target_pairs={{0,1},{1,0},{2,3},{3,2},{4,5},{5,4},{6,7},{7,6},{8,9},{9,8},{10,11... | collective-permute-start | bytes 1572872 | tf_op jit(solution)/shard_map/ppermute | solution.py:44
  85.2 10.9 %all-to-all-start.1 = ((f32[8,16,128]{2,1,0:T(8,128)}), f32[8,16,128]{2,1,0:T(8,128)}, u32[]{:S(2)}, u32[]{:S(2)}) async-start(f32[8,16,128]{2,1,0:T(8,128)} %get-tuple-element.25), calls=%async_computation.1 | async-start | bytes 131072 | tf_op jit(solution)/shard_map/all_to_all | solution.py:512
  114.9 17.9 %collective-permute-start.17 = (bf16[27,32,128]{2,1,0:T(8,128)(2,1)}, bf16[27,32,128]{2,1,0:T(8,128)(2,1)S(1)}, u32[]{:S(2)}, u32[]{:S(2)}) collective-permute-start(bf16[27,32,128]{2,1,0:T(8,128)(2,1)} %get-tuple-element.29), channel_id=1, source_target_pairs={{0,4},{4,8},{8,12},{12,0},{1,5},{5,9},{9,13},{13,1},{2,6},{6,10},{... | collective-permute-start | bytes 663560 | tf_op jit(solution)/shard_map/ppermute | solution.py:468
  115.1 17.9 %collective-permute-start.18 = (bf16[27,32,128]{2,1,0:T(8,128)(2,1)}, bf16[27,32,128]{2,1,0:T(8,128)(2,1)S(1)}, u32[]{:S(2)}, u32[]{:S(2)}) collective-permute-start(bf16[27,32,128]{2,1,0:T(8,128)(2,1)} %get-tuple-element.30), channel_id=1, source_target_pairs={{0,8},{4,12},{8,0},{12,4},{1,9},{5,13},{9,1},{13,5},{2,10},{6,14},... | collective-permute-start | bytes 663560 | tf_op jit(solution)/shard_map/ppermute | solution.py:468
  117.9 19.6 %collective-permute-start.19 = (bf16[27,32,128]{2,1,0:T(8,128)(2,1)}, bf16[27,32,128]{2,1,0:T(8,128)(2,1)S(1)}, u32[]{:S(2)}, u32[]{:S(2)}) collective-permute-start(bf16[27,32,128]{2,1,0:T(8,128)(2,1)} %get-tuple-element.31), channel_id=1, source_target_pairs={{0,12},{4,0},{8,4},{12,8},{1,13},{5,1},{9,5},{13,9},{2,14},{6,2},{... | collective-permute-start | bytes 663560 | tf_op jit(solution)/shard_map/ppermute | solution.py:468
  (7 other events, 35.2 us)
where the time goes:
time: 140 us; the launch traced here: 138 us
  Pallas kernels  57.1 us (41%)
  starting transfers between devices  40.4 us (29%)
  local copies, waits for them, and re-layouts  15.1 us (11%)
  other arithmetic  12 us (9%)
  waiting for transfers between devices  10.2 us (7%)
  matrix products  2.77 us (2%)
    pallas_call x1, Pallas kernels, per_device(): call(backward_body, [sds((frames, cells, chans), F32), sds((parts, 2 * NC...  16.2 us
    pallas_call x1, Pallas kernels, per_device(): call(functools.partial(weight_body, peers, bands, cap, block), [sds((27,...  14.2 us
    pallas_call x1, Pallas kernels, per_device(): call(functools.partial(forward_body, bands), sds(clip_video.shape, BF16),...  13.4 us
    all_to_all x1, starting transfers between devices, per_device(): totals = lax.all_to_all(sums, ('tm', 'height'), 0, 0)  6.96 us
    all_to_all x1, starting transfers between devices, per_device(): got = lax.all_to_all(stats, everyone, 0, 0)  6.55 us
    ppermute x6, starting transfers between devices, sibling(): return lax.ppermute(value, 'chan', ring(2, 1))  6.31 us
    ppermute x2, starting transfers between devices, per_device(): prev_own.append(lax.ppermute(last, ('tm', 'height'), pairs))  6.19 us
    transpose x2, local copies, waits for them, and re-layouts, per_device(): jnp.transpose(weight_back, (0, 1, 2, 4, 3)).reshape(9, 3 * full, chans)  5.27 us
  transfers between devices with their start and end apart: 22, of which 5 were waited for; matrix products, arithmetic and copies ran while one was open for 20% of the time, Pallas kernels for 29%

commit v1 on v0

v1 whole, which is shorter than its diff:
```python
import functools
import jax
import jax.numpy as jnp
from jax import lax
from jax.experimental import pallas as pl
from jax.experimental.pallas import tpu as pltpu
from jax.sharding import PartitionSpec as P

GROUPS = 32
NCLIPS = 8
F32 = jnp.float32
BF16 = jnp.bfloat16
HIGHEST = lax.Precision.HIGHEST
VM = pl.BlockSpec(memory_space=pltpu.VMEM)
SM = pl.BlockSpec(memory_space=pltpu.SMEM)


ANY = pl.BlockSpec(memory_space=pl.ANY)


def call(body, out_shape, in_specs, scratch=(), flops=0, nbytes=0, name=None):
    return pl.pallas_call(
        body,
        out_shape=out_shape,
        in_specs=in_specs,
        out_specs=jax.tree.map(lambda _: VM, out_shape),
        scratch_shapes=list(scratch),
        compiler_params=pltpu.CompilerParams(vmem_limit_bytes=56 * 2**20),
        cost_estimate=pl.CostEstimate(flops=flops, bytes_accessed=nbytes, transcendentals=0),
        name=name,
    )


def fdot(a, b):
    return jnp.dot(a, b, precision=HIGHEST, preferred_element_type=F32)


def bdot(a, b):
    return jnp.dot(a, b, preferred_element_type=F32)


def ring(peers, by):
    return [(i, (i + by) % peers) for i in range(peers)]


def sibling(value):
    return lax.ppermute(value, "chan", ring(2, 1))


def sigmoid(v):
    return 1.0 / (1.0 + jnp.exp(-v))


def start_of(lengths, frame):
    begin = jnp.int32(0)
    end = jnp.int32(0)
    for k in range(NCLIPS):
        end = end + lengths[k]
        begin = jnp.where(end <= frame, end, begin)
    return begin


def clip_of(lengths, frame):
    number = jnp.zeros(frame.shape, jnp.int32)
    end = jnp.int32(0)
    for k in range(NCLIPS):
        end = end + lengths[k]
        number = number + jnp.where(end <= frame, 1, 0)
    return number


def per_clip(lengths, clip, scale):
    inverse = jnp.zeros(clip.shape, F32)
    for k in range(NCLIPS):
        length = jnp.full(clip.shape, lengths[k].astype(F32) * scale, F32)
        inverse = jnp.where(clip == k, 1.0 / length, inverse)
    return inverse


def iota(shape, dim):
    return lax.broadcasted_iota(jnp.int32, shape, dim)


def group_matrix(chans, size):
    return (iota((chans, chans), 0) // size == iota((chans, chans), 1) // size).astype(F32)


def pack_body(peers, cap, frames, grad, video, last, *outs):
    outs, sem = outs[:-1], outs[-1]
    slots = frames.shape[0]
    copy = pltpu.make_async_copy(video.at[pl.ds(slots - 2, 2)], last, sem)
    copy.start()
    tm = lax.axis_index("tm")
    number = [frames[i] for i in range(slots)]
    step = [lax.rem(lax.div(n, slots) - tm + peers, peers) for n in number]
    rank = []
    for i in range(slots):
        r = jnp.int32(0)
        for j in range(i):
            r = r + jnp.where(step[j] == step[i], 1, 0)
        rank.append(r)
    rows = grad.shape[1]
    for k in range(peers):
        for j in range(cap):
            index = jnp.int32(0)
            local = jnp.int32(-1)
            for i in range(slots):
                hit = jnp.logical_and(step[i] == k, rank[i] == j)
                index = jnp.where(hit, i, index)
                local = jnp.where(hit, lax.rem(number[i], slots), local)
            outs[k][j, :rows] = grad[index]
            outs[k][j, rows:] = jnp.full((1,) + grad.shape[2:], local.astype(F32), F32).astype(BF16)
    copy.wait()


def stat_body(size, video, gain, bias, out):
    frames, rows, cols, chans = video.shape
    cells = rows * cols
    average = group_matrix(chans, size) * (1.0 / size)
    sums = [
        jnp.sum(video[t].astype(F32).reshape(cells, chans), axis=0, keepdims=True)
        for t in range(frames)
    ]
    mean = fdot(jnp.concatenate(sums, axis=0) * (1.0 / cells), average)
    squares = []
    for t in range(frames):
        apart = video[t].astype(F32).reshape(cells, chans) - mean[t : t + 1]
        squares.append(jnp.sum(apart * apart, axis=0, keepdims=True))
    var = fdot(jnp.concatenate(squares, axis=0) * (1.0 / cells), average)
    rest = jnp.concatenate(
        [gain[...], bias[...], jnp.zeros((6, chans), F32)], axis=0
    )
    whole = jnp.concatenate([mean, var, rest], axis=0)
    for i in range(out.shape[0]):
        out[i] = whole


def turn_body(weight, out):
    for i in range(9):
        for col in range(3):
            out[i, col * 256 : (col + 1) * 256] = weight[i, col * 256 : (col + 1) * 256].T


def table_body(lengths, got, out):
    peers, bands = got.shape[:2]
    frames = (got.shape[3] - 8) // 2
    first = lax.axis_index("tm") * frames
    count = peers * frames
    clip = clip_of(lengths, iota((count, count), 1))
    inverse = per_clip(lengths, clip, 1.0)
    same = jnp.where(clip_of(lengths, iota((count, count), 0)) == clip, inverse, 0.0)
    near = jnp.clip(first - 2 + iota((16, count), 0), 0, count - 1)
    clip = clip_of(lengths, iota((16, count), 1))
    inverse = per_clip(lengths, clip, 1.0)
    picked = jnp.where(clip_of(lengths, near) == clip, inverse, 0.0)
    for c in range(2):
        mean = [
            jnp.concatenate([got[t, h, c, :frames] for t in range(peers)], axis=0)
            for h in range(bands)
        ]
        var = [
            jnp.concatenate([got[t, h, c, frames : 2 * frames] for t in range(peers)], axis=0)
            for h in range(bands)
        ]
        average = sum(mean[1:], mean[0]) * (1.0 / bands)
        clip_mean = fdot(same, average)
        spread = jnp.zeros_like(average)
        for h in range(bands):
            apart = mean[h] - clip_mean
            spread = spread + (var[h] + apart * apart)
        out[c, :16] = fdot(picked, average)
        out[c, 16:32] = lax.rsqrt(fdot(picked, spread * (1.0 / bands)) + 1e-06)
        out[c, 32:] = got[0, 0, c, 2 * frames :]


def shifts(value):
    length = value.shape[0]
    column = lax.rem(iota(value.shape, 0), 16)
    before = jnp.where(column == 0, 0.0, pltpu.roll(value, 1, 0))
    after = jnp.where(column == 15, 0.0, pltpu.roll(value, length - 1, 0))
    return before, after


def weight_body(peers, bands, cap, block, *refs):
    refs = list(refs)
    lengths, table = refs.pop(0), refs.pop(0)
    take = lambda n: [refs.pop(0) for _ in range(n)]
    own, sib, prev_own, prev_sib = take(bands), take(bands), take(bands), take(bands)
    ups = [take(peers) for _ in range(bands)]
    outs = take(peers)
    active, upright = refs
    frames, rows, cols, chans = own[0].shape
    cells = rows * cols
    width = peers * block
    tm, h, c = lax.axis_index("tm"), lax.axis_index("height"), lax.axis_index("chan")
    first = tm * frames
    band = [lax.rem(h - m + bands, bands) for m in range(bands)]
    place = iota((chans, width), 1)
    wanted = (lax.rem(tm + lax.div(place, block), peers) * bands + h) * block + lax.rem(place, block)
    channel = iota((chans, width), 0)
    pick_own = (c * chans + channel == wanted).astype(F32)
    pick_sib = ((1 - c) * chans + channel == wanted).astype(F32)
    lookup = fdot(table[c], pick_own) + fdot(table[1 - c], pick_sib)
    pick_own, pick_sib = pick_own.astype(BF16), pick_sib.astype(BF16)
    mean, inv = lookup[:16], lookup[16:32]
    scale = inv * lookup[32:33]
    bias = lookup[33:34]
    active[:, 0] = jnp.zeros((active.shape[0], cols, 3 * width), BF16)
    active[:, bands * rows + 1] = jnp.zeros((active.shape[0], cols, 3 * width), BF16)
    for f in range(frames + 2):
        for m in range(bands):
            if f < 2:
                a, b = prev_own[m][f], prev_sib[m][f]
            else:
                a, b = own[m][f - 2], sib[m][f - 2]
            x = bdot(a.reshape(cells, chans), pick_own) + bdot(b.reshape(cells, chans), pick_sib)
            v = (x - mean[f : f + 1]) * scale[f : f + 1] + bias
            v = v * sigmoid(v)
            before, after = shifts(v)
            at = pl.ds(band[m] * rows + 1, rows)
            active[f, at, :, :width] = before.astype(BF16).reshape(rows, cols, width)
            active[f, at, :, width : 2 * width] = v.astype(BF16).reshape(rows, cols, width)
            active[f, at, :, 2 * width :] = after.astype(BF16).reshape(rows, cols, width)
    for k in range(peers):
        for j in range(cap):
            local = jnp.max(ups[0][k][j, rows].astype(F32)).astype(jnp.int32)

            @pl.when(local >= 0)
            def _():
                for m in range(bands):
                    u = ups[m][k][j, :rows].reshape(cells, chans)
                    upright[local, m] = u.T

    begin = [start_of(lengths, first + t) for t in range(frames)]

    def tap(i, carry):
        a = lax.div(i, 3)
        b = lax.rem(i, 3)
        total = jnp.zeros((chans, 3 * width), F32)
        for t in range(frames):
            s = jnp.maximum(first + t - 2 + a, begin[t]) - (first - 2)
            for m in range(bands):
                patch = active[s, pl.ds(band[m] * rows + b, rows)].reshape(cells, 3 * width)
                total = total + bdot(upright[t, m], patch)
        for col in range(3):
            piece = total[:, col * width : (col + 1) * width].T
            for k in range(peers):
                outs[k][i * 3 + col] = piece[k * block : (k + 1) * block].astype(outs[k].dtype)
        return carry

    lax.fori_loop(0, 9, tap, 0)


def forward_body(bands, lengths, table, weight, own, sib, prev_own, prev_sib, *refs):
    above_own, above_sib, below_own, below_sib = refs[:4]
    far_prev = refs[4:8]
    keep, give, active = refs[8:]
    frames, rows, cols, chans = own.shape
    half = rows // 2
    tm, h, c = lax.axis_index("tm"), lax.axis_index("height"), lax.axis_index("chan")
    first = tm * frames
    outer = jnp.logical_or(
        jnp.logical_and(c == 0, h > 0), jnp.logical_and(c == 1, h < bands - 1)
    )
    begin = [start_of(lengths, first + t) for t in range(frames)]

    def put(f, at, lines, value_own, value_sib, ok):
        a, b = value_own.astype(F32), value_sib.astype(F32)
        for side, x in enumerate((jnp.where(c == 0, a, b), jnp.where(c == 0, b, a))):
            mean = table[side, f : f + 1]
            scale = table[side, 16 + f : 17 + f] * table[side, 32:33]
            v = (x - mean) * scale + table[side, 33:34]
            v = v * sigmoid(v)
            if ok is not None:
                v = jnp.where(ok, v, 0.0)
            before, after = shifts(v)
            for n, w in enumerate((before, v, after)):
                lane = n * 2 * chans + side * chans
                active[f, at, :, lane : lane + chans] = w.astype(BF16).reshape(lines, cols, chans)

    def edge(up, down, f):
        return jnp.where(c == 0, up[f, rows - 1].astype(F32), down[f, 0].astype(F32))

    for f in range(frames + 2):
        if f < 2:
            here = (prev_own, prev_sib, f)
            there = far_prev
        else:
            here = (own, sib, f - 2)
            there = (above_own, above_sib, below_own, below_sib)
        g = here[2]
        near = pl.ds((half - 1) * c, half + 1)
        put(
            f, pl.ds(1 - c, half + 1), half + 1,
            here[0][g, near].reshape((half + 1) * cols, chans),
            here[1][g, near].reshape((half + 1) * cols, chans),
            None,
        )
        put(
            f, pl.ds((half + 1) * c, 1), 1,
            edge(there[0], there[2], g), edge(there[1], there[3], g), outer,
        )
    batch = 4
    for t0 in range(0, frames, batch):
        mixed = [jnp.zeros((half * cols, 2 * chans), F32) for _ in range(batch)]
        for a in range(3):
            for b in range(3):
                w = weight[a * 3 + b]
                for q in range(batch):
                    t = t0 + q
                    s = jnp.maximum(first + t - 2 + a, begin[t]) - (first - 2)
                    patch = active[s, b : b + half].reshape(half * cols, 6 * chans)
                    mixed[q] = mixed[q] + bdot(patch, w)
        for q in range(batch):
            t = t0 + q
            mine = pl.ds(c * half, half)
            left, right = mixed[q][:, :chans], mixed[q][:, chans:]
            shape = (half, cols, chans)
            for out, value, x in (
                (keep, jnp.where(c == 0, left, right), own[t, mine]),
                (give, jnp.where(c == 0, right, left), sib[t, mine]),
            ):
                x = x.reshape(half * cols, chans).astype(F32)
                out[t] = (x + value).astype(BF16).reshape(shape)


def order_body(peers, bands, cap, *refs):
    own, above, below = refs[:peers], refs[peers : 2 * peers], refs[2 * peers : 3 * peers]
    out, first = refs[3 * peers :]
    rows = own[0].shape[1] - 1
    h = lax.axis_index("height")
    for k in range(peers):
        for j in range(cap):
            local = jnp.max(own[k][j, rows].astype(F32)).astype(jnp.int32)

            @pl.when(local >= 0)
            def _():
                out[local, 1 : rows + 1] = own[k][j, :rows]
                top = above[k][j, rows - 1].astype(F32)
                bottom = below[k][j, 0].astype(F32)
                out[local, 0] = jnp.where(h > 0, top, 0.0).astype(BF16)
                out[local, rows + 1] = jnp.where(h < bands - 1, bottom, 0.0).astype(BF16)

    first[...] = out[:2]


def backward_body(peers, lengths, table, weight, own, sib, up, up_sib, next_own, next_sib, *refs):
    keep, give, sums, spatial, total = refs
    frames, rows, cols, chans = own.shape
    half = rows // 2
    cells = half * cols
    tm, c = lax.axis_index("tm"), lax.axis_index("chan")
    first = tm * frames
    for f in range(frames + 2):
        a, b, g = (up, up_sib, f) if f < frames else (next_own, next_sib, f - frames)
        a = a[g, pl.ds(c * half, half + 2)].reshape(cells + 2 * cols, chans).astype(F32)
        b = b[g, pl.ds(c * half, half + 2)].reshape(cells + 2 * cols, chans).astype(F32)
        for side, v in enumerate((jnp.where(c == 0, a, b), jnp.where(c == 0, b, a))):
            before, after = shifts(v)
            for n, w in enumerate((after, v, before)):
                at = n * 2 * chans + side * chans
                spatial[f, :, :, at : at + chans] = w.astype(BF16).reshape(half + 2, cols, chans)
    total[...] = jnp.zeros_like(total)

    def frame(t, carry):
        begin = start_of(lengths, first + t)
        for a in range(3):
            s = jnp.maximum(first + t - 2 + a, begin) - first

            @pl.when(jnp.logical_and(s >= 0, s < frames))
            def _():
                grad = jnp.zeros((cells, 2 * chans), F32)
                for b in range(3):
                    patch = spatial[t, 2 - b : 2 - b + half].reshape(cells, 6 * chans)
                    grad = grad + bdot(patch, weight[a * 3 + b])
                total[s] += grad

        return carry

    lax.fori_loop(0, frames + 2, frame, 0)
    mine = pl.ds(c * half, half)
    member = (
        clip_of(lengths, first + iota((NCLIPS, frames), 1)) == iota((NCLIPS, frames), 0)
    ).astype(F32)
    for side in range(2):
        firsts, seconds = [], []
        for t in range(frames):
            a, b = own[t, mine].astype(F32), sib[t, mine].astype(F32)
            x = jnp.where((c == 0) == (side == 0), a, b).reshape(cells, chans)
            hat = (x - table[side, t + 2 : t + 3]) * table[side, t + 18 : t + 19]
            v = hat * table[side, 32:33] + table[side, 33:34]
            s = sigmoid(v)
            grad = total[t, :, side * chans : (side + 1) * chans] * s * (1.0 + v * (1.0 - s))
            total[t, :, side * chans : (side + 1) * chans] = grad
            firsts.append(jnp.sum(grad, axis=0, keepdims=True))
            seconds.append(jnp.sum(grad * hat, axis=0, keepdims=True))
        whole = jnp.concatenate(
            [
                fdot(member, jnp.concatenate(firsts, axis=0)),
                fdot(member, jnp.concatenate(seconds, axis=0)),
            ],
            axis=0,
        )
        for i in range(sums.shape[0] // 2):
            sums[2 * i + side] = whole
    for t in range(frames):
        left, right = total[t, :, :chans], total[t, :, chans:]
        keep[t] = jnp.where(c == 0, left, right)
        give[t] = jnp.where(c == 0, right, left)


def finish_body(size, bands, lengths, table, got, video, keep, other, up, out, small):
    frames, rows, cols, chans = video.shape
    half = rows // 2
    cells = half * cols
    tm, c = lax.axis_index("tm"), lax.axis_index("chan")
    first_frame = tm * frames
    whole = jnp.sum(got[...], axis=0)
    gain = table[c, 32:33]
    small[0:1] = jnp.sum(whole[NCLIPS:], axis=0, keepdims=True)
    small[1:2] = jnp.sum(whole[:NCLIPS], axis=0, keepdims=True)
    small[2:] = jnp.zeros((6, chans), F32)
    group = group_matrix(chans, size)
    clip = iota((frames, NCLIPS), 1)
    inverse = per_clip(lengths, clip, float(rows * bands * cols * size))
    spread = jnp.where(clip_of(lengths, first_frame + iota((frames, NCLIPS), 0)) == clip, inverse, 0.0)
    first = fdot(spread, fdot(whole[:NCLIPS] * gain, group))
    second = fdot(spread, fdot(whole[NCLIPS:] * gain, group))
    for t in range(frames):
        inv = table[c, t + 18 : t + 19]
        for grads, at in ((keep, c * half), (other, (1 - c) * half)):
            x = video[t, pl.ds(at, half)].reshape(cells, chans).astype(F32)
            hat = (x - table[c, t + 2 : t + 3]) * inv
            part = inv * (grads[t] * gain - first[t : t + 1] - hat * second[t : t + 1])
            u = up[t, pl.ds(at + 1, half)].reshape(cells, chans).astype(F32)
            out[t, pl.ds(at, half)] = (u + part).astype(BF16).reshape(half, cols, chans)


def per_device(
    clip_video, norm_gain, norm_bias, conv_weight, clip_lengths, packed_frame, packed_grad
):
    frames, rows, cols, chans = clip_video.shape
    full = conv_weight.shape[3]
    peers = lax.axis_size("tm")
    bands = lax.axis_size("height")
    c = lax.axis_index("chan")
    size = full // GROUPS
    cap = max(1, frames // peers)
    block = full // (peers * bands)
    width = peers * block
    half = rows // 2
    everyone = ("tm", "height", "chan")
    devices = peers * bands * 2
    sds = jax.ShapeDtypeStruct

    piece = sds((cap, rows + 1, cols, chans), BF16)
    last, *pieces = call(
        functools.partial(pack_body, peers, cap),
        [sds((2, rows, cols, chans), BF16)] + [piece] * peers,
        [SM, VM, ANY],
        [pltpu.SemaphoreType.DMA],
        nbytes=2**20, name="pack",
    )(packed_frame, packed_grad, clip_video)
    ups = [[pieces[0]] + [lax.ppermute(pieces[k], "tm", ring(peers, k)) for k in range(1, peers)]]

    own = [clip_video]
    prev_own = []
    for m in range(bands):
        if m > 0:
            own.append(lax.ppermute(clip_video, "height", ring(bands, m)))
        pairs = [
            (t * bands + b, (t + 1) * bands + (b + m) % bands)
            for t in range(peers - 1)
            for b in range(bands)
        ]
        prev_own.append(lax.ppermute(last, ("tm", "height"), pairs))
    sib = [sibling(v) for v in own]
    prev_sib = [sibling(v) for v in prev_own]
    for m in range(1, bands):
        ups.append([lax.ppermute(v, "height", ring(bands, m)) for v in ups[0]])

    stats = call(
        functools.partial(stat_body, size),
        sds((devices, 2 * frames + 8, chans), F32), [VM, VM, VM],
        nbytes=2**20, name="stat",
    )(clip_video, norm_gain[None], norm_bias[None])
    got = lax.all_to_all(stats, everyone, 0, 0)
    got = got.reshape(peers, bands, 2, 2 * frames + 8, chans)
    table = call(
        table_body, sds((2, 40, chans), F32), [SM, VM], nbytes=2**18, name="table"
    )(clip_lengths, got)
    weight = conv_weight.reshape(9, 3 * full, full)
    turned = call(
        turn_body, sds(weight.shape, BF16), [VM], nbytes=8 * 2**20, name="turn"
    )(weight)

    grads = call(
        functools.partial(weight_body, peers, bands, cap, block),
        [sds((27, block, chans), F32)] + [sds((27, block, chans), BF16)] * (peers - 1),
        [SM] + [VM] * (1 + 4 * bands + peers * bands),
        [
            pltpu.VMEM((frames + 2, bands * rows + 2, cols, 3 * width), BF16),
            pltpu.VMEM((frames, bands, chans, rows * cols), BF16),
        ],
        flops=8 * 10**9, nbytes=6 * 2**20, name="weight",
    )(
        clip_lengths, table, *own, *sib, *prev_own, *prev_sib,
        *[v for band in ups for v in band],
    )
    weight_grad = grads[0]
    for k in range(1, peers):
        weight_grad = weight_grad + lax.ppermute(grads[k], "tm", ring(peers, k)).astype(F32)
    weight_grad = weight_grad.reshape(3, 3, 3, block, chans)

    far = bands - 1
    up, up_first = call(
        functools.partial(order_body, peers, bands, cap),
        [sds((frames, rows + 2, cols, chans), BF16), sds((2, rows + 2, cols, chans), BF16)],
        [VM] * (3 * peers),
        nbytes=2 * 2**20, name="order",
    )(*ups[0], *ups[1], *ups[far])
    up_sib = sibling(up)
    next_own = lax.ppermute(up_first, "tm", [(t + 1, t) for t in range(peers - 1)])
    next_sib = sibling(next_own)
    part = sds((frames, half * cols, chans), F32)
    keep, give, sums = call(
        functools.partial(backward_body, peers),
        [part, part, sds((devices, 2 * NCLIPS, chans), F32)],
        [SM] + [VM] * 8,
        [
            pltpu.VMEM((frames + 2, half + 2, cols, 6 * chans), BF16),
            pltpu.VMEM((frames, half * cols, 2 * chans), F32),
        ],
        flops=8 * 10**9, nbytes=6 * 2**20, name="backward",
    )(clip_lengths, table, turned, clip_video, sib[0], up, up_sib, next_own, next_sib)
    totals = lax.all_to_all(sums, everyone, 0, 0)
    other = sibling(give)

    part = sds((frames, half, cols, chans), BF16)
    block_keep, block_give = call(
        functools.partial(forward_body, bands),
        [part, part],
        [SM] + [VM] * 14,
        [pltpu.VMEM((frames + 2, half + 2, cols, 6 * chans), BF16)],
        flops=8 * 10**9, nbytes=6 * 2**20, name="forward",
    )(
        clip_lengths, table, weight, clip_video, sib[0], prev_own[0], prev_sib[0],
        own[1], sib[1], own[far], sib[far],
        prev_own[1], prev_sib[1], prev_own[far], prev_sib[far],
    )
    block_other = sibling(block_give)
    block_out = jnp.where(
        c == 0,
        jnp.concatenate([block_keep, block_other], axis=1),
        jnp.concatenate([block_other, block_keep], axis=1),
    )

    video_grad, small = call(
        functools.partial(finish_body, size, bands),
        [sds(clip_video.shape, BF16), sds((8, chans), F32)],
        [SM] + [VM] * 6,
        nbytes=3 * 2**20, name="finish",
    )(clip_lengths, table, totals, clip_video, keep, other, up)
    return (block_out, video_grad, weight_grad, small[0], small[1])


def solution(mesh):
    placed = (
        P(("groups", "tm"), "height", None, "chan"),
        P("chan"),
        P("chan"),
        P(),
        P("groups"),
        P(("groups", "tm")),
        P(("groups", "tm"), "height", None, "chan"),
    )
    return jax.shard_map(
        per_device,
        mesh=mesh,
        in_specs=placed,
        out_specs=(
            P(("groups", "tm"), "height", None, "chan"),
            P(("groups", "tm"), "height", None, "chan"),
            P("groups", None, None, ("tm", "height"), "chan"),
            P(("groups", "chan")),
            P(("groups", "chan")),
        ),
        check_vma=False,
    )
```

time: 140 us -> 129 us (0.921)
  waiting for transfers between devices: 10.2 us -> 29.9 us
  other arithmetic: 12 us -> 2.76 us
  local copies, waits for them, and re-layouts: 15.1 us -> 6.42 us
  starting transfers between devices: 40.4 us -> 33.7 us
  matrix products: 2.77 us -> 0 us
  Pallas kernels: 57.1 us -> 55.1 us
    ppermute x3, waiting for transfers between devices: 0.01 us -> 10.8 us  [per_device(): lax.ppermute(pieces[k], 'tm', ring(peers, k))]
    transpose x3 -> x0, local copies, waits for them, and re-layouts: 5.92 us -> none  [the longest x2 5.27 us: per_device(): jnp.transpose(weight_back, (0, 1, 2, 4, 3)).reshape(9, 3 * full, chans)]
    ppermute x3, waiting for transfers between devices: 4.72 us -> 9.24 us  [per_device(): lax.ppermute(grads[k], 'tm', ring(peers, k)).astype(F32)]
    unnamed x18 -> x42, local copies, waits for them, and re-layouts: 0.71 us -> 5.15 us
    ppermute x4, waiting for transfers between devices: 2.03 us -> 5.53 us  [per_device(): ups.append([lax.ppermute(v, 'height', ring(bands, m)) for v in ups[0]])]
    squeeze x4 -> x0, local copies, waits for them, and re-layouts: 2.89 us -> none  [edge(): return jnp.concatenate([v[:, row] for v in values], axis=0)]
    dot_general x2 -> x0, matrix products: 2.77 us -> none  [the longest x1 1.39 us: per_device(): picked = jnp.dot(near_member, over.T, precision=HIGHEST)]
    ppermute x1, waiting for transfers between devices: 1.6 us -> 4.24 us  [per_device(): lax.ppermute(up_first, 'tm', [(t + 1, t) for t in range(peers - 1)])]
  transfers between devices with their start and end apart: 22 -> 24, of which waited for: 5 -> 8; matrix products, arithmetic and copies ran while one was open for 20% -> 2% of each run, Pallas kernels for 29% -> 35%
where the time goes in v1:
time: 129 us
  Pallas kernels  55.1 us (43%)
  starting transfers between devices  33.7 us (26%)
  waiting for transfers between devices  29.9 us (23%)
  local copies, waits for them, and re-layouts  6.42 us (5%)
  other arithmetic  2.76 us (2%)
    pallas_call x1, Pallas kernels, per_device(): call(functools.partial(weight_body, peers, bands, cap, block), [sds((27,...  14.2 us
    pallas_call x1, Pallas kernels, per_device(): call(functools.partial(backward_body, peers), [part, part, sds((devices,...  13.4 us
    ppermute x3, waiting for transfers between devices, per_device(): lax.ppermute(pieces[k], 'tm', ring(peers, k))  10.8 us
    ppermute x3, waiting for transfers between devices, per_device(): lax.ppermute(grads[k], 'tm', ring(peers, k)).astype(F32)  9.24 us
    pallas_call x1, Pallas kernels, per_device(): call(functools.partial(forward_body, bands), [part, part], [SM] + [VM] *...  8.93 us
    ppermute x8, starting transfers between devices, sibling(): return lax.ppermute(value, 'chan', ring(2, 1))  6.99 us
    ppermute x4, waiting for transfers between devices, per_device(): ups.append([lax.ppermute(v, 'height', ring(bands, m)) for v in ups[0]])  5.53 us
    ppermute x2, starting transfers between devices, per_device(): prev_own.append(lax.ppermute(last, ('tm', 'height'), pairs))  5.36 us
  transfers between devices with their start and end apart: 24, of which 8 were waited for; matrix products, arithmetic and copies ran while one was open for 2% of the time, Pallas kernels for 35%

profile of v1, /device:TPU:15, one launch (start us, length us, event | category | flops | bytes accessed | tf_op | source)
XLA Modules:
  0.0 128.6 jit_solution(14306353239423574793)
XLA Ops:
  0.6 2.8 %pack.1 = (bf16[2,16,16,128]{3,2,1,0:T(8,128)(2,1)}, bf16[2,17,16,128]{3,2,1,0:T(8,128)(2,1)}, bf16[2,17,16,128]{3,2,1,0:T(8,128)(2,1)}, bf16[2,17,16,128]{3,2,1,0:T(8,128)(2,1)}, bf16[2,17,16,128]{3,2,1,0:T(8,128)(2,1)}) custom-call(s32[8]{0:T(128)} %frames.1, bf16[8,16,16,128]{3,2,1,0:T(8,128)(2,1)} %grad.1, bf16[8,16,16,128]{3,2,1,0:T(8,128)(2,1)} %refs_2_.1), custom_call_target="tpu_custom_call" | custom-call | bytes 1048576 | tf_op jit(solution)/shard_map/pack/pallas_call | solution.py:457
  8.7 7.7 %collective-permute-done.9.refs_2_.refs_12_ = bf16[2,17,16,128]{3,2,1,0:T(8,128)(2,1)S(1)} collective-permute-done((bf16[2,17,16,128]{3,2,1,0:T(8,128)(2,1)}, bf16[2,17,16,128]{3,2,1,0:T(8,128)(2,1)S(1)}, u32[]{:S(2)}, u32[]{:S(2)}) %collective-permute-start.9) | collective-permute-done | bytes 139296 | tf_op jit(solution)/shard_map/ppermute | solution.py:464
  16.7 2.4 %collective-permute-done.10.refs_3_.refs_13_ = bf16[2,17,16,128]{3,2,1,0:T(8,128)(2,1)S(1)} collective-permute-done((bf16[2,17,16,128]{3,2,1,0:T(8,128)(2,1)}, bf16[2,17,16,128]{3,2,1,0:T(8,128)(2,1)S(1)}, u32[]{:S(2)}, u32[]{:S(2)}) %collective-permute-start.10) | collective-permute-done | bytes 139296 | tf_op jit(solution)/shard_map/ppermute | solution.py:464
  19.4 2.5 %collective-permute-done.13.refs_6_.refs_10_.refs_16_ = bf16[2,17,16,128]{3,2,1,0:T(8,128)(2,1)S(1)} collective-permute-done((bf16[2,17,16,128]{3,2,1,0:T(8,128)(2,1)S(1)}, bf16[2,17,16,128]{3,2,1,0:T(8,128)(2,1)S(1)}, u32[]{:S(2)}, u32[]{:S(2)}) %collective-permute-start.13) | collective-permute-done | bytes 139296 | tf_op jit(solution)/shard_map/ppermute | solution.py:480
  21.9 3.0 %collective-permute-done.14.refs_7_.refs_11_.refs_17_ = bf16[2,17,16,128]{3,2,1,0:T(8,128)(2,1)S(1)} collective-permute-done((bf16[2,17,16,128]{3,2,1,0:T(8,128)(2,1)S(1)}, bf16[2,17,16,128]{3,2,1,0:T(8,128)(2,1)S(1)}, u32[]{:S(2)}, u32[]{:S(2)}) %collective-permute-start.14) | collective-permute-done | bytes 139296 | tf_op jit(solution)/shard_map/ppermute | solution.py:480
  25.6 3.4 %order.1 = (bf16[8,18,16,128]{3,2,1,0:T(8,128)(2,1)}, bf16[2,18,16,128]{3,2,1,0:T(8,128)(2,1)}) custom-call(bf16[2,17,16,128]{3,2,1,0:T(8,128)(2,1)} %get-tuple-element.26.refs_0_.refs_10_, bf16[2,17,16,128]{3,2,1,0:T(8,128)(2,1)} %copy-done.8, bf16[2,17,16,128]{3,2,1,0:T(8,128)(2,1)} %copy-done.9, bf16[2,17,16,128]{3,2,1,0:T(8,128)(2,1)} %copy-done.10, ...), custom_call_target="tpu_custom_call" | custom-call | bytes 2097152 | tf_op jit(solution)/shard_map/order/pallas_call | solution.py:516
  29.0 2.1 %collective-permute-start.15 = (bf16[8,18,16,128]{3,2,1,0:T(8,128)(2,1)}, bf16[8,18,16,128]{3,2,1,0:T(8,128)(2,1)S(1)}, u32[]{:S(2)}, u32[]{:S(2)}) collective-permute-start(bf16[8,18,16,128]{3,2,1,0:T(8,128)(2,1)} %get-tuple-element.30.up), channel_id=1, source_target_pairs={{0,1},{1,0},{2,3},{3,2},{4,5},{5,4},{6,7},{7,6},{8,9},{9,8},{10,11... | collective-permute-start | bytes 1769480 | tf_op jit(solution)/shard_map/ppermute | solution.py:47
  31.6 2.4 %stat.1 = f32[16,24,128]{2,1,0:T(8,128)} custom-call(bf16[8,16,16,128]{3,2,1,0:T(8,128)(2,1)} %refs_2_.1, f32[1,128]{1,0:T(1,128)} %bitcast.13, f32[1,128]{1,0:T(1,128)} %bitcast.14), custom_call_target="tpu_custom_call" | custom-call | bytes 1048576 | tf_op jit(solution)/shard_map/stat/pallas_call | solution.py:482
  34.0 5.3 %all-to-all-start = ((f32[16,24,128]{2,1,0:T(8,128)}), f32[16,24,128]{2,1,0:T(8,128)S(1)}, u32[]{:S(2)}, u32[]{:S(2)}) async-start(f32[16,24,128]{2,1,0:T(8,128)} %stat.1), calls=%async_computation | async-start | bytes 393216 | tf_op jit(solution)/shard_map/all_to_all | solution.py:487
  39.3 2.2 %collective-permute-start.16 = (bf16[2,18,16,128]{3,2,1,0:T(8,128)(2,1)}, bf16[2,18,16,128]{3,2,1,0:T(8,128)(2,1)S(1)}, u32[]{:S(2)}, u32[]{:S(2)}) collective-permute-start(bf16[2,18,16,128]{3,2,1,0:T(8,128)(2,1)} %get-tuple-element.31), channel_id=1, source_target_pairs={{4,0},{8,4},{12,8},{5,1},{9,5},{13,9},{6,2},{10,6},{14,10},{7,3},{... | collective-permute-start | bytes 442376 | tf_op jit(solution)/shard_map/ppermute | solution.py:523
  41.5 3.1 %collective-permute-start.5 = (bf16[2,16,16,128]{3,2,1,0:T(8,128)(2,1)}, bf16[2,16,16,128]{3,2,1,0:T(8,128)(2,1)S(1)}, u32[]{:S(2)}, u32[]{:S(2)}) collective-permute-start(bf16[2,16,16,128]{3,2,1,0:T(8,128)(2,1)} %get-tuple-element.23), channel_id=1, source_target_pairs={{0,6},{2,4},{4,10},{6,8},{8,14},{10,12},{1,7},{3,5},{5,11},{7,9},{... | collective-permute-start | bytes 393224 | tf_op jit(solution)/shard_map/ppermute | solution.py:476
  44.6 4.2 %collective-permute-done.16.next_own = bf16[2,18,16,128]{3,2,1,0:T(8,128)(2,1)S(1)} collective-permute-done((bf16[2,18,16,128]{3,2,1,0:T(8,128)(2,1)}, bf16[2,18,16,128]{3,2,1,0:T(8,128)(2,1)S(1)}, u32[]{:S(2)}, u32[]{:S(2)}) %collective-permute-start.16) | collective-permute-done | bytes 147488 | tf_op jit(solution)/shard_map/ppermute | solution.py:523
  49.7 2.3 %collective-permute-start.1 = (bf16[2,16,16,128]{3,2,1,0:T(8,128)(2,1)}, bf16[2,16,16,128]{3,2,1,0:T(8,128)(2,1)S(1)}, u32[]{:S(2)}, u32[]{:S(2)}) collective-permute-start(bf16[2,16,16,128]{3,2,1,0:T(8,128)(2,1)} %get-tuple-element.23), channel_id=1, source_target_pairs={{0,4},{2,6},{4,8},{6,10},{8,12},{10,14},{1,5},{3,7},{5,9},{7,11},{... | collective-permute-start | bytes 393224 | tf_op jit(solution)/shard_map/ppermute | solution.py:476
  52.0 4.7 %turn.1.weight = bf16[9,768,256]{2,1,0:T(8,128)(2,1)} custom-call(bf16[9,768,256]{2,1,0:T(8,128)(2,1)} %bitcast.9), custom_call_target="tpu_custom_call" | custom-call | bytes 8388608 | tf_op jit(solution)/shard_map/turn/pallas_call | solution.py:493
  57.4 2.0 %table.1.refs_1_ = f32[2,40,128]{2,1,0:T(8,128)} custom-call(s32[8]{0:T(128)} %refs_0_.1, f32[4,2,2,24,128]{4,3,2,1,0:T(8,128)} %bitcast.11), custom_call_target="tpu_custom_call" | custom-call | bytes 262144 | tf_op jit(solution)/shard_map/table/pallas_call | solution.py:489
  59.4 1.9 %collective-permute-start.6 = (bf16[2,16,16,128]{3,2,1,0:T(8,128)(2,1)S(1)}, bf16[2,16,16,128]{3,2,1,0:T(8,128)(2,1)S(1)}, u32[]{:S(2)}, u32[]{:S(2)}) collective-permute-start(bf16[2,16,16,128]{3,2,1,0:T(8,128)(2,1)S(1)} %collective-permute-done.5.refs_4_.refs_6_.refs_7_), channel_id=1, source_target_pairs={{0,1},{1,0},{2,3},{3,2},{4,5},{5,4},{6,7},{7,6},{8,9},{9,8},{10,11... | collective-permute-start | bytes 393224 | tf_op jit(solution)/shard_map/ppermute | solution.py:47
  63.2 13.4 %backward.1 = (f32[8,128,128]{2,1,0:T(8,128)}, f32[8,128,128]{2,1,0:T(8,128)}, f32[16,16,128]{2,1,0:T(8,128)}) custom-call(s32[8]{0:T(128)} %refs_0_.1, f32[2,40,128]{2,1,0:T(8,128)} %table.1.refs_1_, bf16[9,768,256]{2,1,0:T(8,128)(2,1)} %turn.1.weight, bf16[8,16,16,128]{3,2,1,0:T(8,128)(2,1)} %refs_2_.1, bf16[8,16,16,128]{3,2,1,0:T(8,128)(2,1)} %copy-done.13, ...), custom_call_target="tpu_custom_call" | custom-call | flops 8000000000 | bytes 6291456 | tf_op jit(solution)/shard_map/backward/pallas_call | solution.py:526
  76.6 5.0 %all-to-all-start.1 = ((f32[16,16,128]{2,1,0:T(8,128)}), f32[16,16,128]{2,1,0:T(8,128)S(1)}, u32[]{:S(2)}, u32[]{:S(2)}) async-start(f32[16,16,128]{2,1,0:T(8,128)} %get-tuple-element.32), calls=%async_computation.1 | async-start | bytes 262144 | tf_op jit(solution)/shard_map/all_to_all | solution.py:536
  83.4 14.2 %weight.1 = (f32[27,32,128]{2,1,0:T(8,128)}, bf16[27,32,128]{2,1,0:T(8,128)(2,1)}, bf16[27,32,128]{2,1,0:T(8,128)(2,1)}, bf16[27,32,128]{2,1,0:T(8,128)(2,1)}) custom-call(s32[8]{0:T(128)} %refs_0_.1, f32[2,40,128]{2,1,0:T(8,128)} %table.1.refs_1_, bf16[8,16,16,128]{3,2,1,0:T(8,128)(2,1)} %refs_2_.1, bf16[8,16,16,128]{3,2,1,0:T(8,128)(2,1)} %copy-done.12, ...), custom_call_target="tpu_custom_call" | custom-call | flops 8000000000 | bytes 6291456 | tf_op jit(solution)/shard_map/weight/pallas_call | solution.py:497
  101.3 8.9 %forward.1 = (bf16[8,8,16,128]{3,2,1,0:T(8,128)(2,1)}, bf16[8,8,16,128]{3,2,1,0:T(8,128)(2,1)}) custom-call(s32[8]{0:T(128)} %refs_0_.1, f32[2,40,128]{2,1,0:T(8,128)} %table.1.refs_1_, bf16[9,768,256]{2,1,0:T(8,128)(2,1)} %bitcast.10, bf16[8,16,16,128]{3,2,1,0:T(8,128)(2,1)} %refs_2_.1, bf16[8,16,16,128]{3,2,1,0:T(8,128)(2,1)} %copy-done.13, ...), custom_call_target="tpu_custom_call" | custom-call | flops 8000000000 | bytes 6291456 | tf_op jit(solution)/shard_map/forward/pallas_call | solution.py:540
  111.2 6.9 %collective-permute-done.20 = bf16[27,32,128]{2,1,0:T(8,128)(2,1)S(1)} collective-permute-done((bf16[27,32,128]{2,1,0:T(8,128)(2,1)}, bf16[27,32,128]{2,1,0:T(8,128)(2,1)S(1)}, u32[]{:S(2)}, u32[]{:S(2)}) %collective-permute-start.20) | collective-permute-done | bytes 221216 | tf_op jit(solution)/shard_map/ppermute | solution.py:512
  118.1 2.3 %collective-permute-done.21 = bf16[27,32,128]{2,1,0:T(8,128)(2,1)S(1)} collective-permute-done((bf16[27,32,128]{2,1,0:T(8,128)(2,1)}, bf16[27,32,128]{2,1,0:T(8,128)(2,1)S(1)}, u32[]{:S(2)}, u32[]{:S(2)}) %collective-permute-start.21) | collective-permute-done | bytes 221216 | tf_op jit(solution)/shard_map/ppermute | solution.py:512
  121.3 1.9 %maximum_select_fusion = bf16[8,16,16,128]{3,2,1,0:T(8,128)(2,1)} fusion(bf16[8,8,16,128]{3,2,1,0:T(8,128)(2,1)S(1)} %collective-permute-done.7, bf16[8,8,16,128]{3,2,1,0:T(8,128)(2,1)} %get-tuple-element.24, pred[]{:T(512)S(6)} %eq.3), kind=kLoop, calls=%fused_computation | loop fusion | flops 786432 | bytes 1048577 | tf_op jit(solution)/shard_map/jit(_where)/select_n | solution.py:552
  124.1 3.3 %finish.1 = (bf16[8,16,16,128]{3,2,1,0:T(8,128)(2,1)}, f32[8,128]{1,0:T(8,128)}) custom-call(s32[8]{0:T(128)} %refs_0_.1, f32[2,40,128]{2,1,0:T(8,128)} %table.1.refs_1_, f32[16,16,128]{2,1,0:T(8,128)} %copy-done.6, bf16[8,16,16,128]{3,2,1,0:T(8,128)(2,1)} %refs_2_.1, f32[8,128,128]{2,1,0:T(8,128)} %get-tuple-element.33.keep, f32[8,128,128]{2,1,0:T(8,128)} %copy-done.5, ...), custom_call_target="tpu_custom_call" | custom-call | bytes 3145728 | tf_op jit(solution)/shard_map/finish/pallas_call | solution.py:558
  (78 shorter events, 20.0 us)
Async XLA Ops:
  3.4 4.8 %collective-permute-start.8 = (bf16[2,17,16,128]{3,2,1,0:T(8,128)(2,1)}, bf16[2,17,16,128]{3,2,1,0:T(8,128)(2,1)S(1)}, u32[]{:S(2)}, u32[]{:S(2)}) collective-permute-start(bf16[2,17,16,128]{3,2,1,0:T(8,128)(2,1)} %get-tuple-element.27), channel_id=1, source_target_pairs={{0,4},{4,8},{8,12},{12,0},{1,5},{5,9},{9,13},{13,1},{2,6},{6,10},{... | collective-permute-start | bytes 417800 | tf_op jit(solution)/shard_map/ppermute | solution.py:464
  4.8 11.6 %collective-permute-start.9 = (bf16[2,17,16,128]{3,2,1,0:T(8,128)(2,1)}, bf16[2,17,16,128]{3,2,1,0:T(8,128)(2,1)S(1)}, u32[]{:S(2)}, u32[]{:S(2)}) collective-permute-start(bf16[2,17,16,128]{3,2,1,0:T(8,128)(2,1)} %get-tuple-element.28), channel_id=1, source_target_pairs={{0,8},{4,12},{8,0},{12,4},{1,9},{5,13},{9,1},{13,5},{2,10},{6,14},... | collective-permute-start | bytes 417800 | tf_op jit(solution)/shard_map/ppermute | solution.py:464
  5.9 13.2 %collective-permute-start.10 = (bf16[2,17,16,128]{3,2,1,0:T(8,128)(2,1)}, bf16[2,17,16,128]{3,2,1,0:T(8,128)(2,1)S(1)}, u32[]{:S(2)}, u32[]{:S(2)}) collective-permute-start(bf16[2,17,16,128]{3,2,1,0:T(8,128)(2,1)} %get-tuple-element.29), channel_id=1, source_target_pairs={{0,12},{4,0},{8,4},{12,8},{1,13},{5,1},{9,5},{13,9},{2,14},{6,2},{... | collective-permute-start | bytes 417800 | tf_op jit(solution)/shard_map/ppermute | solution.py:464
  7.3 12.1 %collective-permute-start.11 = (bf16[2,17,16,128]{3,2,1,0:T(8,128)(2,1)}, bf16[2,17,16,128]{3,2,1,0:T(8,128)(2,1)S(1)}, u32[]{:S(2)}, u32[]{:S(2)}) collective-permute-start(bf16[2,17,16,128]{3,2,1,0:T(8,128)(2,1)} %get-tuple-element.26.refs_0_.refs_10_), channel_id=1, source_target_pairs={{0,2},{2,0},{1,3},{3,1},{4,6},{6,4},{5,7},{7,5},{8,10},{10,8},{9,1... | collective-permute-start | bytes 417800 | tf_op jit(solution)/shard_map/ppermute | solution.py:480
  8.3 11.1 %collective-permute-start.12 = (bf16[2,17,16,128]{3,2,1,0:T(8,128)(2,1)S(1)}, bf16[2,17,16,128]{3,2,1,0:T(8,128)(2,1)S(1)}, u32[]{:S(2)}, u32[]{:S(2)}) collective-permute-start(bf16[2,17,16,128]{3,2,1,0:T(8,128)(2,1)S(1)} %collective-permute-done.8.refs_1_.refs_11_), channel_id=1, source_target_pairs={{0,2},{2,0},{1,3},{3,1},{4,6},{6,4},{5,7},{7,5},{8,10},{10,8},{9,1... | collective-permute-start | bytes 417800 | tf_op jit(solution)/shard_map/ppermute | solution.py:480
  16.4 5.5 %collective-permute-start.13 = (bf16[2,17,16,128]{3,2,1,0:T(8,128)(2,1)S(1)}, bf16[2,17,16,128]{3,2,1,0:T(8,128)(2,1)S(1)}, u32[]{:S(2)}, u32[]{:S(2)}) collective-permute-start(bf16[2,17,16,128]{3,2,1,0:T(8,128)(2,1)S(1)} %collective-permute-done.9.refs_2_.refs_12_), channel_id=1, source_target_pairs={{0,2},{2,0},{1,3},{3,1},{4,6},{6,4},{5,7},{7,5},{8,10},{10,8},{9,1... | collective-permute-start | bytes 417800 | tf_op jit(solution)/shard_map/ppermute | solution.py:480
  19.1 5.8 %collective-permute-start.14 = (bf16[2,17,16,128]{3,2,1,0:T(8,128)(2,1)S(1)}, bf16[2,17,16,128]{3,2,1,0:T(8,128)(2,1)S(1)}, u32[]{:S(2)}, u32[]{:S(2)}) collective-permute-start(bf16[2,17,16,128]{3,2,1,0:T(8,128)(2,1)S(1)} %collective-permute-done.10.refs_3_.refs_13_), channel_id=1, source_target_pairs={{0,2},{2,0},{1,3},{3,1},{4,6},{6,4},{5,7},{7,5},{8,10},{10,8},{9,1... | collective-permute-start | bytes 417800 | tf_op jit(solution)/shard_map/ppermute | solution.py:480
  29.0 32.8 %collective-permute-start.15 = (bf16[8,18,16,128]{3,2,1,0:T(8,128)(2,1)}, bf16[8,18,16,128]{3,2,1,0:T(8,128)(2,1)S(1)}, u32[]{:S(2)}, u32[]{:S(2)}) collective-permute-start(bf16[8,18,16,128]{3,2,1,0:T(8,128)(2,1)} %get-tuple-element.30.up), channel_id=1, source_target_pairs={{0,1},{1,0},{2,3},{3,2},{4,5},{5,4},{6,7},{7,6},{8,9},{9,8},{10,11... | collective-permute-start | bytes 1769480 | tf_op jit(solution)/shard_map/ppermute | solution.py:47
  31.0 30.2 %collective-permute-start.3 = (bf16[8,16,16,128]{3,2,1,0:T(8,128)(2,1)}, bf16[8,16,16,128]{3,2,1,0:T(8,128)(2,1)S(1)}, u32[]{:S(2)}, u32[]{:S(2)}) collective-permute-start(bf16[8,16,16,128]{3,2,1,0:T(8,128)(2,1)} %refs_2_.1), channel_id=1, source_target_pairs={{0,2},{2,0},{1,3},{3,1},{4,6},{6,4},{5,7},{7,5},{8,10},{10,8},{9,1... | collective-permute-start | bytes 1572872 | tf_op jit(solution)/shard_map/ppermute | solution.py:470
  31.3 30.0 %collective-permute-start = (bf16[8,16,16,128]{3,2,1,0:T(8,128)(2,1)}, bf16[8,16,16,128]{3,2,1,0:T(8,128)(2,1)S(1)}, u32[]{:S(2)}, u32[]{:S(2)}) collective-permute-start(bf16[8,16,16,128]{3,2,1,0:T(8,128)(2,1)} %refs_2_.1), channel_id=1, source_target_pairs={{0,1},{1,0},{2,3},{3,2},{4,5},{5,4},{6,7},{7,6},{8,9},{9,8},{10,11... | collective-permute-start | bytes 1572872 | tf_op jit(solution)/shard_map/ppermute | solution.py:47
  34.0 22.7 %all-to-all-start = ((f32[16,24,128]{2,1,0:T(8,128)}), f32[16,24,128]{2,1,0:T(8,128)S(1)}, u32[]{:S(2)}, u32[]{:S(2)}) async-start(f32[16,24,128]{2,1,0:T(8,128)} %stat.1), calls=%async_computation | async-start | bytes 393216 | tf_op jit(solution)/shard_map/all_to_all | solution.py:487
  39.3 9.5 %collective-permute-start.16 = (bf16[2,18,16,128]{3,2,1,0:T(8,128)(2,1)}, bf16[2,18,16,128]{3,2,1,0:T(8,128)(2,1)S(1)}, u32[]{:S(2)}, u32[]{:S(2)}) collective-permute-start(bf16[2,18,16,128]{3,2,1,0:T(8,128)(2,1)} %get-tuple-element.31), channel_id=1, source_target_pairs={{4,0},{8,4},{12,8},{5,1},{9,5},{13,9},{6,2},{10,6},{14,10},{7,3},{... | collective-permute-start | bytes 442376 | tf_op jit(solution)/shard_map/ppermute | solution.py:523
  41.5 8.2 %collective-permute-start.5 = (bf16[2,16,16,128]{3,2,1,0:T(8,128)(2,1)}, bf16[2,16,16,128]{3,2,1,0:T(8,128)(2,1)S(1)}, u32[]{:S(2)}, u32[]{:S(2)}) collective-permute-start(bf16[2,16,16,128]{3,2,1,0:T(8,128)(2,1)} %get-tuple-element.23), channel_id=1, source_target_pairs={{0,6},{2,4},{4,10},{6,8},{8,14},{10,12},{1,7},{3,5},{5,11},{7,9},{... | collective-permute-start | bytes 393224 | tf_op jit(solution)/shard_map/ppermute | solution.py:476
  48.8 12.9 %collective-permute-start.17 = (bf16[2,18,16,128]{3,2,1,0:T(8,128)(2,1)S(1)}, bf16[2,18,16,128]{3,2,1,0:T(8,128)(2,1)S(1)}, u32[]{:S(2)}, u32[]{:S(2)}) collective-permute-start(bf16[2,18,16,128]{3,2,1,0:T(8,128)(2,1)S(1)} %collective-permute-done.16.next_own), channel_id=1, source_target_pairs={{0,1},{1,0},{2,3},{3,2},{4,5},{5,4},{6,7},{7,6},{8,9},{9,8},{10,11... | collective-permute-start | bytes 442376 | tf_op jit(solution)/shard_map/ppermute | solution.py:47
  49.7 9.6 %collective-permute-start.1 = (bf16[2,16,16,128]{3,2,1,0:T(8,128)(2,1)}, bf16[2,16,16,128]{3,2,1,0:T(8,128)(2,1)S(1)}, u32[]{:S(2)}, u32[]{:S(2)}) collective-permute-start(bf16[2,16,16,128]{3,2,1,0:T(8,128)(2,1)} %get-tuple-element.23), channel_id=1, source_target_pairs={{0,4},{2,6},{4,8},{6,10},{8,12},{10,14},{1,5},{3,7},{5,9},{7,11},{... | collective-permute-start | bytes 393224 | tf_op jit(solution)/shard_map/ppermute | solution.py:476
  59.4 22.6 %collective-permute-start.6 = (bf16[2,16,16,128]{3,2,1,0:T(8,128)(2,1)S(1)}, bf16[2,16,16,128]{3,2,1,0:T(8,128)(2,1)S(1)}, u32[]{:S(2)}, u32[]{:S(2)}) collective-permute-start(bf16[2,16,16,128]{3,2,1,0:T(8,128)(2,1)S(1)} %collective-permute-done.5.refs_4_.refs_6_.refs_7_), channel_id=1, source_target_pairs={{0,1},{1,0},{2,3},{3,2},{4,5},{5,4},{6,7},{7,6},{8,9},{9,8},{10,11... | collective-permute-start | bytes 393224 | tf_op jit(solution)/shard_map/ppermute | solution.py:47
  61.2 20.7 %collective-permute-start.2 = (bf16[2,16,16,128]{3,2,1,0:T(8,128)(2,1)S(1)}, bf16[2,16,16,128]{3,2,1,0:T(8,128)(2,1)S(1)}, u32[]{:S(2)}, u32[]{:S(2)}) collective-permute-start(bf16[2,16,16,128]{3,2,1,0:T(8,128)(2,1)S(1)} %collective-permute-done.1.prev_own.refs_6_), channel_id=1, source_target_pairs={{0,1},{1,0},{2,3},{3,2},{4,5},{5,4},{6,7},{7,6},{8,9},{9,8},{10,11... | collective-permute-start | bytes 393224 | tf_op jit(solution)/shard_map/ppermute | solution.py:47
  61.3 20.6 %collective-permute-start.4 = (bf16[8,16,16,128]{3,2,1,0:T(8,128)(2,1)S(1)}, bf16[8,16,16,128]{3,2,1,0:T(8,128)(2,1)S(1)}, u32[]{:S(2)}, u32[]{:S(2)}) collective-permute-start(bf16[8,16,16,128]{3,2,1,0:T(8,128)(2,1)S(1)} %collective-permute-done.3.refs_0_.refs_2_.refs_3_), channel_id=1, source_target_pairs={{0,1},{1,0},{2,3},{3,2},{4,5},{5,4},{6,7},{7,6},{8,9},{9,8},{10,11... | collective-permute-start | bytes 1572872 | tf_op jit(solution)/shard_map/ppermute | solution.py:47
  76.6 46.6 %all-to-all-start.1 = ((f32[16,16,128]{2,1,0:T(8,128)}), f32[16,16,128]{2,1,0:T(8,128)S(1)}, u32[]{:S(2)}, u32[]{:S(2)}) async-start(f32[16,16,128]{2,1,0:T(8,128)} %get-tuple-element.32), calls=%async_computation.1 | async-start | bytes 262144 | tf_op jit(solution)/shard_map/all_to_all | solution.py:536
  81.5 41.7 %collective-permute-start.18 = (f32[8,128,128]{2,1,0:T(8,128)}, f32[8,128,128]{2,1,0:T(8,128)S(1)}, u32[]{:S(2)}, u32[]{:S(2)}) collective-permute-start(f32[8,128,128]{2,1,0:T(8,128)} %get-tuple-element.34), channel_id=1, source_target_pairs={{0,1},{1,0},{2,3},{3,2},{4,5},{5,4},{6,7},{7,6},{8,9},{9,8},{10,11... | collective-permute-start | bytes 1572872 | tf_op jit(solution)/shard_map/ppermute | solution.py:47
  97.7 13.5 %collective-permute-start.19 = (bf16[27,32,128]{2,1,0:T(8,128)(2,1)}, bf16[27,32,128]{2,1,0:T(8,128)(2,1)S(1)}, u32[]{:S(2)}, u32[]{:S(2)}) collective-permute-start(bf16[27,32,128]{2,1,0:T(8,128)(2,1)} %get-tuple-element.37), channel_id=1, source_target_pairs={{0,4},{4,8},{8,12},{12,0},{1,5},{5,9},{9,13},{13,1},{2,6},{6,10},{... | collective-permute-start | bytes 663560 | tf_op jit(solution)/shard_map/ppermute | solution.py:512
  98.9 19.2 %collective-permute-start.20 = (bf16[27,32,128]{2,1,0:T(8,128)(2,1)}, bf16[27,32,128]{2,1,0:T(8,128)(2,1)S(1)}, u32[]{:S(2)}, u32[]{:S(2)}) collective-permute-start(bf16[27,32,128]{2,1,0:T(8,128)(2,1)} %get-tuple-element.38), channel_id=1, source_target_pairs={{0,8},{4,12},{8,0},{12,4},{1,9},{5,13},{9,1},{13,5},{2,10},{6,14},... | collective-permute-start | bytes 663560 | tf_op jit(solution)/shard_map/ppermute | solution.py:512
  100.1 20.4 %collective-permute-start.21 = (bf16[27,32,128]{2,1,0:T(8,128)(2,1)}, bf16[27,32,128]{2,1,0:T(8,128)(2,1)S(1)}, u32[]{:S(2)}, u32[]{:S(2)}) collective-permute-start(bf16[27,32,128]{2,1,0:T(8,128)(2,1)} %get-tuple-element.39), channel_id=1, source_target_pairs={{0,12},{4,0},{8,4},{12,8},{1,13},{5,1},{9,5},{13,9},{2,14},{6,2},{... | collective-permute-start | bytes 663560 | tf_op jit(solution)/shard_map/ppermute | solution.py:512
  110.2 11.1 %collective-permute-start.7 = (bf16[8,8,16,128]{3,2,1,0:T(8,128)(2,1)}, bf16[8,8,16,128]{3,2,1,0:T(8,128)(2,1)S(1)}, u32[]{:S(2)}, u32[]{:S(2)}) collective-permute-start(bf16[8,8,16,128]{3,2,1,0:T(8,128)(2,1)} %get-tuple-element.25), channel_id=1, source_target_pairs={{0,1},{1,0},{2,3},{3,2},{4,5},{5,4},{6,7},{7,6},{8,9},{9,8},{10,11... | collective-permute-start | bytes 786440 | tf_op jit(solution)/shard_map/ppermute | solution.py:47
  (21 other events, 123.0 us)

commit v2 on v1

--- a/solution.py
+++ b/solution.py
@@ -18,14 +18,18 @@
 ANY = pl.BlockSpec(memory_space=pl.ANY)
 
 
-def call(body, out_shape, in_specs, scratch=(), flops=0, nbytes=0, name=None):
+def after(value, *others):
+    return lax.optimization_barrier((value, *others))[0]
+
+
+def call(body, out_shape, in_specs, scratch=(), flops=0, nbytes=0, name=None, room=24):
     return pl.pallas_call(
         body,
         out_shape=out_shape,
         in_specs=in_specs,
         out_specs=jax.tree.map(lambda _: VM, out_shape),
         scratch_shapes=list(scratch),
-        compiler_params=pltpu.CompilerParams(vmem_limit_bytes=56 * 2**20),
+        compiler_params=pltpu.CompilerParams(vmem_limit_bytes=room * 2**20),
         cost_estimate=pl.CostEstimate(flops=flops, bytes_accessed=nbytes, transcendentals=0),
         name=name,
     )
@@ -85,11 +89,20 @@
     return (iota((chans, chans), 0) // size == iota((chans, chans), 1) // size).astype(F32)
 
 
-def pack_body(peers, cap, frames, grad, video, last, *outs):
+def pack_body(peers, cap, frames, grad, video, *outs):
     outs, sem = outs[:-1], outs[-1]
     slots = frames.shape[0]
-    copy = pltpu.make_async_copy(video.at[pl.ds(slots - 2, 2)], last, sem)
-    copy.start()
+    rows = grad.shape[1]
+    copies = [
+        pltpu.make_async_copy(
+            video.at[slots - 2 + i],
+            outs[1].at[pl.ds(cap * (rows + 1) + i * rows, rows)],
+            sem.at[i],
+        )
+        for i in range(2)
+    ]
+    for copy in copies:
+        copy.start()
     tm = lax.axis_index("tm")
     number = [frames[i] for i in range(slots)]
     step = [lax.rem(lax.div(n, slots) - tm + peers, peers) for n in number]
@@ -99,18 +112,19 @@
         for j in range(i):
             r = r + jnp.where(step[j] == step[i], 1, 0)
         rank.append(r)
-    rows = grad.shape[1]
     for k in range(peers):
         for j in range(cap):
+            at = j * (rows + 1)
             index = jnp.int32(0)
             local = jnp.int32(-1)
             for i in range(slots):
                 hit = jnp.logical_and(step[i] == k, rank[i] == j)
                 index = jnp.where(hit, i, index)
                 local = jnp.where(hit, lax.rem(number[i], slots), local)
-            outs[k][j, :rows] = grad[index]
-            outs[k][j, rows:] = jnp.full((1,) + grad.shape[2:], local.astype(F32), F32).astype(BF16)
-    copy.wait()
+            outs[k][at : at + rows] = grad[index]
+            outs[k][at + rows] = jnp.full(grad.shape[2:], local.astype(F32), F32).astype(BF16)
+    for copy in copies:
+        copy.wait()
 
 
 def stat_body(size, video, gain, bias, out):
@@ -185,7 +199,7 @@
     refs = list(refs)
     lengths, table = refs.pop(0), refs.pop(0)
     take = lambda n: [refs.pop(0) for _ in range(n)]
-    own, sib, prev_own, prev_sib = take(bands), take(bands), take(bands), take(bands)
+    own, sib, prev_sib = take(bands), take(bands), take(bands)
     ups = [take(peers) for _ in range(bands)]
     outs = take(peers)
     active, upright = refs
@@ -210,7 +224,8 @@
     for f in range(frames + 2):
         for m in range(bands):
             if f < 2:
-                a, b = prev_own[m][f], prev_sib[m][f]
+                at = cap * (rows + 1) + f * rows
+                a, b = ups[m][1][at : at + rows], prev_sib[m][at : at + rows]
             else:
                 a, b = own[m][f - 2], sib[m][f - 2]
             x = bdot(a.reshape(cells, chans), pick_own) + bdot(b.reshape(cells, chans), pick_sib)
@@ -223,12 +238,13 @@
             active[f, at, :, 2 * width :] = after.astype(BF16).reshape(rows, cols, width)
     for k in range(peers):
         for j in range(cap):
-            local = jnp.max(ups[0][k][j, rows].astype(F32)).astype(jnp.int32)
+            at = j * (rows + 1)
+            local = jnp.max(ups[0][k][at + rows].astype(F32)).astype(jnp.int32)
 
             @pl.when(local >= 0)
             def _():
                 for m in range(bands):
-                    u = ups[m][k][j, :rows].reshape(cells, chans)
+                    u = ups[m][k][at : at + rows].reshape(cells, chans)
                     upright[local, m] = u.T
 
     begin = [start_of(lengths, first + t) for t in range(frames)]
@@ -251,10 +267,11 @@
     lax.fori_loop(0, 9, tap, 0)
 
 
-def forward_body(bands, lengths, table, weight, own, sib, prev_own, prev_sib, *refs):
-    above_own, above_sib, below_own, below_sib = refs[:4]
-    far_prev = refs[4:8]
-    keep, give, active = refs[8:]
+def forward_body(bands, skip, lengths, table, weight, *refs):
+    own, sib, above_own, above_sib, below_own, below_sib = refs[:6]
+    prev_own, prev_sib = refs[6:8]
+    far_prev = refs[8:12]
+    keep, give, active = refs[12:]
     frames, rows, cols, chans = own.shape
     half = rows // 2
     tm, h, c = lax.axis_index("tm"), lax.axis_index("height"), lax.axis_index("chan")
@@ -278,27 +295,26 @@
                 lane = n * 2 * chans + side * chans
                 active[f, at, :, lane : lane + chans] = w.astype(BF16).reshape(lines, cols, chans)
 
-    def edge(up, down, f):
-        return jnp.where(c == 0, up[f, rows - 1].astype(F32), down[f, 0].astype(F32))
+    def edge(up, down):
+        return jnp.where(c == 0, up.astype(F32), down.astype(F32))
 
     for f in range(frames + 2):
         if f < 2:
-            here = (prev_own, prev_sib, f)
-            there = far_prev
+            base = skip + f * rows
+            near = pl.ds(base + (half - 1) * c, half + 1)
+            here = [v[near] for v in (prev_own, prev_sib)]
+            up = [v[base + rows - 1] for v in far_prev[:2]]
+            down = [v[base] for v in far_prev[2:]]
         else:
-            here = (own, sib, f - 2)
-            there = (above_own, above_sib, below_own, below_sib)
-        g = here[2]
-        near = pl.ds((half - 1) * c, half + 1)
-        put(
-            f, pl.ds(1 - c, half + 1), half + 1,
-            here[0][g, near].reshape((half + 1) * cols, chans),
-            here[1][g, near].reshape((half + 1) * cols, chans),
-            None,
-        )
+            near = pl.ds((half - 1) * c, half + 1)
+            here = [v[f - 2, near] for v in (own, sib)]
+            up = [v[f - 2, rows - 1] for v in (above_own, above_sib)]
+            down = [v[f - 2, 0] for v in (below_own, below_sib)]
+        here = [v.reshape((half + 1) * cols, chans) for v in here]
+        put(f, pl.ds(1 - c, half + 1), half + 1, here[0], here[1], None)
         put(
             f, pl.ds((half + 1) * c, 1), 1,
-            edge(there[0], there[2], g), edge(there[1], there[3], g), outer,
+            edge(up[0], down[0]), edge(up[1], down[1]), outer,
         )
     batch = 4
     for t0 in range(0, frames, batch):
@@ -327,17 +343,18 @@
 def order_body(peers, bands, cap, *refs):
     own, above, below = refs[:peers], refs[peers : 2 * peers], refs[2 * peers : 3 * peers]
     out, first = refs[3 * peers :]
-    rows = own[0].shape[1] - 1
+    rows = out.shape[1] - 2
     h = lax.axis_index("height")
     for k in range(peers):
         for j in range(cap):
-            local = jnp.max(own[k][j, rows].astype(F32)).astype(jnp.int32)
+            at = j * (rows + 1)
+            local = jnp.max(own[k][at + rows].astype(F32)).astype(jnp.int32)
 
             @pl.when(local >= 0)
             def _():
-                out[local, 1 : rows + 1] = own[k][j, :rows]
-                top = above[k][j, rows - 1].astype(F32)
-                bottom = below[k][j, 0].astype(F32)
+                out[local, 1 : rows + 1] = own[k][at : at + rows]
+                top = above[k][at + rows - 1].astype(F32)
+                bottom = below[k][at].astype(F32)
                 out[local, 0] = jnp.where(h > 0, top, 0.0).astype(BF16)
                 out[local, rows + 1] = jnp.where(h < bands - 1, bottom, 0.0).astype(BF16)
 
@@ -453,65 +470,57 @@
     devices = peers * bands * 2
     sds = jax.ShapeDtypeStruct
 
-    piece = sds((cap, rows + 1, cols, chans), BF16)
-    last, *pieces = call(
+    skip = cap * (rows + 1)
+    pieces = call(
         functools.partial(pack_body, peers, cap),
-        [sds((2, rows, cols, chans), BF16)] + [piece] * peers,
+        [
+            sds((skip + (2 * rows if k == 1 else 0), cols, chans), BF16)
+            for k in range(peers)
+        ],
         [SM, VM, ANY],
-        [pltpu.SemaphoreType.DMA],
+        [pltpu.SemaphoreType.DMA((2,))],
         nbytes=2**20, name="pack",
     )(packed_frame, packed_grad, clip_video)
     ups = [[pieces[0]] + [lax.ppermute(pieces[k], "tm", ring(peers, k)) for k in range(1, peers)]]
-
-    own = [clip_video]
-    prev_own = []
-    for m in range(bands):
-        if m > 0:
-            own.append(lax.ppermute(clip_video, "height", ring(bands, m)))
-        pairs = [
-            (t * bands + b, (t + 1) * bands + (b + m) % bands)
-            for t in range(peers - 1)
-            for b in range(bands)
-        ]
-        prev_own.append(lax.ppermute(last, ("tm", "height"), pairs))
-    sib = [sibling(v) for v in own]
-    prev_sib = [sibling(v) for v in prev_own]
-    for m in range(1, bands):
-        ups.append([lax.ppermute(v, "height", ring(bands, m)) for v in ups[0]])
 
     stats = call(
         functools.partial(stat_body, size),
         sds((devices, 2 * frames + 8, chans), F32), [VM, VM, VM],
         nbytes=2**20, name="stat",
-    )(clip_video, norm_gain[None], norm_bias[None])
+    )(after(clip_video, pieces[0]), norm_gain[None], norm_bias[None])
+
+    own = [clip_video]
+    for m in range(1, bands):
+        own.append(lax.ppermute(clip_video, "height", ring(bands, m)))
+    sib = [sibling(v) for v in own]
+    for m in range(1, bands):
+        ready = [after(v, stats) if k == 0 else after(v, stats, own[m]) for k, v in enumerate(ups[0])]
+        ups.append([lax.ppermute(v, "height", ring(bands, m)) for v in ready])
+    prev_sib = [sibling(v[1]) for v in ups]
+
     got = lax.all_to_all(stats, everyone, 0, 0)
     got = got.reshape(peers, bands, 2, 2 * frames + 8, chans)
-    table = call(
-        table_body, sds((2, 40, chans), F32), [SM, VM], nbytes=2**18, name="table"
-    )(clip_lengths, got)
     weight = conv_weight.reshape(9, 3 * full, full)
     turned = call(
         turn_body, sds(weight.shape, BF16), [VM], nbytes=8 * 2**20, name="turn"
     )(weight)
+    table = call(
+        table_body, sds((2, 40, chans), F32), [SM, VM], nbytes=2**18, name="table"
+    )(clip_lengths, after(got, turned))
 
     grads = call(
         functools.partial(weight_body, peers, bands, cap, block),
         [sds((27, block, chans), F32)] + [sds((27, block, chans), BF16)] * (peers - 1),
-        [SM] + [VM] * (1 + 4 * bands + peers * bands),
+        [SM] + [VM] * (1 + 3 * bands + peers * bands),
         [
             pltpu.VMEM((frames + 2, bands * rows + 2, cols, 3 * width), BF16),
             pltpu.VMEM((frames, bands, chans, rows * cols), BF16),
         ],
         flops=8 * 10**9, nbytes=6 * 2**20, name="weight",
     )(
-        clip_lengths, table, *own, *sib, *prev_own, *prev_sib,
+        clip_lengths, table, *own, *sib, *prev_sib,
         *[v for band in ups for v in band],
     )
-    weight_grad = grads[0]
-    for k in range(1, peers):
-        weight_grad = weight_grad + lax.ppermute(grads[k], "tm", ring(peers, k)).astype(F32)
-    weight_grad = weight_grad.reshape(3, 3, 3, block, chans)
-
     far = bands - 1
     up, up_first = call(
         functools.partial(order_body, peers, bands, cap),
@@ -532,21 +541,20 @@
             pltpu.VMEM((frames, half * cols, 2 * chans), F32),
         ],
         flops=8 * 10**9, nbytes=6 * 2**20, name="backward",
-    )(clip_lengths, table, turned, clip_video, sib[0], up, up_sib, next_own, next_sib)
+    )(clip_lengths, table, after(turned, grads[0]), clip_video, sib[0], up, up_sib, next_own, next_sib)
     totals = lax.all_to_all(sums, everyone, 0, 0)
     other = sibling(give)
 
     part = sds((frames, half, cols, chans), BF16)
     block_keep, block_give = call(
-        functools.partial(forward_body, bands),
+        functools.partial(forward_body, bands, skip),
         [part, part],
         [SM] + [VM] * 14,
         [pltpu.VMEM((frames + 2, half + 2, cols, 6 * chans), BF16)],
         flops=8 * 10**9, nbytes=6 * 2**20, name="forward",
     )(
-        clip_lengths, table, weight, clip_video, sib[0], prev_own[0], prev_sib[0],
-        own[1], sib[1], own[far], sib[far],
-        prev_own[1], prev_sib[1], prev_own[far], prev_sib[far],
+        clip_lengths, table, after(weight, sums), own[0], sib[0], own[1], sib[1], own[far], sib[far],
+        ups[0][1], prev_sib[0], ups[1][1], prev_sib[1], ups[far][1], prev_sib[far],
     )
     block_other = sibling(block_give)
     block_out = jnp.where(
@@ -561,6 +569,10 @@
         [SM] + [VM] * 6,
         nbytes=3 * 2**20, name="finish",
     )(clip_lengths, table, totals, clip_video, keep, other, up)
+    weight_grad = after(grads[0], small)
+    for k in range(1, peers):
+        weight_grad = weight_grad + lax.ppermute(grads[k], "tm", ring(peers, k)).astype(F32)
+    weight_grad = weight_grad.reshape(3, 3, 3, block, chans)
     return (block_out, video_grad, weight_grad, small[0], small[1])
 
 

time: 129 us -> 119 us (0.922)
  waiting for transfers between devices: 29.9 us -> 18.2 us
  Pallas kernels: 55.1 us -> 46.8 us
  local copies, waits for them, and re-layouts: 6.42 us -> 12.2 us
  starting transfers between devices: 33.7 us -> 36.9 us
    ppermute x3, waiting for transfers between devices: 10.8 us -> 1.15 us  [per_device(): lax.ppermute(pieces[k], 'tm', ring(peers, k))]
    all_to_all x1, waiting for transfers between devices: 0.01 us -> 9.46 us  [per_device(): totals = lax.all_to_all(sums, everyone, 0, 0)]
    unnamed x42 -> x50, local copies, waits for them, and re-layouts: 5.15 us -> 11.7 us
    ppermute x3, waiting for transfers between devices: 9.24 us -> 2.86 us  [per_device(): lax.ppermute(grads[k], 'tm', ring(peers, k)).astype(F32)]
    ppermute x8, starting transfers between devices: 6.99 us -> 13.1 us  [sibling(): return lax.ppermute(value, 'chan', ring(2, 1))]
    ppermute x6 -> x4, starting transfers between devices: 6.62 us -> 2.1 us  [per_device(): ups.append([lax.ppermute(v, 'height', ring(bands, m)) for v in ready])]
    ppermute x1, waiting for transfers between devices: 4.24 us -> 0.01 us  [per_device(): lax.ppermute(up_first, 'tm', [(t + 1, t) for t in range(peers - 1)])]
    pallas_call x1, Pallas kernels: 4.72 us -> 0.96 us  [per_device(): call(turn_body, sds(weight.shape, BF16), [VM], nbytes=8 * 2 ** 20, name='...]
  transfers between devices with their start and end apart: 24 -> 22, of which waited for: 8 -> 6; matrix products, arithmetic and copies ran while one was open for 2% -> 2% of each run, Pallas kernels for 35% -> 29%
where the time goes in v2:
time: 119 us; the launch traced here: 118 us
  Pallas kernels  46.8 us (39%)
  starting transfers between devices  36.9 us (31%)
  waiting for transfers between devices  18.2 us (15%)
  local copies, waits for them, and re-layouts  12.2 us (10%)
  other arithmetic  2.79 us (2%)
    pallas_call x1, Pallas kernels, per_device(): call(functools.partial(weight_body, peers, bands, cap, block), [sds((27,...  13.5 us
    ppermute x8, starting transfers between devices, sibling(): return lax.ppermute(value, 'chan', ring(2, 1))  13.1 us
    pallas_call x1, Pallas kernels, per_device(): call(functools.partial(backward_body, peers), [part, part, sds((devices,...  13 us
    unnamed x50, local copies, waits for them, and re-layouts  11.7 us
    all_to_all x1, waiting for transfers between devices, per_device(): totals = lax.all_to_all(sums, everyone, 0, 0)  9.46 us
    pallas_call x1, Pallas kernels, per_device(): call(functools.partial(forward_body, bands, skip), [part, part], [SM] + [...  8.15 us
    all_to_all x1, starting transfers between devices, per_device(): got = lax.all_to_all(stats, everyone, 0, 0)  6.35 us
    all_to_all x1, starting transfers between devices, per_device(): totals = lax.all_to_all(sums, everyone, 0, 0)  4.91 us
  transfers between devices with their start and end apart: 22, of which 6 were waited for; matrix products, arithmetic and copies ran while one was open for 2% of the time, Pallas kernels for 29%

profile of v2, /device:TPU:15, one launch (start us, length us, event | category | flops | bytes accessed | tf_op | source)
XLA Modules:
  0.0 117.7 jit_solution(3307019747680613503)
XLA Ops:
  1.0 1.2 %copy-done.11 = bf16[8,16,16,128]{3,2,1,0:T(8,128)(2,1)S(1)} copy-done((bf16[8,16,16,128]{3,2,1,0:T(8,128)(2,1)S(1)}, bf16[8,16,16,128]{3,2,1,0:T(8,128)(2,1)}, u32[]{:S(2)}) %copy-start.11) | copy-done | bytes 524312
  2.8 2.1 %pack.1 = (bf16[34,16,128]{2,1,0:T(8,128)(2,1)}, bf16[66,16,128]{2,1,0:T(8,128)(2,1)S(1)}, bf16[34,16,128]{2,1,0:T(8,128)(2,1)S(1)}, bf16[34,16,128]{2,1,0:T(8,128)(2,1)S(1)}) custom-call(s32[8]{0:T(128)S(1)} %copy-done.19, bf16[8,16,16,128]{3,2,1,0:T(8,128)(2,1)S(1)} %copy-done.11, bf16[8,16,16,128]{3,2,1,0:T(8,128)(2,1)} %video.4), custom_call_target="tpu_custom_call" | custom-call | bytes 1048576 | tf_op jit(solution)/shard_map/pack/pallas_call | solution.py:474
  4.9 1.3 %collective-permute-start.3 = (bf16[66,16,128]{2,1,0:T(8,128)(2,1)S(1)}, bf16[66,16,128]{2,1,0:T(8,128)(2,1)}, u32[]{:S(2)}, u32[]{:S(2)}) collective-permute-start(bf16[66,16,128]{2,1,0:T(8,128)(2,1)S(1)} %get-tuple-element.34), channel_id=1, source_target_pairs={{0,4},{4,8},{8,12},{12,0},{1,5},{5,9},{9,13},{13,1},{2,6},{6,10},{... | collective-permute-start | bytes 811016 | tf_op jit(solution)/shard_map/ppermute | solution.py:484
  7.4 1.4 %collective-permute-start.8 = (bf16[34,16,128]{2,1,0:T(8,128)(2,1)S(1)}, bf16[34,16,128]{2,1,0:T(8,128)(2,1)}, u32[]{:S(2)}, u32[]{:S(2)}) collective-permute-start(bf16[34,16,128]{2,1,0:T(8,128)(2,1)S(1)} %get-tuple-element.37), channel_id=1, source_target_pairs={{0,12},{4,0},{8,4},{12,8},{1,13},{5,1},{9,5},{13,9},{2,14},{6,2},{... | collective-permute-start | bytes 417800 | tf_op jit(solution)/shard_map/ppermute | solution.py:484
  10.1 1.7 %stat.1 = f32[16,24,128]{2,1,0:T(8,128)S(1)} custom-call(bf16[8,16,16,128]{3,2,1,0:T(8,128)(2,1)} %video.4, f32[1,128]{1,0:T(1,128)S(1)} %bitcast.11, f32[1,128]{1,0:T(1,128)S(1)} %bitcast.12), custom_call_target="tpu_custom_call" | custom-call | bytes 1048576 | tf_op jit(solution)/shard_map/stat/pallas_call | solution.py:486
  12.5 1.4 %collective-permute-done.refs_3_.refs_2_.refs_4_ = bf16[8,16,16,128]{3,2,1,0:T(8,128)(2,1)} collective-permute-done((bf16[8,16,16,128]{3,2,1,0:T(8,128)(2,1)}, bf16[8,16,16,128]{3,2,1,0:T(8,128)(2,1)}, u32[]{:S(2)}, u32[]{:S(2)}) %collective-permute-start) | collective-permute-done | bytes 524320 | tf_op jit(solution)/shard_map/ppermute | solution.py:494
  14.1 7.7 %collective-permute-start.1 = (bf16[8,16,16,128]{3,2,1,0:T(8,128)(2,1)}, bf16[8,16,16,128]{3,2,1,0:T(8,128)(2,1)}, u32[]{:S(2)}, u32[]{:S(2)}) collective-permute-start(bf16[8,16,16,128]{3,2,1,0:T(8,128)(2,1)} %video.4), channel_id=1, source_target_pairs={{0,1},{1,0},{2,3},{3,2},{4,5},{5,4},{6,7},{7,6},{8,9},{9,8},{10,11... | collective-permute-start | bytes 1572872 | tf_op jit(solution)/shard_map/ppermute | solution.py:51
  24.4 6.3 %all-to-all-start = ((f32[16,24,128]{2,1,0:T(8,128)}), f32[16,24,128]{2,1,0:T(8,128)}, u32[]{:S(2)}, u32[]{:S(2)}) async-start(f32[16,24,128]{2,1,0:T(8,128)} %copy-done.3), calls=%async_computation | async-start | bytes 393216 | tf_op jit(solution)/shard_map/all_to_all | solution.py:501
  31.1 2.5 %collective-permute-start.4 = (bf16[66,16,128]{2,1,0:T(8,128)(2,1)}, bf16[66,16,128]{2,1,0:T(8,128)(2,1)}, u32[]{:S(2)}, u32[]{:S(2)}) collective-permute-start(bf16[66,16,128]{2,1,0:T(8,128)(2,1)} %collective-permute-done.3.refs_9_.refs_1_.refs_6_), channel_id=1, source_target_pairs={{0,1},{1,0},{2,3},{3,2},{4,5},{5,4},{6,7},{7,6},{8,9},{9,8},{10,11... | collective-permute-start | bytes 811016 | tf_op jit(solution)/shard_map/ppermute | solution.py:51
  33.6 3.3 %collective-permute-done.11.refs_15_.refs_7_.refs_11_ = bf16[34,16,128]{2,1,0:T(8,128)(2,1)S(1)} collective-permute-done((bf16[34,16,128]{2,1,0:T(8,128)(2,1)}, bf16[34,16,128]{2,1,0:T(8,128)(2,1)S(1)}, u32[]{:S(2)}, u32[]{:S(2)}) %collective-permute-start.11) | collective-permute-done | bytes 139296 | tf_op jit(solution)/shard_map/ppermute | solution.py:498
  36.9 3.2 %order.1 = (bf16[8,18,16,128]{3,2,1,0:T(8,128)(2,1)S(1)}, bf16[2,18,16,128]{3,2,1,0:T(8,128)(2,1)}) custom-call(bf16[34,16,128]{2,1,0:T(8,128)(2,1)} %get-tuple-element.38.refs_8_.refs_0_, bf16[66,16,128]{2,1,0:T(8,128)(2,1)} %collective-permute-done.3.refs_9_.refs_1_.refs_6_, bf16[34,16,128]{2,1,0:T(8,128)(2,1)} %collective-permute-done.7.refs_10_.refs_2_, ...), custom_call_target="tpu_custom_call" | custom-call | bytes 2097152 | tf_op jit(solution)/shard_map/order/pallas_call | solution.py:525
  40.9 2.7 %collective-permute-start.13 = (bf16[2,18,16,128]{3,2,1,0:T(8,128)(2,1)}, bf16[2,18,16,128]{3,2,1,0:T(8,128)(2,1)}, u32[]{:S(2)}, u32[]{:S(2)}) collective-permute-start(bf16[2,18,16,128]{3,2,1,0:T(8,128)(2,1)} %get-tuple-element.44), channel_id=1, source_target_pairs={{4,0},{8,4},{12,8},{5,1},{9,5},{13,9},{6,2},{10,6},{14,10},{7,3},{... | collective-permute-start | bytes 442376 | tf_op jit(solution)/shard_map/ppermute | solution.py:532
  44.7 1.7 %copy-done.1 = bf16[9,768,256]{2,1,0:T(8,128)(2,1)} copy-done((bf16[9,768,256]{2,1,0:T(8,128)(2,1)}, bf16[9,768,256]{2,1,0:T(8,128)(2,1)S(1)}, u32[]{:S(2)}) %copy-start.1) | copy-done | bytes 3538968
  46.4 1.3 %table.1.refs_1_ = f32[2,40,128]{2,1,0:T(8,128)S(1)} custom-call(s32[8]{0:T(128)S(1)} %copy-done.18, f32[4,2,2,24,128]{4,3,2,1,0:T(8,128)} %bitcast.2.got), custom_call_target="tpu_custom_call" | custom-call | bytes 262144 | tf_op jit(solution)/shard_map/table/pallas_call | solution.py:507
  47.8 1.3 %collective-permute-start.12 = (bf16[8,18,16,128]{3,2,1,0:T(8,128)(2,1)}, bf16[8,18,16,128]{3,2,1,0:T(8,128)(2,1)S(1)}, u32[]{:S(2)}, u32[]{:S(2)}) collective-permute-start(bf16[8,18,16,128]{3,2,1,0:T(8,128)(2,1)} %copy-done.4), channel_id=1, source_target_pairs={{0,1},{1,0},{2,3},{3,2},{4,5},{5,4},{6,7},{7,6},{8,9},{9,8},{10,11... | collective-permute-start | bytes 1769480 | tf_op jit(solution)/shard_map/ppermute | solution.py:51
  51.1 13.5 %weight.1 = (f32[27,32,128]{2,1,0:T(8,128)S(1)}, bf16[27,32,128]{2,1,0:T(8,128)(2,1)S(1)}, bf16[27,32,128]{2,1,0:T(8,128)(2,1)S(1)}, bf16[27,32,128]{2,1,0:T(8,128)(2,1)S(1)}) custom-call(s32[8]{0:T(128)S(1)} %copy-done.18, f32[2,40,128]{2,1,0:T(8,128)S(1)} %table.1.refs_1_, bf16[8,16,16,128]{3,2,1,0:T(8,128)(2,1)} %video.4, ...), custom_call_target="tpu_custom_call" | custom-call | flops 8000000000 | bytes 6291456 | tf_op jit(solution)/shard_map/weight/pallas_call | solution.py:511
  65.4 13.0 %backward.1 = (f32[8,128,128]{2,1,0:T(8,128)S(1)}, f32[8,128,128]{2,1,0:T(8,128)}, f32[16,16,128]{2,1,0:T(8,128)S(1)}) custom-call(s32[8]{0:T(128)S(1)} %copy-done.18, f32[2,40,128]{2,1,0:T(8,128)S(1)} %table.1.refs_1_, bf16[9,768,256]{2,1,0:T(8,128)(2,1)S(1)} %copy-done.2, bf16[8,16,16,128]{3,2,1,0:T(8,128)(2,1)} %video.4, ...), custom_call_target="tpu_custom_call" | custom-call | flops 8000000000 | bytes 6291456 | tf_op jit(solution)/shard_map/backward/pallas_call | solution.py:535
  78.6 8.2 %forward.1 = (bf16[8,8,16,128]{3,2,1,0:T(8,128)(2,1)S(1)}, bf16[8,8,16,128]{3,2,1,0:T(8,128)(2,1)}) custom-call(s32[8]{0:T(128)S(1)} %copy-done.18, f32[2,40,128]{2,1,0:T(8,128)S(1)} %table.1.refs_1_, bf16[9,768,256]{2,1,0:T(8,128)(2,1)S(1)} %bitcast.10, bf16[8,16,16,128]{3,2,1,0:T(8,128)(2,1)} %video.4, ...), custom_call_target="tpu_custom_call" | custom-call | flops 8000000000 | bytes 6291456 | tf_op jit(solution)/shard_map/forward/pallas_call | solution.py:549
  87.9 4.9 %all-to-all-start.1 = ((f32[16,16,128]{2,1,0:T(8,128)}), f32[16,16,128]{2,1,0:T(8,128)S(1)}, u32[]{:S(2)}, u32[]{:S(2)}) async-start(f32[16,16,128]{2,1,0:T(8,128)} %copy-done.17), calls=%async_computation.1 | async-start | bytes 262144 | tf_op jit(solution)/shard_map/all_to_all | solution.py:545
  95.1 1.2 %collective-permute-start.19 = (bf16[27,32,128]{2,1,0:T(8,128)(2,1)}, bf16[27,32,128]{2,1,0:T(8,128)(2,1)S(1)}, u32[]{:S(2)}, u32[]{:S(2)}) collective-permute-start(bf16[27,32,128]{2,1,0:T(8,128)(2,1)} %copy-done.22), channel_id=1, source_target_pairs={{0,12},{4,0},{8,4},{12,8},{1,13},{5,1},{9,5},{13,9},{2,14},{6,2},{... | collective-permute-start | bytes 663560 | tf_op jit(solution)/shard_map/ppermute | solution.py:574
  96.3 1.9 %maximum_select_fusion = bf16[8,16,16,128]{3,2,1,0:T(8,128)(2,1)} fusion(bf16[8,8,16,128]{3,2,1,0:T(8,128)(2,1)S(1)} %collective-permute-done.15, bf16[8,8,16,128]{3,2,1,0:T(8,128)(2,1)} %copy-done.14, pred[]{:T(512)S(6)} %eq.3), kind=kLoop, calls=%fused_computation | loop fusion | flops 786432 | bytes 1048577 | tf_op jit(solution)/shard_map/jit(_where)/select_n | solution.py:560
  98.2 9.5 %all-to-all-done.1.got = f32[16,16,128]{2,1,0:T(8,128)S(1)} async-done(((f32[16,16,128]{2,1,0:T(8,128)}), f32[16,16,128]{2,1,0:T(8,128)S(1)}, u32[]{:S(2)}, u32[]{:S(2)}) %all-to-all-start.1) | async-done | bytes 131104 | tf_op jit(solution)/shard_map/all_to_all | solution.py:545
  110.6 2.9 %finish.1 = (bf16[8,16,16,128]{3,2,1,0:T(8,128)(2,1)}, f32[8,128]{1,0:T(8,128)S(1)}) custom-call(s32[8]{0:T(128)S(1)} %copy-done.18, f32[2,40,128]{2,1,0:T(8,128)S(1)} %copy-done.16, f32[16,16,128]{2,1,0:T(8,128)S(1)} %all-to-all-done.1.got, bf16[8,16,16,128]{3,2,1,0:T(8,128)(2,1)} %video.4, f32[8,128,128]{2,1,0:T(8,128)S(1)} %copy-done.10, ...), custom_call_target="tpu_custom_call" | custom-call | bytes 3145728 | tf_op jit(solution)/shard_map/finish/pallas_call | solution.py:566
  115.2 1.7 %collective-permute-done.19 = bf16[27,32,128]{2,1,0:T(8,128)(2,1)S(1)} collective-permute-done((bf16[27,32,128]{2,1,0:T(8,128)(2,1)}, bf16[27,32,128]{2,1,0:T(8,128)(2,1)S(1)}, u32[]{:S(2)}, u32[]{:S(2)}) %collective-permute-start.19) | collective-permute-done | bytes 221216 | tf_op jit(solution)/shard_map/ppermute | solution.py:574
  (82 shorter events, 21.0 us)
Async XLA Ops:
  0.6 43.0 %copy-start = (bf16[3,3,3,256,256]{4,3,2,1,0:T(8,128)(2,1)S(1)}, bf16[3,3,3,256,256]{4,3,2,1,0:T(8,128)(2,1)}, u32[]{:S(2)}) copy-start(bf16[3,3,3,256,256]{4,3,2,1,0:T(8,128)(2,1)} %param.10) | copy-start | bytes 10616836
  0.6 13.2 %collective-permute-start = (bf16[8,16,16,128]{3,2,1,0:T(8,128)(2,1)}, bf16[8,16,16,128]{3,2,1,0:T(8,128)(2,1)}, u32[]{:S(2)}, u32[]{:S(2)}) collective-permute-start(bf16[8,16,16,128]{3,2,1,0:T(8,128)(2,1)} %video.4), channel_id=1, source_target_pairs={{0,2},{2,0},{1,3},{3,1},{4,6},{6,4},{5,7},{7,5},{8,10},{10,8},{9,1... | collective-permute-start | bytes 1572872 | tf_op jit(solution)/shard_map/ppermute | solution.py:494
  4.9 7.5 %collective-permute-start.3 = (bf16[66,16,128]{2,1,0:T(8,128)(2,1)S(1)}, bf16[66,16,128]{2,1,0:T(8,128)(2,1)}, u32[]{:S(2)}, u32[]{:S(2)}) collective-permute-start(bf16[66,16,128]{2,1,0:T(8,128)(2,1)S(1)} %get-tuple-element.34), channel_id=1, source_target_pairs={{0,4},{4,8},{8,12},{12,0},{1,5},{5,9},{9,13},{13,1},{2,6},{6,10},{... | collective-permute-start | bytes 811016 | tf_op jit(solution)/shard_map/ppermute | solution.py:484
  6.3 15.5 %collective-permute-start.7 = (bf16[34,16,128]{2,1,0:T(8,128)(2,1)S(1)}, bf16[34,16,128]{2,1,0:T(8,128)(2,1)}, u32[]{:S(2)}, u32[]{:S(2)}) collective-permute-start(bf16[34,16,128]{2,1,0:T(8,128)(2,1)S(1)} %get-tuple-element.36), channel_id=1, source_target_pairs={{0,8},{4,12},{8,0},{12,4},{1,9},{5,13},{9,1},{13,5},{2,10},{6,14},... | collective-permute-start | bytes 417800 | tf_op jit(solution)/shard_map/ppermute | solution.py:484
  7.4 16.0 %collective-permute-start.8 = (bf16[34,16,128]{2,1,0:T(8,128)(2,1)S(1)}, bf16[34,16,128]{2,1,0:T(8,128)(2,1)}, u32[]{:S(2)}, u32[]{:S(2)}) collective-permute-start(bf16[34,16,128]{2,1,0:T(8,128)(2,1)S(1)} %get-tuple-element.37), channel_id=1, source_target_pairs={{0,12},{4,0},{8,4},{12,8},{1,13},{5,1},{9,5},{13,9},{2,14},{6,2},{... | collective-permute-start | bytes 417800 | tf_op jit(solution)/shard_map/ppermute | solution.py:484
  13.8 19.8 %collective-permute-start.5 = (bf16[66,16,128]{2,1,0:T(8,128)(2,1)}, bf16[66,16,128]{2,1,0:T(8,128)(2,1)}, u32[]{:S(2)}, u32[]{:S(2)}) collective-permute-start(bf16[66,16,128]{2,1,0:T(8,128)(2,1)} %collective-permute-done.3.refs_9_.refs_1_.refs_6_), channel_id=1, source_target_pairs={{0,2},{2,0},{1,3},{3,1},{4,6},{6,4},{5,7},{7,5},{8,10},{10,8},{9,1... | collective-permute-start | bytes 811016 | tf_op jit(solution)/shard_map/ppermute | solution.py:498
  14.1 33.7 %collective-permute-start.1 = (bf16[8,16,16,128]{3,2,1,0:T(8,128)(2,1)}, bf16[8,16,16,128]{3,2,1,0:T(8,128)(2,1)}, u32[]{:S(2)}, u32[]{:S(2)}) collective-permute-start(bf16[8,16,16,128]{3,2,1,0:T(8,128)(2,1)} %video.4), channel_id=1, source_target_pairs={{0,1},{1,0},{2,3},{3,2},{4,5},{5,4},{6,7},{7,6},{8,9},{9,8},{10,11... | collective-permute-start | bytes 1572872 | tf_op jit(solution)/shard_map/ppermute | solution.py:51
  21.7 28.4 %collective-permute-start.2 = (bf16[8,16,16,128]{3,2,1,0:T(8,128)(2,1)}, bf16[8,16,16,128]{3,2,1,0:T(8,128)(2,1)}, u32[]{:S(2)}, u32[]{:S(2)}) collective-permute-start(bf16[8,16,16,128]{3,2,1,0:T(8,128)(2,1)} %collective-permute-done.refs_3_.refs_2_.refs_4_), channel_id=1, source_target_pairs={{0,1},{1,0},{2,3},{3,2},{4,5},{5,4},{6,7},{7,6},{8,9},{9,8},{10,11... | collective-permute-start | bytes 1572872 | tf_op jit(solution)/shard_map/ppermute | solution.py:51
  21.7 9.0 %collective-permute-start.9 = (bf16[34,16,128]{2,1,0:T(8,128)(2,1)}, bf16[34,16,128]{2,1,0:T(8,128)(2,1)}, u32[]{:S(2)}, u32[]{:S(2)}) collective-permute-start(bf16[34,16,128]{2,1,0:T(8,128)(2,1)} %get-tuple-element.38.refs_8_.refs_0_), channel_id=1, source_target_pairs={{0,2},{2,0},{1,3},{3,1},{4,6},{6,4},{5,7},{7,5},{8,10},{10,8},{9,1... | collective-permute-start | bytes 417800 | tf_op jit(solution)/shard_map/ppermute | solution.py:498
  23.3 7.8 %collective-permute-start.10 = (bf16[34,16,128]{2,1,0:T(8,128)(2,1)}, bf16[34,16,128]{2,1,0:T(8,128)(2,1)}, u32[]{:S(2)}, u32[]{:S(2)}) collective-permute-start(bf16[34,16,128]{2,1,0:T(8,128)(2,1)} %collective-permute-done.7.refs_10_.refs_2_), channel_id=1, source_target_pairs={{0,2},{2,0},{1,3},{3,1},{4,6},{6,4},{5,7},{7,5},{8,10},{10,8},{9,1... | collective-permute-start | bytes 417800 | tf_op jit(solution)/shard_map/ppermute | solution.py:498
  24.4 22.0 %all-to-all-start = ((f32[16,24,128]{2,1,0:T(8,128)}), f32[16,24,128]{2,1,0:T(8,128)}, u32[]{:S(2)}, u32[]{:S(2)}) async-start(f32[16,24,128]{2,1,0:T(8,128)} %copy-done.3), calls=%async_computation | async-start | bytes 393216 | tf_op jit(solution)/shard_map/all_to_all | solution.py:501
  30.7 6.2 %collective-permute-start.11 = (bf16[34,16,128]{2,1,0:T(8,128)(2,1)}, bf16[34,16,128]{2,1,0:T(8,128)(2,1)S(1)}, u32[]{:S(2)}, u32[]{:S(2)}) collective-permute-start(bf16[34,16,128]{2,1,0:T(8,128)(2,1)} %collective-permute-done.8.refs_11_.refs_3_), channel_id=1, source_target_pairs={{0,2},{2,0},{1,3},{3,1},{4,6},{6,4},{5,7},{7,5},{8,10},{10,8},{9,1... | collective-permute-start | bytes 417800 | tf_op jit(solution)/shard_map/ppermute | solution.py:498
  31.1 19.1 %collective-permute-start.4 = (bf16[66,16,128]{2,1,0:T(8,128)(2,1)}, bf16[66,16,128]{2,1,0:T(8,128)(2,1)}, u32[]{:S(2)}, u32[]{:S(2)}) collective-permute-start(bf16[66,16,128]{2,1,0:T(8,128)(2,1)} %collective-permute-done.3.refs_9_.refs_1_.refs_6_), channel_id=1, source_target_pairs={{0,1},{1,0},{2,3},{3,2},{4,5},{5,4},{6,7},{7,6},{8,9},{9,8},{10,11... | collective-permute-start | bytes 811016 | tf_op jit(solution)/shard_map/ppermute | solution.py:51
  33.6 16.6 %collective-permute-start.6 = (bf16[66,16,128]{2,1,0:T(8,128)(2,1)}, bf16[66,16,128]{2,1,0:T(8,128)(2,1)}, u32[]{:S(2)}, u32[]{:S(2)}) collective-permute-start(bf16[66,16,128]{2,1,0:T(8,128)(2,1)} %collective-permute-done.5.refs_13_.refs_5_.refs_9_.refs_8_.refs_10_), channel_id=1, source_target_pairs={{0,1},{1,0},{2,3},{3,2},{4,5},{5,4},{6,7},{7,6},{8,9},{9,8},{10,11... | collective-permute-start | bytes 811016 | tf_op jit(solution)/shard_map/ppermute | solution.py:51
  40.9 8.2 %collective-permute-start.13 = (bf16[2,18,16,128]{3,2,1,0:T(8,128)(2,1)}, bf16[2,18,16,128]{3,2,1,0:T(8,128)(2,1)}, u32[]{:S(2)}, u32[]{:S(2)}) collective-permute-start(bf16[2,18,16,128]{3,2,1,0:T(8,128)(2,1)} %get-tuple-element.44), channel_id=1, source_target_pairs={{4,0},{8,4},{12,8},{5,1},{9,5},{13,9},{6,2},{10,6},{14,10},{7,3},{... | collective-permute-start | bytes 442376 | tf_op jit(solution)/shard_map/ppermute | solution.py:532
  47.7 30.9 %copy-start.15 = (f32[2,40,128]{2,1,0:T(8,128)}, f32[2,40,128]{2,1,0:T(8,128)S(1)}, u32[]{:S(2)}) copy-start(f32[2,40,128]{2,1,0:T(8,128)S(1)} %table.1.refs_1_) | copy-start | bytes 122884
  47.8 17.6 %collective-permute-start.12 = (bf16[8,18,16,128]{3,2,1,0:T(8,128)(2,1)}, bf16[8,18,16,128]{3,2,1,0:T(8,128)(2,1)S(1)}, u32[]{:S(2)}, u32[]{:S(2)}) collective-permute-start(bf16[8,18,16,128]{3,2,1,0:T(8,128)(2,1)} %copy-done.4), channel_id=1, source_target_pairs={{0,1},{1,0},{2,3},{3,2},{4,5},{5,4},{6,7},{7,6},{8,9},{9,8},{10,11... | collective-permute-start | bytes 1769480 | tf_op jit(solution)/shard_map/ppermute | solution.py:51
  49.1 16.3 %collective-permute-start.14 = (bf16[2,18,16,128]{3,2,1,0:T(8,128)(2,1)}, bf16[2,18,16,128]{3,2,1,0:T(8,128)(2,1)S(1)}, u32[]{:S(2)}, u32[]{:S(2)}) collective-permute-start(bf16[2,18,16,128]{3,2,1,0:T(8,128)(2,1)} %collective-permute-done.13.next_own), channel_id=1, source_target_pairs={{0,1},{1,0},{2,3},{3,2},{4,5},{5,4},{6,7},{7,6},{8,9},{9,8},{10,11... | collective-permute-start | bytes 442376 | tf_op jit(solution)/shard_map/ppermute | solution.py:51
  78.5 29.2 %collective-permute-start.16 = (f32[8,128,128]{2,1,0:T(8,128)}, f32[8,128,128]{2,1,0:T(8,128)}, u32[]{:S(2)}, u32[]{:S(2)}) collective-permute-start(f32[8,128,128]{2,1,0:T(8,128)} %get-tuple-element.50), channel_id=1, source_target_pairs={{0,1},{1,0},{2,3},{3,2},{4,5},{5,4},{6,7},{7,6},{8,9},{9,8},{10,11... | collective-permute-start | bytes 1572872 | tf_op jit(solution)/shard_map/ppermute | solution.py:51
  87.5 8.9 %collective-permute-start.15 = (bf16[8,8,16,128]{3,2,1,0:T(8,128)(2,1)}, bf16[8,8,16,128]{3,2,1,0:T(8,128)(2,1)S(1)}, u32[]{:S(2)}, u32[]{:S(2)}) collective-permute-start(bf16[8,8,16,128]{3,2,1,0:T(8,128)(2,1)} %get-tuple-element.48), channel_id=1, source_target_pairs={{0,1},{1,0},{2,3},{3,2},{4,5},{5,4},{6,7},{7,6},{8,9},{9,8},{10,11... | collective-permute-start | bytes 786440 | tf_op jit(solution)/shard_map/ppermute | solution.py:51
  87.9 19.8 %all-to-all-start.1 = ((f32[16,16,128]{2,1,0:T(8,128)}), f32[16,16,128]{2,1,0:T(8,128)S(1)}, u32[]{:S(2)}, u32[]{:S(2)}) async-start(f32[16,16,128]{2,1,0:T(8,128)} %copy-done.17), calls=%async_computation.1 | async-start | bytes 262144 | tf_op jit(solution)/shard_map/all_to_all | solution.py:545
  92.8 21.2 %collective-permute-start.17 = (bf16[27,32,128]{2,1,0:T(8,128)(2,1)}, bf16[27,32,128]{2,1,0:T(8,128)(2,1)S(1)}, u32[]{:S(2)}, u32[]{:S(2)}) collective-permute-start(bf16[27,32,128]{2,1,0:T(8,128)(2,1)} %copy-done.24), channel_id=1, source_target_pairs={{0,4},{4,8},{8,12},{12,0},{1,5},{5,9},{9,13},{13,1},{2,6},{6,10},{... | collective-permute-start | bytes 663560 | tf_op jit(solution)/shard_map/ppermute | solution.py:574
  94.0 21.2 %collective-permute-start.18 = (bf16[27,32,128]{2,1,0:T(8,128)(2,1)}, bf16[27,32,128]{2,1,0:T(8,128)(2,1)S(1)}, u32[]{:S(2)}, u32[]{:S(2)}) collective-permute-start(bf16[27,32,128]{2,1,0:T(8,128)(2,1)} %copy-done.23), channel_id=1, source_target_pairs={{0,8},{4,12},{8,0},{12,4},{1,9},{5,13},{9,1},{13,5},{2,10},{6,14},... | collective-permute-start | bytes 663560 | tf_op jit(solution)/shard_map/ppermute | solution.py:574
  95.1 21.7 %collective-permute-start.19 = (bf16[27,32,128]{2,1,0:T(8,128)(2,1)}, bf16[27,32,128]{2,1,0:T(8,128)(2,1)S(1)}, u32[]{:S(2)}, u32[]{:S(2)}) collective-permute-start(bf16[27,32,128]{2,1,0:T(8,128)(2,1)} %copy-done.22), channel_id=1, source_target_pairs={{0,12},{4,0},{8,4},{12,8},{1,13},{5,1},{9,5},{13,9},{2,14},{6,2},{... | collective-permute-start | bytes 663560 | tf_op jit(solution)/shard_map/ppermute | solution.py:574
  (23 other events, 141.7 us)

commit v3 on v2

--- a/solution.py
+++ b/solution.py
@@ -22,15 +22,15 @@
     return lax.optimization_barrier((value, *others))[0]
 
 
-def call(body, out_shape, in_specs, scratch=(), flops=0, nbytes=0, name=None, room=24):
+def call(body, out_shape, in_specs, scratch=(), name=None, room=24, where=VM, work=1024):
     return pl.pallas_call(
         body,
         out_shape=out_shape,
         in_specs=in_specs,
-        out_specs=jax.tree.map(lambda _: VM, out_shape),
+        out_specs=jax.tree.map(lambda _: where, out_shape),
         scratch_shapes=list(scratch),
         compiler_params=pltpu.CompilerParams(vmem_limit_bytes=room * 2**20),
-        cost_estimate=pl.CostEstimate(flops=flops, bytes_accessed=nbytes, transcendentals=0),
+        cost_estimate=pl.CostEstimate(flops=work, bytes_accessed=1024, transcendentals=0),
         name=name,
     )
 
@@ -89,20 +89,10 @@
     return (iota((chans, chans), 0) // size == iota((chans, chans), 1) // size).astype(F32)
 
 
-def pack_body(peers, cap, frames, grad, video, *outs):
-    outs, sem = outs[:-1], outs[-1]
+def pack_body(peers, cap, frames, grad, video, *refs):
+    outs, names, sem = refs[:peers], refs[peers], refs[peers + 1]
     slots = frames.shape[0]
     rows = grad.shape[1]
-    copies = [
-        pltpu.make_async_copy(
-            video.at[slots - 2 + i],
-            outs[1].at[pl.ds(cap * (rows + 1) + i * rows, rows)],
-            sem.at[i],
-        )
-        for i in range(2)
-    ]
-    for copy in copies:
-        copy.start()
     tm = lax.axis_index("tm")
     number = [frames[i] for i in range(slots)]
     step = [lax.rem(lax.div(n, slots) - tm + peers, peers) for n in number]
@@ -112,6 +102,7 @@
         for j in range(i):
             r = r + jnp.where(step[j] == step[i], 1, 0)
         rank.append(r)
+    copies = []
     for k in range(peers):
         for j in range(cap):
             at = j * (rows + 1)
@@ -121,10 +112,33 @@
                 hit = jnp.logical_and(step[i] == k, rank[i] == j)
                 index = jnp.where(hit, i, index)
                 local = jnp.where(hit, lax.rem(number[i], slots), local)
-            outs[k][at : at + rows] = grad[index]
-            outs[k][at + rows] = jnp.full(grad.shape[2:], local.astype(F32), F32).astype(BF16)
+            n = 2 * (k * cap + j)
+            names[k * cap + j] = jnp.full(grad.shape[2:], local.astype(F32), F32).astype(BF16)
+            copies += [
+                pltpu.make_async_copy(grad.at[index], outs[k].at[pl.ds(at, rows)], sem.at[n]),
+                pltpu.make_async_copy(
+                    names.at[pl.ds(k * cap + j, 1)], outs[k].at[pl.ds(at + rows, 1)], sem.at[n + 1]
+                ),
+            ]
+            copies[-2].start()
+            copies[-1].start()
+    for i in range(2):
+        copies.append(
+            pltpu.make_async_copy(
+                video.at[slots - 2 + i],
+                outs[1].at[pl.ds(cap * (rows + 1) + i * rows, rows)],
+                sem.at[2 * peers * cap + i],
+            )
+        )
+        copies[-1].start()
     for copy in copies:
         copy.wait()
+
+
+def named(piece, rows, cap):
+    return [
+        jnp.max(piece[j * (rows + 1) + rows].astype(F32)).astype(jnp.int32) for j in range(cap)
+    ]
 
 
 def stat_body(size, video, gain, bias, out):
@@ -219,8 +233,10 @@
     mean, inv = lookup[:16], lookup[16:32]
     scale = inv * lookup[32:33]
     bias = lookup[33:34]
-    active[:, 0] = jnp.zeros((active.shape[0], cols, 3 * width), BF16)
-    active[:, bands * rows + 1] = jnp.zeros((active.shape[0], cols, 3 * width), BF16)
+    names = [named(ups[0][k], rows, cap) for k in range(peers)]
+    for col in range(3):
+        active[col, :, 0] = jnp.zeros((frames + 2, cols, width), BF16)
+        active[col, :, bands * rows + 1] = jnp.zeros((frames + 2, cols, width), BF16)
     for f in range(frames + 2):
         for m in range(bands):
             if f < 2:
@@ -233,13 +249,12 @@
             v = v * sigmoid(v)
             before, after = shifts(v)
             at = pl.ds(band[m] * rows + 1, rows)
-            active[f, at, :, :width] = before.astype(BF16).reshape(rows, cols, width)
-            active[f, at, :, width : 2 * width] = v.astype(BF16).reshape(rows, cols, width)
-            active[f, at, :, 2 * width :] = after.astype(BF16).reshape(rows, cols, width)
+            for col, moved in enumerate((before, v, after)):
+                active[col, f, at] = moved.astype(BF16).reshape(rows, cols, width)
     for k in range(peers):
         for j in range(cap):
             at = j * (rows + 1)
-            local = jnp.max(ups[0][k][at + rows].astype(F32)).astype(jnp.int32)
+            local = names[k][j]
 
             @pl.when(local >= 0)
             def _():
@@ -249,22 +264,33 @@
 
     begin = [start_of(lengths, first + t) for t in range(frames)]
 
-    def tap(i, carry):
-        a = lax.div(i, 3)
-        b = lax.rem(i, 3)
-        total = jnp.zeros((chans, 3 * width), F32)
+    def taps(i, count):
+        where = []
+        for n in range(count):
+            tap = 2 * i + n
+            a = lax.div(tap, 9)
+            where.append((a, lax.rem(lax.div(tap, 3), 3), lax.rem(tap, 3)))
+        total = jnp.zeros((chans, count * width), F32)
         for t in range(frames):
-            s = jnp.maximum(first + t - 2 + a, begin[t]) - (first - 2)
             for m in range(bands):
-                patch = active[s, pl.ds(band[m] * rows + b, rows)].reshape(cells, 3 * width)
+                patch = []
+                for a, b, col in where:
+                    s = jnp.maximum(first + t - 2 + a, begin[t]) - (first - 2)
+                    lines = active[col, s, pl.ds(band[m] * rows + b, rows)]
+                    patch.append(lines.reshape(cells, width))
+                patch = jnp.concatenate(patch, axis=1) if count > 1 else patch[0]
                 total = total + bdot(upright[t, m], patch)
-        for col in range(3):
-            piece = total[:, col * width : (col + 1) * width].T
+        for n in range(count):
+            piece = total[:, n * width : (n + 1) * width].T
             for k in range(peers):
-                outs[k][i * 3 + col] = piece[k * block : (k + 1) * block].astype(outs[k].dtype)
+                outs[k][2 * i + n] = piece[k * block : (k + 1) * block].astype(outs[k].dtype)
+
+    def pair(i, carry):
+        taps(i, 2)
         return carry
 
-    lax.fori_loop(0, 9, tap, 0)
+    lax.fori_loop(0, 13, pair, 0)
+    taps(jnp.int32(13), 1)
 
 
 def forward_body(bands, skip, lengths, table, weight, *refs):
@@ -345,10 +371,11 @@
     out, first = refs[3 * peers :]
     rows = out.shape[1] - 2
     h = lax.axis_index("height")
+    names = [named(own[k], rows, cap) for k in range(peers)]
     for k in range(peers):
         for j in range(cap):
             at = j * (rows + 1)
-            local = jnp.max(own[k][at + rows].astype(F32)).astype(jnp.int32)
+            local = names[k][j]
 
             @pl.when(local >= 0)
             def _():
@@ -379,22 +406,20 @@
                 spatial[f, :, :, at : at + chans] = w.astype(BF16).reshape(half + 2, cols, chans)
     total[...] = jnp.zeros_like(total)
 
-    def frame(t, carry):
-        begin = start_of(lengths, first + t)
-        for a in range(3):
-            s = jnp.maximum(first + t - 2 + a, begin) - first
-
-            @pl.when(jnp.logical_and(s >= 0, s < frames))
-            def _():
-                grad = jnp.zeros((cells, 2 * chans), F32)
-                for b in range(3):
+    begin = [start_of(lengths, first + t) for t in range(frames + 2)]
+    for a in range(3):
+        last = frames + 2 - a
+        for low, high in ((0, last // 2), (last // 2, last)):
+            grads = [jnp.zeros((cells, 2 * chans), F32) for _ in range(low, high)]
+            for b in range(3):
+                w = weight[a * 3 + b]
+                for t in range(low, high):
                     patch = spatial[t, 2 - b : 2 - b + half].reshape(cells, 6 * chans)
-                    grad = grad + bdot(patch, weight[a * 3 + b])
-                total[s] += grad
-
-        return carry
-
-    lax.fori_loop(0, frames + 2, frame, 0)
+                    grads[t - low] = grads[t - low] + bdot(patch, w)
+            for t in range(low, high):
+                s = jnp.maximum(first + t - 2 + a, begin[t]) - first
+                s = jnp.where(jnp.logical_and(s >= 0, s < frames), s, frames)
+                total[s] += grads[t - low]
     mine = pl.ds(c * half, half)
     member = (
         clip_of(lengths, first + iota((NCLIPS, frames), 1)) == iota((NCLIPS, frames), 0)
@@ -426,6 +451,15 @@
         give[t] = jnp.where(c == 0, right, left)
 
 
+def collect_body(own, *refs):
+    terms, out = refs[:-1], refs[-1]
+    for tap in range(own.shape[0]):
+        total = own[tap]
+        for term in terms:
+            total = total + term[tap].astype(F32)
+        out[tap] = total
+
+
 def finish_body(size, bands, lengths, table, got, video, keep, other, up, out, small):
     frames, rows, cols, chans = video.shape
     half = rows // 2
@@ -477,35 +511,38 @@
             sds((skip + (2 * rows if k == 1 else 0), cols, chans), BF16)
             for k in range(peers)
         ],
-        [SM, VM, ANY],
-        [pltpu.SemaphoreType.DMA((2,))],
-        nbytes=2**20, name="pack",
+        [SM, ANY, ANY],
+        [
+            pltpu.VMEM((peers * cap, cols, chans), BF16),
+            pltpu.SemaphoreType.DMA((2 * peers * cap + 2,)),
+        ],
+        name="pack", where=ANY,
     )(packed_frame, packed_grad, clip_video)
     ups = [[pieces[0]] + [lax.ppermute(pieces[k], "tm", ring(peers, k)) for k in range(1, peers)]]
 
     stats = call(
         functools.partial(stat_body, size),
         sds((devices, 2 * frames + 8, chans), F32), [VM, VM, VM],
-        nbytes=2**20, name="stat",
+        name="stat",
     )(after(clip_video, pieces[0]), norm_gain[None], norm_bias[None])
+
+    got = lax.all_to_all(stats, everyone, 0, 0)
+    got = got.reshape(peers, bands, 2, 2 * frames + 8, chans)
 
     own = [clip_video]
     for m in range(1, bands):
-        own.append(lax.ppermute(clip_video, "height", ring(bands, m)))
+        own.append(lax.ppermute(after(clip_video, pieces[0]), "height", ring(bands, m)))
     sib = [sibling(v) for v in own]
     for m in range(1, bands):
-        ready = [after(v, stats) if k == 0 else after(v, stats, own[m]) for k, v in enumerate(ups[0])]
-        ups.append([lax.ppermute(v, "height", ring(bands, m)) for v in ready])
+        ups.append([lax.ppermute(after(v, got), "height", ring(bands, m)) for v in ups[0]])
     prev_sib = [sibling(v[1]) for v in ups]
 
-    got = lax.all_to_all(stats, everyone, 0, 0)
-    got = got.reshape(peers, bands, 2, 2 * frames + 8, chans)
     weight = conv_weight.reshape(9, 3 * full, full)
     turned = call(
-        turn_body, sds(weight.shape, BF16), [VM], nbytes=8 * 2**20, name="turn"
+        turn_body, sds(weight.shape, BF16), [VM], name="turn"
     )(weight)
     table = call(
-        table_body, sds((2, 40, chans), F32), [SM, VM], nbytes=2**18, name="table"
+        table_body, sds((2, 40, chans), F32), [SM, VM], name="table"
     )(clip_lengths, after(got, turned))
 
     grads = call(
@@ -513,10 +550,10 @@
         [sds((27, block, chans), F32)] + [sds((27, block, chans), BF16)] * (peers - 1),
         [SM] + [VM] * (1 + 3 * bands + peers * bands),
         [
-            pltpu.VMEM((frames + 2, bands * rows + 2, cols, 3 * width), BF16),
+            pltpu.VMEM((3, frames + 2, bands * rows + 2, cols, width), BF16),
             pltpu.VMEM((frames, bands, chans, rows * cols), BF16),
         ],
-        flops=8 * 10**9, nbytes=6 * 2**20, name="weight",
+        name="weight",
     )(
         clip_lengths, table, *own, *sib, *prev_sib,
         *[v for band in ups for v in band],
@@ -526,7 +563,7 @@
         functools.partial(order_body, peers, bands, cap),
         [sds((frames, rows + 2, cols, chans), BF16), sds((2, rows + 2, cols, chans), BF16)],
         [VM] * (3 * peers),
-        nbytes=2 * 2**20, name="order",
+        name="order",
     )(*ups[0], *ups[1], *ups[far])
     up_sib = sibling(up)
     next_own = lax.ppermute(up_first, "tm", [(t + 1, t) for t in range(peers - 1)])
@@ -538,9 +575,9 @@
         [SM] + [VM] * 8,
         [
             pltpu.VMEM((frames + 2, half + 2, cols, 6 * chans), BF16),
-            pltpu.VMEM((frames, half * cols, 2 * chans), F32),
+            pltpu.VMEM((frames + 1, half * cols, 2 * chans), F32),
         ],
-        flops=8 * 10**9, nbytes=6 * 2**20, name="backward",
+        name="backward",
     )(clip_lengths, table, after(turned, grads[0]), clip_video, sib[0], up, up_sib, next_own, next_sib)
     totals = lax.all_to_all(sums, everyone, 0, 0)
     other = sibling(give)
@@ -551,7 +588,7 @@
         [part, part],
         [SM] + [VM] * 14,
         [pltpu.VMEM((frames + 2, half + 2, cols, 6 * chans), BF16)],
-        flops=8 * 10**9, nbytes=6 * 2**20, name="forward",
+        name="forward",
     )(
         clip_lengths, table, after(weight, sums), own[0], sib[0], own[1], sib[1], own[far], sib[far],
         ups[0][1], prev_sib[0], ups[1][1], prev_sib[1], ups[far][1], prev_sib[far],
@@ -563,16 +600,18 @@
         jnp.concatenate([block_other, block_keep], axis=1),
     )
 
+    terms = [lax.ppermute(grads[k], "tm", ring(peers, k)) for k in range(1, peers)]
+    weight_grad = call(
+        collect_body, sds((27, block, chans), F32), [VM] * peers, name="collect", work=10**13
+    )(after(grads[0], block_out), *terms)
+    weight_grad = weight_grad.reshape(3, 3, 3, block, chans)
+
     video_grad, small = call(
         functools.partial(finish_body, size, bands),
         [sds(clip_video.shape, BF16), sds((8, chans), F32)],
         [SM] + [VM] * 6,
-        nbytes=3 * 2**20, name="finish",
-    )(clip_lengths, table, totals, clip_video, keep, other, up)
-    weight_grad = after(grads[0], small)
-    for k in range(1, peers):
-        weight_grad = weight_grad + lax.ppermute(grads[k], "tm", ring(peers, k)).astype(F32)
-    weight_grad = weight_grad.reshape(3, 3, 3, block, chans)
+        name="finish",
+    )(clip_lengths, table, after(totals, weight_grad), clip_video, keep, other, up)
     return (block_out, video_grad, weight_grad, small[0], small[1])
 
 

time: 119 us -> 116 us (0.975)
  waiting for transfers between devices: 18.2 us -> 41.7 us
  Pallas kernels: 46.8 us -> 33 us
  starting transfers between devices: 36.9 us -> 28.6 us
  local copies, waits for them, and re-layouts: 12.2 us -> 9.75 us
  other arithmetic: 2.79 us -> 0.84 us
    ppermute x8, waiting for transfers between devices: 7.54 us -> 22.1 us  [the longest x3 12.8 us: per_device(): lax.ppermute(grads[k], 'tm', ring(peers, k))]
    all_to_all x1, waiting for transfers between devices: 0.01 us -> 12.3 us  [per_device(): got = lax.all_to_all(stats, everyone, 0, 0)]
    all_to_all x1, waiting for transfers between devices: 9.46 us -> 0.01 us  [per_device(): totals = lax.all_to_all(sums, everyone, 0, 0)]
    ppermute x8, starting transfers between devices: 13.1 us -> 3.7 us  [sibling(): return lax.ppermute(value, 'chan', ring(2, 1))]
    pallas_call x1, Pallas kernels: 13 us -> 6.91 us  [per_device(): call(functools.partial(backward_body, peers), [part, part, sds((devices,...]
    ppermute x1, waiting for transfers between devices: 0.01 us -> 4.38 us  [per_device(): lax.ppermute(up_first, 'tm', [(t + 1, t) for t in range(peers - 1)])]
    pallas_call x1, Pallas kernels: 3.19 us -> 0.24 us  [per_device(): call(functools.partial(order_body, peers, bands, cap), [sds((frames, rows...]
    pallas_call x1, Pallas kernels: 8.15 us -> 5.64 us  [per_device(): call(functools.partial(forward_body, bands, skip), [part, part], [SM] + [...]
  transfers between devices with their start and end apart: 22 -> 22, of which waited for: 6 -> 8; matrix products, arithmetic and copies ran while one was open for 2% -> 1% of each run, Pallas kernels for 29% -> 12%
where the time goes in v3:
time: 116 us; the launch traced here: 115 us
  waiting for transfers between devices  41.7 us (36%)
  Pallas kernels  33 us (28%)
  starting transfers between devices  28.6 us (25%)
  local copies, waits for them, and re-layouts  9.75 us (8%)
    ppermute x3, waiting for transfers between devices, per_device(): lax.ppermute(grads[k], 'tm', ring(peers, k))  12.8 us
    all_to_all x1, waiting for transfers between devices, per_device(): got = lax.all_to_all(stats, everyone, 0, 0)  12.3 us
    pallas_call x1, Pallas kernels, per_device(): call(functools.partial(weight_body, peers, bands, cap, block), [sds((27,...  11.3 us
    unnamed x36, local copies, waits for them, and re-layouts  9.24 us
    ppermute x4, waiting for transfers between devices, per_device(): lax.ppermute(after(v, got), 'height', ring(bands, m))  9.23 us
    all_to_all x1, starting transfers between devices, per_device(): totals = lax.all_to_all(sums, everyone, 0, 0)  7.31 us
    pallas_call x1, Pallas kernels, per_device(): call(functools.partial(backward_body, peers), [part, part, sds((devices,...  6.91 us
    all_to_all x1, starting transfers between devices, per_device(): got = lax.all_to_all(stats, everyone, 0, 0)  6.55 us
  transfers between devices with their start and end apart: 22, of which 8 were waited for; matrix products, arithmetic and copies ran while one was open for 1% of the time, Pallas kernels for 12%

profile of v3, /device:TPU:15, one launch (start us, length us, event | category | flops | bytes accessed | tf_op | source)
XLA Modules:
  0.0 114.7 jit_solution(2966096674081795377)
XLA Ops:
  1.7 1.0 copy-done.10
  3.4 2.0 %pack.1 = (bf16[34,16,128]{2,1,0:T(8,128)(2,1)S(1)}, bf16[66,16,128]{2,1,0:T(8,128)(2,1)S(1)}, bf16[34,16,128]{2,1,0:T(8,128)(2,1)S(1)}, bf16[34,16,128]{2,1,0:T(8,128)(2,1)S(1)}) custom-call(s32[8]{0:T(128)S(1)} %copy-done.13, bf16[8,16,16,128]{3,2,1,0:T(8,128)(2,1)S(1)} %copy-done.10, bf16[8,16,16,128]{3,2,1,0:T(8,128)(2,1)S(1)} %copy-done), custom_call_target="tpu_custom_call" | custom-call | flops 1024 | bytes 1024 | tf_op jit(solution)/shard_map/pack/pallas_call | solution.py:508
  7.7 1.4 %stat.1 = f32[16,24,128]{2,1,0:T(8,128)} custom-call(bf16[8,16,16,128]{3,2,1,0:T(8,128)(2,1)S(1)} %copy-done.1, f32[1,128]{1,0:T(1,128)S(1)} %bitcast.12, f32[1,128]{1,0:T(1,128)S(1)} %bitcast.13), custom_call_target="tpu_custom_call" | custom-call | flops 1024 | bytes 1024 | tf_op jit(solution)/shard_map/stat/pallas_call | solution.py:523
  9.1 6.6 %all-to-all-start = ((f32[16,24,128]{2,1,0:T(8,128)}), f32[16,24,128]{2,1,0:T(8,128)S(1)}, u32[]{:S(2)}, u32[]{:S(2)}) async-start(f32[16,24,128]{2,1,0:T(8,128)} %stat.1), calls=%async_computation | async-start | bytes 393216 | tf_op jit(solution)/shard_map/all_to_all | solution.py:529
  15.7 1.2 %collective-permute-start.3 = (bf16[66,16,128]{2,1,0:T(8,128)(2,1)S(1)}, bf16[66,16,128]{2,1,0:T(8,128)(2,1)S(1)}, u32[]{:S(2)}, u32[]{:S(2)}) collective-permute-start(bf16[66,16,128]{2,1,0:T(8,128)(2,1)S(1)} %get-tuple-element.35), channel_id=1, source_target_pairs={{0,4},{4,8},{8,12},{12,0},{1,5},{5,9},{9,13},{13,1},{2,6},{6,10},{... | collective-permute-start | bytes 811016 | tf_op jit(solution)/shard_map/ppermute | solution.py:521
  18.1 1.4 %collective-permute-start.8 = (bf16[34,16,128]{2,1,0:T(8,128)(2,1)S(1)}, bf16[34,16,128]{2,1,0:T(8,128)(2,1)S(1)}, u32[]{:S(2)}, u32[]{:S(2)}) collective-permute-start(bf16[34,16,128]{2,1,0:T(8,128)(2,1)S(1)} %get-tuple-element.38), channel_id=1, source_target_pairs={{0,12},{4,0},{8,4},{12,8},{1,13},{5,1},{9,5},{13,9},{2,14},{6,2},{... | collective-permute-start | bytes 417800 | tf_op jit(solution)/shard_map/ppermute | solution.py:521
  19.5 12.3 %all-to-all-done = f32[16,24,128]{2,1,0:T(8,128)S(1)} async-done(((f32[16,24,128]{2,1,0:T(8,128)}), f32[16,24,128]{2,1,0:T(8,128)S(1)}, u32[]{:S(2)}, u32[]{:S(2)}) %all-to-all-start) | async-done | bytes 196640 | tf_op jit(solution)/shard_map/all_to_all | solution.py:529
  33.2 1.9 %collective-permute-done.7.refs_10_.refs_2_ = bf16[34,16,128]{2,1,0:T(8,128)(2,1)S(1)} collective-permute-done((bf16[34,16,128]{2,1,0:T(8,128)(2,1)S(1)}, bf16[34,16,128]{2,1,0:T(8,128)(2,1)S(1)}, u32[]{:S(2)}, u32[]{:S(2)}) %collective-permute-start.7) | collective-permute-done | bytes 139296 | tf_op jit(solution)/shard_map/ppermute | solution.py:521
  35.7 1.0 collective-permute-done.8.refs_11_.refs_3_
  37.1 1.2 %collective-permute-start.11 = (bf16[34,16,128]{2,1,0:T(8,128)(2,1)S(1)}, bf16[34,16,128]{2,1,0:T(8,128)(2,1)S(1)}, u32[]{:S(2)}, u32[]{:S(2)}) collective-permute-start(bf16[34,16,128]{2,1,0:T(8,128)(2,1)S(1)} %collective-permute-done.8.refs_11_.refs_3_), channel_id=1, source_target_pairs={{0,2},{2,0},{1,3},{3,1},{4,6},{6,4},{5,7},{7,5},{8,10},{10,8},{9,1... | collective-permute-start | bytes 417800 | tf_op jit(solution)/shard_map/ppermute | solution.py:537
  38.2 6.2 %collective-permute-done.10.refs_14_.refs_6_.refs_10_ = bf16[34,16,128]{2,1,0:T(8,128)(2,1)S(1)} collective-permute-done((bf16[34,16,128]{2,1,0:T(8,128)(2,1)S(1)}, bf16[34,16,128]{2,1,0:T(8,128)(2,1)S(1)}, u32[]{:S(2)}, u32[]{:S(2)}) %collective-permute-start.10) | collective-permute-done | bytes 139296 | tf_op jit(solution)/shard_map/ppermute | solution.py:537
  44.5 3.0 %collective-permute-done.11.refs_15_.refs_7_.refs_11_ = bf16[34,16,128]{2,1,0:T(8,128)(2,1)S(1)} collective-permute-done((bf16[34,16,128]{2,1,0:T(8,128)(2,1)S(1)}, bf16[34,16,128]{2,1,0:T(8,128)(2,1)S(1)}, u32[]{:S(2)}, u32[]{:S(2)}) %collective-permute-start.11) | collective-permute-done | bytes 139296 | tf_op jit(solution)/shard_map/ppermute | solution.py:537
  48.5 1.9 %collective-permute-start.13 = (bf16[2,18,16,128]{3,2,1,0:T(8,128)(2,1)S(1)}, bf16[2,18,16,128]{3,2,1,0:T(8,128)(2,1)S(1)}, u32[]{:S(2)}, u32[]{:S(2)}) collective-permute-start(bf16[2,18,16,128]{3,2,1,0:T(8,128)(2,1)S(1)} %get-tuple-element.45), channel_id=1, source_target_pairs={{4,0},{8,4},{12,8},{5,1},{9,5},{13,9},{6,2},{10,6},{14,10},{7,3},{... | collective-permute-start | bytes 442376 | tf_op jit(solution)/shard_map/ppermute | solution.py:569
  51.0 4.4 %collective-permute-done.13.next_own = bf16[2,18,16,128]{3,2,1,0:T(8,128)(2,1)S(1)} collective-permute-done((bf16[2,18,16,128]{3,2,1,0:T(8,128)(2,1)S(1)}, bf16[2,18,16,128]{3,2,1,0:T(8,128)(2,1)S(1)}, u32[]{:S(2)}, u32[]{:S(2)}) %collective-permute-start.13) | collective-permute-done | bytes 147488 | tf_op jit(solution)/shard_map/ppermute | solution.py:569
  55.4 1.3 %collective-permute-start.14 = (bf16[2,18,16,128]{3,2,1,0:T(8,128)(2,1)S(1)}, bf16[2,18,16,128]{3,2,1,0:T(8,128)(2,1)S(1)}, u32[]{:S(2)}, u32[]{:S(2)}) collective-permute-start(bf16[2,18,16,128]{3,2,1,0:T(8,128)(2,1)S(1)} %collective-permute-done.13.next_own), channel_id=1, source_target_pairs={{0,1},{1,0},{2,3},{3,2},{4,5},{5,4},{6,7},{7,6},{8,9},{9,8},{10,11... | collective-permute-start | bytes 442376 | tf_op jit(solution)/shard_map/ppermute | solution.py:51
  56.7 2.0 %copy-done.4 = bf16[3,3,3,256,256]{4,3,2,1,0:T(8,128)(2,1)S(1)} copy-done((bf16[3,3,3,256,256]{4,3,2,1,0:T(8,128)(2,1)S(1)}, bf16[3,3,3,256,256]{4,3,2,1,0:T(8,128)(2,1)}, u32[]{:S(2)}) %copy-start.4) | copy-done | bytes 3538968
  60.6 11.3 %weight.1 = (f32[27,32,128]{2,1,0:T(8,128)S(1)}, bf16[27,32,128]{2,1,0:T(8,128)(2,1)S(1)}, bf16[27,32,128]{2,1,0:T(8,128)(2,1)S(1)}, bf16[27,32,128]{2,1,0:T(8,128)(2,1)S(1)}) custom-call(s32[8]{0:T(128)S(1)} %copy-done.11, f32[2,40,128]{2,1,0:T(8,128)S(1)} %table.1.refs_1_, bf16[8,16,16,128]{3,2,1,0:T(8,128)(2,1)S(1)} %copy-done.2, ...), custom_call_target="tpu_custom_call" | custom-call | flops 1024 | bytes 1024 | tf_op jit(solution)/shard_map/weight/pallas_call | solution.py:548
  72.0 6.9 %backward.1 = (f32[8,128,128]{2,1,0:T(8,128)S(1)}, f32[8,128,128]{2,1,0:T(8,128)}, f32[16,16,128]{2,1,0:T(8,128)}) custom-call(s32[8]{0:T(128)S(1)} %copy-done.11, f32[2,40,128]{2,1,0:T(8,128)S(1)} %table.1.refs_1_, bf16[9,768,256]{2,1,0:T(8,128)(2,1)S(1)} %turn.1.weight, bf16[8,16,16,128]{3,2,1,0:T(8,128)(2,1)S(1)} %copy-done.2, ...), custom_call_target="tpu_custom_call" | custom-call | flops 1024 | bytes 1024 | tf_op jit(solution)/shard_map/backward/pallas_call | solution.py:572
  78.9 5.6 %forward.1 = (bf16[8,8,16,128]{3,2,1,0:T(8,128)(2,1)S(1)}, bf16[8,8,16,128]{3,2,1,0:T(8,128)(2,1)S(1)}) custom-call(s32[8]{0:T(128)S(1)} %copy-done.11, f32[2,40,128]{2,1,0:T(8,128)S(1)} %table.1.refs_1_, bf16[9,768,256]{2,1,0:T(8,128)(2,1)S(1)} %bitcast.10, bf16[8,16,16,128]{3,2,1,0:T(8,128)(2,1)S(1)} %copy-done.2, ...), custom_call_target="tpu_custom_call" | custom-call | flops 1024 | bytes 1024 | tf_op jit(solution)/shard_map/forward/pallas_call | solution.py:586
  84.6 1.1 collective-permute-start.16
  87.0 7.3 %all-to-all-start.1 = ((f32[16,16,128]{2,1,0:T(8,128)}), f32[16,16,128]{2,1,0:T(8,128)}, u32[]{:S(2)}, u32[]{:S(2)}) async-start(f32[16,16,128]{2,1,0:T(8,128)} %get-tuple-element.46), calls=%async_computation.1 | async-start | bytes 262144 | tf_op jit(solution)/shard_map/all_to_all | solution.py:582
  95.5 10.2 %collective-permute-done.17.refs_1_ = bf16[27,32,128]{2,1,0:T(8,128)(2,1)S(1)} collective-permute-done((bf16[27,32,128]{2,1,0:T(8,128)(2,1)S(1)}, bf16[27,32,128]{2,1,0:T(8,128)(2,1)S(1)}, u32[]{:S(2)}, u32[]{:S(2)}) %collective-permute-start.17) | collective-permute-done | bytes 221216 | tf_op jit(solution)/shard_map/ppermute | solution.py:603
  105.7 2.6 %collective-permute-done.18.refs_2_ = bf16[27,32,128]{2,1,0:T(8,128)(2,1)S(1)} collective-permute-done((bf16[27,32,128]{2,1,0:T(8,128)(2,1)S(1)}, bf16[27,32,128]{2,1,0:T(8,128)(2,1)S(1)}, u32[]{:S(2)}, u32[]{:S(2)}) %collective-permute-start.18) | collective-permute-done | bytes 221216 | tf_op jit(solution)/shard_map/ppermute | solution.py:603
  111.4 2.8 %finish.1 = (bf16[8,16,16,128]{3,2,1,0:T(8,128)(2,1)}, f32[8,128]{1,0:T(8,128)S(1)}) custom-call(s32[8]{0:T(128)S(1)} %copy-done.12, f32[2,40,128]{2,1,0:T(8,128)S(1)} %copy-done.9, f32[16,16,128]{2,1,0:T(8,128)} %all-to-all-done.1.got, bf16[8,16,16,128]{3,2,1,0:T(8,128)(2,1)S(1)} %copy-done.3, f32[8,128,128]{2,1,0:T(8,128)S(1)} %get-tuple-element.55.keep, ...), custom_call_target="tpu_custom_call" | custom-call | flops 1024 | bytes 1024 | tf_op jit(solution)/shard_map/finish/pallas_call | solution.py:609
  (68 shorter events, 17.3 us)
Async XLA Ops:
  9.1 22.6 %all-to-all-start = ((f32[16,24,128]{2,1,0:T(8,128)}), f32[16,24,128]{2,1,0:T(8,128)S(1)}, u32[]{:S(2)}, u32[]{:S(2)}) async-start(f32[16,24,128]{2,1,0:T(8,128)} %stat.1), calls=%async_computation | async-start | bytes 393216 | tf_op jit(solution)/shard_map/all_to_all | solution.py:529
  15.7 16.6 %collective-permute-start.3 = (bf16[66,16,128]{2,1,0:T(8,128)(2,1)S(1)}, bf16[66,16,128]{2,1,0:T(8,128)(2,1)S(1)}, u32[]{:S(2)}, u32[]{:S(2)}) collective-permute-start(bf16[66,16,128]{2,1,0:T(8,128)(2,1)S(1)} %get-tuple-element.35), channel_id=1, source_target_pairs={{0,4},{4,8},{8,12},{12,0},{1,5},{5,9},{9,13},{13,1},{2,6},{6,10},{... | collective-permute-start | bytes 811016 | tf_op jit(solution)/shard_map/ppermute | solution.py:521
  16.8 31.6 %collective-permute-start = (bf16[8,16,16,128]{3,2,1,0:T(8,128)(2,1)}, bf16[8,16,16,128]{3,2,1,0:T(8,128)(2,1)S(1)}, u32[]{:S(2)}, u32[]{:S(2)}) collective-permute-start(bf16[8,16,16,128]{3,2,1,0:T(8,128)(2,1)} %video.4), channel_id=1, source_target_pairs={{0,2},{2,0},{1,3},{3,1},{4,6},{6,4},{5,7},{7,5},{8,10},{10,8},{9,1... | collective-permute-start | bytes 1572872 | tf_op jit(solution)/shard_map/ppermute | solution.py:534
  17.1 18.0 %collective-permute-start.7 = (bf16[34,16,128]{2,1,0:T(8,128)(2,1)S(1)}, bf16[34,16,128]{2,1,0:T(8,128)(2,1)S(1)}, u32[]{:S(2)}, u32[]{:S(2)}) collective-permute-start(bf16[34,16,128]{2,1,0:T(8,128)(2,1)S(1)} %get-tuple-element.37), channel_id=1, source_target_pairs={{0,8},{4,12},{8,0},{12,4},{1,9},{5,13},{9,1},{13,5},{2,10},{6,14},... | collective-permute-start | bytes 417800 | tf_op jit(solution)/shard_map/ppermute | solution.py:521
  18.1 18.7 %collective-permute-start.8 = (bf16[34,16,128]{2,1,0:T(8,128)(2,1)S(1)}, bf16[34,16,128]{2,1,0:T(8,128)(2,1)S(1)}, u32[]{:S(2)}, u32[]{:S(2)}) collective-permute-start(bf16[34,16,128]{2,1,0:T(8,128)(2,1)S(1)} %get-tuple-element.38), channel_id=1, source_target_pairs={{0,12},{4,0},{8,4},{12,8},{1,13},{5,1},{9,5},{13,9},{2,14},{6,2},{... | collective-permute-start | bytes 417800 | tf_op jit(solution)/shard_map/ppermute | solution.py:521
  31.7 5.3 %collective-permute-start.9 = (bf16[34,16,128]{2,1,0:T(8,128)(2,1)S(1)}, bf16[34,16,128]{2,1,0:T(8,128)(2,1)S(1)}, u32[]{:S(2)}, u32[]{:S(2)}) collective-permute-start(bf16[34,16,128]{2,1,0:T(8,128)(2,1)S(1)} %get-tuple-element.39.refs_8_.refs_0_), channel_id=1, source_target_pairs={{0,2},{2,0},{1,3},{3,1},{4,6},{6,4},{5,7},{7,5},{8,10},{10,8},{9,1... | collective-permute-start | bytes 417800 | tf_op jit(solution)/shard_map/ppermute | solution.py:537
  32.3 15.2 %collective-permute-start.5 = (bf16[66,16,128]{2,1,0:T(8,128)(2,1)S(1)}, bf16[66,16,128]{2,1,0:T(8,128)(2,1)S(1)}, u32[]{:S(2)}, u32[]{:S(2)}) collective-permute-start(bf16[66,16,128]{2,1,0:T(8,128)(2,1)S(1)} %collective-permute-done.3.refs_9_.refs_1_.refs_6_), channel_id=1, source_target_pairs={{0,2},{2,0},{1,3},{3,1},{4,6},{6,4},{5,7},{7,5},{8,10},{10,8},{9,1... | collective-permute-start | bytes 811016 | tf_op jit(solution)/shard_map/ppermute | solution.py:537
  35.1 15.8 %collective-permute-start.1 = (bf16[8,16,16,128]{3,2,1,0:T(8,128)(2,1)}, bf16[8,16,16,128]{3,2,1,0:T(8,128)(2,1)S(1)}, u32[]{:S(2)}, u32[]{:S(2)}) collective-permute-start(bf16[8,16,16,128]{3,2,1,0:T(8,128)(2,1)} %video.4), channel_id=1, source_target_pairs={{0,1},{1,0},{2,3},{3,2},{4,5},{5,4},{6,7},{7,6},{8,9},{9,8},{10,11... | collective-permute-start | bytes 1572872 | tf_op jit(solution)/shard_map/ppermute | solution.py:51
  36.8 7.7 %collective-permute-start.10 = (bf16[34,16,128]{2,1,0:T(8,128)(2,1)S(1)}, bf16[34,16,128]{2,1,0:T(8,128)(2,1)S(1)}, u32[]{:S(2)}, u32[]{:S(2)}) collective-permute-start(bf16[34,16,128]{2,1,0:T(8,128)(2,1)S(1)} %collective-permute-done.7.refs_10_.refs_2_), channel_id=1, source_target_pairs={{0,2},{2,0},{1,3},{3,1},{4,6},{6,4},{5,7},{7,5},{8,10},{10,8},{9,1... | collective-permute-start | bytes 417800 | tf_op jit(solution)/shard_map/ppermute | solution.py:537
  37.1 10.4 %collective-permute-start.11 = (bf16[34,16,128]{2,1,0:T(8,128)(2,1)S(1)}, bf16[34,16,128]{2,1,0:T(8,128)(2,1)S(1)}, u32[]{:S(2)}, u32[]{:S(2)}) collective-permute-start(bf16[34,16,128]{2,1,0:T(8,128)(2,1)S(1)} %collective-permute-done.8.refs_11_.refs_3_), channel_id=1, source_target_pairs={{0,2},{2,0},{1,3},{3,1},{4,6},{6,4},{5,7},{7,5},{8,10},{10,8},{9,1... | collective-permute-start | bytes 417800 | tf_op jit(solution)/shard_map/ppermute | solution.py:537
  47.7 24.3 %copy-start.6 = (bf16[8,18,16,128]{3,2,1,0:T(8,128)(2,1)}, bf16[8,18,16,128]{3,2,1,0:T(8,128)(2,1)S(1)}, u32[]{:S(2)}) copy-start(bf16[8,18,16,128]{3,2,1,0:T(8,128)(2,1)S(1)} %get-tuple-element.44.up) | copy-start | bytes 1769476
  47.7 24.2 %collective-permute-start.12 = (bf16[8,18,16,128]{3,2,1,0:T(8,128)(2,1)S(1)}, bf16[8,18,16,128]{3,2,1,0:T(8,128)(2,1)S(1)}, u32[]{:S(2)}, u32[]{:S(2)}) collective-permute-start(bf16[8,18,16,128]{3,2,1,0:T(8,128)(2,1)S(1)} %get-tuple-element.44.up), channel_id=1, source_target_pairs={{0,1},{1,0},{2,3},{3,2},{4,5},{5,4},{6,7},{7,6},{8,9},{9,8},{10,11... | collective-permute-start | bytes 1769480 | tf_op jit(solution)/shard_map/ppermute | solution.py:51
  48.4 12.2 %collective-permute-start.2 = (bf16[8,16,16,128]{3,2,1,0:T(8,128)(2,1)S(1)}, bf16[8,16,16,128]{3,2,1,0:T(8,128)(2,1)S(1)}, u32[]{:S(2)}, u32[]{:S(2)}) collective-permute-start(bf16[8,16,16,128]{3,2,1,0:T(8,128)(2,1)S(1)} %collective-permute-done.refs_3_.refs_2_.refs_4_), channel_id=1, source_target_pairs={{0,1},{1,0},{2,3},{3,2},{4,5},{5,4},{6,7},{7,6},{8,9},{9,8},{10,11... | collective-permute-start | bytes 1572872 | tf_op jit(solution)/shard_map/ppermute | solution.py:51
  48.5 6.9 %collective-permute-start.13 = (bf16[2,18,16,128]{3,2,1,0:T(8,128)(2,1)S(1)}, bf16[2,18,16,128]{3,2,1,0:T(8,128)(2,1)S(1)}, u32[]{:S(2)}, u32[]{:S(2)}) collective-permute-start(bf16[2,18,16,128]{3,2,1,0:T(8,128)(2,1)S(1)} %get-tuple-element.45), channel_id=1, source_target_pairs={{4,0},{8,4},{12,8},{5,1},{9,5},{13,9},{6,2},{10,6},{14,10},{7,3},{... | collective-permute-start | bytes 442376 | tf_op jit(solution)/shard_map/ppermute | solution.py:569
  50.4 10.1 %collective-permute-start.4 = (bf16[66,16,128]{2,1,0:T(8,128)(2,1)S(1)}, bf16[66,16,128]{2,1,0:T(8,128)(2,1)S(1)}, u32[]{:S(2)}, u32[]{:S(2)}) collective-permute-start(bf16[66,16,128]{2,1,0:T(8,128)(2,1)S(1)} %collective-permute-done.3.refs_9_.refs_1_.refs_6_), channel_id=1, source_target_pairs={{0,1},{1,0},{2,3},{3,2},{4,5},{5,4},{6,7},{7,6},{8,9},{9,8},{10,11... | collective-permute-start | bytes 811016 | tf_op jit(solution)/shard_map/ppermute | solution.py:51
  50.9 9.7 %collective-permute-start.6 = (bf16[66,16,128]{2,1,0:T(8,128)(2,1)S(1)}, bf16[66,16,128]{2,1,0:T(8,128)(2,1)S(1)}, u32[]{:S(2)}, u32[]{:S(2)}) collective-permute-start(bf16[66,16,128]{2,1,0:T(8,128)(2,1)S(1)} %collective-permute-done.5.refs_13_.refs_5_.refs_9_.refs_8_.refs_10_), channel_id=1, source_target_pairs={{0,1},{1,0},{2,3},{3,2},{4,5},{5,4},{6,7},{7,6},{8,9},{9,8},{10,11... | collective-permute-start | bytes 811016 | tf_op jit(solution)/shard_map/ppermute | solution.py:51
  55.4 16.6 %collective-permute-start.14 = (bf16[2,18,16,128]{3,2,1,0:T(8,128)(2,1)S(1)}, bf16[2,18,16,128]{3,2,1,0:T(8,128)(2,1)S(1)}, u32[]{:S(2)}, u32[]{:S(2)}) collective-permute-start(bf16[2,18,16,128]{3,2,1,0:T(8,128)(2,1)S(1)} %collective-permute-done.13.next_own), channel_id=1, source_target_pairs={{0,1},{1,0},{2,3},{3,2},{4,5},{5,4},{6,7},{7,6},{8,9},{9,8},{10,11... | collective-permute-start | bytes 442376 | tf_op jit(solution)/shard_map/ppermute | solution.py:51
  60.6 18.3 %copy-start.8 = (f32[2,40,128]{2,1,0:T(8,128)}, f32[2,40,128]{2,1,0:T(8,128)S(1)}, u32[]{:S(2)}) copy-start(f32[2,40,128]{2,1,0:T(8,128)S(1)} %table.1.refs_1_) | copy-start | bytes 122884
  84.5 10.1 %collective-permute-start.15 = (bf16[8,8,16,128]{3,2,1,0:T(8,128)(2,1)S(1)}, bf16[8,8,16,128]{3,2,1,0:T(8,128)(2,1)S(1)}, u32[]{:S(2)}, u32[]{:S(2)}) collective-permute-start(bf16[8,8,16,128]{3,2,1,0:T(8,128)(2,1)S(1)} %get-tuple-element.49), channel_id=1, source_target_pairs={{0,1},{1,0},{2,3},{3,2},{4,5},{5,4},{6,7},{7,6},{8,9},{9,8},{10,11... | collective-permute-start | bytes 786440 | tf_op jit(solution)/shard_map/ppermute | solution.py:51
  84.6 10.9 %collective-permute-start.16 = (bf16[27,32,128]{2,1,0:T(8,128)(2,1)S(1)}, bf16[27,32,128]{2,1,0:T(8,128)(2,1)S(1)}, u32[]{:S(2)}, u32[]{:S(2)}) collective-permute-start(bf16[27,32,128]{2,1,0:T(8,128)(2,1)S(1)} %get-tuple-element.51), channel_id=1, source_target_pairs={{0,4},{4,8},{8,12},{12,0},{1,5},{5,9},{9,13},{13,1},{2,6},{6,10},{... | collective-permute-start | bytes 663560 | tf_op jit(solution)/shard_map/ppermute | solution.py:603
  85.7 20.0 %collective-permute-start.17 = (bf16[27,32,128]{2,1,0:T(8,128)(2,1)S(1)}, bf16[27,32,128]{2,1,0:T(8,128)(2,1)S(1)}, u32[]{:S(2)}, u32[]{:S(2)}) collective-permute-start(bf16[27,32,128]{2,1,0:T(8,128)(2,1)S(1)} %get-tuple-element.52), channel_id=1, source_target_pairs={{0,8},{4,12},{8,0},{12,4},{1,9},{5,13},{9,1},{13,5},{2,10},{6,14},... | collective-permute-start | bytes 663560 | tf_op jit(solution)/shard_map/ppermute | solution.py:603
  86.8 21.6 %collective-permute-start.18 = (bf16[27,32,128]{2,1,0:T(8,128)(2,1)S(1)}, bf16[27,32,128]{2,1,0:T(8,128)(2,1)S(1)}, u32[]{:S(2)}, u32[]{:S(2)}) collective-permute-start(bf16[27,32,128]{2,1,0:T(8,128)(2,1)S(1)} %get-tuple-element.53), channel_id=1, source_target_pairs={{0,12},{4,0},{8,4},{12,8},{1,13},{5,1},{9,5},{13,9},{2,14},{6,2},{... | collective-permute-start | bytes 663560 | tf_op jit(solution)/shard_map/ppermute | solution.py:603
  87.0 23.8 %all-to-all-start.1 = ((f32[16,16,128]{2,1,0:T(8,128)}), f32[16,16,128]{2,1,0:T(8,128)}, u32[]{:S(2)}, u32[]{:S(2)}) async-start(f32[16,16,128]{2,1,0:T(8,128)} %get-tuple-element.46), calls=%async_computation.1 | async-start | bytes 262144 | tf_op jit(solution)/shard_map/all_to_all | solution.py:582
  94.3 16.5 %collective-permute-start.19 = (f32[8,128,128]{2,1,0:T(8,128)}, f32[8,128,128]{2,1,0:T(8,128)}, u32[]{:S(2)}, u32[]{:S(2)}) collective-permute-start(f32[8,128,128]{2,1,0:T(8,128)} %get-tuple-element.56), channel_id=1, source_target_pairs={{0,1},{1,0},{2,3},{3,2},{4,5},{5,4},{6,7},{7,6},{8,9},{9,8},{10,11... | collective-permute-start | bytes 1572872 | tf_op jit(solution)/shard_map/ppermute | solution.py:51
  (16 other events, 23.9 us)

commit v4 on v3

--- a/solution.py
+++ b/solution.py
@@ -16,13 +16,14 @@
 
 
 ANY = pl.BlockSpec(memory_space=pl.ANY)
+HB = pl.BlockSpec(memory_space=pltpu.HBM)
 
 
 def after(value, *others):
     return lax.optimization_barrier((value, *others))[0]
 
 
-def call(body, out_shape, in_specs, scratch=(), name=None, room=24, where=VM, work=1024):
+def call(body, out_shape, in_specs, scratch=(), name=None, room=20, where=VM, work=1024):
     return pl.pallas_call(
         body,
         out_shape=out_shape,
@@ -89,10 +90,25 @@
     return (iota((chans, chans), 0) // size == iota((chans, chans), 1) // size).astype(F32)
 
 
-def pack_body(peers, cap, frames, grad, video, *refs):
-    outs, names, sem = refs[:peers], refs[peers], refs[peers + 1]
-    slots = frames.shape[0]
-    rows = grad.shape[1]
+def split(value):
+    parts = []
+    for _ in range(3):
+        part = value.astype(BF16)
+        parts.append(part)
+        value = value - part.astype(F32)
+    return parts
+
+
+def pack_body(peers, cap, size, frames, grad, video_far, *refs):
+    outs = refs[:peers]
+    names, video, stats, sem, far, done = refs[peers:]
+    slots, rows, cols, chans = grad.shape
+    cells = rows * cols
+    loads = [
+        pltpu.make_async_copy(video_far.at[t], video.at[t], far.at[t]) for t in range(slots)
+    ]
+    for load in loads:
+        load.start()
     tm = lax.axis_index("tm")
     number = [frames[i] for i in range(slots)]
     step = [lax.rem(lax.div(n, slots) - tm + peers, peers) for n in number]
@@ -122,15 +138,32 @@
             ]
             copies[-2].start()
             copies[-1].start()
+    base = cap * (rows + 1)
     for i in range(2):
         copies.append(
             pltpu.make_async_copy(
-                video.at[slots - 2 + i],
-                outs[1].at[pl.ds(cap * (rows + 1) + i * rows, rows)],
+                video_far.at[slots - 2 + i],
+                outs[1].at[pl.ds(base + 3 + i * rows, rows)],
                 sem.at[2 * peers * cap + i],
             )
         )
         copies[-1].start()
+    average = group_matrix(chans, size) * (1.0 / size)
+    sums = []
+    for t in range(slots):
+        loads[t].wait()
+        sums.append(jnp.sum(video[t].astype(F32).reshape(cells, chans), axis=0, keepdims=True))
+    mean = fdot(jnp.concatenate(sums, axis=0) * (1.0 / cells), average)
+    squares = []
+    for t in range(slots):
+        apart = video[t].astype(F32).reshape(cells, chans) - mean[t : t + 1]
+        squares.append(jnp.sum(apart * apart, axis=0, keepdims=True))
+    var = fdot(jnp.concatenate(squares, axis=0) * (1.0 / cells), average)
+    for n, part in enumerate(split(jnp.concatenate([mean, var], axis=0))):
+        stats[n] = part
+    for k in range(peers):
+        copies.append(pltpu.make_async_copy(stats, outs[k].at[pl.ds(base, 3)], done.at[k]))
+        copies[-1].start()
     for copy in copies:
         copy.wait()
 
@@ -141,64 +174,10 @@
     ]
 
 
-def stat_body(size, video, gain, bias, out):
-    frames, rows, cols, chans = video.shape
-    cells = rows * cols
-    average = group_matrix(chans, size) * (1.0 / size)
-    sums = [
-        jnp.sum(video[t].astype(F32).reshape(cells, chans), axis=0, keepdims=True)
-        for t in range(frames)
-    ]
-    mean = fdot(jnp.concatenate(sums, axis=0) * (1.0 / cells), average)
-    squares = []
-    for t in range(frames):
-        apart = video[t].astype(F32).reshape(cells, chans) - mean[t : t + 1]
-        squares.append(jnp.sum(apart * apart, axis=0, keepdims=True))
-    var = fdot(jnp.concatenate(squares, axis=0) * (1.0 / cells), average)
-    rest = jnp.concatenate(
-        [gain[...], bias[...], jnp.zeros((6, chans), F32)], axis=0
-    )
-    whole = jnp.concatenate([mean, var, rest], axis=0)
-    for i in range(out.shape[0]):
-        out[i] = whole
-
-
 def turn_body(weight, out):
     for i in range(9):
         for col in range(3):
             out[i, col * 256 : (col + 1) * 256] = weight[i, col * 256 : (col + 1) * 256].T
-
-
-def table_body(lengths, got, out):
-    peers, bands = got.shape[:2]
-    frames = (got.shape[3] - 8) // 2
-    first = lax.axis_index("tm") * frames
-    count = peers * frames
-    clip = clip_of(lengths, iota((count, count), 1))
-    inverse = per_clip(lengths, clip, 1.0)
-    same = jnp.where(clip_of(lengths, iota((count, count), 0)) == clip, inverse, 0.0)
-    near = jnp.clip(first - 2 + iota((16, count), 0), 0, count - 1)
-    clip = clip_of(lengths, iota((16, count), 1))
-    inverse = per_clip(lengths, clip, 1.0)
-    picked = jnp.where(clip_of(lengths, near) == clip, inverse, 0.0)
-    for c in range(2):
-        mean = [
-            jnp.concatenate([got[t, h, c, :frames] for t in range(peers)], axis=0)
-            for h in range(bands)
-        ]
-        var = [
-            jnp.concatenate([got[t, h, c, frames : 2 * frames] for t in range(peers)], axis=0)
-            for h in range(bands)
-        ]
-        average = sum(mean[1:], mean[0]) * (1.0 / bands)
-        clip_mean = fdot(same, average)
-        spread = jnp.zeros_like(average)
-        for h in range(bands):
-            apart = mean[h] - clip_mean
-            spread = spread + (var[h] + apart * apart)
-        out[c, :16] = fdot(picked, average)
-        out[c, 16:32] = lax.rsqrt(fdot(picked, spread * (1.0 / bands)) + 1e-06)
-        out[c, 32:] = got[0, 0, c, 2 * frames :]
 
 
 def shifts(value):
@@ -211,7 +190,7 @@
 
 def weight_body(peers, bands, cap, block, *refs):
     refs = list(refs)
-    lengths, table = refs.pop(0), refs.pop(0)
+    lengths, table, table_sib = [refs.pop(0) for _ in range(3)]
     take = lambda n: [refs.pop(0) for _ in range(n)]
     own, sib, prev_sib = take(bands), take(bands), take(bands)
     ups = [take(peers) for _ in range(bands)]
@@ -228,7 +207,7 @@
     channel = iota((chans, width), 0)
     pick_own = (c * chans + channel == wanted).astype(F32)
     pick_sib = ((1 - c) * chans + channel == wanted).astype(F32)
-    lookup = fdot(table[c], pick_own) + fdot(table[1 - c], pick_sib)
+    lookup = fdot(table[...], pick_own) + fdot(table_sib[...], pick_sib)
     pick_own, pick_sib = pick_own.astype(BF16), pick_sib.astype(BF16)
     mean, inv = lookup[:16], lookup[16:32]
     scale = inv * lookup[32:33]
@@ -240,7 +219,7 @@
     for f in range(frames + 2):
         for m in range(bands):
             if f < 2:
-                at = cap * (rows + 1) + f * rows
+                at = cap * (rows + 1) + 3 + f * rows
                 a, b = ups[m][1][at : at + rows], prev_sib[m][at : at + rows]
             else:
                 a, b = own[m][f - 2], sib[m][f - 2]
@@ -293,55 +272,94 @@
     taps(jnp.int32(13), 1)
 
 
-def forward_body(bands, skip, lengths, table, weight, *refs):
-    own, sib, above_own, above_sib, below_own, below_sib = refs[:6]
-    prev_own, prev_sib = refs[6:8]
-    far_prev = refs[8:12]
-    keep, give, active = refs[12:]
-    frames, rows, cols, chans = own.shape
+def both(c, table, table_sib):
+    return (
+        jnp.where(c == 0, table[...], table_sib[...]),
+        jnp.where(c == 0, table_sib[...], table[...]),
+    )
+
+
+def forward_body(bands, skip, lengths, table, table_sib, weight_far, *refs):
+    core, above, below = refs[:2], refs[2:4], refs[4:6]
+    before, before_above, before_below = refs[6:8], refs[8:10], refs[10:12]
+    keep, give, active, here, weight, sem = refs[12:]
+    frames, rows, cols, chans = core[0].shape
     half = rows // 2
     tm, h, c = lax.axis_index("tm"), lax.axis_index("height"), lax.axis_index("chan")
     first = tm * frames
+    load = pltpu.make_async_copy(weight_far, weight, sem.at[12])
+    near, place = pl.ds((half - 1) * c, half + 1), pl.ds(1 - c, half + 1)
+    outside = pl.ds((half + 1) * c, 1)
+    waits = []
+    for n in range(2):
+        waits.append(
+            pltpu.make_async_copy(
+                core[n].at[:, near], here.at[n, pl.ds(2, frames), place], sem.at[6 * n]
+            )
+        )
+        waits[-1].start()
+        for f in range(2):
+            line = skip + f * rows
+            waits.append(
+                pltpu.make_async_copy(
+                    before[n].at[pl.ds(line + (half - 1) * c, half + 1)],
+                    here.at[n, f, place],
+                    sem.at[6 * n + 1 + f],
+                )
+            )
+            waits[-1].start()
+        for side, rim, rim_before, row in (
+            (0, above[n], before_above[n], rows - 1),
+            (1, below[n], before_below[n], 0),
+        ):
+            edges = [
+                pltpu.make_async_copy(
+                    rim.at[:, pl.ds(row, 1)],
+                    here.at[n, pl.ds(2, frames), outside],
+                    sem.at[6 * n + 3],
+                )
+            ]
+            for f in range(2):
+                edges.append(
+                    pltpu.make_async_copy(
+                        rim_before.at[pl.ds(skip + f * rows + row, 1)],
+                        here.at[n, f, outside],
+                        sem.at[6 * n + 4 + f],
+                    )
+                )
+
+            @pl.when(c == side)
+            def _():
+                for edge in edges:
+                    edge.start()
+
+        waits += edges
+    load.start()
+    for wait in waits:
+        wait.wait()
     outer = jnp.logical_or(
         jnp.logical_and(c == 0, h > 0), jnp.logical_and(c == 1, h < bands - 1)
     )
     begin = [start_of(lengths, first + t) for t in range(frames)]
-
-    def put(f, at, lines, value_own, value_sib, ok):
-        a, b = value_own.astype(F32), value_sib.astype(F32)
+    tables = both(c, table, table_sib)
+    cells = (half + 2) * cols
+    line = iota((cells, chans), 0)
+    rim = jnp.logical_or(
+        jnp.logical_and(line < cols, c == 0), jnp.logical_and(line >= cells - cols, c == 1)
+    )
+    ok = jnp.logical_or(jnp.logical_not(rim), outer)
+    for f in range(frames + 2):
+        a, b = [here[n, f].reshape(cells, chans).astype(F32) for n in range(2)]
         for side, x in enumerate((jnp.where(c == 0, a, b), jnp.where(c == 0, b, a))):
-            mean = table[side, f : f + 1]
-            scale = table[side, 16 + f : 17 + f] * table[side, 32:33]
-            v = (x - mean) * scale + table[side, 33:34]
-            v = v * sigmoid(v)
-            if ok is not None:
-                v = jnp.where(ok, v, 0.0)
-            before, after = shifts(v)
-            for n, w in enumerate((before, v, after)):
+            info = tables[side]
+            scale = info[16 + f : 17 + f] * info[32:33]
+            v = (x - info[f : f + 1]) * scale + info[33:34]
+            v = jnp.where(ok, v * sigmoid(v), 0.0)
+            left, right = shifts(v)
+            for n, w in enumerate((left, v, right)):
                 lane = n * 2 * chans + side * chans
-                active[f, at, :, lane : lane + chans] = w.astype(BF16).reshape(lines, cols, chans)
-
-    def edge(up, down):
-        return jnp.where(c == 0, up.astype(F32), down.astype(F32))
-
-    for f in range(frames + 2):
-        if f < 2:
-            base = skip + f * rows
-            near = pl.ds(base + (half - 1) * c, half + 1)
-            here = [v[near] for v in (prev_own, prev_sib)]
-            up = [v[base + rows - 1] for v in far_prev[:2]]
-            down = [v[base] for v in far_prev[2:]]
-        else:
-            near = pl.ds((half - 1) * c, half + 1)
-            here = [v[f - 2, near] for v in (own, sib)]
-            up = [v[f - 2, rows - 1] for v in (above_own, above_sib)]
-            down = [v[f - 2, 0] for v in (below_own, below_sib)]
-        here = [v.reshape((half + 1) * cols, chans) for v in here]
-        put(f, pl.ds(1 - c, half + 1), half + 1, here[0], here[1], None)
-        put(
-            f, pl.ds((half + 1) * c, 1), 1,
-            edge(up[0], down[0]), edge(up[1], down[1]), outer,
-        )
+                active[f, :, :, lane : lane + chans] = w.astype(BF16).reshape(half + 2, cols, chans)
+    load.wait()
     batch = 4
     for t0 in range(0, frames, batch):
         mixed = [jnp.zeros((half * cols, 2 * chans), F32) for _ in range(batch)]
@@ -355,20 +373,53 @@
                     mixed[q] = mixed[q] + bdot(patch, w)
         for q in range(batch):
             t = t0 + q
-            mine = pl.ds(c * half, half)
+            mine = slice(1, half + 1)
             left, right = mixed[q][:, :chans], mixed[q][:, chans:]
             shape = (half, cols, chans)
             for out, value, x in (
-                (keep, jnp.where(c == 0, left, right), own[t, mine]),
-                (give, jnp.where(c == 0, right, left), sib[t, mine]),
+                (keep, jnp.where(c == 0, left, right), here[0, t + 2, mine]),
+                (give, jnp.where(c == 0, right, left), here[1, t + 2, mine]),
             ):
                 x = x.reshape(half * cols, chans).astype(F32)
                 out[t] = (x + value).astype(BF16).reshape(shape)
 
 
-def order_body(peers, bands, cap, *refs):
-    own, above, below = refs[:peers], refs[peers : 2 * peers], refs[2 * peers : 3 * peers]
-    out, first = refs[3 * peers :]
+def order_body(peers, bands, cap, lengths, gain, bias, *refs):
+    pieces = [refs[m * peers : (m + 1) * peers] for m in range(bands)]
+    out, first, table = refs[bands * peers :]
+    own, above, below = pieces[0], pieces[1], pieces[bands - 1]
+    frames = out.shape[0]
+    base = cap * (out.shape[1] - 1)
+    tm = lax.axis_index("tm")
+    count = peers * frames
+
+    def frame_of(index):
+        slab = lax.rem(tm - lax.div(index, frames) + peers, peers)
+        return slab * frames + lax.rem(index, frames)
+
+    means, spreads = [], []
+    for m in range(bands):
+        stats = [
+            sum(piece[base + n].astype(F32) for n in (2, 1, 0)) for piece in pieces[m]
+        ]
+        means.append(jnp.concatenate([v[:frames] for v in stats], axis=0))
+        spreads.append(jnp.concatenate([v[frames:] for v in stats], axis=0))
+    clip = clip_of(lengths, frame_of(iota((count, count), 1)))
+    inverse = per_clip(lengths, clip, 1.0)
+    same = jnp.where(clip_of(lengths, frame_of(iota((count, count), 0))) == clip, inverse, 0.0)
+    near = jnp.clip(tm * frames - 2 + iota((16, count), 0), 0, count - 1)
+    picked = jnp.where(clip_of(lengths, near) == clip[:16], inverse[:16], 0.0)
+    average = sum(means[1:], means[0]) * (1.0 / bands)
+    clip_mean = fdot(same, average)
+    spread = jnp.zeros_like(average)
+    for m in range(bands):
+        apart = means[m] - clip_mean
+        spread = spread + (spreads[m] + apart * apart)
+    table[:16] = fdot(picked, average)
+    table[16:32] = lax.rsqrt(fdot(picked, spread * (1.0 / bands)) + 1e-06)
+    table[32:33] = gain[...]
+    table[33:34] = bias[...]
+    table[34:] = jnp.zeros((6, table.shape[1]), F32)
     rows = out.shape[1] - 2
     h = lax.axis_index("height")
     names = [named(own[k], rows, cap) for k in range(peers)]
@@ -388,7 +439,7 @@
     first[...] = out[:2]
 
 
-def backward_body(peers, lengths, table, weight, own, sib, up, up_sib, next_own, next_sib, *refs):
+def backward_body(peers, lengths, table, table_sib, weight, own, sib, up, up_sib, next_own, next_sib, *refs):
     keep, give, sums, spatial, total = refs
     frames, rows, cols, chans = own.shape
     half = rows // 2
@@ -405,6 +456,7 @@
                 at = n * 2 * chans + side * chans
                 spatial[f, :, :, at : at + chans] = w.astype(BF16).reshape(half + 2, cols, chans)
     total[...] = jnp.zeros_like(total)
+    tables = both(c, table, table_sib)
 
     begin = [start_of(lengths, first + t) for t in range(frames + 2)]
     for a in range(3):
@@ -429,8 +481,9 @@
         for t in range(frames):
             a, b = own[t, mine].astype(F32), sib[t, mine].astype(F32)
             x = jnp.where((c == 0) == (side == 0), a, b).reshape(cells, chans)
-            hat = (x - table[side, t + 2 : t + 3]) * table[side, t + 18 : t + 19]
-            v = hat * table[side, 32:33] + table[side, 33:34]
+            info = tables[side]
+            hat = (x - info[t + 2 : t + 3]) * info[t + 18 : t + 19]
+            v = hat * info[32:33] + info[33:34]
             s = sigmoid(v)
             grad = total[t, :, side * chans : (side + 1) * chans] * s * (1.0 + v * (1.0 - s))
             total[t, :, side * chans : (side + 1) * chans] = grad
@@ -467,7 +520,7 @@
     tm, c = lax.axis_index("tm"), lax.axis_index("chan")
     first_frame = tm * frames
     whole = jnp.sum(got[...], axis=0)
-    gain = table[c, 32:33]
+    gain = table[32:33]
     small[0:1] = jnp.sum(whole[NCLIPS:], axis=0, keepdims=True)
     small[1:2] = jnp.sum(whole[:NCLIPS], axis=0, keepdims=True)
     small[2:] = jnp.zeros((6, chans), F32)
@@ -478,10 +531,10 @@
     first = fdot(spread, fdot(whole[:NCLIPS] * gain, group))
     second = fdot(spread, fdot(whole[NCLIPS:] * gain, group))
     for t in range(frames):
-        inv = table[c, t + 18 : t + 19]
+        inv = table[t + 18 : t + 19]
         for grads, at in ((keep, c * half), (other, (1 - c) * half)):
             x = video[t, pl.ds(at, half)].reshape(cells, chans).astype(F32)
-            hat = (x - table[c, t + 2 : t + 3]) * inv
+            hat = (x - table[t + 2 : t + 3]) * inv
             part = inv * (grads[t] * gain - first[t : t + 1] - hat * second[t : t + 1])
             u = up[t, pl.ds(at + 1, half)].reshape(cells, chans).astype(F32)
             out[t, pl.ds(at, half)] = (u + part).astype(BF16).reshape(half, cols, chans)
@@ -504,67 +557,69 @@
     devices = peers * bands * 2
     sds = jax.ShapeDtypeStruct
 
-    skip = cap * (rows + 1)
+    skip = cap * (rows + 1) + 3
     pieces = call(
-        functools.partial(pack_body, peers, cap),
+        functools.partial(pack_body, peers, cap, size),
         [
             sds((skip + (2 * rows if k == 1 else 0), cols, chans), BF16)
             for k in range(peers)
         ],
-        [SM, ANY, ANY],
+        [SM, HB, HB],
         [
             pltpu.VMEM((peers * cap, cols, chans), BF16),
+            pltpu.VMEM(clip_video.shape, BF16),
+            pltpu.VMEM((3, 2 * frames, chans), BF16),
             pltpu.SemaphoreType.DMA((2 * peers * cap + 2,)),
+            pltpu.SemaphoreType.DMA((frames,)),
+            pltpu.SemaphoreType.DMA((peers,)),
         ],
         name="pack", where=ANY,
     )(packed_frame, packed_grad, clip_video)
     ups = [[pieces[0]] + [lax.ppermute(pieces[k], "tm", ring(peers, k)) for k in range(1, peers)]]
-
-    stats = call(
-        functools.partial(stat_body, size),
-        sds((devices, 2 * frames + 8, chans), F32), [VM, VM, VM],
-        name="stat",
-    )(after(clip_video, pieces[0]), norm_gain[None], norm_bias[None])
-
-    got = lax.all_to_all(stats, everyone, 0, 0)
-    got = got.reshape(peers, bands, 2, 2 * frames + 8, chans)
 
     own = [clip_video]
     for m in range(1, bands):
         own.append(lax.ppermute(after(clip_video, pieces[0]), "height", ring(bands, m)))
     sib = [sibling(v) for v in own]
     for m in range(1, bands):
-        ups.append([lax.ppermute(after(v, got), "height", ring(bands, m)) for v in ups[0]])
+        ready = [v if k == 0 else after(v, own[m]) for k, v in enumerate(ups[0])]
+        ups.append([lax.ppermute(v, "height", ring(bands, m)) for v in ready])
     prev_sib = [sibling(v[1]) for v in ups]
 
     weight = conv_weight.reshape(9, 3 * full, full)
     turned = call(
         turn_body, sds(weight.shape, BF16), [VM], name="turn"
     )(weight)
-    table = call(
-        table_body, sds((2, 40, chans), F32), [SM, VM], name="table"
-    )(clip_lengths, after(got, turned))
+
+    up, up_first, table = call(
+        functools.partial(order_body, peers, bands, cap),
+        [
+            sds((frames, rows + 2, cols, chans), BF16),
+            sds((2, rows + 2, cols, chans), BF16),
+            sds((40, chans), F32),
+        ],
+        [SM] + [VM] * (2 + bands * peers),
+        name="order",
+    )(
+        clip_lengths, norm_gain[None], norm_bias[None], after(ups[0][0], turned),
+        *ups[0][1:], *[v for band in ups[1:] for v in band],
+    )
+    table_sib = sibling(table)
 
     grads = call(
         functools.partial(weight_body, peers, bands, cap, block),
         [sds((27, block, chans), F32)] + [sds((27, block, chans), BF16)] * (peers - 1),
-        [SM] + [VM] * (1 + 3 * bands + peers * bands),
+        [SM] + [VM] * (2 + 3 * bands + peers * bands),
         [
             pltpu.VMEM((3, frames + 2, bands * rows + 2, cols, width), BF16),
             pltpu.VMEM((frames, bands, chans, rows * cols), BF16),
         ],
         name="weight",
     )(
-        clip_lengths, table, *own, *sib, *prev_sib,
+        clip_lengths, table, table_sib, *own, *sib, *prev_sib,
         *[v for band in ups for v in band],
     )
     far = bands - 1
-    up, up_first = call(
-        functools.partial(order_body, peers, bands, cap),
-        [sds((frames, rows + 2, cols, chans), BF16), sds((2, rows + 2, cols, chans), BF16)],
-        [VM] * (3 * peers),
-        name="order",
-    )(*ups[0], *ups[1], *ups[far])
     up_sib = sibling(up)
     next_own = lax.ppermute(up_first, "tm", [(t + 1, t) for t in range(peers - 1)])
     next_sib = sibling(next_own)
@@ -572,13 +627,13 @@
     keep, give, sums = call(
         functools.partial(backward_body, peers),
         [part, part, sds((devices, 2 * NCLIPS, chans), F32)],
-        [SM] + [VM] * 8,
+        [SM] + [VM] * 9,
         [
             pltpu.VMEM((frames + 2, half + 2, cols, 6 * chans), BF16),
             pltpu.VMEM((frames + 1, half * cols, 2 * chans), F32),
         ],
         name="backward",
-    )(clip_lengths, table, after(turned, grads[0]), clip_video, sib[0], up, up_sib, next_own, next_sib)
+    )(clip_lengths, table, table_sib, after(turned, grads[0]), clip_video, sib[0], up, up_sib, next_own, next_sib)
     totals = lax.all_to_all(sums, everyone, 0, 0)
     other = sibling(give)
 
@@ -586,24 +641,22 @@
     block_keep, block_give = call(
         functools.partial(forward_body, bands, skip),
         [part, part],
-        [SM] + [VM] * 14,
-        [pltpu.VMEM((frames + 2, half + 2, cols, 6 * chans), BF16)],
+        [SM, VM, VM] + [HB] * 13,
+        [
+            pltpu.VMEM((frames + 2, half + 2, cols, 6 * chans), BF16),
+            pltpu.VMEM((2, frames + 2, half + 2, cols, chans), BF16),
+            pltpu.VMEM(weight.shape, BF16),
+            pltpu.SemaphoreType.DMA((13,)),
+        ],
         name="forward",
     )(
-        clip_lengths, table, after(weight, sums), own[0], sib[0], own[1], sib[1], own[far], sib[far],
+        clip_lengths, table, table_sib, after(weight, sums), own[0], sib[0], own[1], sib[1], own[far], sib[far],
         ups[0][1], prev_sib[0], ups[1][1], prev_sib[1], ups[far][1], prev_sib[far],
     )
-    block_other = sibling(block_give)
-    block_out = jnp.where(
-        c == 0,
-        jnp.concatenate([block_keep, block_other], axis=1),
-        jnp.concatenate([block_other, block_keep], axis=1),
-    )
-
     terms = [lax.ppermute(grads[k], "tm", ring(peers, k)) for k in range(1, peers)]
     weight_grad = call(
         collect_body, sds((27, block, chans), F32), [VM] * peers, name="collect", work=10**13
-    )(after(grads[0], block_out), *terms)
+    )(after(grads[0], block_give), *terms)
     weight_grad = weight_grad.reshape(3, 3, 3, block, chans)
 
     video_grad, small = call(
@@ -612,6 +665,12 @@
         [SM] + [VM] * 6,
         name="finish",
     )(clip_lengths, table, after(totals, weight_grad), clip_video, keep, other, up)
+    block_other = sibling(after(block_give, small))
+    block_out = jnp.where(
+        c == 0,
+        jnp.concatenate([block_keep, block_other], axis=1),
+        jnp.concatenate([block_other, block_keep], axis=1),
+    )
     return (block_out, video_grad, weight_grad, small[0], small[1])
 
 

time: 116 us -> 100 us (0.86)
  waiting for transfers between devices: 41.7 us -> 16.6 us
  local copies, waits for them, and re-layouts: 9.75 us -> 15.5 us
  Pallas kernels: 33 us -> 36.4 us
    ppermute x3, waiting for transfers between devices: 12.8 us -> 0.01 us  [per_device(): lax.ppermute(grads[k], 'tm', ring(peers, k))]
    all_to_all x1 -> x0, waiting for transfers between devices: 12.3 us -> none  [per_device(): got = lax.all_to_all(stats, everyone, 0, 0)]
    all_to_all x1 -> x0, starting transfers between devices: 6.55 us -> none  [per_device(): got = lax.all_to_all(stats, everyone, 0, 0)]
    unnamed x36 -> x74, local copies, waits for them, and re-layouts: 9.24 us -> 15 us
    ppermute x8 -> x9, starting transfers between devices: 3.7 us -> 9.2 us  [sibling(): return lax.ppermute(value, 'chan', ring(2, 1))]
    ppermute x1, waiting for transfers between devices: 0.01 us -> 5.45 us  [per_device(): lax.ppermute(after(clip_video, pieces[0]), 'height', ring(bands, m))]
    ppermute x4, waiting for transfers between devices: 9.23 us -> 4.83 us  [per_device(): ups.append([lax.ppermute(v, 'height', ring(bands, m)) for v in ready])]
    ppermute x1, waiting for transfers between devices: 4.38 us -> 0.01 us  [per_device(): lax.ppermute(up_first, 'tm', [(t + 1, t) for t in range(peers - 1)])]
  transfers between devices with their start and end apart: 22 -> 22, of which waited for: 8 -> 8; matrix products, arithmetic and copies ran while one was open for 1% -> 1% of each run, Pallas kernels for 12% -> 31%
where the time goes in v4:
time: 100 us; the launch traced here: 98.5 us
  Pallas kernels  36.4 us (36%)
  starting transfers between devices  28.2 us (28%)
  waiting for transfers between devices  16.6 us (17%)
  local copies, waits for them, and re-layouts  15.5 us (16%)
    unnamed x74, local copies, waits for them, and re-layouts  15 us
    pallas_call x1, Pallas kernels, per_device(): call(functools.partial(weight_body, peers, bands, cap, block), [sds((27,...  12.8 us
    ppermute x9, starting transfers between devices, sibling(): return lax.ppermute(value, 'chan', ring(2, 1))  9.2 us
    pallas_call x1, Pallas kernels, per_device(): call(functools.partial(backward_body, peers), [part, part, sds((devices,...  7.16 us
    pallas_call x1, Pallas kernels, per_device(): call(functools.partial(forward_body, bands, skip), [part, part], [SM, VM,...  6.6 us
    all_to_all x1, starting transfers between devices, per_device(): totals = lax.all_to_all(sums, everyone, 0, 0)  5.87 us
    ppermute x1, waiting for transfers between devices, per_device(): lax.ppermute(after(clip_video, pieces[0]), 'height', ring(bands, m))  5.45 us
    ppermute x4, waiting for transfers between devices, per_device(): ups.append([lax.ppermute(v, 'height', ring(bands, m)) for v in ready])  4.83 us
  transfers between devices with their start and end apart: 22, of which 8 were waited for; matrix products, arithmetic and copies ran while one was open for 1% of the time, Pallas kernels for 31%

profile of v4, /device:TPU:15, one launch (start us, length us, event | category | flops | bytes accessed | tf_op | source)
XLA Modules:
  0.0 98.5 jit_solution(12407019298240485830)
XLA Ops:
  2.3 2.9 %pack.1 = (bf16[37,16,128]{2,1,0:T(8,128)(2,1)S(1)}, bf16[69,16,128]{2,1,0:T(8,128)(2,1)S(1)}, bf16[37,16,128]{2,1,0:T(8,128)(2,1)S(1)}, bf16[37,16,128]{2,1,0:T(8,128)(2,1)S(1)}) custom-call(s32[8]{0:T(128)S(1)} %copy-done.30, bf16[8,16,16,128]{3,2,1,0:T(8,128)(2,1)S(1)} %copy-done.20, bf16[8,16,16,128]{3,2,1,0:T(8,128)(2,1)} %video.1), custom_call_target="tpu_custom_call" | custom-call | flops 1024 | bytes 1024 | tf_op jit(solution)/shard_map/pack/pallas_call | solution.py:561
  5.5 1.3 %collective-permute-start = (bf16[69,16,128]{2,1,0:T(8,128)(2,1)S(1)}, bf16[69,16,128]{2,1,0:T(8,128)(2,1)S(1)}, u32[]{:S(2)}, u32[]{:S(2)}) collective-permute-start(bf16[69,16,128]{2,1,0:T(8,128)(2,1)S(1)} %get-tuple-element.35), channel_id=1, source_target_pairs={{0,4},{4,8},{8,12},{12,0},{1,5},{5,9},{9,13},{13,1},{2,6},{6,10},{... | collective-permute-start | bytes 847880 | tf_op jit(solution)/shard_map/ppermute | solution.py:578
  7.9 1.5 %collective-permute-start.2 = (bf16[37,16,128]{2,1,0:T(8,128)(2,1)S(1)}, bf16[37,16,128]{2,1,0:T(8,128)(2,1)S(1)}, u32[]{:S(2)}, u32[]{:S(2)}) collective-permute-start(bf16[37,16,128]{2,1,0:T(8,128)(2,1)S(1)} %get-tuple-element.37), channel_id=1, source_target_pairs={{0,12},{4,0},{8,4},{12,8},{1,13},{5,1},{9,5},{13,9},{2,14},{6,2},{... | collective-permute-start | bytes 454664 | tf_op jit(solution)/shard_map/ppermute | solution.py:578
  9.3 1.2 %collective-permute-start.3 = (bf16[37,16,128]{2,1,0:T(8,128)(2,1)S(1)}, bf16[37,16,128]{2,1,0:T(8,128)(2,1)S(1)}, u32[]{:S(2)}, u32[]{:S(2)}) collective-permute-start(bf16[37,16,128]{2,1,0:T(8,128)(2,1)S(1)} %get-tuple-element.34.refs_0_.refs_9_), channel_id=1, source_target_pairs={{0,2},{2,0},{1,3},{3,1},{4,6},{6,4},{5,7},{7,5},{8,10},{10,8},{9,1... | collective-permute-start | bytes 454664 | tf_op jit(solution)/shard_map/ppermute | solution.py:586
  10.5 2.3 %collective-permute-done.refs_1_.refs_10_.refs_6_ = bf16[69,16,128]{2,1,0:T(8,128)(2,1)S(1)} collective-permute-done((bf16[69,16,128]{2,1,0:T(8,128)(2,1)S(1)}, bf16[69,16,128]{2,1,0:T(8,128)(2,1)S(1)}, u32[]{:S(2)}, u32[]{:S(2)}) %collective-permute-start) | collective-permute-done | bytes 282656 | tf_op jit(solution)/shard_map/ppermute | solution.py:578
  12.8 5.4 %collective-permute-done.4.refs_4_.refs_2_ = bf16[8,16,16,128]{3,2,1,0:T(8,128)(2,1)S(1)} collective-permute-done((bf16[8,16,16,128]{3,2,1,0:T(8,128)(2,1)}, bf16[8,16,16,128]{3,2,1,0:T(8,128)(2,1)S(1)}, u32[]{:S(2)}, u32[]{:S(2)}) %collective-permute-start.4) | collective-permute-done | bytes 524320 | tf_op jit(solution)/shard_map/ppermute | solution.py:582
  18.5 4.7 %collective-permute-start.9 = (bf16[8,16,16,128]{3,2,1,0:T(8,128)(2,1)}, bf16[8,16,16,128]{3,2,1,0:T(8,128)(2,1)S(1)}, u32[]{:S(2)}, u32[]{:S(2)}) collective-permute-start(bf16[8,16,16,128]{3,2,1,0:T(8,128)(2,1)} %video.1), channel_id=1, source_target_pairs={{0,1},{1,0},{2,3},{3,2},{4,5},{5,4},{6,7},{7,6},{8,9},{9,8},{10,11... | collective-permute-start | bytes 1572872 | tf_op jit(solution)/shard_map/ppermute | solution.py:52
  23.5 1.3 %collective-permute-done.2.refs_3_.refs_12_ = bf16[37,16,128]{2,1,0:T(8,128)(2,1)S(1)} collective-permute-done((bf16[37,16,128]{2,1,0:T(8,128)(2,1)S(1)}, bf16[37,16,128]{2,1,0:T(8,128)(2,1)S(1)}, u32[]{:S(2)}, u32[]{:S(2)}) %collective-permute-start.2) | collective-permute-done | bytes 151584 | tf_op jit(solution)/shard_map/ppermute | solution.py:578
  24.8 1.2 %collective-permute-start.6 = (bf16[37,16,128]{2,1,0:T(8,128)(2,1)S(1)}, bf16[37,16,128]{2,1,0:T(8,128)(2,1)S(1)}, u32[]{:S(2)}, u32[]{:S(2)}) collective-permute-start(bf16[37,16,128]{2,1,0:T(8,128)(2,1)S(1)} %collective-permute-done.1.refs_2_.refs_11_), channel_id=1, source_target_pairs={{0,2},{2,0},{1,3},{3,1},{4,6},{6,4},{5,7},{7,5},{8,10},{10,8},{9,1... | collective-permute-start | bytes 454664 | tf_op jit(solution)/shard_map/ppermute | solution.py:586
  26.3 2.0 %copy-done = bf16[3,3,3,256,256]{4,3,2,1,0:T(8,128)(2,1)S(1)} copy-done((bf16[3,3,3,256,256]{4,3,2,1,0:T(8,128)(2,1)S(1)}, bf16[3,3,3,256,256]{4,3,2,1,0:T(8,128)(2,1)}, u32[]{:S(2)}) %copy-start) | copy-done | bytes 3538968
  29.3 1.6 %collective-permute-done.6.refs_6_.refs_15_ = bf16[37,16,128]{2,1,0:T(8,128)(2,1)S(1)} collective-permute-done((bf16[37,16,128]{2,1,0:T(8,128)(2,1)S(1)}, bf16[37,16,128]{2,1,0:T(8,128)(2,1)S(1)}, u32[]{:S(2)}, u32[]{:S(2)}) %collective-permute-start.6) | collective-permute-done | bytes 151584 | tf_op jit(solution)/shard_map/ppermute | solution.py:586
  30.9 3.2 %collective-permute-done.7.refs_7_.refs_16_ = bf16[37,16,128]{2,1,0:T(8,128)(2,1)S(1)} collective-permute-done((bf16[37,16,128]{2,1,0:T(8,128)(2,1)S(1)}, bf16[37,16,128]{2,1,0:T(8,128)(2,1)S(1)}, u32[]{:S(2)}, u32[]{:S(2)}) %collective-permute-start.7) | collective-permute-done | bytes 151584 | tf_op jit(solution)/shard_map/ppermute | solution.py:586
  35.1 1.6 %collective-permute-start.13 = (bf16[8,18,16,128]{3,2,1,0:T(8,128)(2,1)S(1)}, bf16[8,18,16,128]{3,2,1,0:T(8,128)(2,1)S(1)}, u32[]{:S(2)}, u32[]{:S(2)}) collective-permute-start(bf16[8,18,16,128]{3,2,1,0:T(8,128)(2,1)S(1)} %get-tuple-element.45.up), channel_id=1, source_target_pairs={{0,1},{1,0},{2,3},{3,2},{4,5},{5,4},{6,7},{7,6},{8,9},{9,8},{10,11... | collective-permute-start | bytes 1769480 | tf_op jit(solution)/shard_map/ppermute | solution.py:52
  37.3 2.1 %collective-permute-start.14 = (bf16[2,18,16,128]{3,2,1,0:T(8,128)(2,1)S(1)}, bf16[2,18,16,128]{3,2,1,0:T(8,128)(2,1)S(1)}, u32[]{:S(2)}, u32[]{:S(2)}) collective-permute-start(bf16[2,18,16,128]{3,2,1,0:T(8,128)(2,1)S(1)} %get-tuple-element.46), channel_id=1, source_target_pairs={{4,0},{8,4},{12,8},{5,1},{9,5},{13,9},{6,2},{10,6},{14,10},{7,3},{... | collective-permute-start | bytes 442376 | tf_op jit(solution)/shard_map/ppermute | solution.py:624
  40.7 12.8 %weight.1 = (f32[27,32,128]{2,1,0:T(8,128)S(1)}, bf16[27,32,128]{2,1,0:T(8,128)(2,1)}, bf16[27,32,128]{2,1,0:T(8,128)(2,1)}, bf16[27,32,128]{2,1,0:T(8,128)(2,1)}) custom-call(s32[8]{0:T(128)S(1)} %copy-done.29, f32[40,128]{1,0:T(8,128)S(1)} %get-tuple-element.42.refs_1_.table, f32[40,128]{1,0:T(8,128)S(1)} %collective-permute-done.8.refs_2_.table_sib, ...), custom_call_target="tpu_custom_call" | custom-call | flops 1024 | bytes 1024 | tf_op jit(solution)/shard_map/weight/pallas_call | solution.py:609
  53.4 1.4 %collective-permute-start.16 = (bf16[27,32,128]{2,1,0:T(8,128)(2,1)}, bf16[27,32,128]{2,1,0:T(8,128)(2,1)}, u32[]{:S(2)}, u32[]{:S(2)}) collective-permute-start(bf16[27,32,128]{2,1,0:T(8,128)(2,1)} %get-tuple-element.52), channel_id=1, source_target_pairs={{0,4},{4,8},{8,12},{12,0},{1,5},{5,9},{9,13},{13,1},{2,6},{6,10},{... | collective-permute-start | bytes 663560 | tf_op jit(solution)/shard_map/ppermute | solution.py:656
  54.8 1.2 %collective-permute-start.17 = (bf16[27,32,128]{2,1,0:T(8,128)(2,1)}, bf16[27,32,128]{2,1,0:T(8,128)(2,1)}, u32[]{:S(2)}, u32[]{:S(2)}) collective-permute-start(bf16[27,32,128]{2,1,0:T(8,128)(2,1)} %get-tuple-element.53), channel_id=1, source_target_pairs={{0,8},{4,12},{8,0},{12,4},{1,9},{5,13},{9,1},{13,5},{2,10},{6,14},... | collective-permute-start | bytes 663560 | tf_op jit(solution)/shard_map/ppermute | solution.py:656
  56.0 1.4 %collective-permute-start.18 = (bf16[27,32,128]{2,1,0:T(8,128)(2,1)}, bf16[27,32,128]{2,1,0:T(8,128)(2,1)}, u32[]{:S(2)}, u32[]{:S(2)}) collective-permute-start(bf16[27,32,128]{2,1,0:T(8,128)(2,1)} %get-tuple-element.54), channel_id=1, source_target_pairs={{0,12},{4,0},{8,4},{12,8},{1,13},{5,1},{9,5},{13,9},{2,14},{6,2},{... | collective-permute-start | bytes 663560 | tf_op jit(solution)/shard_map/ppermute | solution.py:656
  57.4 1.2 %collective-permute-start.15 = (bf16[2,18,16,128]{3,2,1,0:T(8,128)(2,1)S(1)}, bf16[2,18,16,128]{3,2,1,0:T(8,128)(2,1)S(1)}, u32[]{:S(2)}, u32[]{:S(2)}) collective-permute-start(bf16[2,18,16,128]{3,2,1,0:T(8,128)(2,1)S(1)} %collective-permute-done.14.next_own), channel_id=1, source_target_pairs={{0,1},{1,0},{2,3},{3,2},{4,5},{5,4},{6,7},{7,6},{8,9},{9,8},{10,11... | collective-permute-start | bytes 442376 | tf_op jit(solution)/shard_map/ppermute | solution.py:52
  59.6 7.2 %backward.1 = (f32[8,128,128]{2,1,0:T(8,128)S(1)}, f32[8,128,128]{2,1,0:T(8,128)}, f32[16,16,128]{2,1,0:T(8,128)S(1)}) custom-call(s32[8]{0:T(128)S(1)} %copy-done.29, f32[40,128]{1,0:T(8,128)S(1)} %get-tuple-element.42.refs_1_.table, f32[40,128]{1,0:T(8,128)S(1)} %collective-permute-done.8.refs_2_.table_sib, bf16[9,768,256]{2,1,0:T(8,128)(2,1)S(1)} %turn.1.weight, ...), custom_call_target="tpu_custom_call" | custom-call | flops 1024 | bytes 1024 | tf_op jit(solution)/shard_map/backward/pallas_call | solution.py:627
  68.3 5.9 %all-to-all-start = ((f32[16,16,128]{2,1,0:T(8,128)}), f32[16,16,128]{2,1,0:T(8,128)}, u32[]{:S(2)}, u32[]{:S(2)}) async-start(f32[16,16,128]{2,1,0:T(8,128)} %copy-done.28), calls=%async_computation | async-start | bytes 262144 | tf_op jit(solution)/shard_map/all_to_all | solution.py:637
  82.6 6.6 %forward.1 = (bf16[8,8,16,128]{3,2,1,0:T(8,128)(2,1)S(1)}, bf16[8,8,16,128]{3,2,1,0:T(8,128)(2,1)S(1)}) custom-call(s32[8]{0:T(128)S(1)} %copy-done.29, f32[40,128]{1,0:T(8,128)S(1)} %copy-done.22, f32[40,128]{1,0:T(8,128)S(1)} %copy-done.27, bf16[9,768,256]{2,1,0:T(8,128)(2,1)S(1)} %bitcast.9, bf16[8,16,16,128]{3,2,1,0:T(8,128)(2,1)} %video.1, ...), custom_call_target="tpu_custom_call" | custom-call | flops 1024 | bytes 1024 | tf_op jit(solution)/shard_map/forward/pallas_call | solution.py:641
  91.0 2.1 %collect.1 = f32[27,32,128]{2,1,0:T(8,128)} custom-call(f32[27,32,128]{2,1,0:T(8,128)S(1)} %copy-done.34, bf16[27,32,128]{2,1,0:T(8,128)(2,1)} %collective-permute-done.16.refs_0_, bf16[27,32,128]{2,1,0:T(8,128)(2,1)} %collective-permute-done.17.refs_1_, bf16[27,32,128]{2,1,0:T(8,128)(2,1)} %collective-permute-done.18.refs_2_), custom_call_target="tpu_custom_call" | custom-call | flops 9999999827968 | bytes 1024 | tf_op jit(solution)/shard_map/collect/pallas_call | solution.py:657
  93.2 2.9 %finish.1 = (bf16[8,16,16,128]{3,2,1,0:T(8,128)(2,1)}, f32[8,128]{1,0:T(8,128)S(1)}) custom-call(s32[8]{0:T(128)S(1)} %copy-done.29, f32[40,128]{1,0:T(8,128)S(1)} %copy-done.23, f32[16,16,128]{2,1,0:T(8,128)} %all-to-all-done.got, bf16[8,16,16,128]{3,2,1,0:T(8,128)(2,1)} %video.1, f32[8,128,128]{2,1,0:T(8,128)S(1)} %copy-done.19, ...), custom_call_target="tpu_custom_call" | custom-call | flops 1024 | bytes 1024 | tf_op jit(solution)/shard_map/finish/pallas_call | solution.py:662
  (104 shorter events, 22.6 us)
Async XLA Ops:
  5.2 13.1 %collective-permute-start.4 = (bf16[8,16,16,128]{3,2,1,0:T(8,128)(2,1)}, bf16[8,16,16,128]{3,2,1,0:T(8,128)(2,1)S(1)}, u32[]{:S(2)}, u32[]{:S(2)}) collective-permute-start(bf16[8,16,16,128]{3,2,1,0:T(8,128)(2,1)} %video.1), channel_id=1, source_target_pairs={{0,2},{2,0},{1,3},{3,1},{4,6},{6,4},{5,7},{7,5},{8,10},{10,8},{9,1... | collective-permute-start | bytes 1572872 | tf_op jit(solution)/shard_map/ppermute | solution.py:582
  5.5 7.3 %collective-permute-start = (bf16[69,16,128]{2,1,0:T(8,128)(2,1)S(1)}, bf16[69,16,128]{2,1,0:T(8,128)(2,1)S(1)}, u32[]{:S(2)}, u32[]{:S(2)}) collective-permute-start(bf16[69,16,128]{2,1,0:T(8,128)(2,1)S(1)} %get-tuple-element.35), channel_id=1, source_target_pairs={{0,4},{4,8},{8,12},{12,0},{1,5},{5,9},{9,13},{13,1},{2,6},{6,10},{... | collective-permute-start | bytes 847880 | tf_op jit(solution)/shard_map/ppermute | solution.py:578
  6.8 16.4 %collective-permute-start.1 = (bf16[37,16,128]{2,1,0:T(8,128)(2,1)S(1)}, bf16[37,16,128]{2,1,0:T(8,128)(2,1)S(1)}, u32[]{:S(2)}, u32[]{:S(2)}) collective-permute-start(bf16[37,16,128]{2,1,0:T(8,128)(2,1)S(1)} %get-tuple-element.36), channel_id=1, source_target_pairs={{0,8},{4,12},{8,0},{12,4},{1,9},{5,13},{9,1},{13,5},{2,10},{6,14},... | collective-permute-start | bytes 454664 | tf_op jit(solution)/shard_map/ppermute | solution.py:578
  7.9 17.0 %collective-permute-start.2 = (bf16[37,16,128]{2,1,0:T(8,128)(2,1)S(1)}, bf16[37,16,128]{2,1,0:T(8,128)(2,1)S(1)}, u32[]{:S(2)}, u32[]{:S(2)}) collective-permute-start(bf16[37,16,128]{2,1,0:T(8,128)(2,1)S(1)} %get-tuple-element.37), channel_id=1, source_target_pairs={{0,12},{4,0},{8,4},{12,8},{1,13},{5,1},{9,5},{13,9},{2,14},{6,2},{... | collective-permute-start | bytes 454664 | tf_op jit(solution)/shard_map/ppermute | solution.py:578
  9.3 16.7 %collective-permute-start.3 = (bf16[37,16,128]{2,1,0:T(8,128)(2,1)S(1)}, bf16[37,16,128]{2,1,0:T(8,128)(2,1)S(1)}, u32[]{:S(2)}, u32[]{:S(2)}) collective-permute-start(bf16[37,16,128]{2,1,0:T(8,128)(2,1)S(1)} %get-tuple-element.34.refs_0_.refs_9_), channel_id=1, source_target_pairs={{0,2},{2,0},{1,3},{3,1},{4,6},{6,4},{5,7},{7,5},{8,10},{10,8},{9,1... | collective-permute-start | bytes 454664 | tf_op jit(solution)/shard_map/ppermute | solution.py:586
  18.3 15.8 %collective-permute-start.5 = (bf16[69,16,128]{2,1,0:T(8,128)(2,1)S(1)}, bf16[69,16,128]{2,1,0:T(8,128)(2,1)S(1)}, u32[]{:S(2)}, u32[]{:S(2)}) collective-permute-start(bf16[69,16,128]{2,1,0:T(8,128)(2,1)S(1)} %collective-permute-done.refs_1_.refs_10_.refs_6_), channel_id=1, source_target_pairs={{0,2},{2,0},{1,3},{3,1},{4,6},{6,4},{5,7},{7,5},{8,10},{10,8},{9,1... | collective-permute-start | bytes 847880 | tf_op jit(solution)/shard_map/ppermute | solution.py:586
  18.5 18.7 %collective-permute-start.9 = (bf16[8,16,16,128]{3,2,1,0:T(8,128)(2,1)}, bf16[8,16,16,128]{3,2,1,0:T(8,128)(2,1)S(1)}, u32[]{:S(2)}, u32[]{:S(2)}) collective-permute-start(bf16[8,16,16,128]{3,2,1,0:T(8,128)(2,1)} %video.1), channel_id=1, source_target_pairs={{0,1},{1,0},{2,3},{3,2},{4,5},{5,4},{6,7},{7,6},{8,9},{9,8},{10,11... | collective-permute-start | bytes 1572872 | tf_op jit(solution)/shard_map/ppermute | solution.py:52
  23.3 17.4 %collective-permute-start.10 = (bf16[8,16,16,128]{3,2,1,0:T(8,128)(2,1)S(1)}, bf16[8,16,16,128]{3,2,1,0:T(8,128)(2,1)S(1)}, u32[]{:S(2)}, u32[]{:S(2)}) collective-permute-start(bf16[8,16,16,128]{3,2,1,0:T(8,128)(2,1)S(1)} %collective-permute-done.4.refs_4_.refs_2_), channel_id=1, source_target_pairs={{0,1},{1,0},{2,3},{3,2},{4,5},{5,4},{6,7},{7,6},{8,9},{9,8},{10,11... | collective-permute-start | bytes 1572872 | tf_op jit(solution)/shard_map/ppermute | solution.py:52
  24.8 6.0 %collective-permute-start.6 = (bf16[37,16,128]{2,1,0:T(8,128)(2,1)S(1)}, bf16[37,16,128]{2,1,0:T(8,128)(2,1)S(1)}, u32[]{:S(2)}, u32[]{:S(2)}) collective-permute-start(bf16[37,16,128]{2,1,0:T(8,128)(2,1)S(1)} %collective-permute-done.1.refs_2_.refs_11_), channel_id=1, source_target_pairs={{0,2},{2,0},{1,3},{3,1},{4,6},{6,4},{5,7},{7,5},{8,10},{10,8},{9,1... | collective-permute-start | bytes 454664 | tf_op jit(solution)/shard_map/ppermute | solution.py:586
  26.1 8.1 %collective-permute-start.7 = (bf16[37,16,128]{2,1,0:T(8,128)(2,1)S(1)}, bf16[37,16,128]{2,1,0:T(8,128)(2,1)S(1)}, u32[]{:S(2)}, u32[]{:S(2)}) collective-permute-start(bf16[37,16,128]{2,1,0:T(8,128)(2,1)S(1)} %collective-permute-done.2.refs_3_.refs_12_), channel_id=1, source_target_pairs={{0,2},{2,0},{1,3},{3,1},{4,6},{6,4},{5,7},{7,5},{8,10},{10,8},{9,1... | collective-permute-start | bytes 454664 | tf_op jit(solution)/shard_map/ppermute | solution.py:586
  35.1 31.7 %copy-start.14 = (bf16[8,18,16,128]{3,2,1,0:T(8,128)(2,1)}, bf16[8,18,16,128]{3,2,1,0:T(8,128)(2,1)S(1)}, u32[]{:S(2)}) copy-start(bf16[8,18,16,128]{3,2,1,0:T(8,128)(2,1)S(1)} %get-tuple-element.45.up) | copy-start | bytes 1769476
  35.1 31.7 %copy-start.21 = (f32[40,128]{1,0:T(8,128)}, f32[40,128]{1,0:T(8,128)S(1)}, u32[]{:S(2)}) copy-start(f32[40,128]{1,0:T(8,128)S(1)} %get-tuple-element.42.refs_1_.table) | copy-start | bytes 61444
  35.1 24.5 %collective-permute-start.13 = (bf16[8,18,16,128]{3,2,1,0:T(8,128)(2,1)S(1)}, bf16[8,18,16,128]{3,2,1,0:T(8,128)(2,1)S(1)}, u32[]{:S(2)}, u32[]{:S(2)}) collective-permute-start(bf16[8,18,16,128]{3,2,1,0:T(8,128)(2,1)S(1)} %get-tuple-element.45.up), channel_id=1, source_target_pairs={{0,1},{1,0},{2,3},{3,2},{4,5},{5,4},{6,7},{7,6},{8,9},{9,8},{10,11... | collective-permute-start | bytes 1769480 | tf_op jit(solution)/shard_map/ppermute | solution.py:52
  36.7 2.6 %collective-permute-start.11 = (bf16[69,16,128]{2,1,0:T(8,128)(2,1)S(1)}, bf16[69,16,128]{2,1,0:T(8,128)(2,1)S(1)}, u32[]{:S(2)}, u32[]{:S(2)}) collective-permute-start(bf16[69,16,128]{2,1,0:T(8,128)(2,1)S(1)} %collective-permute-done.refs_1_.refs_10_.refs_6_), channel_id=1, source_target_pairs={{0,1},{1,0},{2,3},{3,2},{4,5},{5,4},{6,7},{7,6},{8,9},{9,8},{10,11... | collective-permute-start | bytes 847880 | tf_op jit(solution)/shard_map/ppermute | solution.py:52
  36.8 3.8 %collective-permute-start.12 = (bf16[69,16,128]{2,1,0:T(8,128)(2,1)S(1)}, bf16[69,16,128]{2,1,0:T(8,128)(2,1)S(1)}, u32[]{:S(2)}, u32[]{:S(2)}) collective-permute-start(bf16[69,16,128]{2,1,0:T(8,128)(2,1)S(1)} %collective-permute-done.5.refs_5_.refs_14_.refs_8_.refs_10_), channel_id=1, source_target_pairs={{0,1},{1,0},{2,3},{3,2},{4,5},{5,4},{6,7},{7,6},{8,9},{9,8},{10,11... | collective-permute-start | bytes 847880 | tf_op jit(solution)/shard_map/ppermute | solution.py:52
  37.3 20.2 %collective-permute-start.14 = (bf16[2,18,16,128]{3,2,1,0:T(8,128)(2,1)S(1)}, bf16[2,18,16,128]{3,2,1,0:T(8,128)(2,1)S(1)}, u32[]{:S(2)}, u32[]{:S(2)}) collective-permute-start(bf16[2,18,16,128]{3,2,1,0:T(8,128)(2,1)S(1)} %get-tuple-element.46), channel_id=1, source_target_pairs={{4,0},{8,4},{12,8},{5,1},{9,5},{13,9},{6,2},{10,6},{14,10},{7,3},{... | collective-permute-start | bytes 442376 | tf_op jit(solution)/shard_map/ppermute | solution.py:624
  39.4 1.3 %collective-permute-start.8 = (f32[40,128]{1,0:T(8,128)S(1)}, f32[40,128]{1,0:T(8,128)S(1)}, u32[]{:S(2)}, u32[]{:S(2)}) collective-permute-start(f32[40,128]{1,0:T(8,128)S(1)} %get-tuple-element.42.refs_1_.table), channel_id=1, source_target_pairs={{0,1},{1,0},{2,3},{3,2},{4,5},{5,4},{6,7},{7,6},{8,9},{9,8},{10,11... | collective-permute-start | bytes 61448 | tf_op jit(solution)/shard_map/ppermute | solution.py:52
  53.4 37.5 %collective-permute-start.16 = (bf16[27,32,128]{2,1,0:T(8,128)(2,1)}, bf16[27,32,128]{2,1,0:T(8,128)(2,1)}, u32[]{:S(2)}, u32[]{:S(2)}) collective-permute-start(bf16[27,32,128]{2,1,0:T(8,128)(2,1)} %get-tuple-element.52), channel_id=1, source_target_pairs={{0,4},{4,8},{8,12},{12,0},{1,5},{5,9},{9,13},{13,1},{2,6},{6,10},{... | collective-permute-start | bytes 663560 | tf_op jit(solution)/shard_map/ppermute | solution.py:656
  54.8 36.2 %collective-permute-start.17 = (bf16[27,32,128]{2,1,0:T(8,128)(2,1)}, bf16[27,32,128]{2,1,0:T(8,128)(2,1)}, u32[]{:S(2)}, u32[]{:S(2)}) collective-permute-start(bf16[27,32,128]{2,1,0:T(8,128)(2,1)} %get-tuple-element.53), channel_id=1, source_target_pairs={{0,8},{4,12},{8,0},{12,4},{1,9},{5,13},{9,1},{13,5},{2,10},{6,14},... | collective-permute-start | bytes 663560 | tf_op jit(solution)/shard_map/ppermute | solution.py:656
  56.0 34.9 %collective-permute-start.18 = (bf16[27,32,128]{2,1,0:T(8,128)(2,1)}, bf16[27,32,128]{2,1,0:T(8,128)(2,1)}, u32[]{:S(2)}, u32[]{:S(2)}) collective-permute-start(bf16[27,32,128]{2,1,0:T(8,128)(2,1)} %get-tuple-element.54), channel_id=1, source_target_pairs={{0,12},{4,0},{8,4},{12,8},{1,13},{5,1},{9,5},{13,9},{2,14},{6,2},{... | collective-permute-start | bytes 663560 | tf_op jit(solution)/shard_map/ppermute | solution.py:656
  57.4 2.2 %collective-permute-start.15 = (bf16[2,18,16,128]{3,2,1,0:T(8,128)(2,1)S(1)}, bf16[2,18,16,128]{3,2,1,0:T(8,128)(2,1)S(1)}, u32[]{:S(2)}, u32[]{:S(2)}) collective-permute-start(bf16[2,18,16,128]{3,2,1,0:T(8,128)(2,1)S(1)} %collective-permute-done.14.next_own), channel_id=1, source_target_pairs={{0,1},{1,0},{2,3},{3,2},{4,5},{5,4},{6,7},{7,6},{8,9},{9,8},{10,11... | collective-permute-start | bytes 442376 | tf_op jit(solution)/shard_map/ppermute | solution.py:52
  68.3 24.9 %all-to-all-start = ((f32[16,16,128]{2,1,0:T(8,128)}), f32[16,16,128]{2,1,0:T(8,128)}, u32[]{:S(2)}, u32[]{:S(2)}) async-start(f32[16,16,128]{2,1,0:T(8,128)} %copy-done.28), calls=%async_computation | async-start | bytes 262144 | tf_op jit(solution)/shard_map/all_to_all | solution.py:637
  90.6 2.6 %collective-permute-start.19 = (f32[8,128,128]{2,1,0:T(8,128)}, f32[8,128,128]{2,1,0:T(8,128)}, u32[]{:S(2)}, u32[]{:S(2)}) collective-permute-start(f32[8,128,128]{2,1,0:T(8,128)} %get-tuple-element.57), channel_id=1, source_target_pairs={{0,1},{1,0},{2,3},{3,2},{4,5},{5,4},{6,7},{7,6},{8,9},{9,8},{10,11... | collective-permute-start | bytes 1572872 | tf_op jit(solution)/shard_map/ppermute | solution.py:52
  96.1 1.5 %collective-permute-start.20 = (bf16[8,8,16,128]{3,2,1,0:T(8,128)(2,1)S(1)}, bf16[8,8,16,128]{3,2,1,0:T(8,128)(2,1)S(1)}, u32[]{:S(2)}, u32[]{:S(2)}) collective-permute-start(bf16[8,8,16,128]{3,2,1,0:T(8,128)(2,1)S(1)} %copy-done.36), channel_id=1, source_target_pairs={{0,1},{1,0},{2,3},{3,2},{4,5},{5,4},{6,7},{7,6},{8,9},{9,8},{10,11... | collective-permute-start | bytes 786440 | tf_op jit(solution)/shard_map/ppermute | solution.py:52
  (35 other events, 284.8 us)

commit v5 on v4

--- a/solution.py
+++ b/solution.py
@@ -34,6 +34,10 @@
         cost_estimate=pl.CostEstimate(flops=work, bytes_accessed=1024, transcendentals=0),
         name=name,
     )
+
+
+def far_away(*values):
+    return [pltpu.with_memory_space_constraint(v, pltpu.HBM) for v in values]
 
 
 def fdot(a, b):
@@ -504,16 +508,24 @@
         give[t] = jnp.where(c == 0, right, left)
 
 
-def collect_body(own, *refs):
-    terms, out = refs[:-1], refs[-1]
-    for tap in range(own.shape[0]):
-        total = own[tap]
-        for term in terms:
+def collect_body(*refs):
+    count = len(refs) // 2 - 1
+    far, out, near, sem = refs[:count], refs[count], refs[count + 1 : -1], refs[-1]
+    loads = [pltpu.make_async_copy(far[n], near[n], sem.at[n]) for n in range(count)]
+    for load in loads:
+        load.start()
+    for load in loads:
+        load.wait()
+    for tap in range(out.shape[0]):
+        total = near[0][tap]
+        for term in near[1:]:
             total = total + term[tap].astype(F32)
         out[tap] = total
 
 
-def finish_body(size, bands, lengths, table, got, video, keep, other, up, out, small):
+def finish_body(size, bands, lengths, table, got, video, keep_far, other, up, block_keep, block_other, out, block, small, keep, sem):
+    load = pltpu.make_async_copy(keep_far, keep, sem)
+    load.start()
     frames, rows, cols, chans = video.shape
     half = rows // 2
     cells = half * cols
@@ -530,7 +542,10 @@
     spread = jnp.where(clip_of(lengths, first_frame + iota((frames, NCLIPS), 0)) == clip, inverse, 0.0)
     first = fdot(spread, fdot(whole[:NCLIPS] * gain, group))
     second = fdot(spread, fdot(whole[NCLIPS:] * gain, group))
+    load.wait()
     for t in range(frames):
+        block[t, pl.ds(c * half, half)] = block_keep[t]
+        block[t, pl.ds((1 - c) * half, half)] = block_other[t]
         inv = table[t + 18 : t + 19]
         for grads, at in ((keep, c * half), (other, (1 - c) * half)):
             x = video[t, pl.ds(at, half)].reshape(cells, chans).astype(F32)
@@ -574,7 +589,7 @@
             pltpu.SemaphoreType.DMA((peers,)),
         ],
         name="pack", where=ANY,
-    )(packed_frame, packed_grad, clip_video)
+    )(packed_frame, *far_away(packed_grad, clip_video))
     ups = [[pieces[0]] + [lax.ppermute(pieces[k], "tm", ring(peers, k)) for k in range(1, peers)]]
 
     own = [clip_video]
@@ -650,27 +665,29 @@
         ],
         name="forward",
     )(
-        clip_lengths, table, table_sib, after(weight, sums), own[0], sib[0], own[1], sib[1], own[far], sib[far],
-        ups[0][1], prev_sib[0], ups[1][1], prev_sib[1], ups[far][1], prev_sib[far],
+        clip_lengths, table, table_sib, *far_away(
+            after(weight, sums), own[0], sib[0], own[1], sib[1], own[far], sib[far],
+            ups[0][1], prev_sib[0], ups[1][1], prev_sib[1], ups[far][1], prev_sib[far],
+        ),
     )
     terms = [lax.ppermute(grads[k], "tm", ring(peers, k)) for k in range(1, peers)]
     weight_grad = call(
-        collect_body, sds((27, block, chans), F32), [VM] * peers, name="collect", work=10**13
-    )(after(grads[0], block_give), *terms)
+        collect_body, sds((27, block, chans), F32), [HB] * peers,
+        [pltpu.VMEM((27, block, chans), F32)]
+        + [pltpu.VMEM((27, block, chans), BF16)] * (peers - 1)
+        + [pltpu.SemaphoreType.DMA((peers,))],
+        name="collect", work=10**13,
+    )(*far_away(after(grads[0], block_give), *terms))
     weight_grad = weight_grad.reshape(3, 3, 3, block, chans)
 
-    video_grad, small = call(
+    block_other = sibling(after(block_give, terms[-1]))
+    video_grad, block_out, small = call(
         functools.partial(finish_body, size, bands),
-        [sds(clip_video.shape, BF16), sds((8, chans), F32)],
-        [SM] + [VM] * 6,
+        [sds(clip_video.shape, BF16)] * 2 + [sds((8, chans), F32)],
+        [SM] + [VM] * 3 + [HB] + [VM] * 4,
+        [pltpu.VMEM((frames, half * cols, chans), F32), pltpu.SemaphoreType.DMA],
         name="finish",
-    )(clip_lengths, table, after(totals, weight_grad), clip_video, keep, other, up)
-    block_other = sibling(after(block_give, small))
-    block_out = jnp.where(
-        c == 0,
-        jnp.concatenate([block_keep, block_other], axis=1),
-        jnp.concatenate([block_other, block_keep], axis=1),
-    )
+    )(clip_lengths, table, after(totals, weight_grad), clip_video, *far_away(keep), other, up, block_keep, block_other)
     return (block_out, video_grad, weight_grad, small[0], small[1])
 
 

time: 100 us -> 87.9 us (0.88)
  local copies, waits for them, and re-layouts: 15.5 us -> 4.79 us
  waiting for transfers between devices: 16.6 us -> 14.8 us
  starting transfers between devices: 28.2 us -> 29.3 us
    unnamed x74 -> x40, local copies, waits for them, and re-layouts: 15 us -> 4.28 us
    ppermute x3, starting transfers between devices: 3.99 us -> 5.74 us  [per_device(): lax.ppermute(grads[k], 'tm', ring(peers, k))]
    all_to_all x1, starting transfers between devices: 5.87 us -> 4.24 us  [per_device(): totals = lax.all_to_all(sums, everyone, 0, 0)]
    ppermute x3, waiting for transfers between devices: 3.61 us -> 2.31 us  [per_device(): lax.ppermute(pieces[k], 'tm', ring(peers, k))]
  transfers between devices with their start and end apart: 22 -> 22, of which waited for: 8 -> 6; matrix products, arithmetic and copies ran while one was open for 1% -> 0% of each run, Pallas kernels for 31% -> 35%
where the time goes in v5:
time: 87.9 us; the launch traced here: 86.5 us
  Pallas kernels  36.7 us (42%)
  starting transfers between devices  29.3 us (33%)
  waiting for transfers between devices  14.8 us (17%)
  local copies, waits for them, and re-layouts  4.79 us (5%)
  between operations  0.91 us (1%)
    pallas_call x1, Pallas kernels, per_device(): call(functools.partial(weight_body, peers, bands, cap, block), [sds((27,...  11.9 us
    ppermute x9, starting transfers between devices, sibling(): return lax.ppermute(value, 'chan', ring(2, 1))  10.2 us
    pallas_call x1, Pallas kernels, per_device(): call(functools.partial(forward_body, bands, skip), [part, part], [SM, VM,...  7.54 us
    pallas_call x1, Pallas kernels, per_device(): call(functools.partial(backward_body, peers), [part, part, sds((devices,...  6.9 us
    ppermute x3, starting transfers between devices, per_device(): lax.ppermute(grads[k], 'tm', ring(peers, k))  5.74 us
    ppermute x1, waiting for transfers between devices, per_device(): lax.ppermute(after(clip_video, pieces[0]), 'height', ring(bands, m))  5.45 us
    ppermute x4, waiting for transfers between devices, per_device(): ups.append([lax.ppermute(v, 'height', ring(bands, m)) for v in ready])  5.15 us
    unnamed x40, local copies, waits for them, and re-layouts  4.28 us
  transfers between devices with their start and end apart: 22, of which 6 were waited for; matrix products, arithmetic and copies ran while one was open for 0% of the time, Pallas kernels for 35%

profile of v5, /device:TPU:15, one launch (start us, length us, event | category | flops | bytes accessed | tf_op | source)
XLA Modules:
  0.0 86.5 jit_solution(16336582989639213538)
XLA Ops:
  1.3 2.6 %pack.1 = (bf16[37,16,128]{2,1,0:T(8,128)(2,1)S(1)}, bf16[69,16,128]{2,1,0:T(8,128)(2,1)S(1)}, bf16[37,16,128]{2,1,0:T(8,128)(2,1)S(1)}, bf16[37,16,128]{2,1,0:T(8,128)(2,1)S(1)}) custom-call(s32[8]{0:T(128)S(1)} %copy-done.14, bf16[8,16,16,128]{3,2,1,0:T(8,128)(2,1)} %grad.1, bf16[8,16,16,128]{3,2,1,0:T(8,128)(2,1)} %video.1), custom_call_target="tpu_custom_call" | custom-call | flops 1024 | bytes 1024 | tf_op jit(solution)/shard_map/pack/pallas_call | solution.py:576
  4.2 1.3 %collective-permute-start = (bf16[69,16,128]{2,1,0:T(8,128)(2,1)S(1)}, bf16[69,16,128]{2,1,0:T(8,128)(2,1)S(1)}, u32[]{:S(2)}, u32[]{:S(2)}) collective-permute-start(bf16[69,16,128]{2,1,0:T(8,128)(2,1)S(1)} %get-tuple-element.36), channel_id=1, source_target_pairs={{0,4},{4,8},{8,12},{12,0},{1,5},{5,9},{9,13},{13,1},{2,6},{6,10},{... | collective-permute-start | bytes 847880 | tf_op jit(solution)/shard_map/ppermute | solution.py:593
  5.7 2.3 %collective-permute-start.1 = (bf16[37,16,128]{2,1,0:T(8,128)(2,1)S(1)}, bf16[37,16,128]{2,1,0:T(8,128)(2,1)S(1)}, u32[]{:S(2)}, u32[]{:S(2)}) collective-permute-start(bf16[37,16,128]{2,1,0:T(8,128)(2,1)S(1)} %get-tuple-element.37), channel_id=1, source_target_pairs={{0,8},{4,12},{8,0},{12,4},{1,9},{5,13},{9,1},{13,5},{2,10},{6,14},... | collective-permute-start | bytes 454664 | tf_op jit(solution)/shard_map/ppermute | solution.py:593
  8.0 1.2 %collective-permute-start.3 = (bf16[37,16,128]{2,1,0:T(8,128)(2,1)S(1)}, bf16[37,16,128]{2,1,0:T(8,128)(2,1)S(1)}, u32[]{:S(2)}, u32[]{:S(2)}) collective-permute-start(bf16[37,16,128]{2,1,0:T(8,128)(2,1)S(1)} %get-tuple-element.35.refs_0_.refs_9_), channel_id=1, source_target_pairs={{0,2},{2,0},{1,3},{3,1},{4,6},{6,4},{5,7},{7,5},{8,10},{10,8},{9,1... | collective-permute-start | bytes 454664 | tf_op jit(solution)/shard_map/ppermute | solution.py:601
  9.2 2.3 %collective-permute-done.refs_1_.refs_10_.refs_6_ = bf16[69,16,128]{2,1,0:T(8,128)(2,1)S(1)} collective-permute-done((bf16[69,16,128]{2,1,0:T(8,128)(2,1)S(1)}, bf16[69,16,128]{2,1,0:T(8,128)(2,1)S(1)}, u32[]{:S(2)}, u32[]{:S(2)}) %collective-permute-start) | collective-permute-done | bytes 282656 | tf_op jit(solution)/shard_map/ppermute | solution.py:593
  11.5 5.4 %collective-permute-done.4.refs_4_.refs_2_ = bf16[8,16,16,128]{3,2,1,0:T(8,128)(2,1)S(1)} collective-permute-done((bf16[8,16,16,128]{3,2,1,0:T(8,128)(2,1)}, bf16[8,16,16,128]{3,2,1,0:T(8,128)(2,1)S(1)}, u32[]{:S(2)}, u32[]{:S(2)}) %collective-permute-start.4) | collective-permute-done | bytes 524320 | tf_op jit(solution)/shard_map/ppermute | solution.py:597
  17.3 4.7 %collective-permute-start.9 = (bf16[8,16,16,128]{3,2,1,0:T(8,128)(2,1)}, bf16[8,16,16,128]{3,2,1,0:T(8,128)(2,1)S(1)}, u32[]{:S(2)}, u32[]{:S(2)}) collective-permute-start(bf16[8,16,16,128]{3,2,1,0:T(8,128)(2,1)} %video.1), channel_id=1, source_target_pairs={{0,1},{1,0},{2,3},{3,2},{4,5},{5,4},{6,7},{7,6},{8,9},{9,8},{10,11... | collective-permute-start | bytes 1572872 | tf_op jit(solution)/shard_map/ppermute | solution.py:56
  22.3 1.2 %collective-permute-start.7 = (bf16[37,16,128]{2,1,0:T(8,128)(2,1)S(1)}, bf16[37,16,128]{2,1,0:T(8,128)(2,1)S(1)}, u32[]{:S(2)}, u32[]{:S(2)}) collective-permute-start(bf16[37,16,128]{2,1,0:T(8,128)(2,1)S(1)} %collective-permute-done.2.refs_3_.refs_12_), channel_id=1, source_target_pairs={{0,2},{2,0},{1,3},{3,1},{4,6},{6,4},{5,7},{7,5},{8,10},{10,8},{9,1... | collective-permute-start | bytes 454664 | tf_op jit(solution)/shard_map/ppermute | solution.py:601
  23.5 2.0 %copy-done = bf16[3,3,3,256,256]{4,3,2,1,0:T(8,128)(2,1)S(1)} copy-done((bf16[3,3,3,256,256]{4,3,2,1,0:T(8,128)(2,1)S(1)}, bf16[3,3,3,256,256]{4,3,2,1,0:T(8,128)(2,1)}, u32[]{:S(2)}) %copy-start) | copy-done | bytes 3538968
  26.5 1.9 %collective-permute-done.6.refs_6_.refs_15_ = bf16[37,16,128]{2,1,0:T(8,128)(2,1)S(1)} collective-permute-done((bf16[37,16,128]{2,1,0:T(8,128)(2,1)S(1)}, bf16[37,16,128]{2,1,0:T(8,128)(2,1)S(1)}, u32[]{:S(2)}, u32[]{:S(2)}) %collective-permute-start.6) | collective-permute-done | bytes 151584 | tf_op jit(solution)/shard_map/ppermute | solution.py:601
  28.4 3.2 %collective-permute-done.7.refs_7_.refs_16_ = bf16[37,16,128]{2,1,0:T(8,128)(2,1)S(1)} collective-permute-done((bf16[37,16,128]{2,1,0:T(8,128)(2,1)S(1)}, bf16[37,16,128]{2,1,0:T(8,128)(2,1)S(1)}, u32[]{:S(2)}, u32[]{:S(2)}) %collective-permute-start.7) | collective-permute-done | bytes 151584 | tf_op jit(solution)/shard_map/ppermute | solution.py:601
  31.7 1.0 %order.1 = (bf16[8,18,16,128]{3,2,1,0:T(8,128)(2,1)S(1)}, bf16[2,18,16,128]{3,2,1,0:T(8,128)(2,1)S(1)}, f32[40,128]{1,0:T(8,128)S(1)}) custom-call(s32[8]{0:T(128)S(1)} %copy-done.13, f32[1,128]{1,0:T(1,128)S(1)} %bitcast.10, f32[1,128]{1,0:T(1,128)S(1)} %bitcast.11, bf16[37,16,128]{2,1,0:T(8,128)(2,1)S(1)} %get-tuple-element.35.refs_0_.refs_9_, ...), custom_call_target="tpu_custom_call" | custom-call | flops 1024 | bytes 1024 | tf_op jit(solution)/shard_map/order/pallas_call | solution.py:609
  32.7 2.8 %collective-permute-start.13 = (bf16[8,18,16,128]{3,2,1,0:T(8,128)(2,1)S(1)}, bf16[8,18,16,128]{3,2,1,0:T(8,128)(2,1)S(1)}, u32[]{:S(2)}, u32[]{:S(2)}) collective-permute-start(bf16[8,18,16,128]{3,2,1,0:T(8,128)(2,1)S(1)} %get-tuple-element.46.up), channel_id=1, source_target_pairs={{0,1},{1,0},{2,3},{3,2},{4,5},{5,4},{6,7},{7,6},{8,9},{9,8},{10,11... | collective-permute-start | bytes 1769480 | tf_op jit(solution)/shard_map/ppermute | solution.py:56
  35.9 2.1 %collective-permute-start.14 = (bf16[2,18,16,128]{3,2,1,0:T(8,128)(2,1)S(1)}, bf16[2,18,16,128]{3,2,1,0:T(8,128)(2,1)S(1)}, u32[]{:S(2)}, u32[]{:S(2)}) collective-permute-start(bf16[2,18,16,128]{3,2,1,0:T(8,128)(2,1)S(1)} %get-tuple-element.47), channel_id=1, source_target_pairs={{4,0},{8,4},{12,8},{5,1},{9,5},{13,9},{6,2},{10,6},{14,10},{7,3},{... | collective-permute-start | bytes 442376 | tf_op jit(solution)/shard_map/ppermute | solution.py:639
  39.4 11.9 %weight.1 = (f32[27,32,128]{2,1,0:T(8,128)S(1)}, bf16[27,32,128]{2,1,0:T(8,128)(2,1)}, bf16[27,32,128]{2,1,0:T(8,128)(2,1)S(1)}, bf16[27,32,128]{2,1,0:T(8,128)(2,1)}) custom-call(s32[8]{0:T(128)S(1)} %copy-done.13, f32[40,128]{1,0:T(8,128)S(1)} %get-tuple-element.43.refs_1_.table, f32[40,128]{1,0:T(8,128)S(1)} %collective-permute-done.8.refs_2_.table_sib, ...), custom_call_target="tpu_custom_call" | custom-call | flops 1024 | bytes 1024 | tf_op jit(solution)/shard_map/weight/pallas_call | solution.py:624
  51.3 1.5 %collective-permute-start.16 = (bf16[27,32,128]{2,1,0:T(8,128)(2,1)}, bf16[27,32,128]{2,1,0:T(8,128)(2,1)S(1)}, u32[]{:S(2)}, u32[]{:S(2)}) collective-permute-start(bf16[27,32,128]{2,1,0:T(8,128)(2,1)} %get-tuple-element.52), channel_id=1, source_target_pairs={{0,4},{4,8},{8,12},{12,0},{1,5},{5,9},{9,13},{13,1},{2,6},{6,10},{... | collective-permute-start | bytes 663560 | tf_op jit(solution)/shard_map/ppermute | solution.py:673
  52.8 4.3 %collective-permute-start.17 = (bf16[27,32,128]{2,1,0:T(8,128)(2,1)S(1)}, bf16[27,32,128]{2,1,0:T(8,128)(2,1)}, u32[]{:S(2)}, u32[]{:S(2)}) collective-permute-start(bf16[27,32,128]{2,1,0:T(8,128)(2,1)S(1)} %get-tuple-element.53), channel_id=1, source_target_pairs={{0,8},{4,12},{8,0},{12,4},{1,9},{5,13},{9,1},{13,5},{2,10},{6,14},... | collective-permute-start | bytes 663560 | tf_op jit(solution)/shard_map/ppermute | solution.py:673
  57.0 1.2 %collective-permute-start.15 = (bf16[2,18,16,128]{3,2,1,0:T(8,128)(2,1)S(1)}, bf16[2,18,16,128]{3,2,1,0:T(8,128)(2,1)S(1)}, u32[]{:S(2)}, u32[]{:S(2)}) collective-permute-start(bf16[2,18,16,128]{3,2,1,0:T(8,128)(2,1)S(1)} %collective-permute-done.14.next_own), channel_id=1, source_target_pairs={{0,1},{1,0},{2,3},{3,2},{4,5},{5,4},{6,7},{7,6},{8,9},{9,8},{10,11... | collective-permute-start | bytes 442376 | tf_op jit(solution)/shard_map/ppermute | solution.py:56
  58.2 1.0 %collective-permute-done.15.next_sib = bf16[2,18,16,128]{3,2,1,0:T(8,128)(2,1)S(1)} collective-permute-done((bf16[2,18,16,128]{3,2,1,0:T(8,128)(2,1)S(1)}, bf16[2,18,16,128]{3,2,1,0:T(8,128)(2,1)S(1)}, u32[]{:S(2)}, u32[]{:S(2)}) %collective-permute-start.15) | collective-permute-done | bytes 147488 | tf_op jit(solution)/shard_map/ppermute | solution.py:56
  59.2 6.9 %backward.1 = (f32[8,128,128]{2,1,0:T(8,128)S(1)}, f32[8,128,128]{2,1,0:T(8,128)}, f32[16,16,128]{2,1,0:T(8,128)}) custom-call(s32[8]{0:T(128)S(1)} %copy-done.13, f32[40,128]{1,0:T(8,128)S(1)} %get-tuple-element.43.refs_1_.table, f32[40,128]{1,0:T(8,128)S(1)} %collective-permute-done.8.refs_2_.table_sib, bf16[9,768,256]{2,1,0:T(8,128)(2,1)S(1)} %turn.1.weight, ...), custom_call_target="tpu_custom_call" | custom-call | flops 1024 | bytes 1024 | tf_op jit(solution)/shard_map/backward/pallas_call | solution.py:642
  67.0 4.2 %all-to-all-start = ((f32[16,16,128]{2,1,0:T(8,128)}), f32[16,16,128]{2,1,0:T(8,128)}, u32[]{:S(2)}, u32[]{:S(2)}) async-start(f32[16,16,128]{2,1,0:T(8,128)} %get-tuple-element.48), calls=%async_computation | async-start | bytes 262144 | tf_op jit(solution)/shard_map/all_to_all | solution.py:652
  71.2 7.5 %forward.1 = (bf16[8,8,16,128]{3,2,1,0:T(8,128)(2,1)S(1)}, bf16[8,8,16,128]{3,2,1,0:T(8,128)(2,1)}) custom-call(s32[8]{0:T(128)S(1)} %copy-done.13, f32[40,128]{1,0:T(8,128)S(1)} %get-tuple-element.43.refs_1_.table, f32[40,128]{1,0:T(8,128)S(1)} %collective-permute-done.8.refs_2_.table_sib, bf16[9,768,256]{2,1,0:T(8,128)(2,1)} %bitcast.8, ...), custom_call_target="tpu_custom_call" | custom-call | flops 1024 | bytes 1024 | tf_op jit(solution)/shard_map/forward/pallas_call | solution.py:656
  80.2 2.2 %collect.1 = f32[27,32,128]{2,1,0:T(8,128)} custom-call(f32[27,32,128]{2,1,0:T(8,128)} %copy-done.17, bf16[27,32,128]{2,1,0:T(8,128)(2,1)} %copy-done.19, bf16[27,32,128]{2,1,0:T(8,128)(2,1)} %collective-permute-done.17.refs_2_, bf16[27,32,128]{2,1,0:T(8,128)(2,1)} %copy-done.18), custom_call_target="tpu_custom_call" | custom-call | flops 9999999827968 | bytes 1024 | tf_op jit(solution)/shard_map/collect/pallas_call | solution.py:674
  82.4 3.6 %finish.1 = (bf16[8,16,16,128]{3,2,1,0:T(8,128)(2,1)}, bf16[8,16,16,128]{3,2,1,0:T(8,128)(2,1)}, f32[8,128]{1,0:T(8,128)S(1)}) custom-call(s32[8]{0:T(128)S(1)} %copy-done.13, f32[40,128]{1,0:T(8,128)S(1)} %get-tuple-element.43.refs_1_.table, f32[16,16,128]{2,1,0:T(8,128)} %all-to-all-done.got, bf16[8,16,16,128]{3,2,1,0:T(8,128)(2,1)S(1)} %copy-done.2, ...), custom_call_target="tpu_custom_call" | custom-call | flops 1024 | bytes 1024 | tf_op jit(solution)/shard_map/finish/pallas_call | solution.py:684
  (69 shorter events, 7.2 us)
Async XLA Ops:
  3.9 13.1 %collective-permute-start.4 = (bf16[8,16,16,128]{3,2,1,0:T(8,128)(2,1)}, bf16[8,16,16,128]{3,2,1,0:T(8,128)(2,1)S(1)}, u32[]{:S(2)}, u32[]{:S(2)}) collective-permute-start(bf16[8,16,16,128]{3,2,1,0:T(8,128)(2,1)} %video.1), channel_id=1, source_target_pairs={{0,2},{2,0},{1,3},{3,1},{4,6},{6,4},{5,7},{7,5},{8,10},{10,8},{9,1... | collective-permute-start | bytes 1572872 | tf_op jit(solution)/shard_map/ppermute | solution.py:597
  4.2 7.3 %collective-permute-start = (bf16[69,16,128]{2,1,0:T(8,128)(2,1)S(1)}, bf16[69,16,128]{2,1,0:T(8,128)(2,1)S(1)}, u32[]{:S(2)}, u32[]{:S(2)}) collective-permute-start(bf16[69,16,128]{2,1,0:T(8,128)(2,1)S(1)} %get-tuple-element.36), channel_id=1, source_target_pairs={{0,4},{4,8},{8,12},{12,0},{1,5},{5,9},{9,13},{13,1},{2,6},{6,10},{... | collective-permute-start | bytes 847880 | tf_op jit(solution)/shard_map/ppermute | solution.py:593
  5.5 16.4 %collective-permute-start.2 = (bf16[37,16,128]{2,1,0:T(8,128)(2,1)S(1)}, bf16[37,16,128]{2,1,0:T(8,128)(2,1)S(1)}, u32[]{:S(2)}, u32[]{:S(2)}) collective-permute-start(bf16[37,16,128]{2,1,0:T(8,128)(2,1)S(1)} %get-tuple-element.38), channel_id=1, source_target_pairs={{0,12},{4,0},{8,4},{12,8},{1,13},{5,1},{9,5},{13,9},{2,14},{6,2},{... | collective-permute-start | bytes 454664 | tf_op jit(solution)/shard_map/ppermute | solution.py:593
  5.7 16.3 %collective-permute-start.1 = (bf16[37,16,128]{2,1,0:T(8,128)(2,1)S(1)}, bf16[37,16,128]{2,1,0:T(8,128)(2,1)S(1)}, u32[]{:S(2)}, u32[]{:S(2)}) collective-permute-start(bf16[37,16,128]{2,1,0:T(8,128)(2,1)S(1)} %get-tuple-element.37), channel_id=1, source_target_pairs={{0,8},{4,12},{8,0},{12,4},{1,9},{5,13},{9,1},{13,5},{2,10},{6,14},... | collective-permute-start | bytes 454664 | tf_op jit(solution)/shard_map/ppermute | solution.py:593
  8.0 14.3 %collective-permute-start.3 = (bf16[37,16,128]{2,1,0:T(8,128)(2,1)S(1)}, bf16[37,16,128]{2,1,0:T(8,128)(2,1)S(1)}, u32[]{:S(2)}, u32[]{:S(2)}) collective-permute-start(bf16[37,16,128]{2,1,0:T(8,128)(2,1)S(1)} %get-tuple-element.35.refs_0_.refs_9_), channel_id=1, source_target_pairs={{0,2},{2,0},{1,3},{3,1},{4,6},{6,4},{5,7},{7,5},{8,10},{10,8},{9,1... | collective-permute-start | bytes 454664 | tf_op jit(solution)/shard_map/ppermute | solution.py:601
  17.0 14.6 %collective-permute-start.5 = (bf16[69,16,128]{2,1,0:T(8,128)(2,1)S(1)}, bf16[69,16,128]{2,1,0:T(8,128)(2,1)S(1)}, u32[]{:S(2)}, u32[]{:S(2)}) collective-permute-start(bf16[69,16,128]{2,1,0:T(8,128)(2,1)S(1)} %collective-permute-done.refs_1_.refs_10_.refs_6_), channel_id=1, source_target_pairs={{0,2},{2,0},{1,3},{3,1},{4,6},{6,4},{5,7},{7,5},{8,10},{10,8},{9,1... | collective-permute-start | bytes 847880 | tf_op jit(solution)/shard_map/ppermute | solution.py:601
  17.3 18.7 %collective-permute-start.9 = (bf16[8,16,16,128]{3,2,1,0:T(8,128)(2,1)}, bf16[8,16,16,128]{3,2,1,0:T(8,128)(2,1)S(1)}, u32[]{:S(2)}, u32[]{:S(2)}) collective-permute-start(bf16[8,16,16,128]{3,2,1,0:T(8,128)(2,1)} %video.1), channel_id=1, source_target_pairs={{0,1},{1,0},{2,3},{3,2},{4,5},{5,4},{6,7},{7,6},{8,9},{9,8},{10,11... | collective-permute-start | bytes 1572872 | tf_op jit(solution)/shard_map/ppermute | solution.py:56
  22.0 17.3 %collective-permute-start.10 = (bf16[8,16,16,128]{3,2,1,0:T(8,128)(2,1)S(1)}, bf16[8,16,16,128]{3,2,1,0:T(8,128)(2,1)S(1)}, u32[]{:S(2)}, u32[]{:S(2)}) collective-permute-start(bf16[8,16,16,128]{3,2,1,0:T(8,128)(2,1)S(1)} %collective-permute-done.4.refs_4_.refs_2_), channel_id=1, source_target_pairs={{0,1},{1,0},{2,3},{3,2},{4,5},{5,4},{6,7},{7,6},{8,9},{9,8},{10,11... | collective-permute-start | bytes 1572872 | tf_op jit(solution)/shard_map/ppermute | solution.py:56
  22.0 6.4 %collective-permute-start.6 = (bf16[37,16,128]{2,1,0:T(8,128)(2,1)S(1)}, bf16[37,16,128]{2,1,0:T(8,128)(2,1)S(1)}, u32[]{:S(2)}, u32[]{:S(2)}) collective-permute-start(bf16[37,16,128]{2,1,0:T(8,128)(2,1)S(1)} %collective-permute-done.1.refs_2_.refs_11_), channel_id=1, source_target_pairs={{0,2},{2,0},{1,3},{3,1},{4,6},{6,4},{5,7},{7,5},{8,10},{10,8},{9,1... | collective-permute-start | bytes 454664 | tf_op jit(solution)/shard_map/ppermute | solution.py:601
  22.3 9.3 %collective-permute-start.7 = (bf16[37,16,128]{2,1,0:T(8,128)(2,1)S(1)}, bf16[37,16,128]{2,1,0:T(8,128)(2,1)S(1)}, u32[]{:S(2)}, u32[]{:S(2)}) collective-permute-start(bf16[37,16,128]{2,1,0:T(8,128)(2,1)S(1)} %collective-permute-done.2.refs_3_.refs_12_), channel_id=1, source_target_pairs={{0,2},{2,0},{1,3},{3,1},{4,6},{6,4},{5,7},{7,5},{8,10},{10,8},{9,1... | collective-permute-start | bytes 454664 | tf_op jit(solution)/shard_map/ppermute | solution.py:601
  31.6 34.5 %copy-start.6 = (bf16[69,16,128]{2,1,0:T(8,128)(2,1)}, bf16[69,16,128]{2,1,0:T(8,128)(2,1)S(1)}, u32[]{:S(2)}) copy-start(bf16[69,16,128]{2,1,0:T(8,128)(2,1)S(1)} %collective-permute-done.5.refs_5_.refs_14_.refs_8_.refs_10_) | copy-start | bytes 847876
  32.6 33.5 %copy-start.9 = (bf16[8,18,16,128]{3,2,1,0:T(8,128)(2,1)}, bf16[8,18,16,128]{3,2,1,0:T(8,128)(2,1)S(1)}, u32[]{:S(2)}) copy-start(bf16[8,18,16,128]{3,2,1,0:T(8,128)(2,1)S(1)} %get-tuple-element.46.up) | copy-start | bytes 1769476
  32.7 26.6 %collective-permute-start.13 = (bf16[8,18,16,128]{3,2,1,0:T(8,128)(2,1)S(1)}, bf16[8,18,16,128]{3,2,1,0:T(8,128)(2,1)S(1)}, u32[]{:S(2)}, u32[]{:S(2)}) collective-permute-start(bf16[8,18,16,128]{3,2,1,0:T(8,128)(2,1)S(1)} %get-tuple-element.46.up), channel_id=1, source_target_pairs={{0,1},{1,0},{2,3},{3,2},{4,5},{5,4},{6,7},{7,6},{8,9},{9,8},{10,11... | collective-permute-start | bytes 1769480 | tf_op jit(solution)/shard_map/ppermute | solution.py:56
  35.4 2.6 %collective-permute-start.11 = (bf16[69,16,128]{2,1,0:T(8,128)(2,1)S(1)}, bf16[69,16,128]{2,1,0:T(8,128)(2,1)S(1)}, u32[]{:S(2)}, u32[]{:S(2)}) collective-permute-start(bf16[69,16,128]{2,1,0:T(8,128)(2,1)S(1)} %collective-permute-done.refs_1_.refs_10_.refs_6_), channel_id=1, source_target_pairs={{0,1},{1,0},{2,3},{3,2},{4,5},{5,4},{6,7},{7,6},{8,9},{9,8},{10,11... | collective-permute-start | bytes 847880 | tf_op jit(solution)/shard_map/ppermute | solution.py:56
  35.5 3.8 %collective-permute-start.12 = (bf16[69,16,128]{2,1,0:T(8,128)(2,1)S(1)}, bf16[69,16,128]{2,1,0:T(8,128)(2,1)S(1)}, u32[]{:S(2)}, u32[]{:S(2)}) collective-permute-start(bf16[69,16,128]{2,1,0:T(8,128)(2,1)S(1)} %collective-permute-done.5.refs_5_.refs_14_.refs_8_.refs_10_), channel_id=1, source_target_pairs={{0,1},{1,0},{2,3},{3,2},{4,5},{5,4},{6,7},{7,6},{8,9},{9,8},{10,11... | collective-permute-start | bytes 847880 | tf_op jit(solution)/shard_map/ppermute | solution.py:56
  35.9 21.1 %collective-permute-start.14 = (bf16[2,18,16,128]{3,2,1,0:T(8,128)(2,1)S(1)}, bf16[2,18,16,128]{3,2,1,0:T(8,128)(2,1)S(1)}, u32[]{:S(2)}, u32[]{:S(2)}) collective-permute-start(bf16[2,18,16,128]{3,2,1,0:T(8,128)(2,1)S(1)} %get-tuple-element.47), channel_id=1, source_target_pairs={{4,0},{8,4},{12,8},{5,1},{9,5},{13,9},{6,2},{10,6},{14,10},{7,3},{... | collective-permute-start | bytes 442376 | tf_op jit(solution)/shard_map/ppermute | solution.py:639
  38.1 1.3 %collective-permute-start.8 = (f32[40,128]{1,0:T(8,128)S(1)}, f32[40,128]{1,0:T(8,128)S(1)}, u32[]{:S(2)}, u32[]{:S(2)}) collective-permute-start(f32[40,128]{1,0:T(8,128)S(1)} %get-tuple-element.43.refs_1_.table), channel_id=1, source_target_pairs={{0,1},{1,0},{2,3},{3,2},{4,5},{5,4},{6,7},{7,6},{8,9},{9,8},{10,11... | collective-permute-start | bytes 61448 | tf_op jit(solution)/shard_map/ppermute | solution.py:56
  51.3 27.5 %collective-permute-start.18 = (bf16[27,32,128]{2,1,0:T(8,128)(2,1)}, bf16[27,32,128]{2,1,0:T(8,128)(2,1)S(1)}, u32[]{:S(2)}, u32[]{:S(2)}) collective-permute-start(bf16[27,32,128]{2,1,0:T(8,128)(2,1)} %get-tuple-element.54), channel_id=1, source_target_pairs={{0,12},{4,0},{8,4},{12,8},{1,13},{5,1},{9,5},{13,9},{2,14},{6,2},{... | collective-permute-start | bytes 663560 | tf_op jit(solution)/shard_map/ppermute | solution.py:673
  51.3 28.1 %collective-permute-start.16 = (bf16[27,32,128]{2,1,0:T(8,128)(2,1)}, bf16[27,32,128]{2,1,0:T(8,128)(2,1)S(1)}, u32[]{:S(2)}, u32[]{:S(2)}) collective-permute-start(bf16[27,32,128]{2,1,0:T(8,128)(2,1)} %get-tuple-element.52), channel_id=1, source_target_pairs={{0,4},{4,8},{8,12},{12,0},{1,5},{5,9},{9,13},{13,1},{2,6},{6,10},{... | collective-permute-start | bytes 663560 | tf_op jit(solution)/shard_map/ppermute | solution.py:673
  52.8 27.4 %collective-permute-start.17 = (bf16[27,32,128]{2,1,0:T(8,128)(2,1)S(1)}, bf16[27,32,128]{2,1,0:T(8,128)(2,1)}, u32[]{:S(2)}, u32[]{:S(2)}) collective-permute-start(bf16[27,32,128]{2,1,0:T(8,128)(2,1)S(1)} %get-tuple-element.53), channel_id=1, source_target_pairs={{0,8},{4,12},{8,0},{12,4},{1,9},{5,13},{9,1},{13,5},{2,10},{6,14},... | collective-permute-start | bytes 663560 | tf_op jit(solution)/shard_map/ppermute | solution.py:673
  57.0 2.2 %collective-permute-start.15 = (bf16[2,18,16,128]{3,2,1,0:T(8,128)(2,1)S(1)}, bf16[2,18,16,128]{3,2,1,0:T(8,128)(2,1)S(1)}, u32[]{:S(2)}, u32[]{:S(2)}) collective-permute-start(bf16[2,18,16,128]{3,2,1,0:T(8,128)(2,1)S(1)} %collective-permute-done.14.next_own), channel_id=1, source_target_pairs={{0,1},{1,0},{2,3},{3,2},{4,5},{5,4},{6,7},{7,6},{8,9},{9,8},{10,11... | collective-permute-start | bytes 442376 | tf_op jit(solution)/shard_map/ppermute | solution.py:56
  67.0 15.4 %all-to-all-start = ((f32[16,16,128]{2,1,0:T(8,128)}), f32[16,16,128]{2,1,0:T(8,128)}, u32[]{:S(2)}, u32[]{:S(2)}) async-start(f32[16,16,128]{2,1,0:T(8,128)} %get-tuple-element.48), calls=%async_computation | async-start | bytes 262144 | tf_op jit(solution)/shard_map/all_to_all | solution.py:652
  78.8 3.6 %collective-permute-start.20 = (bf16[8,8,16,128]{3,2,1,0:T(8,128)(2,1)}, bf16[8,8,16,128]{3,2,1,0:T(8,128)(2,1)}, u32[]{:S(2)}, u32[]{:S(2)}) collective-permute-start(bf16[8,8,16,128]{3,2,1,0:T(8,128)(2,1)} %get-tuple-element.59), channel_id=1, source_target_pairs={{0,1},{1,0},{2,3},{3,2},{4,5},{5,4},{6,7},{7,6},{8,9},{9,8},{10,11... | collective-permute-start | bytes 786440 | tf_op jit(solution)/shard_map/ppermute | solution.py:56
  79.2 3.2 %collective-permute-start.19 = (f32[8,128,128]{2,1,0:T(8,128)}, f32[8,128,128]{2,1,0:T(8,128)}, u32[]{:S(2)}, u32[]{:S(2)}) collective-permute-start(f32[8,128,128]{2,1,0:T(8,128)} %get-tuple-element.57), channel_id=1, source_target_pairs={{0,1},{1,0},{2,3},{3,2},{4,5},{5,4},{6,7},{7,6},{8,9},{9,8},{10,11... | collective-permute-start | bytes 1572872 | tf_op jit(solution)/shard_map/ppermute | solution.py:56
  (18 other events, 218.5 us)

commit v6 on v5

--- a/solution.py
+++ b/solution.py
@@ -143,15 +143,6 @@
             copies[-2].start()
             copies[-1].start()
     base = cap * (rows + 1)
-    for i in range(2):
-        copies.append(
-            pltpu.make_async_copy(
-                video_far.at[slots - 2 + i],
-                outs[1].at[pl.ds(base + 3 + i * rows, rows)],
-                sem.at[2 * peers * cap + i],
-            )
-        )
-        copies[-1].start()
     average = group_matrix(chans, size) * (1.0 / size)
     sums = []
     for t in range(slots):
@@ -196,7 +187,8 @@
     refs = list(refs)
     lengths, table, table_sib = [refs.pop(0) for _ in range(3)]
     take = lambda n: [refs.pop(0) for _ in range(n)]
-    own, sib, prev_sib = take(bands), take(bands), take(bands)
+    own, sib = take(bands), take(bands)
+    prev, prev_sib = take(2)
     ups = [take(peers) for _ in range(bands)]
     outs = take(peers)
     active, upright = refs
@@ -223,8 +215,8 @@
     for f in range(frames + 2):
         for m in range(bands):
             if f < 2:
-                at = cap * (rows + 1) + 3 + f * rows
-                a, b = ups[m][1][at : at + rows], prev_sib[m][at : at + rows]
+                at = (2 * m + f) * rows
+                a, b = prev[at : at + rows], prev_sib[at : at + rows]
             else:
                 a, b = own[m][f - 2], sib[m][f - 2]
             x = bdot(a.reshape(cells, chans), pick_own) + bdot(b.reshape(cells, chans), pick_sib)
@@ -283,10 +275,10 @@
     )
 
 
-def forward_body(bands, skip, lengths, table, table_sib, weight_far, *refs):
+def forward_body(bands, lengths, table, table_sib, weight_far, *refs):
     core, above, below = refs[:2], refs[2:4], refs[4:6]
-    before, before_above, before_below = refs[6:8], refs[8:10], refs[10:12]
-    keep, give, active, here, weight, sem = refs[12:]
+    before = refs[6:8]
+    keep, give, active, here, weight, sem = refs[8:]
     frames, rows, cols, chans = core[0].shape
     half = rows // 2
     tm, h, c = lax.axis_index("tm"), lax.axis_index("height"), lax.axis_index("chan")
@@ -303,7 +295,7 @@
         )
         waits[-1].start()
         for f in range(2):
-            line = skip + f * rows
+            line = f * rows
             waits.append(
                 pltpu.make_async_copy(
                     before[n].at[pl.ds(line + (half - 1) * c, half + 1)],
@@ -312,9 +304,9 @@
                 )
             )
             waits[-1].start()
-        for side, rim, rim_before, row in (
-            (0, above[n], before_above[n], rows - 1),
-            (1, below[n], before_below[n], 0),
+        for side, rim, row, line in (
+            (0, above[n], rows - 1, 2 * rows),
+            (1, below[n], 0, 2 * (bands - 1) * rows),
         ):
             edges = [
                 pltpu.make_async_copy(
@@ -326,7 +318,7 @@
             for f in range(2):
                 edges.append(
                     pltpu.make_async_copy(
-                        rim_before.at[pl.ds(skip + f * rows + row, 1)],
+                        before[n].at[pl.ds(line + f * rows + row, 1)],
                         here.at[n, f, outside],
                         sem.at[6 * n + 4 + f],
                     )
@@ -572,19 +564,15 @@
     devices = peers * bands * 2
     sds = jax.ShapeDtypeStruct
 
-    skip = cap * (rows + 1) + 3
     pieces = call(
         functools.partial(pack_body, peers, cap, size),
-        [
-            sds((skip + (2 * rows if k == 1 else 0), cols, chans), BF16)
-            for k in range(peers)
-        ],
+        [sds((cap * (rows + 1) + 3, cols, chans), BF16)] * peers,
         [SM, HB, HB],
         [
             pltpu.VMEM((peers * cap, cols, chans), BF16),
             pltpu.VMEM(clip_video.shape, BF16),
             pltpu.VMEM((3, 2 * frames, chans), BF16),
-            pltpu.SemaphoreType.DMA((2 * peers * cap + 2,)),
+            pltpu.SemaphoreType.DMA((2 * peers * cap,)),
             pltpu.SemaphoreType.DMA((frames,)),
             pltpu.SemaphoreType.DMA((peers,)),
         ],
@@ -597,9 +585,12 @@
         own.append(lax.ppermute(after(clip_video, pieces[0]), "height", ring(bands, m)))
     sib = [sibling(v) for v in own]
     for m in range(1, bands):
-        ready = [v if k == 0 else after(v, own[m]) for k, v in enumerate(ups[0])]
+        ready = [v for k, v in enumerate(ups[0])]
         ups.append([lax.ppermute(v, "height", ring(bands, m)) for v in ready])
-    prev_sib = [sibling(v[1]) for v in ups]
+    prev = jnp.concatenate([v[frames - 2 :] for v in own], axis=0)
+    prev = prev.reshape(2 * bands * rows, cols, chans)
+    prev = lax.ppermute(prev, "tm", [(t, t + 1) for t in range(peers - 1)])
+    prev_sib = sibling(prev)
 
     weight = conv_weight.reshape(9, 3 * full, full)
     turned = call(
@@ -624,14 +615,14 @@
     grads = call(
         functools.partial(weight_body, peers, bands, cap, block),
         [sds((27, block, chans), F32)] + [sds((27, block, chans), BF16)] * (peers - 1),
-        [SM] + [VM] * (2 + 3 * bands + peers * bands),
+        [SM] + [VM] * (4 + 2 * bands + peers * bands),
         [
             pltpu.VMEM((3, frames + 2, bands * rows + 2, cols, width), BF16),
             pltpu.VMEM((frames, bands, chans, rows * cols), BF16),
         ],
         name="weight",
     )(
-        clip_lengths, table, table_sib, *own, *sib, *prev_sib,
+        clip_lengths, table, table_sib, *own, *sib, prev, prev_sib,
         *[v for band in ups for v in band],
     )
     far = bands - 1
@@ -654,9 +645,9 @@
 
     part = sds((frames, half, cols, chans), BF16)
     block_keep, block_give = call(
-        functools.partial(forward_body, bands, skip),
+        functools.partial(forward_body, bands),
         [part, part],
-        [SM, VM, VM] + [HB] * 13,
+        [SM, VM, VM] + [HB] * 9,
         [
             pltpu.VMEM((frames + 2, half + 2, cols, 6 * chans), BF16),
             pltpu.VMEM((2, frames + 2, half + 2, cols, chans), BF16),
@@ -667,7 +658,7 @@
     )(
         clip_lengths, table, table_sib, *far_away(
             after(weight, sums), own[0], sib[0], own[1], sib[1], own[far], sib[far],
-            ups[0][1], prev_sib[0], ups[1][1], prev_sib[1], ups[far][1], prev_sib[far],
+            prev, prev_sib,
         ),
     )
     terms = [lax.ppermute(grads[k], "tm", ring(peers, k)) for k in range(1, peers)]

time: 87.9 us -> 86 us (0.978)
  waiting for transfers between devices: 14.8 us -> 12.6 us
    ppermute x0 -> x1, starting transfers between devices: none -> 3.2 us  [per_device(): prev = lax.ppermute(prev, 'tm', [(t, t + 1) for t in range(peers - 1)])]
    ppermute x3, waiting for transfers between devices: 2.31 us -> 0.01 us  [per_device(): lax.ppermute(pieces[k], 'tm', ring(peers, k))]
    ppermute x9 -> x8, starting transfers between devices: 10.2 us -> 8.34 us  [sibling(): return lax.ppermute(value, 'chan', ring(2, 1))]
    ppermute x3, starting transfers between devices: 5.74 us -> 4.47 us  [per_device(): lax.ppermute(grads[k], 'tm', ring(peers, k))]
    ppermute x4, waiting for transfers between devices: 5.15 us -> 3.89 us  [per_device(): ups.append([lax.ppermute(v, 'height', ring(bands, m)) for v in ready])]
    slice x0 -> x2, local copies, waits for them, and re-layouts: none -> 0.92 us  [per_device(): prev = jnp.concatenate([v[frames - 2:] for v in own], axis=0)]
    ppermute x9 -> x8, waiting for transfers between devices: 1.87 us -> 2.54 us  [sibling(): return lax.ppermute(value, 'chan', ring(2, 1))]
    unnamed x40 -> x36, local copies, waits for them, and re-layouts: 4.28 us -> 4.2 us
  transfers between devices with their start and end apart: 22 -> 22, of which waited for: 6 -> 5; matrix products, arithmetic and copies ran while one was open for 0% -> 1% of each run, Pallas kernels for 35% -> 35%
where the time goes in v6:
time: 86 us; the launch traced here: 84.7 us
  Pallas kernels  35.9 us (42%)
  starting transfers between devices  29.6 us (34%)
  waiting for transfers between devices  12.6 us (15%)
  local copies, waits for them, and re-layouts  5.64 us (7%)
  between operations  0.92 us (1%)
    pallas_call x1, Pallas kernels, per_device(): call(functools.partial(weight_body, peers, bands, cap, block), [sds((27,...  11.1 us
    ppermute x8, starting transfers between devices, sibling(): return lax.ppermute(value, 'chan', ring(2, 1))  8.34 us
    pallas_call x1, Pallas kernels, per_device(): call(functools.partial(forward_body, bands), [part, part], [SM, VM, VM] +...  7.52 us
    pallas_call x1, Pallas kernels, per_device(): call(functools.partial(backward_body, peers), [part, part, sds((devices,...  6.91 us
    ppermute x1, waiting for transfers between devices, per_device(): lax.ppermute(after(clip_video, pieces[0]), 'height', ring(bands, m))  6.13 us
    ppermute x3, starting transfers between devices, per_device(): lax.ppermute(grads[k], 'tm', ring(peers, k))  4.47 us
    all_to_all x1, starting transfers between devices, per_device(): totals = lax.all_to_all(sums, everyone, 0, 0)  4.22 us
    unnamed x36, local copies, waits for them, and re-layouts  4.2 us
  transfers between devices with their start and end apart: 22, of which 5 were waited for; matrix products, arithmetic and copies ran while one was open for 1% of the time, Pallas kernels for 35%

profile of v6, /device:TPU:15, one launch (start us, length us, event | category | flops | bytes accessed | tf_op | source)
XLA Modules:
  0.0 84.7 jit_solution(12837232836610878936)
XLA Ops:
  1.3 2.6 %pack.1 = (bf16[37,16,128]{2,1,0:T(8,128)(2,1)S(1)}, bf16[37,16,128]{2,1,0:T(8,128)(2,1)S(1)}, bf16[37,16,128]{2,1,0:T(8,128)(2,1)S(1)}, bf16[37,16,128]{2,1,0:T(8,128)(2,1)S(1)}) custom-call(s32[8]{0:T(128)S(1)} %copy-done.14, bf16[8,16,16,128]{3,2,1,0:T(8,128)(2,1)} %grad.1, bf16[8,16,16,128]{3,2,1,0:T(8,128)(2,1)} %video.1), custom_call_target="tpu_custom_call" | custom-call | flops 1024 | bytes 1024 | tf_op jit(solution)/shard_map/pack/pallas_call | solution.py:567
  4.2 1.3 %collective-permute-start = (bf16[37,16,128]{2,1,0:T(8,128)(2,1)S(1)}, bf16[37,16,128]{2,1,0:T(8,128)(2,1)S(1)}, u32[]{:S(2)}, u32[]{:S(2)}) collective-permute-start(bf16[37,16,128]{2,1,0:T(8,128)(2,1)S(1)} %get-tuple-element.33), channel_id=1, source_target_pairs={{0,4},{4,8},{8,12},{12,0},{1,5},{5,9},{9,13},{13,1},{2,6},{6,10},{... | collective-permute-start | bytes 454664 | tf_op jit(solution)/shard_map/ppermute | solution.py:581
  5.5 1.0 %collective-permute-start.1 = (bf16[37,16,128]{2,1,0:T(8,128)(2,1)S(1)}, bf16[37,16,128]{2,1,0:T(8,128)(2,1)S(1)}, u32[]{:S(2)}, u32[]{:S(2)}) collective-permute-start(bf16[37,16,128]{2,1,0:T(8,128)(2,1)S(1)} %get-tuple-element.34), channel_id=1, source_target_pairs={{0,8},{4,12},{8,0},{12,4},{1,9},{5,13},{9,1},{13,5},{2,10},{6,14},... | collective-permute-start | bytes 454664 | tf_op jit(solution)/shard_map/ppermute | solution.py:581
  6.5 1.5 %collective-permute-start.2 = (bf16[37,16,128]{2,1,0:T(8,128)(2,1)S(1)}, bf16[37,16,128]{2,1,0:T(8,128)(2,1)S(1)}, u32[]{:S(2)}, u32[]{:S(2)}) collective-permute-start(bf16[37,16,128]{2,1,0:T(8,128)(2,1)S(1)} %get-tuple-element.35), channel_id=1, source_target_pairs={{0,12},{4,0},{8,4},{12,8},{1,13},{5,1},{9,5},{13,9},{2,14},{6,2},{... | collective-permute-start | bytes 454664 | tf_op jit(solution)/shard_map/ppermute | solution.py:581
  8.0 1.2 %collective-permute-start.3 = (bf16[37,16,128]{2,1,0:T(8,128)(2,1)S(1)}, bf16[37,16,128]{2,1,0:T(8,128)(2,1)S(1)}, u32[]{:S(2)}, u32[]{:S(2)}) collective-permute-start(bf16[37,16,128]{2,1,0:T(8,128)(2,1)S(1)} %get-tuple-element.32.refs_0_.refs_9_), channel_id=1, source_target_pairs={{0,2},{2,0},{1,3},{3,1},{4,6},{6,4},{5,7},{7,5},{8,10},{10,8},{9,1... | collective-permute-start | bytes 454664 | tf_op jit(solution)/shard_map/ppermute | solution.py:589
  10.8 6.1 %collective-permute-done.8.refs_4_.refs_2_ = bf16[8,16,16,128]{3,2,1,0:T(8,128)(2,1)S(1)} collective-permute-done((bf16[8,16,16,128]{3,2,1,0:T(8,128)(2,1)}, bf16[8,16,16,128]{3,2,1,0:T(8,128)(2,1)S(1)}, u32[]{:S(2)}, u32[]{:S(2)}) %collective-permute-start.8) | collective-permute-done | bytes 524320 | tf_op jit(solution)/shard_map/ppermute | solution.py:585
  17.0 3.2 %collective-permute-start.11 = (bf16[64,16,128]{2,1,0:T(8,128)(2,1)S(1)}, bf16[64,16,128]{2,1,0:T(8,128)(2,1)S(1)}, u32[]{:S(2)}, u32[]{:S(2)}) collective-permute-start(bf16[64,16,128]{2,1,0:T(8,128)(2,1)S(1)} %bitcast.13), channel_id=1, source_target_pairs={{0,4},{4,8},{8,12},{1,5},{5,9},{9,13},{2,6},{6,10},{10,14},{3,7},{... | collective-permute-start | bytes 786440 | tf_op jit(solution)/shard_map/ppermute | solution.py:592
  20.2 4.3 %collective-permute-start.9 = (bf16[8,16,16,128]{3,2,1,0:T(8,128)(2,1)}, bf16[8,16,16,128]{3,2,1,0:T(8,128)(2,1)S(1)}, u32[]{:S(2)}, u32[]{:S(2)}) collective-permute-start(bf16[8,16,16,128]{3,2,1,0:T(8,128)(2,1)} %video.1), channel_id=1, source_target_pairs={{0,1},{1,0},{2,3},{3,2},{4,5},{5,4},{6,7},{7,6},{8,9},{9,8},{10,11... | collective-permute-start | bytes 1572872 | tf_op jit(solution)/shard_map/ppermute | solution.py:56
  24.9 1.2 %collective-permute-start.6 = (bf16[37,16,128]{2,1,0:T(8,128)(2,1)S(1)}, bf16[37,16,128]{2,1,0:T(8,128)(2,1)S(1)}, u32[]{:S(2)}, u32[]{:S(2)}) collective-permute-start(bf16[37,16,128]{2,1,0:T(8,128)(2,1)S(1)} %collective-permute-done.2.refs_3_.refs_12_), channel_id=1, source_target_pairs={{0,2},{2,0},{1,3},{3,1},{4,6},{6,4},{5,7},{7,5},{8,10},{10,8},{9,1... | collective-permute-start | bytes 454664 | tf_op jit(solution)/shard_map/ppermute | solution.py:589
  26.2 2.0 %copy-done.2 = bf16[3,3,3,256,256]{4,3,2,1,0:T(8,128)(2,1)S(1)} copy-done((bf16[3,3,3,256,256]{4,3,2,1,0:T(8,128)(2,1)S(1)}, bf16[3,3,3,256,256]{4,3,2,1,0:T(8,128)(2,1)}, u32[]{:S(2)}) %copy-start.2) | copy-done | bytes 3538968
  29.8 3.2 %collective-permute-done.6.refs_7_.refs_16_ = bf16[37,16,128]{2,1,0:T(8,128)(2,1)S(1)} collective-permute-done((bf16[37,16,128]{2,1,0:T(8,128)(2,1)S(1)}, bf16[37,16,128]{2,1,0:T(8,128)(2,1)S(1)}, u32[]{:S(2)}, u32[]{:S(2)}) %collective-permute-start.6) | collective-permute-done | bytes 151584 | tf_op jit(solution)/shard_map/ppermute | solution.py:589
  34.0 1.3 %collective-permute-start.13 = (bf16[8,18,16,128]{3,2,1,0:T(8,128)(2,1)S(1)}, bf16[8,18,16,128]{3,2,1,0:T(8,128)(2,1)S(1)}, u32[]{:S(2)}, u32[]{:S(2)}) collective-permute-start(bf16[8,18,16,128]{3,2,1,0:T(8,128)(2,1)S(1)} %get-tuple-element.40.up), channel_id=1, source_target_pairs={{0,1},{1,0},{2,3},{3,2},{4,5},{5,4},{6,7},{7,6},{8,9},{9,8},{10,11... | collective-permute-start | bytes 1769480 | tf_op jit(solution)/shard_map/ppermute | solution.py:56
  35.9 1.5 %collective-permute-done.7.refs_2_.table_sib = f32[40,128]{1,0:T(8,128)S(1)} collective-permute-done((f32[40,128]{1,0:T(8,128)S(1)}, f32[40,128]{1,0:T(8,128)S(1)}, u32[]{:S(2)}, u32[]{:S(2)}) %collective-permute-start.7) | collective-permute-done | bytes 20512 | tf_op jit(solution)/shard_map/ppermute | solution.py:56
  37.4 1.9 %collective-permute-start.14 = (bf16[2,18,16,128]{3,2,1,0:T(8,128)(2,1)S(1)}, bf16[2,18,16,128]{3,2,1,0:T(8,128)(2,1)S(1)}, u32[]{:S(2)}, u32[]{:S(2)}) collective-permute-start(bf16[2,18,16,128]{3,2,1,0:T(8,128)(2,1)S(1)} %get-tuple-element.41), channel_id=1, source_target_pairs={{4,0},{8,4},{12,8},{5,1},{9,5},{13,9},{6,2},{10,6},{14,10},{7,3},{... | collective-permute-start | bytes 442376 | tf_op jit(solution)/shard_map/ppermute | solution.py:630
  39.4 11.1 %weight.1 = (f32[27,32,128]{2,1,0:T(8,128)S(1)}, bf16[27,32,128]{2,1,0:T(8,128)(2,1)S(1)}, bf16[27,32,128]{2,1,0:T(8,128)(2,1)S(1)}, bf16[27,32,128]{2,1,0:T(8,128)(2,1)S(1)}) custom-call(s32[8]{0:T(128)S(1)} %copy-done.11, f32[40,128]{1,0:T(8,128)S(1)} %get-tuple-element.36.refs_1_.table, f32[40,128]{1,0:T(8,128)S(1)} %collective-permute-done.7.refs_2_.table_sib, ...), custom_call_target="tpu_custom_call" | custom-call | flops 1024 | bytes 1024 | tf_op jit(solution)/shard_map/weight/pallas_call | solution.py:615
  50.6 1.7 %collective-permute-start.16 = (bf16[27,32,128]{2,1,0:T(8,128)(2,1)S(1)}, bf16[27,32,128]{2,1,0:T(8,128)(2,1)S(1)}, u32[]{:S(2)}, u32[]{:S(2)}) collective-permute-start(bf16[27,32,128]{2,1,0:T(8,128)(2,1)S(1)} %get-tuple-element.46), channel_id=1, source_target_pairs={{0,4},{4,8},{8,12},{12,0},{1,5},{5,9},{9,13},{13,1},{2,6},{6,10},{... | collective-permute-start | bytes 663560 | tf_op jit(solution)/shard_map/ppermute | solution.py:664
  52.3 2.7 %collective-permute-start.17 = (bf16[27,32,128]{2,1,0:T(8,128)(2,1)S(1)}, bf16[27,32,128]{2,1,0:T(8,128)(2,1)}, u32[]{:S(2)}, u32[]{:S(2)}) collective-permute-start(bf16[27,32,128]{2,1,0:T(8,128)(2,1)S(1)} %get-tuple-element.47), channel_id=1, source_target_pairs={{0,8},{4,12},{8,0},{12,4},{1,9},{5,13},{9,1},{13,5},{2,10},{6,14},... | collective-permute-start | bytes 663560 | tf_op jit(solution)/shard_map/ppermute | solution.py:664
  55.0 1.5 %collective-permute-start.15 = (bf16[2,18,16,128]{3,2,1,0:T(8,128)(2,1)S(1)}, bf16[2,18,16,128]{3,2,1,0:T(8,128)(2,1)S(1)}, u32[]{:S(2)}, u32[]{:S(2)}) collective-permute-start(bf16[2,18,16,128]{3,2,1,0:T(8,128)(2,1)S(1)} %collective-permute-done.14.next_own), channel_id=1, source_target_pairs={{0,1},{1,0},{2,3},{3,2},{4,5},{5,4},{6,7},{7,6},{8,9},{9,8},{10,11... | collective-permute-start | bytes 442376 | tf_op jit(solution)/shard_map/ppermute | solution.py:56
  56.5 1.0 %collective-permute-done.15.next_sib = bf16[2,18,16,128]{3,2,1,0:T(8,128)(2,1)S(1)} collective-permute-done((bf16[2,18,16,128]{3,2,1,0:T(8,128)(2,1)S(1)}, bf16[2,18,16,128]{3,2,1,0:T(8,128)(2,1)S(1)}, u32[]{:S(2)}, u32[]{:S(2)}) %collective-permute-start.15) | collective-permute-done | bytes 147488 | tf_op jit(solution)/shard_map/ppermute | solution.py:56
  57.5 6.9 %backward.1 = (f32[8,128,128]{2,1,0:T(8,128)S(1)}, f32[8,128,128]{2,1,0:T(8,128)}, f32[16,16,128]{2,1,0:T(8,128)}) custom-call(s32[8]{0:T(128)S(1)} %copy-done.11, f32[40,128]{1,0:T(8,128)S(1)} %get-tuple-element.36.refs_1_.table, f32[40,128]{1,0:T(8,128)S(1)} %collective-permute-done.7.refs_2_.table_sib, bf16[9,768,256]{2,1,0:T(8,128)(2,1)S(1)} %turn.1.weight, ...), custom_call_target="tpu_custom_call" | custom-call | flops 1024 | bytes 1024 | tf_op jit(solution)/shard_map/backward/pallas_call | solution.py:633
  65.3 4.2 %all-to-all-start = ((f32[16,16,128]{2,1,0:T(8,128)}), f32[16,16,128]{2,1,0:T(8,128)}, u32[]{:S(2)}, u32[]{:S(2)}) async-start(f32[16,16,128]{2,1,0:T(8,128)} %get-tuple-element.42), calls=%async_computation | async-start | bytes 262144 | tf_op jit(solution)/shard_map/all_to_all | solution.py:643
  69.5 7.5 %forward.1 = (bf16[8,8,16,128]{3,2,1,0:T(8,128)(2,1)S(1)}, bf16[8,8,16,128]{3,2,1,0:T(8,128)(2,1)}) custom-call(s32[8]{0:T(128)S(1)} %copy-done.11, f32[40,128]{1,0:T(8,128)S(1)} %get-tuple-element.36.refs_1_.table, f32[40,128]{1,0:T(8,128)S(1)} %collective-permute-done.7.refs_2_.table_sib, bf16[9,768,256]{2,1,0:T(8,128)(2,1)} %bitcast.9, ...), custom_call_target="tpu_custom_call" | custom-call | flops 1024 | bytes 1024 | tf_op jit(solution)/shard_map/forward/pallas_call | solution.py:647
  78.3 2.2 %collect.1 = f32[27,32,128]{2,1,0:T(8,128)} custom-call(f32[27,32,128]{2,1,0:T(8,128)} %copy-done.15, bf16[27,32,128]{2,1,0:T(8,128)(2,1)} %copy-done.17, bf16[27,32,128]{2,1,0:T(8,128)(2,1)} %collective-permute-done.17.refs_2_, bf16[27,32,128]{2,1,0:T(8,128)(2,1)} %copy-done.16), custom_call_target="tpu_custom_call" | custom-call | flops 9999999827968 | bytes 1024 | tf_op jit(solution)/shard_map/collect/pallas_call | solution.py:665
  80.6 3.6 %finish.1 = (bf16[8,16,16,128]{3,2,1,0:T(8,128)(2,1)}, bf16[8,16,16,128]{3,2,1,0:T(8,128)(2,1)}, f32[8,128]{1,0:T(8,128)S(1)}) custom-call(s32[8]{0:T(128)S(1)} %copy-done.11, f32[40,128]{1,0:T(8,128)S(1)} %get-tuple-element.36.refs_1_.table, f32[16,16,128]{2,1,0:T(8,128)} %all-to-all-done.got, bf16[8,16,16,128]{3,2,1,0:T(8,128)(2,1)S(1)} %copy-done.1, ...), custom_call_target="tpu_custom_call" | custom-call | flops 1024 | bytes 1024 | tf_op jit(solution)/shard_map/finish/pallas_call | solution.py:675
  (68 shorter events, 8.8 us)
Async XLA Ops:
  3.9 13.1 %collective-permute-start.8 = (bf16[8,16,16,128]{3,2,1,0:T(8,128)(2,1)}, bf16[8,16,16,128]{3,2,1,0:T(8,128)(2,1)S(1)}, u32[]{:S(2)}, u32[]{:S(2)}) collective-permute-start(bf16[8,16,16,128]{3,2,1,0:T(8,128)(2,1)} %video.1), channel_id=1, source_target_pairs={{0,2},{2,0},{1,3},{3,1},{4,6},{6,4},{5,7},{7,5},{8,10},{10,8},{9,1... | collective-permute-start | bytes 1572872 | tf_op jit(solution)/shard_map/ppermute | solution.py:585
  4.2 5.0 %collective-permute-start = (bf16[37,16,128]{2,1,0:T(8,128)(2,1)S(1)}, bf16[37,16,128]{2,1,0:T(8,128)(2,1)S(1)}, u32[]{:S(2)}, u32[]{:S(2)}) collective-permute-start(bf16[37,16,128]{2,1,0:T(8,128)(2,1)S(1)} %get-tuple-element.33), channel_id=1, source_target_pairs={{0,4},{4,8},{8,12},{12,0},{1,5},{5,9},{9,13},{13,1},{2,6},{6,10},{... | collective-permute-start | bytes 454664 | tf_op jit(solution)/shard_map/ppermute | solution.py:581
  5.5 14.7 %collective-permute-start.1 = (bf16[37,16,128]{2,1,0:T(8,128)(2,1)S(1)}, bf16[37,16,128]{2,1,0:T(8,128)(2,1)S(1)}, u32[]{:S(2)}, u32[]{:S(2)}) collective-permute-start(bf16[37,16,128]{2,1,0:T(8,128)(2,1)S(1)} %get-tuple-element.34), channel_id=1, source_target_pairs={{0,8},{4,12},{8,0},{12,4},{1,9},{5,13},{9,1},{13,5},{2,10},{6,14},... | collective-permute-start | bytes 454664 | tf_op jit(solution)/shard_map/ppermute | solution.py:581
  6.5 18.1 %collective-permute-start.2 = (bf16[37,16,128]{2,1,0:T(8,128)(2,1)S(1)}, bf16[37,16,128]{2,1,0:T(8,128)(2,1)S(1)}, u32[]{:S(2)}, u32[]{:S(2)}) collective-permute-start(bf16[37,16,128]{2,1,0:T(8,128)(2,1)S(1)} %get-tuple-element.35), channel_id=1, source_target_pairs={{0,12},{4,0},{8,4},{12,8},{1,13},{5,1},{9,5},{13,9},{2,14},{6,2},{... | collective-permute-start | bytes 454664 | tf_op jit(solution)/shard_map/ppermute | solution.py:581
  8.0 16.7 %collective-permute-start.3 = (bf16[37,16,128]{2,1,0:T(8,128)(2,1)S(1)}, bf16[37,16,128]{2,1,0:T(8,128)(2,1)S(1)}, u32[]{:S(2)}, u32[]{:S(2)}) collective-permute-start(bf16[37,16,128]{2,1,0:T(8,128)(2,1)S(1)} %get-tuple-element.32.refs_0_.refs_9_), channel_id=1, source_target_pairs={{0,2},{2,0},{1,3},{3,1},{4,6},{6,4},{5,7},{7,5},{8,10},{10,8},{9,1... | collective-permute-start | bytes 454664 | tf_op jit(solution)/shard_map/ppermute | solution.py:589
  9.2 15.7 %collective-permute-start.4 = (bf16[37,16,128]{2,1,0:T(8,128)(2,1)S(1)}, bf16[37,16,128]{2,1,0:T(8,128)(2,1)S(1)}, u32[]{:S(2)}, u32[]{:S(2)}) collective-permute-start(bf16[37,16,128]{2,1,0:T(8,128)(2,1)S(1)} %collective-permute-done.refs_1_.refs_10_), channel_id=1, source_target_pairs={{0,2},{2,0},{1,3},{3,1},{4,6},{6,4},{5,7},{7,5},{8,10},{10,8},{9,1... | collective-permute-start | bytes 454664 | tf_op jit(solution)/shard_map/ppermute | solution.py:589
  17.0 18.3 %collective-permute-start.11 = (bf16[64,16,128]{2,1,0:T(8,128)(2,1)S(1)}, bf16[64,16,128]{2,1,0:T(8,128)(2,1)S(1)}, u32[]{:S(2)}, u32[]{:S(2)}) collective-permute-start(bf16[64,16,128]{2,1,0:T(8,128)(2,1)S(1)} %bitcast.13), channel_id=1, source_target_pairs={{0,4},{4,8},{8,12},{1,5},{5,9},{9,13},{2,6},{6,10},{10,14},{3,7},{... | collective-permute-start | bytes 786440 | tf_op jit(solution)/shard_map/ppermute | solution.py:592
  20.2 19.1 %collective-permute-start.9 = (bf16[8,16,16,128]{3,2,1,0:T(8,128)(2,1)}, bf16[8,16,16,128]{3,2,1,0:T(8,128)(2,1)S(1)}, u32[]{:S(2)}, u32[]{:S(2)}) collective-permute-start(bf16[8,16,16,128]{3,2,1,0:T(8,128)(2,1)} %video.1), channel_id=1, source_target_pairs={{0,1},{1,0},{2,3},{3,2},{4,5},{5,4},{6,7},{7,6},{8,9},{9,8},{10,11... | collective-permute-start | bytes 1572872 | tf_op jit(solution)/shard_map/ppermute | solution.py:56
  24.6 14.8 %collective-permute-start.10 = (bf16[8,16,16,128]{3,2,1,0:T(8,128)(2,1)S(1)}, bf16[8,16,16,128]{3,2,1,0:T(8,128)(2,1)S(1)}, u32[]{:S(2)}, u32[]{:S(2)}) collective-permute-start(bf16[8,16,16,128]{3,2,1,0:T(8,128)(2,1)S(1)} %collective-permute-done.8.refs_4_.refs_2_), channel_id=1, source_target_pairs={{0,1},{1,0},{2,3},{3,2},{4,5},{5,4},{6,7},{7,6},{8,9},{9,8},{10,11... | collective-permute-start | bytes 1572872 | tf_op jit(solution)/shard_map/ppermute | solution.py:56
  24.7 5.1 %collective-permute-start.5 = (bf16[37,16,128]{2,1,0:T(8,128)(2,1)S(1)}, bf16[37,16,128]{2,1,0:T(8,128)(2,1)S(1)}, u32[]{:S(2)}, u32[]{:S(2)}) collective-permute-start(bf16[37,16,128]{2,1,0:T(8,128)(2,1)S(1)} %collective-permute-done.1.refs_2_.refs_11_), channel_id=1, source_target_pairs={{0,2},{2,0},{1,3},{3,1},{4,6},{6,4},{5,7},{7,5},{8,10},{10,8},{9,1... | collective-permute-start | bytes 454664 | tf_op jit(solution)/shard_map/ppermute | solution.py:589
  24.9 8.1 %collective-permute-start.6 = (bf16[37,16,128]{2,1,0:T(8,128)(2,1)S(1)}, bf16[37,16,128]{2,1,0:T(8,128)(2,1)S(1)}, u32[]{:S(2)}, u32[]{:S(2)}) collective-permute-start(bf16[37,16,128]{2,1,0:T(8,128)(2,1)S(1)} %collective-permute-done.2.refs_3_.refs_12_), channel_id=1, source_target_pairs={{0,2},{2,0},{1,3},{3,1},{4,6},{6,4},{5,7},{7,5},{8,10},{10,8},{9,1... | collective-permute-start | bytes 454664 | tf_op jit(solution)/shard_map/ppermute | solution.py:589
  34.0 30.4 %copy-start.6 = (bf16[8,18,16,128]{3,2,1,0:T(8,128)(2,1)}, bf16[8,18,16,128]{3,2,1,0:T(8,128)(2,1)S(1)}, u32[]{:S(2)}) copy-start(bf16[8,18,16,128]{3,2,1,0:T(8,128)(2,1)S(1)} %get-tuple-element.40.up) | copy-start | bytes 1769476
  34.0 23.5 %collective-permute-start.13 = (bf16[8,18,16,128]{3,2,1,0:T(8,128)(2,1)S(1)}, bf16[8,18,16,128]{3,2,1,0:T(8,128)(2,1)S(1)}, u32[]{:S(2)}, u32[]{:S(2)}) collective-permute-start(bf16[8,18,16,128]{3,2,1,0:T(8,128)(2,1)S(1)} %get-tuple-element.40.up), channel_id=1, source_target_pairs={{0,1},{1,0},{2,3},{3,2},{4,5},{5,4},{6,7},{7,6},{8,9},{9,8},{10,11... | collective-permute-start | bytes 1769480 | tf_op jit(solution)/shard_map/ppermute | solution.py:56
  35.4 29.1 %copy-start.8 = (bf16[64,16,128]{2,1,0:T(8,128)(2,1)}, bf16[64,16,128]{2,1,0:T(8,128)(2,1)S(1)}, u32[]{:S(2)}) copy-start(bf16[64,16,128]{2,1,0:T(8,128)(2,1)S(1)} %collective-permute-done.11.refs_7_.refs_6_) | copy-start | bytes 786436
  35.4 4.0 %collective-permute-start.12 = (bf16[64,16,128]{2,1,0:T(8,128)(2,1)S(1)}, bf16[64,16,128]{2,1,0:T(8,128)(2,1)S(1)}, u32[]{:S(2)}, u32[]{:S(2)}) collective-permute-start(bf16[64,16,128]{2,1,0:T(8,128)(2,1)S(1)} %collective-permute-done.11.refs_7_.refs_6_), channel_id=1, source_target_pairs={{0,1},{1,0},{2,3},{3,2},{4,5},{5,4},{6,7},{7,6},{8,9},{9,8},{10,11... | collective-permute-start | bytes 786440 | tf_op jit(solution)/shard_map/ppermute | solution.py:56
  35.5 1.9 %collective-permute-start.7 = (f32[40,128]{1,0:T(8,128)S(1)}, f32[40,128]{1,0:T(8,128)S(1)}, u32[]{:S(2)}, u32[]{:S(2)}) collective-permute-start(f32[40,128]{1,0:T(8,128)S(1)} %get-tuple-element.36.refs_1_.table), channel_id=1, source_target_pairs={{0,1},{1,0},{2,3},{3,2},{4,5},{5,4},{6,7},{7,6},{8,9},{9,8},{10,11... | collective-permute-start | bytes 61448 | tf_op jit(solution)/shard_map/ppermute | solution.py:56
  37.4 17.6 %collective-permute-start.14 = (bf16[2,18,16,128]{3,2,1,0:T(8,128)(2,1)S(1)}, bf16[2,18,16,128]{3,2,1,0:T(8,128)(2,1)S(1)}, u32[]{:S(2)}, u32[]{:S(2)}) collective-permute-start(bf16[2,18,16,128]{3,2,1,0:T(8,128)(2,1)S(1)} %get-tuple-element.41), channel_id=1, source_target_pairs={{4,0},{8,4},{12,8},{5,1},{9,5},{13,9},{6,2},{10,6},{14,10},{7,3},{... | collective-permute-start | bytes 442376 | tf_op jit(solution)/shard_map/ppermute | solution.py:630
  50.5 26.9 %collective-permute-start.18 = (bf16[27,32,128]{2,1,0:T(8,128)(2,1)S(1)}, bf16[27,32,128]{2,1,0:T(8,128)(2,1)S(1)}, u32[]{:S(2)}, u32[]{:S(2)}) collective-permute-start(bf16[27,32,128]{2,1,0:T(8,128)(2,1)S(1)} %get-tuple-element.48), channel_id=1, source_target_pairs={{0,12},{4,0},{8,4},{12,8},{1,13},{5,1},{9,5},{13,9},{2,14},{6,2},{... | collective-permute-start | bytes 663560 | tf_op jit(solution)/shard_map/ppermute | solution.py:664
  50.6 27.0 %collective-permute-start.16 = (bf16[27,32,128]{2,1,0:T(8,128)(2,1)S(1)}, bf16[27,32,128]{2,1,0:T(8,128)(2,1)S(1)}, u32[]{:S(2)}, u32[]{:S(2)}) collective-permute-start(bf16[27,32,128]{2,1,0:T(8,128)(2,1)S(1)} %get-tuple-element.46), channel_id=1, source_target_pairs={{0,4},{4,8},{8,12},{12,0},{1,5},{5,9},{9,13},{13,1},{2,6},{6,10},{... | collective-permute-start | bytes 663560 | tf_op jit(solution)/shard_map/ppermute | solution.py:664
  52.3 26.0 %collective-permute-start.17 = (bf16[27,32,128]{2,1,0:T(8,128)(2,1)S(1)}, bf16[27,32,128]{2,1,0:T(8,128)(2,1)}, u32[]{:S(2)}, u32[]{:S(2)}) collective-permute-start(bf16[27,32,128]{2,1,0:T(8,128)(2,1)S(1)} %get-tuple-element.47), channel_id=1, source_target_pairs={{0,8},{4,12},{8,0},{12,4},{1,9},{5,13},{9,1},{13,5},{2,10},{6,14},... | collective-permute-start | bytes 663560 | tf_op jit(solution)/shard_map/ppermute | solution.py:664
  55.0 2.5 %collective-permute-start.15 = (bf16[2,18,16,128]{3,2,1,0:T(8,128)(2,1)S(1)}, bf16[2,18,16,128]{3,2,1,0:T(8,128)(2,1)S(1)}, u32[]{:S(2)}, u32[]{:S(2)}) collective-permute-start(bf16[2,18,16,128]{3,2,1,0:T(8,128)(2,1)S(1)} %collective-permute-done.14.next_own), channel_id=1, source_target_pairs={{0,1},{1,0},{2,3},{3,2},{4,5},{5,4},{6,7},{7,6},{8,9},{9,8},{10,11... | collective-permute-start | bytes 442376 | tf_op jit(solution)/shard_map/ppermute | solution.py:56
  65.3 15.3 %all-to-all-start = ((f32[16,16,128]{2,1,0:T(8,128)}), f32[16,16,128]{2,1,0:T(8,128)}, u32[]{:S(2)}, u32[]{:S(2)}) async-start(f32[16,16,128]{2,1,0:T(8,128)} %get-tuple-element.42), calls=%async_computation | async-start | bytes 262144 | tf_op jit(solution)/shard_map/all_to_all | solution.py:643
  77.0 3.5 %collective-permute-start.19 = (f32[8,128,128]{2,1,0:T(8,128)}, f32[8,128,128]{2,1,0:T(8,128)}, u32[]{:S(2)}, u32[]{:S(2)}) collective-permute-start(f32[8,128,128]{2,1,0:T(8,128)} %get-tuple-element.51), channel_id=1, source_target_pairs={{0,1},{1,0},{2,3},{3,2},{4,5},{5,4},{6,7},{7,6},{8,9},{9,8},{10,11... | collective-permute-start | bytes 1572872 | tf_op jit(solution)/shard_map/ppermute | solution.py:56
  77.5 3.1 %collective-permute-start.20 = (bf16[8,8,16,128]{3,2,1,0:T(8,128)(2,1)}, bf16[8,8,16,128]{3,2,1,0:T(8,128)(2,1)}, u32[]{:S(2)}, u32[]{:S(2)}) collective-permute-start(bf16[8,8,16,128]{3,2,1,0:T(8,128)(2,1)} %get-tuple-element.53), channel_id=1, source_target_pairs={{0,1},{1,0},{2,3},{3,2},{4,5},{5,4},{6,7},{7,6},{8,9},{9,8},{10,11... | collective-permute-start | bytes 786440 | tf_op jit(solution)/shard_map/ppermute | solution.py:56
  (16 other events, 147.0 us)

commit v7 on v6

--- a/solution.py
+++ b/solution.py
@@ -28,7 +28,7 @@
         body,
         out_shape=out_shape,
         in_specs=in_specs,
-        out_specs=jax.tree.map(lambda _: where, out_shape),
+        out_specs=where if isinstance(where, list) else jax.tree.map(lambda _: where, out_shape),
         scratch_shapes=list(scratch),
         compiler_params=pltpu.CompilerParams(vmem_limit_bytes=room * 2**20),
         cost_estimate=pl.CostEstimate(flops=work, bytes_accessed=1024, transcendentals=0),
@@ -500,28 +500,30 @@
         give[t] = jnp.where(c == 0, right, left)
 
 
-def collect_body(*refs):
-    count = len(refs) // 2 - 1
-    far, out, near, sem = refs[:count], refs[count], refs[count + 1 : -1], refs[-1]
-    loads = [pltpu.make_async_copy(far[n], near[n], sem.at[n]) for n in range(count)]
-    for load in loads:
-        load.start()
-    for load in loads:
-        load.wait()
-    for tap in range(out.shape[0]):
-        total = near[0][tap]
-        for term in near[1:]:
-            total = total + term[tap].astype(F32)
-        out[tap] = total
-
-
-def finish_body(size, bands, lengths, table, got, video, keep_far, other, up, block_keep, block_other, out, block, small, keep, sem):
-    load = pltpu.make_async_copy(keep_far, keep, sem)
-    load.start()
+def arrive_body(*refs):
+    refs[-1][...] = jnp.zeros(refs[-1].shape, F32)
+
+
+def finish_body(size, bands, count, lengths, table, got, token, video, other, up, *refs):
+    block_keep, block_other, keep_far = refs[:3]
+    terms_far = refs[3 : 3 + count]
+    out_far, block, small, grad_far = refs[3 + count : 7 + count]
+    keep, out, *terms, grad, sem, done = refs[7 + count :]
     frames, rows, cols, chans = video.shape
     half = rows // 2
     cells = half * cols
     tm, c = lax.axis_index("tm"), lax.axis_index("chan")
+    loads = [pltpu.make_async_copy(keep_far, keep, sem.at[count])]
+    for n in range(count):
+        loads.append(pltpu.make_async_copy(terms_far[n], terms[n], sem.at[n]))
+    stores = [
+        pltpu.make_async_copy(block_keep, block.at[:, pl.ds(c * half, half)], done.at[frames]),
+        pltpu.make_async_copy(
+            block_other, block.at[:, pl.ds((1 - c) * half, half)], done.at[frames + 1]
+        ),
+    ]
+    for copy in loads + stores:
+        copy.start()
     first_frame = tm * frames
     whole = jnp.sum(got[...], axis=0)
     gain = table[32:33]
@@ -534,10 +536,8 @@
     spread = jnp.where(clip_of(lengths, first_frame + iota((frames, NCLIPS), 0)) == clip, inverse, 0.0)
     first = fdot(spread, fdot(whole[:NCLIPS] * gain, group))
     second = fdot(spread, fdot(whole[NCLIPS:] * gain, group))
-    load.wait()
+    loads[0].wait()
     for t in range(frames):
-        block[t, pl.ds(c * half, half)] = block_keep[t]
-        block[t, pl.ds((1 - c) * half, half)] = block_other[t]
         inv = table[t + 18 : t + 19]
         for grads, at in ((keep, c * half), (other, (1 - c) * half)):
             x = video[t, pl.ds(at, half)].reshape(cells, chans).astype(F32)
@@ -545,6 +545,19 @@
             part = inv * (grads[t] * gain - first[t : t + 1] - hat * second[t : t + 1])
             u = up[t, pl.ds(at + 1, half)].reshape(cells, chans).astype(F32)
             out[t, pl.ds(at, half)] = (u + part).astype(BF16).reshape(half, cols, chans)
+        stores.append(pltpu.make_async_copy(out.at[t], out_far.at[t], done.at[t]))
+        stores[-1].start()
+    for load in loads[1:]:
+        load.wait()
+    for tap in range(grad.shape[0]):
+        total = terms[0][tap]
+        for term in terms[1:]:
+            total = total + term[tap].astype(F32)
+        grad[tap] = total
+    stores.append(pltpu.make_async_copy(grad, grad_far, done.at[frames + 2]))
+    stores[-1].start()
+    for store in stores:
+        store.wait()
 
 
 def per_device(
@@ -582,7 +595,7 @@
 
     own = [clip_video]
     for m in range(1, bands):
-        own.append(lax.ppermute(after(clip_video, pieces[0]), "height", ring(bands, m)))
+        own.append(lax.ppermute(clip_video, "height", ring(bands, m)))
     sib = [sibling(v) for v in own]
     for m in range(1, bands):
         ready = [v for k, v in enumerate(ups[0])]
@@ -661,24 +674,34 @@
             prev, prev_sib,
         ),
     )
-    terms = [lax.ppermute(grads[k], "tm", ring(peers, k)) for k in range(1, peers)]
-    weight_grad = call(
-        collect_body, sds((27, block, chans), F32), [HB] * peers,
-        [pltpu.VMEM((27, block, chans), F32)]
+    arrived = [lax.ppermute(grads[k], "tm", ring(peers, k)) for k in range(1, peers)]
+    terms = far_away(after(grads[0], block_give), *arrived)
+    token = call(
+        arrive_body, sds((8, chans), F32), [HB] * peers, name="arrive", work=10**13
+    )(*terms)
+    block_other = sibling(after(block_give, arrived[-1]))
+    video_grad, block_out, small, weight_grad = call(
+        functools.partial(finish_body, size, bands, peers),
+        [sds(clip_video.shape, BF16)] * 2
+        + [sds((8, chans), F32), sds((27, block, chans), F32)],
+        [SM] + [VM] * 8 + [HB] * (1 + peers),
+        [
+            pltpu.VMEM((frames, half * cols, chans), F32),
+            pltpu.VMEM(clip_video.shape, BF16),
+            pltpu.VMEM((27, block, chans), F32),
+        ]
         + [pltpu.VMEM((27, block, chans), BF16)] * (peers - 1)
-        + [pltpu.SemaphoreType.DMA((peers,))],
-        name="collect", work=10**13,
-    )(*far_away(after(grads[0], block_give), *terms))
+        + [
+            pltpu.VMEM((27, block, chans), F32),
+            pltpu.SemaphoreType.DMA((peers + 1,)),
+            pltpu.SemaphoreType.DMA((frames + 3,)),
+        ],
+        name="finish", where=[ANY, ANY, VM, ANY],
+    )(
+        clip_lengths, table, totals, token, clip_video, other, up, block_keep, block_other,
+        *far_away(keep), *terms,
+    )
     weight_grad = weight_grad.reshape(3, 3, 3, block, chans)
-
-    block_other = sibling(after(block_give, terms[-1]))
-    video_grad, block_out, small = call(
-        functools.partial(finish_body, size, bands),
-        [sds(clip_video.shape, BF16)] * 2 + [sds((8, chans), F32)],
-        [SM] + [VM] * 3 + [HB] + [VM] * 4,
-        [pltpu.VMEM((frames, half * cols, chans), F32), pltpu.SemaphoreType.DMA],
-        name="finish",
-    )(clip_lengths, table, after(totals, weight_grad), clip_video, *far_away(keep), other, up, block_keep, block_other)
     return (block_out, video_grad, weight_grad, small[0], small[1])
 
 

time: 86 us -> 85.8 us (level)
  starting transfers between devices: 29.6 us -> 32.1 us
  Pallas kernels: 35.9 us -> 33.9 us
  waiting for transfers between devices: 12.6 us -> 11.3 us
    ppermute x1, waiting for transfers between devices: 6.13 us -> 2.8 us  [per_device(): own.append(lax.ppermute(clip_video, 'height', ring(bands, m)))]
    ppermute x8, starting transfers between devices: 8.34 us -> 11 us  [sibling(): return lax.ppermute(value, 'chan', ring(2, 1))]
    pallas_call x2, Pallas kernels: 5.8 us -> 3.74 us  [the longest x1 3.73 us: per_device(): call(functools.partial(finish_body, size, bands, peers), [sds(clip_video....]
    ppermute x8, waiting for transfers between devices: 2.54 us -> 3.92 us  [sibling(): return lax.ppermute(value, 'chan', ring(2, 1))]
  transfers between devices with their start and end apart: 22 -> 22, of which waited for: 5 -> 7; matrix products, arithmetic and copies ran while one was open for 1% -> 1% of each run, Pallas kernels for 35% -> 36%
where the time goes in v7:
time: 85.8 us; the launch traced here: 84.5 us
  Pallas kernels  33.9 us (40%)
  starting transfers between devices  32.1 us (37%)
  waiting for transfers between devices  11.3 us (13%)
  local copies, waits for them, and re-layouts  6.42 us (7%)
  between operations  0.87 us (1%)
    pallas_call x1, Pallas kernels, per_device(): call(functools.partial(weight_body, peers, bands, cap, block), [sds((27,...  11.1 us
    ppermute x8, starting transfers between devices, sibling(): return lax.ppermute(value, 'chan', ring(2, 1))  11 us
    pallas_call x1, Pallas kernels, per_device(): call(functools.partial(forward_body, bands), [part, part], [SM, VM, VM] +...  7.53 us
    pallas_call x1, Pallas kernels, per_device(): call(functools.partial(backward_body, peers), [part, part, sds((devices,...  6.91 us
    unnamed x36, local copies, waits for them, and re-layouts  4.98 us
    all_to_all x1, starting transfers between devices, per_device(): totals = lax.all_to_all(sums, everyone, 0, 0)  4.22 us
    ppermute x3, starting transfers between devices, per_device(): lax.ppermute(grads[k], 'tm', ring(peers, k))  4.17 us
    ppermute x8, waiting for transfers between devices, sibling(): return lax.ppermute(value, 'chan', ring(2, 1))  3.92 us
  transfers between devices with their start and end apart: 22, of which 7 were waited for; matrix products, arithmetic and copies ran while one was open for 1% of the time, Pallas kernels for 36%

profile of v7, /device:TPU:15, one launch (start us, length us, event | category | flops | bytes accessed | tf_op | source)
XLA Modules:
  0.0 84.5 jit_solution(18154691264203352243)
XLA Ops:
  1.6 2.6 %pack.1 = (bf16[37,16,128]{2,1,0:T(8,128)(2,1)S(1)}, bf16[37,16,128]{2,1,0:T(8,128)(2,1)S(1)}, bf16[37,16,128]{2,1,0:T(8,128)(2,1)S(1)}, bf16[37,16,128]{2,1,0:T(8,128)(2,1)S(1)}) custom-call(s32[8]{0:T(128)S(1)} %copy-done.15, bf16[8,16,16,128]{3,2,1,0:T(8,128)(2,1)} %grad.1, bf16[8,16,16,128]{3,2,1,0:T(8,128)(2,1)} %video.1), custom_call_target="tpu_custom_call" | custom-call | flops 1024 | bytes 1024 | tf_op jit(solution)/shard_map/pack/pallas_call | solution.py:580
  4.2 1.3 %collective-permute-start = (bf16[37,16,128]{2,1,0:T(8,128)(2,1)S(1)}, bf16[37,16,128]{2,1,0:T(8,128)(2,1)S(1)}, u32[]{:S(2)}, u32[]{:S(2)}) collective-permute-start(bf16[37,16,128]{2,1,0:T(8,128)(2,1)S(1)} %get-tuple-element.32), channel_id=1, source_target_pairs={{0,4},{4,8},{8,12},{12,0},{1,5},{5,9},{9,13},{13,1},{2,6},{6,10},{... | collective-permute-start | bytes 454664 | tf_op jit(solution)/shard_map/ppermute | solution.py:594
  5.6 1.1 %collective-permute-start.1 = (bf16[37,16,128]{2,1,0:T(8,128)(2,1)S(1)}, bf16[37,16,128]{2,1,0:T(8,128)(2,1)S(1)}, u32[]{:S(2)}, u32[]{:S(2)}) collective-permute-start(bf16[37,16,128]{2,1,0:T(8,128)(2,1)S(1)} %get-tuple-element.33), channel_id=1, source_target_pairs={{0,8},{4,12},{8,0},{12,4},{1,9},{5,13},{9,1},{13,5},{2,10},{6,14},... | collective-permute-start | bytes 454664 | tf_op jit(solution)/shard_map/ppermute | solution.py:594
  6.7 1.4 %collective-permute-start.2 = (bf16[37,16,128]{2,1,0:T(8,128)(2,1)S(1)}, bf16[37,16,128]{2,1,0:T(8,128)(2,1)S(1)}, u32[]{:S(2)}, u32[]{:S(2)}) collective-permute-start(bf16[37,16,128]{2,1,0:T(8,128)(2,1)S(1)} %get-tuple-element.34), channel_id=1, source_target_pairs={{0,12},{4,0},{8,4},{12,8},{1,13},{5,1},{9,5},{13,9},{2,14},{6,2},{... | collective-permute-start | bytes 454664 | tf_op jit(solution)/shard_map/ppermute | solution.py:594
  8.1 1.2 %collective-permute-start.3 = (bf16[37,16,128]{2,1,0:T(8,128)(2,1)S(1)}, bf16[37,16,128]{2,1,0:T(8,128)(2,1)S(1)}, u32[]{:S(2)}, u32[]{:S(2)}) collective-permute-start(bf16[37,16,128]{2,1,0:T(8,128)(2,1)S(1)} %get-tuple-element.31.refs_0_.refs_9_), channel_id=1, source_target_pairs={{0,2},{2,0},{1,3},{3,1},{4,6},{6,4},{5,7},{7,5},{8,10},{10,8},{9,1... | collective-permute-start | bytes 454664 | tf_op jit(solution)/shard_map/ppermute | solution.py:602
  10.9 2.8 %collective-permute-done.8.refs_4_.refs_2_ = bf16[8,16,16,128]{3,2,1,0:T(8,128)(2,1)S(1)} collective-permute-done((bf16[8,16,16,128]{3,2,1,0:T(8,128)(2,1)}, bf16[8,16,16,128]{3,2,1,0:T(8,128)(2,1)S(1)}, u32[]{:S(2)}, u32[]{:S(2)}) %collective-permute-start.8) | collective-permute-done | bytes 524320 | tf_op jit(solution)/shard_map/ppermute | solution.py:598
  13.7 3.2 %collective-permute-start.11 = (bf16[64,16,128]{2,1,0:T(8,128)(2,1)S(1)}, bf16[64,16,128]{2,1,0:T(8,128)(2,1)S(1)}, u32[]{:S(2)}, u32[]{:S(2)}) collective-permute-start(bf16[64,16,128]{2,1,0:T(8,128)(2,1)S(1)} %bitcast.13), channel_id=1, source_target_pairs={{0,4},{4,8},{8,12},{1,5},{5,9},{9,13},{2,6},{6,10},{10,14},{3,7},{... | collective-permute-start | bytes 786440 | tf_op jit(solution)/shard_map/ppermute | solution.py:605
  17.6 7.0 %collective-permute-start.9 = (bf16[8,16,16,128]{3,2,1,0:T(8,128)(2,1)}, bf16[8,16,16,128]{3,2,1,0:T(8,128)(2,1)S(1)}, u32[]{:S(2)}, u32[]{:S(2)}) collective-permute-start(bf16[8,16,16,128]{3,2,1,0:T(8,128)(2,1)} %video.1), channel_id=1, source_target_pairs={{0,1},{1,0},{2,3},{3,2},{4,5},{5,4},{6,7},{7,6},{8,9},{9,8},{10,11... | collective-permute-start | bytes 1572872 | tf_op jit(solution)/shard_map/ppermute | solution.py:56
  25.0 1.2 %collective-permute-start.6 = (bf16[37,16,128]{2,1,0:T(8,128)(2,1)S(1)}, bf16[37,16,128]{2,1,0:T(8,128)(2,1)S(1)}, u32[]{:S(2)}, u32[]{:S(2)}) collective-permute-start(bf16[37,16,128]{2,1,0:T(8,128)(2,1)S(1)} %collective-permute-done.2.refs_3_.refs_12_), channel_id=1, source_target_pairs={{0,2},{2,0},{1,3},{3,1},{4,6},{6,4},{5,7},{7,5},{8,10},{10,8},{9,1... | collective-permute-start | bytes 454664 | tf_op jit(solution)/shard_map/ppermute | solution.py:602
  26.2 2.0 %copy-done.2 = bf16[3,3,3,256,256]{4,3,2,1,0:T(8,128)(2,1)S(1)} copy-done((bf16[3,3,3,256,256]{4,3,2,1,0:T(8,128)(2,1)S(1)}, bf16[3,3,3,256,256]{4,3,2,1,0:T(8,128)(2,1)}, u32[]{:S(2)}) %copy-start.2) | copy-done | bytes 3538968
  29.8 3.2 %collective-permute-done.6.refs_7_.refs_16_ = bf16[37,16,128]{2,1,0:T(8,128)(2,1)S(1)} collective-permute-done((bf16[37,16,128]{2,1,0:T(8,128)(2,1)S(1)}, bf16[37,16,128]{2,1,0:T(8,128)(2,1)S(1)}, u32[]{:S(2)}, u32[]{:S(2)}) %collective-permute-start.6) | collective-permute-done | bytes 151584 | tf_op jit(solution)/shard_map/ppermute | solution.py:602
  34.1 1.3 %collective-permute-start.13 = (bf16[8,18,16,128]{3,2,1,0:T(8,128)(2,1)S(1)}, bf16[8,18,16,128]{3,2,1,0:T(8,128)(2,1)S(1)}, u32[]{:S(2)}, u32[]{:S(2)}) collective-permute-start(bf16[8,18,16,128]{3,2,1,0:T(8,128)(2,1)S(1)} %get-tuple-element.38.up), channel_id=1, source_target_pairs={{0,1},{1,0},{2,3},{3,2},{4,5},{5,4},{6,7},{7,6},{8,9},{9,8},{10,11... | collective-permute-start | bytes 1769480 | tf_op jit(solution)/shard_map/ppermute | solution.py:56
  35.9 1.5 %collective-permute-done.7.refs_2_.table_sib = f32[40,128]{1,0:T(8,128)S(1)} collective-permute-done((f32[40,128]{1,0:T(8,128)S(1)}, f32[40,128]{1,0:T(8,128)S(1)}, u32[]{:S(2)}, u32[]{:S(2)}) %collective-permute-start.7) | collective-permute-done | bytes 20512 | tf_op jit(solution)/shard_map/ppermute | solution.py:56
  37.4 1.9 %collective-permute-start.14 = (bf16[2,18,16,128]{3,2,1,0:T(8,128)(2,1)S(1)}, bf16[2,18,16,128]{3,2,1,0:T(8,128)(2,1)S(1)}, u32[]{:S(2)}, u32[]{:S(2)}) collective-permute-start(bf16[2,18,16,128]{3,2,1,0:T(8,128)(2,1)S(1)} %get-tuple-element.39), channel_id=1, source_target_pairs={{4,0},{8,4},{12,8},{5,1},{9,5},{13,9},{6,2},{10,6},{14,10},{7,3},{... | collective-permute-start | bytes 442376 | tf_op jit(solution)/shard_map/ppermute | solution.py:643
  39.4 11.1 %weight.1 = (f32[27,32,128]{2,1,0:T(8,128)S(1)}, bf16[27,32,128]{2,1,0:T(8,128)(2,1)S(1)}, bf16[27,32,128]{2,1,0:T(8,128)(2,1)S(1)}, bf16[27,32,128]{2,1,0:T(8,128)(2,1)S(1)}) custom-call(s32[8]{0:T(128)S(1)} %copy-done.12, f32[40,128]{1,0:T(8,128)S(1)} %get-tuple-element.35.refs_1_.table, f32[40,128]{1,0:T(8,128)S(1)} %collective-permute-done.7.refs_2_.table_sib, ...), custom_call_target="tpu_custom_call" | custom-call | flops 1024 | bytes 1024 | tf_op jit(solution)/shard_map/weight/pallas_call | solution.py:628
  51.4 1.5 %collective-permute-start.16 = (bf16[27,32,128]{2,1,0:T(8,128)(2,1)S(1)}, bf16[27,32,128]{2,1,0:T(8,128)(2,1)S(1)}, u32[]{:S(2)}, u32[]{:S(2)}) collective-permute-start(bf16[27,32,128]{2,1,0:T(8,128)(2,1)S(1)} %get-tuple-element.44), channel_id=1, source_target_pairs={{0,4},{4,8},{8,12},{12,0},{1,5},{5,9},{9,13},{13,1},{2,6},{6,10},{... | collective-permute-start | bytes 663560 | tf_op jit(solution)/shard_map/ppermute | solution.py:677
  52.8 2.7 %collective-permute-start.17 = (bf16[27,32,128]{2,1,0:T(8,128)(2,1)S(1)}, bf16[27,32,128]{2,1,0:T(8,128)(2,1)}, u32[]{:S(2)}, u32[]{:S(2)}) collective-permute-start(bf16[27,32,128]{2,1,0:T(8,128)(2,1)S(1)} %get-tuple-element.45), channel_id=1, source_target_pairs={{0,8},{4,12},{8,0},{12,4},{1,9},{5,13},{9,1},{13,5},{2,10},{6,14},... | collective-permute-start | bytes 663560 | tf_op jit(solution)/shard_map/ppermute | solution.py:677
  55.5 1.5 %collective-permute-start.15 = (bf16[2,18,16,128]{3,2,1,0:T(8,128)(2,1)S(1)}, bf16[2,18,16,128]{3,2,1,0:T(8,128)(2,1)S(1)}, u32[]{:S(2)}, u32[]{:S(2)}) collective-permute-start(bf16[2,18,16,128]{3,2,1,0:T(8,128)(2,1)S(1)} %collective-permute-done.14.next_own), channel_id=1, source_target_pairs={{0,1},{1,0},{2,3},{3,2},{4,5},{5,4},{6,7},{7,6},{8,9},{9,8},{10,11... | collective-permute-start | bytes 442376 | tf_op jit(solution)/shard_map/ppermute | solution.py:56
  57.0 1.0 %collective-permute-done.15.next_sib = bf16[2,18,16,128]{3,2,1,0:T(8,128)(2,1)S(1)} collective-permute-done((bf16[2,18,16,128]{3,2,1,0:T(8,128)(2,1)S(1)}, bf16[2,18,16,128]{3,2,1,0:T(8,128)(2,1)S(1)}, u32[]{:S(2)}, u32[]{:S(2)}) %collective-permute-start.15) | collective-permute-done | bytes 147488 | tf_op jit(solution)/shard_map/ppermute | solution.py:56
  58.0 6.9 %backward.1 = (f32[8,128,128]{2,1,0:T(8,128)S(1)}, f32[8,128,128]{2,1,0:T(8,128)}, f32[16,16,128]{2,1,0:T(8,128)}) custom-call(s32[8]{0:T(128)S(1)} %copy-done.12, f32[40,128]{1,0:T(8,128)S(1)} %get-tuple-element.35.refs_1_.table, f32[40,128]{1,0:T(8,128)S(1)} %collective-permute-done.7.refs_2_.table_sib, bf16[9,768,256]{2,1,0:T(8,128)(2,1)S(1)} %turn.1.weight, ...), custom_call_target="tpu_custom_call" | custom-call | flops 1024 | bytes 1024 | tf_op jit(solution)/shard_map/backward/pallas_call | solution.py:646
  65.8 4.2 %all-to-all-start = ((f32[16,16,128]{2,1,0:T(8,128)}), f32[16,16,128]{2,1,0:T(8,128)}, u32[]{:S(2)}, u32[]{:S(2)}) async-start(f32[16,16,128]{2,1,0:T(8,128)} %get-tuple-element.40), calls=%async_computation | async-start | bytes 262144 | tf_op jit(solution)/shard_map/all_to_all | solution.py:656
  70.0 7.5 %forward.1 = (bf16[8,8,16,128]{3,2,1,0:T(8,128)(2,1)S(1)}, bf16[8,8,16,128]{3,2,1,0:T(8,128)(2,1)}) custom-call(s32[8]{0:T(128)S(1)} %copy-done.12, f32[40,128]{1,0:T(8,128)S(1)} %get-tuple-element.35.refs_1_.table, f32[40,128]{1,0:T(8,128)S(1)} %collective-permute-done.7.refs_2_.table_sib, bf16[9,768,256]{2,1,0:T(8,128)(2,1)} %bitcast.9, ...), custom_call_target="tpu_custom_call" | custom-call | flops 1024 | bytes 1024 | tf_op jit(solution)/shard_map/forward/pallas_call | solution.py:660
  78.9 1.4 %collective-permute-done.20.refs_1_ = bf16[8,8,16,128]{3,2,1,0:T(8,128)(2,1)} collective-permute-done((bf16[8,8,16,128]{3,2,1,0:T(8,128)(2,1)}, bf16[8,8,16,128]{3,2,1,0:T(8,128)(2,1)}, u32[]{:S(2)}, u32[]{:S(2)}) %collective-permute-start.20) | collective-permute-done | bytes 262176 | tf_op jit(solution)/shard_map/ppermute | solution.py:56
  80.3 3.7 %finish.1 = (bf16[8,16,16,128]{3,2,1,0:T(8,128)(2,1)}, bf16[8,16,16,128]{3,2,1,0:T(8,128)(2,1)}, f32[8,128]{1,0:T(8,128)S(1)}, f32[27,32,128]{2,1,0:T(8,128)}) custom-call(s32[8]{0:T(128)S(1)} %copy-done.12, f32[40,128]{1,0:T(8,128)S(1)} %get-tuple-element.35.refs_1_.table, f32[16,16,128]{2,1,0:T(8,128)} %all-to-all-done.got, f32[8,128]{1,0:T(8,128)S(1)} %arrive.1.token, ...), custom_call_target="tpu_custom_call" | custom-call | flops 1024 | bytes 1024 | tf_op jit(solution)/shard_map/finish/pallas_call | solution.py:683
  (68 shorter events, 10.2 us)
Async XLA Ops:
  0.6 13.1 %collective-permute-start.8 = (bf16[8,16,16,128]{3,2,1,0:T(8,128)(2,1)}, bf16[8,16,16,128]{3,2,1,0:T(8,128)(2,1)S(1)}, u32[]{:S(2)}, u32[]{:S(2)}) collective-permute-start(bf16[8,16,16,128]{3,2,1,0:T(8,128)(2,1)} %video.1), channel_id=1, source_target_pairs={{0,2},{2,0},{1,3},{3,1},{4,6},{6,4},{5,7},{7,5},{8,10},{10,8},{9,1... | collective-permute-start | bytes 1572872 | tf_op jit(solution)/shard_map/ppermute | solution.py:598
  4.2 5.0 %collective-permute-start = (bf16[37,16,128]{2,1,0:T(8,128)(2,1)S(1)}, bf16[37,16,128]{2,1,0:T(8,128)(2,1)S(1)}, u32[]{:S(2)}, u32[]{:S(2)}) collective-permute-start(bf16[37,16,128]{2,1,0:T(8,128)(2,1)S(1)} %get-tuple-element.32), channel_id=1, source_target_pairs={{0,4},{4,8},{8,12},{12,0},{1,5},{5,9},{9,13},{13,1},{2,6},{6,10},{... | collective-permute-start | bytes 454664 | tf_op jit(solution)/shard_map/ppermute | solution.py:594
  5.6 12.0 %collective-permute-start.1 = (bf16[37,16,128]{2,1,0:T(8,128)(2,1)S(1)}, bf16[37,16,128]{2,1,0:T(8,128)(2,1)S(1)}, u32[]{:S(2)}, u32[]{:S(2)}) collective-permute-start(bf16[37,16,128]{2,1,0:T(8,128)(2,1)S(1)} %get-tuple-element.33), channel_id=1, source_target_pairs={{0,8},{4,12},{8,0},{12,4},{1,9},{5,13},{9,1},{13,5},{2,10},{6,14},... | collective-permute-start | bytes 454664 | tf_op jit(solution)/shard_map/ppermute | solution.py:594
  6.7 18.0 %collective-permute-start.2 = (bf16[37,16,128]{2,1,0:T(8,128)(2,1)S(1)}, bf16[37,16,128]{2,1,0:T(8,128)(2,1)S(1)}, u32[]{:S(2)}, u32[]{:S(2)}) collective-permute-start(bf16[37,16,128]{2,1,0:T(8,128)(2,1)S(1)} %get-tuple-element.34), channel_id=1, source_target_pairs={{0,12},{4,0},{8,4},{12,8},{1,13},{5,1},{9,5},{13,9},{2,14},{6,2},{... | collective-permute-start | bytes 454664 | tf_op jit(solution)/shard_map/ppermute | solution.py:594
  8.1 16.7 %collective-permute-start.3 = (bf16[37,16,128]{2,1,0:T(8,128)(2,1)S(1)}, bf16[37,16,128]{2,1,0:T(8,128)(2,1)S(1)}, u32[]{:S(2)}, u32[]{:S(2)}) collective-permute-start(bf16[37,16,128]{2,1,0:T(8,128)(2,1)S(1)} %get-tuple-element.31.refs_0_.refs_9_), channel_id=1, source_target_pairs={{0,2},{2,0},{1,3},{3,1},{4,6},{6,4},{5,7},{7,5},{8,10},{10,8},{9,1... | collective-permute-start | bytes 454664 | tf_op jit(solution)/shard_map/ppermute | solution.py:602
  9.3 15.7 %collective-permute-start.4 = (bf16[37,16,128]{2,1,0:T(8,128)(2,1)S(1)}, bf16[37,16,128]{2,1,0:T(8,128)(2,1)S(1)}, u32[]{:S(2)}, u32[]{:S(2)}) collective-permute-start(bf16[37,16,128]{2,1,0:T(8,128)(2,1)S(1)} %collective-permute-done.refs_1_.refs_10_), channel_id=1, source_target_pairs={{0,2},{2,0},{1,3},{3,1},{4,6},{6,4},{5,7},{7,5},{8,10},{10,8},{9,1... | collective-permute-start | bytes 454664 | tf_op jit(solution)/shard_map/ppermute | solution.py:602
  13.7 21.7 %collective-permute-start.11 = (bf16[64,16,128]{2,1,0:T(8,128)(2,1)S(1)}, bf16[64,16,128]{2,1,0:T(8,128)(2,1)S(1)}, u32[]{:S(2)}, u32[]{:S(2)}) collective-permute-start(bf16[64,16,128]{2,1,0:T(8,128)(2,1)S(1)} %bitcast.13), channel_id=1, source_target_pairs={{0,4},{4,8},{8,12},{1,5},{5,9},{9,13},{2,6},{6,10},{10,14},{3,7},{... | collective-permute-start | bytes 786440 | tf_op jit(solution)/shard_map/ppermute | solution.py:605
  17.6 21.8 %collective-permute-start.9 = (bf16[8,16,16,128]{3,2,1,0:T(8,128)(2,1)}, bf16[8,16,16,128]{3,2,1,0:T(8,128)(2,1)S(1)}, u32[]{:S(2)}, u32[]{:S(2)}) collective-permute-start(bf16[8,16,16,128]{3,2,1,0:T(8,128)(2,1)} %video.1), channel_id=1, source_target_pairs={{0,1},{1,0},{2,3},{3,2},{4,5},{5,4},{6,7},{7,6},{8,9},{9,8},{10,11... | collective-permute-start | bytes 1572872 | tf_op jit(solution)/shard_map/ppermute | solution.py:56
  24.6 14.8 %collective-permute-start.10 = (bf16[8,16,16,128]{3,2,1,0:T(8,128)(2,1)S(1)}, bf16[8,16,16,128]{3,2,1,0:T(8,128)(2,1)S(1)}, u32[]{:S(2)}, u32[]{:S(2)}) collective-permute-start(bf16[8,16,16,128]{3,2,1,0:T(8,128)(2,1)S(1)} %collective-permute-done.8.refs_4_.refs_2_), channel_id=1, source_target_pairs={{0,1},{1,0},{2,3},{3,2},{4,5},{5,4},{6,7},{7,6},{8,9},{9,8},{10,11... | collective-permute-start | bytes 1572872 | tf_op jit(solution)/shard_map/ppermute | solution.py:56
  24.7 5.1 %collective-permute-start.5 = (bf16[37,16,128]{2,1,0:T(8,128)(2,1)S(1)}, bf16[37,16,128]{2,1,0:T(8,128)(2,1)S(1)}, u32[]{:S(2)}, u32[]{:S(2)}) collective-permute-start(bf16[37,16,128]{2,1,0:T(8,128)(2,1)S(1)} %collective-permute-done.1.refs_2_.refs_11_), channel_id=1, source_target_pairs={{0,2},{2,0},{1,3},{3,1},{4,6},{6,4},{5,7},{7,5},{8,10},{10,8},{9,1... | collective-permute-start | bytes 454664 | tf_op jit(solution)/shard_map/ppermute | solution.py:602
  25.0 8.1 %collective-permute-start.6 = (bf16[37,16,128]{2,1,0:T(8,128)(2,1)S(1)}, bf16[37,16,128]{2,1,0:T(8,128)(2,1)S(1)}, u32[]{:S(2)}, u32[]{:S(2)}) collective-permute-start(bf16[37,16,128]{2,1,0:T(8,128)(2,1)S(1)} %collective-permute-done.2.refs_3_.refs_12_), channel_id=1, source_target_pairs={{0,2},{2,0},{1,3},{3,1},{4,6},{6,4},{5,7},{7,5},{8,10},{10,8},{9,1... | collective-permute-start | bytes 454664 | tf_op jit(solution)/shard_map/ppermute | solution.py:602
  34.1 30.9 %copy-start.6 = (bf16[8,18,16,128]{3,2,1,0:T(8,128)(2,1)}, bf16[8,18,16,128]{3,2,1,0:T(8,128)(2,1)S(1)}, u32[]{:S(2)}) copy-start(bf16[8,18,16,128]{3,2,1,0:T(8,128)(2,1)S(1)} %get-tuple-element.38.up) | copy-start | bytes 1769476
  34.1 24.0 %collective-permute-start.13 = (bf16[8,18,16,128]{3,2,1,0:T(8,128)(2,1)S(1)}, bf16[8,18,16,128]{3,2,1,0:T(8,128)(2,1)S(1)}, u32[]{:S(2)}, u32[]{:S(2)}) collective-permute-start(bf16[8,18,16,128]{3,2,1,0:T(8,128)(2,1)S(1)} %get-tuple-element.38.up), channel_id=1, source_target_pairs={{0,1},{1,0},{2,3},{3,2},{4,5},{5,4},{6,7},{7,6},{8,9},{9,8},{10,11... | collective-permute-start | bytes 1769480 | tf_op jit(solution)/shard_map/ppermute | solution.py:56
  35.4 29.5 %copy-start.8 = (bf16[64,16,128]{2,1,0:T(8,128)(2,1)}, bf16[64,16,128]{2,1,0:T(8,128)(2,1)S(1)}, u32[]{:S(2)}) copy-start(bf16[64,16,128]{2,1,0:T(8,128)(2,1)S(1)} %collective-permute-done.11.refs_7_.refs_6_) | copy-start | bytes 786436
  35.4 4.0 %collective-permute-start.12 = (bf16[64,16,128]{2,1,0:T(8,128)(2,1)S(1)}, bf16[64,16,128]{2,1,0:T(8,128)(2,1)S(1)}, u32[]{:S(2)}, u32[]{:S(2)}) collective-permute-start(bf16[64,16,128]{2,1,0:T(8,128)(2,1)S(1)} %collective-permute-done.11.refs_7_.refs_6_), channel_id=1, source_target_pairs={{0,1},{1,0},{2,3},{3,2},{4,5},{5,4},{6,7},{7,6},{8,9},{9,8},{10,11... | collective-permute-start | bytes 786440 | tf_op jit(solution)/shard_map/ppermute | solution.py:56
  35.5 1.9 %collective-permute-start.7 = (f32[40,128]{1,0:T(8,128)S(1)}, f32[40,128]{1,0:T(8,128)S(1)}, u32[]{:S(2)}, u32[]{:S(2)}) collective-permute-start(f32[40,128]{1,0:T(8,128)S(1)} %get-tuple-element.35.refs_1_.table), channel_id=1, source_target_pairs={{0,1},{1,0},{2,3},{3,2},{4,5},{5,4},{6,7},{7,6},{8,9},{9,8},{10,11... | collective-permute-start | bytes 61448 | tf_op jit(solution)/shard_map/ppermute | solution.py:56
  37.4 18.1 %collective-permute-start.14 = (bf16[2,18,16,128]{3,2,1,0:T(8,128)(2,1)S(1)}, bf16[2,18,16,128]{3,2,1,0:T(8,128)(2,1)S(1)}, u32[]{:S(2)}, u32[]{:S(2)}) collective-permute-start(bf16[2,18,16,128]{3,2,1,0:T(8,128)(2,1)S(1)} %get-tuple-element.39), channel_id=1, source_target_pairs={{4,0},{8,4},{12,8},{5,1},{9,5},{13,9},{6,2},{10,6},{14,10},{7,3},{... | collective-permute-start | bytes 442376 | tf_op jit(solution)/shard_map/ppermute | solution.py:643
  51.4 26.6 %collective-permute-start.18 = (bf16[27,32,128]{2,1,0:T(8,128)(2,1)S(1)}, bf16[27,32,128]{2,1,0:T(8,128)(2,1)S(1)}, u32[]{:S(2)}, u32[]{:S(2)}) collective-permute-start(bf16[27,32,128]{2,1,0:T(8,128)(2,1)S(1)} %get-tuple-element.46), channel_id=1, source_target_pairs={{0,12},{4,0},{8,4},{12,8},{1,13},{5,1},{9,5},{13,9},{2,14},{6,2},{... | collective-permute-start | bytes 663560 | tf_op jit(solution)/shard_map/ppermute | solution.py:677
  51.4 26.8 %collective-permute-start.16 = (bf16[27,32,128]{2,1,0:T(8,128)(2,1)S(1)}, bf16[27,32,128]{2,1,0:T(8,128)(2,1)S(1)}, u32[]{:S(2)}, u32[]{:S(2)}) collective-permute-start(bf16[27,32,128]{2,1,0:T(8,128)(2,1)S(1)} %get-tuple-element.44), channel_id=1, source_target_pairs={{0,4},{4,8},{8,12},{12,0},{1,5},{5,9},{9,13},{13,1},{2,6},{6,10},{... | collective-permute-start | bytes 663560 | tf_op jit(solution)/shard_map/ppermute | solution.py:677
  52.8 26.0 %collective-permute-start.17 = (bf16[27,32,128]{2,1,0:T(8,128)(2,1)S(1)}, bf16[27,32,128]{2,1,0:T(8,128)(2,1)}, u32[]{:S(2)}, u32[]{:S(2)}) collective-permute-start(bf16[27,32,128]{2,1,0:T(8,128)(2,1)S(1)} %get-tuple-element.45), channel_id=1, source_target_pairs={{0,8},{4,12},{8,0},{12,4},{1,9},{5,13},{9,1},{13,5},{2,10},{6,14},... | collective-permute-start | bytes 663560 | tf_op jit(solution)/shard_map/ppermute | solution.py:677
  55.5 2.5 %collective-permute-start.15 = (bf16[2,18,16,128]{3,2,1,0:T(8,128)(2,1)S(1)}, bf16[2,18,16,128]{3,2,1,0:T(8,128)(2,1)S(1)}, u32[]{:S(2)}, u32[]{:S(2)}) collective-permute-start(bf16[2,18,16,128]{3,2,1,0:T(8,128)(2,1)S(1)} %collective-permute-done.14.next_own), channel_id=1, source_target_pairs={{0,1},{1,0},{2,3},{3,2},{4,5},{5,4},{6,7},{7,6},{8,9},{9,8},{10,11... | collective-permute-start | bytes 442376 | tf_op jit(solution)/shard_map/ppermute | solution.py:56
  65.8 13.1 %all-to-all-start = ((f32[16,16,128]{2,1,0:T(8,128)}), f32[16,16,128]{2,1,0:T(8,128)}, u32[]{:S(2)}, u32[]{:S(2)}) async-start(f32[16,16,128]{2,1,0:T(8,128)} %get-tuple-element.40), calls=%async_computation | async-start | bytes 262144 | tf_op jit(solution)/shard_map/all_to_all | solution.py:656
  77.5 2.7 %collective-permute-start.19 = (f32[8,128,128]{2,1,0:T(8,128)}, f32[8,128,128]{2,1,0:T(8,128)}, u32[]{:S(2)}, u32[]{:S(2)}) collective-permute-start(f32[8,128,128]{2,1,0:T(8,128)} %get-tuple-element.47), channel_id=1, source_target_pairs={{0,1},{1,0},{2,3},{3,2},{4,5},{5,4},{6,7},{7,6},{8,9},{9,8},{10,11... | collective-permute-start | bytes 1572872 | tf_op jit(solution)/shard_map/ppermute | solution.py:56
  78.0 2.3 %collective-permute-start.20 = (bf16[8,8,16,128]{3,2,1,0:T(8,128)(2,1)}, bf16[8,8,16,128]{3,2,1,0:T(8,128)(2,1)}, u32[]{:S(2)}, u32[]{:S(2)}) collective-permute-start(bf16[8,8,16,128]{3,2,1,0:T(8,128)(2,1)} %get-tuple-element.49), channel_id=1, source_target_pairs={{0,1},{1,0},{2,3},{3,2},{4,5},{5,4},{6,7},{7,6},{8,9},{9,8},{10,11... | collective-permute-start | bytes 786440 | tf_op jit(solution)/shard_map/ppermute | solution.py:56
  (16 other events, 136.9 us)

commit v8 on v6

--- a/solution.py
+++ b/solution.py
@@ -235,7 +235,8 @@
             def _():
                 for m in range(bands):
                     u = ups[m][k][at : at + rows].reshape(cells, chans)
-                    upright[local, m] = u.T
+                    at_lane = pl.multiple_of(band[m] * cells, cells)
+                    upright[local, :, pl.ds(at_lane, cells)] = u.T
 
     begin = [start_of(lengths, first + t) for t in range(frames)]
 
@@ -247,14 +248,13 @@
             where.append((a, lax.rem(lax.div(tap, 3), 3), lax.rem(tap, 3)))
         total = jnp.zeros((chans, count * width), F32)
         for t in range(frames):
-            for m in range(bands):
-                patch = []
-                for a, b, col in where:
-                    s = jnp.maximum(first + t - 2 + a, begin[t]) - (first - 2)
-                    lines = active[col, s, pl.ds(band[m] * rows + b, rows)]
-                    patch.append(lines.reshape(cells, width))
-                patch = jnp.concatenate(patch, axis=1) if count > 1 else patch[0]
-                total = total + bdot(upright[t, m], patch)
+            patch = []
+            for a, b, col in where:
+                s = jnp.maximum(first + t - 2 + a, begin[t]) - (first - 2)
+                lines = active[col, s, pl.ds(b, bands * rows)]
+                patch.append(lines.reshape(bands * cells, width))
+            patch = jnp.concatenate(patch, axis=1) if count > 1 else patch[0]
+            total = total + bdot(upright[t], patch)
         for n in range(count):
             piece = total[:, n * width : (n + 1) * width].T
             for k in range(peers):
@@ -618,7 +618,7 @@
         [SM] + [VM] * (4 + 2 * bands + peers * bands),
         [
             pltpu.VMEM((3, frames + 2, bands * rows + 2, cols, width), BF16),
-            pltpu.VMEM((frames, bands, chans, rows * cols), BF16),
+            pltpu.VMEM((frames, chans, bands * rows * cols), BF16),
         ],
         name="weight",
     )(

time: 86 us -> 85.9 us (level)
  no operation moved by 1% of the time
where the time goes in v8:
time: 85.9 us; the launch traced here: 84.5 us
  Pallas kernels  35.7 us (42%)
  starting transfers between devices  29.6 us (34%)
  waiting for transfers between devices  12.6 us (15%)
  local copies, waits for them, and re-layouts  5.64 us (7%)
  between operations  0.93 us (1%)
    pallas_call x1, Pallas kernels, per_device(): call(functools.partial(weight_body, peers, bands, cap, block), [sds((27,...  11 us
    ppermute x8, starting transfers between devices, sibling(): return lax.ppermute(value, 'chan', ring(2, 1))  8.33 us
    pallas_call x1, Pallas kernels, per_device(): call(functools.partial(forward_body, bands), [part, part], [SM, VM, VM] +...  7.53 us
    pallas_call x1, Pallas kernels, per_device(): call(functools.partial(backward_body, peers), [part, part, sds((devices,...  6.91 us
    ppermute x1, waiting for transfers between devices, per_device(): lax.ppermute(after(clip_video, pieces[0]), 'height', ring(bands, m))  6.13 us
    ppermute x3, starting transfers between devices, per_device(): lax.ppermute(grads[k], 'tm', ring(peers, k))  4.49 us
    all_to_all x1, starting transfers between devices, per_device(): totals = lax.all_to_all(sums, everyone, 0, 0)  4.22 us
    unnamed x36, local copies, waits for them, and re-layouts  4.2 us
  transfers between devices with their start and end apart: 22, of which 5 were waited for; matrix products, arithmetic and copies ran while one was open for 1% of the time, Pallas kernels for 35%

profile of v8, /device:TPU:15, one launch (start us, length us, event | category | flops | bytes accessed | tf_op | source)
XLA Modules:
  0.0 84.5 jit_solution(12183939224582915928)
XLA Ops:
  1.3 2.6 %pack.1 = (bf16[37,16,128]{2,1,0:T(8,128)(2,1)S(1)}, bf16[37,16,128]{2,1,0:T(8,128)(2,1)S(1)}, bf16[37,16,128]{2,1,0:T(8,128)(2,1)S(1)}, bf16[37,16,128]{2,1,0:T(8,128)(2,1)S(1)}) custom-call(s32[8]{0:T(128)S(1)} %copy-done.14, bf16[8,16,16,128]{3,2,1,0:T(8,128)(2,1)} %grad.1, bf16[8,16,16,128]{3,2,1,0:T(8,128)(2,1)} %video.1), custom_call_target="tpu_custom_call" | custom-call | flops 1024 | bytes 1024 | tf_op jit(solution)/shard_map/pack/pallas_call | solution.py:567
  4.2 1.3 %collective-permute-start = (bf16[37,16,128]{2,1,0:T(8,128)(2,1)S(1)}, bf16[37,16,128]{2,1,0:T(8,128)(2,1)S(1)}, u32[]{:S(2)}, u32[]{:S(2)}) collective-permute-start(bf16[37,16,128]{2,1,0:T(8,128)(2,1)S(1)} %get-tuple-element.33), channel_id=1, source_target_pairs={{0,4},{4,8},{8,12},{12,0},{1,5},{5,9},{9,13},{13,1},{2,6},{6,10},{... | collective-permute-start | bytes 454664 | tf_op jit(solution)/shard_map/ppermute | solution.py:581
  5.5 1.0 %collective-permute-start.1 = (bf16[37,16,128]{2,1,0:T(8,128)(2,1)S(1)}, bf16[37,16,128]{2,1,0:T(8,128)(2,1)S(1)}, u32[]{:S(2)}, u32[]{:S(2)}) collective-permute-start(bf16[37,16,128]{2,1,0:T(8,128)(2,1)S(1)} %get-tuple-element.34), channel_id=1, source_target_pairs={{0,8},{4,12},{8,0},{12,4},{1,9},{5,13},{9,1},{13,5},{2,10},{6,14},... | collective-permute-start | bytes 454664 | tf_op jit(solution)/shard_map/ppermute | solution.py:581
  6.5 1.5 %collective-permute-start.2 = (bf16[37,16,128]{2,1,0:T(8,128)(2,1)S(1)}, bf16[37,16,128]{2,1,0:T(8,128)(2,1)S(1)}, u32[]{:S(2)}, u32[]{:S(2)}) collective-permute-start(bf16[37,16,128]{2,1,0:T(8,128)(2,1)S(1)} %get-tuple-element.35), channel_id=1, source_target_pairs={{0,12},{4,0},{8,4},{12,8},{1,13},{5,1},{9,5},{13,9},{2,14},{6,2},{... | collective-permute-start | bytes 454664 | tf_op jit(solution)/shard_map/ppermute | solution.py:581
  8.0 1.2 %collective-permute-start.3 = (bf16[37,16,128]{2,1,0:T(8,128)(2,1)S(1)}, bf16[37,16,128]{2,1,0:T(8,128)(2,1)S(1)}, u32[]{:S(2)}, u32[]{:S(2)}) collective-permute-start(bf16[37,16,128]{2,1,0:T(8,128)(2,1)S(1)} %get-tuple-element.32.refs_0_.refs_9_), channel_id=1, source_target_pairs={{0,2},{2,0},{1,3},{3,1},{4,6},{6,4},{5,7},{7,5},{8,10},{10,8},{9,1... | collective-permute-start | bytes 454664 | tf_op jit(solution)/shard_map/ppermute | solution.py:589
  10.8 6.1 %collective-permute-done.8.refs_4_.refs_2_ = bf16[8,16,16,128]{3,2,1,0:T(8,128)(2,1)S(1)} collective-permute-done((bf16[8,16,16,128]{3,2,1,0:T(8,128)(2,1)}, bf16[8,16,16,128]{3,2,1,0:T(8,128)(2,1)S(1)}, u32[]{:S(2)}, u32[]{:S(2)}) %collective-permute-start.8) | collective-permute-done | bytes 524320 | tf_op jit(solution)/shard_map/ppermute | solution.py:585
  17.0 3.2 %collective-permute-start.11 = (bf16[64,16,128]{2,1,0:T(8,128)(2,1)S(1)}, bf16[64,16,128]{2,1,0:T(8,128)(2,1)S(1)}, u32[]{:S(2)}, u32[]{:S(2)}) collective-permute-start(bf16[64,16,128]{2,1,0:T(8,128)(2,1)S(1)} %bitcast.13), channel_id=1, source_target_pairs={{0,4},{4,8},{8,12},{1,5},{5,9},{9,13},{2,6},{6,10},{10,14},{3,7},{... | collective-permute-start | bytes 786440 | tf_op jit(solution)/shard_map/ppermute | solution.py:592
  20.2 4.3 %collective-permute-start.9 = (bf16[8,16,16,128]{3,2,1,0:T(8,128)(2,1)}, bf16[8,16,16,128]{3,2,1,0:T(8,128)(2,1)S(1)}, u32[]{:S(2)}, u32[]{:S(2)}) collective-permute-start(bf16[8,16,16,128]{3,2,1,0:T(8,128)(2,1)} %video.1), channel_id=1, source_target_pairs={{0,1},{1,0},{2,3},{3,2},{4,5},{5,4},{6,7},{7,6},{8,9},{9,8},{10,11... | collective-permute-start | bytes 1572872 | tf_op jit(solution)/shard_map/ppermute | solution.py:56
  24.9 1.2 %collective-permute-start.6 = (bf16[37,16,128]{2,1,0:T(8,128)(2,1)S(1)}, bf16[37,16,128]{2,1,0:T(8,128)(2,1)S(1)}, u32[]{:S(2)}, u32[]{:S(2)}) collective-permute-start(bf16[37,16,128]{2,1,0:T(8,128)(2,1)S(1)} %collective-permute-done.2.refs_3_.refs_12_), channel_id=1, source_target_pairs={{0,2},{2,0},{1,3},{3,1},{4,6},{6,4},{5,7},{7,5},{8,10},{10,8},{9,1... | collective-permute-start | bytes 454664 | tf_op jit(solution)/shard_map/ppermute | solution.py:589
  26.2 2.0 %copy-done.2 = bf16[3,3,3,256,256]{4,3,2,1,0:T(8,128)(2,1)S(1)} copy-done((bf16[3,3,3,256,256]{4,3,2,1,0:T(8,128)(2,1)S(1)}, bf16[3,3,3,256,256]{4,3,2,1,0:T(8,128)(2,1)}, u32[]{:S(2)}) %copy-start.2) | copy-done | bytes 3538968
  29.8 3.2 %collective-permute-done.6.refs_7_.refs_16_ = bf16[37,16,128]{2,1,0:T(8,128)(2,1)S(1)} collective-permute-done((bf16[37,16,128]{2,1,0:T(8,128)(2,1)S(1)}, bf16[37,16,128]{2,1,0:T(8,128)(2,1)S(1)}, u32[]{:S(2)}, u32[]{:S(2)}) %collective-permute-start.6) | collective-permute-done | bytes 151584 | tf_op jit(solution)/shard_map/ppermute | solution.py:589
  34.0 1.3 %collective-permute-start.13 = (bf16[8,18,16,128]{3,2,1,0:T(8,128)(2,1)S(1)}, bf16[8,18,16,128]{3,2,1,0:T(8,128)(2,1)S(1)}, u32[]{:S(2)}, u32[]{:S(2)}) collective-permute-start(bf16[8,18,16,128]{3,2,1,0:T(8,128)(2,1)S(1)} %get-tuple-element.40.up), channel_id=1, source_target_pairs={{0,1},{1,0},{2,3},{3,2},{4,5},{5,4},{6,7},{7,6},{8,9},{9,8},{10,11... | collective-permute-start | bytes 1769480 | tf_op jit(solution)/shard_map/ppermute | solution.py:56
  35.9 1.5 %collective-permute-done.7.refs_2_.table_sib = f32[40,128]{1,0:T(8,128)S(1)} collective-permute-done((f32[40,128]{1,0:T(8,128)S(1)}, f32[40,128]{1,0:T(8,128)S(1)}, u32[]{:S(2)}, u32[]{:S(2)}) %collective-permute-start.7) | collective-permute-done | bytes 20512 | tf_op jit(solution)/shard_map/ppermute | solution.py:56
  37.4 1.9 %collective-permute-start.14 = (bf16[2,18,16,128]{3,2,1,0:T(8,128)(2,1)S(1)}, bf16[2,18,16,128]{3,2,1,0:T(8,128)(2,1)S(1)}, u32[]{:S(2)}, u32[]{:S(2)}) collective-permute-start(bf16[2,18,16,128]{3,2,1,0:T(8,128)(2,1)S(1)} %get-tuple-element.41), channel_id=1, source_target_pairs={{4,0},{8,4},{12,8},{5,1},{9,5},{13,9},{6,2},{10,6},{14,10},{7,3},{... | collective-permute-start | bytes 442376 | tf_op jit(solution)/shard_map/ppermute | solution.py:630
  39.4 11.0 %weight.1 = (f32[27,32,128]{2,1,0:T(8,128)S(1)}, bf16[27,32,128]{2,1,0:T(8,128)(2,1)S(1)}, bf16[27,32,128]{2,1,0:T(8,128)(2,1)S(1)}, bf16[27,32,128]{2,1,0:T(8,128)(2,1)S(1)}) custom-call(s32[8]{0:T(128)S(1)} %copy-done.11, f32[40,128]{1,0:T(8,128)S(1)} %get-tuple-element.36.refs_1_.table, f32[40,128]{1,0:T(8,128)S(1)} %collective-permute-done.7.refs_2_.table_sib, ...), custom_call_target="tpu_custom_call" | custom-call | flops 1024 | bytes 1024 | tf_op jit(solution)/shard_map/weight/pallas_call | solution.py:615
  50.4 1.7 %collective-permute-start.16 = (bf16[27,32,128]{2,1,0:T(8,128)(2,1)S(1)}, bf16[27,32,128]{2,1,0:T(8,128)(2,1)S(1)}, u32[]{:S(2)}, u32[]{:S(2)}) collective-permute-start(bf16[27,32,128]{2,1,0:T(8,128)(2,1)S(1)} %get-tuple-element.46), channel_id=1, source_target_pairs={{0,4},{4,8},{8,12},{12,0},{1,5},{5,9},{9,13},{13,1},{2,6},{6,10},{... | collective-permute-start | bytes 663560 | tf_op jit(solution)/shard_map/ppermute | solution.py:664
  52.1 2.7 %collective-permute-start.17 = (bf16[27,32,128]{2,1,0:T(8,128)(2,1)S(1)}, bf16[27,32,128]{2,1,0:T(8,128)(2,1)}, u32[]{:S(2)}, u32[]{:S(2)}) collective-permute-start(bf16[27,32,128]{2,1,0:T(8,128)(2,1)S(1)} %get-tuple-element.47), channel_id=1, source_target_pairs={{0,8},{4,12},{8,0},{12,4},{1,9},{5,13},{9,1},{13,5},{2,10},{6,14},... | collective-permute-start | bytes 663560 | tf_op jit(solution)/shard_map/ppermute | solution.py:664
  54.9 1.5 %collective-permute-start.15 = (bf16[2,18,16,128]{3,2,1,0:T(8,128)(2,1)S(1)}, bf16[2,18,16,128]{3,2,1,0:T(8,128)(2,1)S(1)}, u32[]{:S(2)}, u32[]{:S(2)}) collective-permute-start(bf16[2,18,16,128]{3,2,1,0:T(8,128)(2,1)S(1)} %collective-permute-done.14.next_own), channel_id=1, source_target_pairs={{0,1},{1,0},{2,3},{3,2},{4,5},{5,4},{6,7},{7,6},{8,9},{9,8},{10,11... | collective-permute-start | bytes 442376 | tf_op jit(solution)/shard_map/ppermute | solution.py:56
  56.3 1.0 %collective-permute-done.15.next_sib = bf16[2,18,16,128]{3,2,1,0:T(8,128)(2,1)S(1)} collective-permute-done((bf16[2,18,16,128]{3,2,1,0:T(8,128)(2,1)S(1)}, bf16[2,18,16,128]{3,2,1,0:T(8,128)(2,1)S(1)}, u32[]{:S(2)}, u32[]{:S(2)}) %collective-permute-start.15) | collective-permute-done | bytes 147488 | tf_op jit(solution)/shard_map/ppermute | solution.py:56
  57.4 6.9 %backward.1 = (f32[8,128,128]{2,1,0:T(8,128)S(1)}, f32[8,128,128]{2,1,0:T(8,128)}, f32[16,16,128]{2,1,0:T(8,128)}) custom-call(s32[8]{0:T(128)S(1)} %copy-done.11, f32[40,128]{1,0:T(8,128)S(1)} %get-tuple-element.36.refs_1_.table, f32[40,128]{1,0:T(8,128)S(1)} %collective-permute-done.7.refs_2_.table_sib, bf16[9,768,256]{2,1,0:T(8,128)(2,1)S(1)} %turn.1.weight, ...), custom_call_target="tpu_custom_call" | custom-call | flops 1024 | bytes 1024 | tf_op jit(solution)/shard_map/backward/pallas_call | solution.py:633
  65.1 4.2 %all-to-all-start = ((f32[16,16,128]{2,1,0:T(8,128)}), f32[16,16,128]{2,1,0:T(8,128)}, u32[]{:S(2)}, u32[]{:S(2)}) async-start(f32[16,16,128]{2,1,0:T(8,128)} %get-tuple-element.42), calls=%async_computation | async-start | bytes 262144 | tf_op jit(solution)/shard_map/all_to_all | solution.py:643
  69.3 7.5 %forward.1 = (bf16[8,8,16,128]{3,2,1,0:T(8,128)(2,1)S(1)}, bf16[8,8,16,128]{3,2,1,0:T(8,128)(2,1)}) custom-call(s32[8]{0:T(128)S(1)} %copy-done.11, f32[40,128]{1,0:T(8,128)S(1)} %get-tuple-element.36.refs_1_.table, f32[40,128]{1,0:T(8,128)S(1)} %collective-permute-done.7.refs_2_.table_sib, bf16[9,768,256]{2,1,0:T(8,128)(2,1)} %bitcast.9, ...), custom_call_target="tpu_custom_call" | custom-call | flops 1024 | bytes 1024 | tf_op jit(solution)/shard_map/forward/pallas_call | solution.py:647
  78.2 2.2 %collect.1 = f32[27,32,128]{2,1,0:T(8,128)} custom-call(f32[27,32,128]{2,1,0:T(8,128)} %copy-done.15, bf16[27,32,128]{2,1,0:T(8,128)(2,1)} %copy-done.17, bf16[27,32,128]{2,1,0:T(8,128)(2,1)} %collective-permute-done.17.refs_2_, bf16[27,32,128]{2,1,0:T(8,128)(2,1)} %copy-done.16), custom_call_target="tpu_custom_call" | custom-call | flops 9999999827968 | bytes 1024 | tf_op jit(solution)/shard_map/collect/pallas_call | solution.py:665
  80.4 3.6 %finish.1 = (bf16[8,16,16,128]{3,2,1,0:T(8,128)(2,1)}, bf16[8,16,16,128]{3,2,1,0:T(8,128)(2,1)}, f32[8,128]{1,0:T(8,128)S(1)}) custom-call(s32[8]{0:T(128)S(1)} %copy-done.11, f32[40,128]{1,0:T(8,128)S(1)} %get-tuple-element.36.refs_1_.table, f32[16,16,128]{2,1,0:T(8,128)} %all-to-all-done.got, bf16[8,16,16,128]{3,2,1,0:T(8,128)(2,1)S(1)} %copy-done.1, ...), custom_call_target="tpu_custom_call" | custom-call | flops 1024 | bytes 1024 | tf_op jit(solution)/shard_map/finish/pallas_call | solution.py:675
  (68 shorter events, 8.8 us)
Async XLA Ops:
  3.9 13.1 %collective-permute-start.8 = (bf16[8,16,16,128]{3,2,1,0:T(8,128)(2,1)}, bf16[8,16,16,128]{3,2,1,0:T(8,128)(2,1)S(1)}, u32[]{:S(2)}, u32[]{:S(2)}) collective-permute-start(bf16[8,16,16,128]{3,2,1,0:T(8,128)(2,1)} %video.1), channel_id=1, source_target_pairs={{0,2},{2,0},{1,3},{3,1},{4,6},{6,4},{5,7},{7,5},{8,10},{10,8},{9,1... | collective-permute-start | bytes 1572872 | tf_op jit(solution)/shard_map/ppermute | solution.py:585
  4.2 5.0 %collective-permute-start = (bf16[37,16,128]{2,1,0:T(8,128)(2,1)S(1)}, bf16[37,16,128]{2,1,0:T(8,128)(2,1)S(1)}, u32[]{:S(2)}, u32[]{:S(2)}) collective-permute-start(bf16[37,16,128]{2,1,0:T(8,128)(2,1)S(1)} %get-tuple-element.33), channel_id=1, source_target_pairs={{0,4},{4,8},{8,12},{12,0},{1,5},{5,9},{9,13},{13,1},{2,6},{6,10},{... | collective-permute-start | bytes 454664 | tf_op jit(solution)/shard_map/ppermute | solution.py:581
  5.5 14.7 %collective-permute-start.1 = (bf16[37,16,128]{2,1,0:T(8,128)(2,1)S(1)}, bf16[37,16,128]{2,1,0:T(8,128)(2,1)S(1)}, u32[]{:S(2)}, u32[]{:S(2)}) collective-permute-start(bf16[37,16,128]{2,1,0:T(8,128)(2,1)S(1)} %get-tuple-element.34), channel_id=1, source_target_pairs={{0,8},{4,12},{8,0},{12,4},{1,9},{5,13},{9,1},{13,5},{2,10},{6,14},... | collective-permute-start | bytes 454664 | tf_op jit(solution)/shard_map/ppermute | solution.py:581
  6.5 18.1 %collective-permute-start.2 = (bf16[37,16,128]{2,1,0:T(8,128)(2,1)S(1)}, bf16[37,16,128]{2,1,0:T(8,128)(2,1)S(1)}, u32[]{:S(2)}, u32[]{:S(2)}) collective-permute-start(bf16[37,16,128]{2,1,0:T(8,128)(2,1)S(1)} %get-tuple-element.35), channel_id=1, source_target_pairs={{0,12},{4,0},{8,4},{12,8},{1,13},{5,1},{9,5},{13,9},{2,14},{6,2},{... | collective-permute-start | bytes 454664 | tf_op jit(solution)/shard_map/ppermute | solution.py:581
  8.0 16.7 %collective-permute-start.3 = (bf16[37,16,128]{2,1,0:T(8,128)(2,1)S(1)}, bf16[37,16,128]{2,1,0:T(8,128)(2,1)S(1)}, u32[]{:S(2)}, u32[]{:S(2)}) collective-permute-start(bf16[37,16,128]{2,1,0:T(8,128)(2,1)S(1)} %get-tuple-element.32.refs_0_.refs_9_), channel_id=1, source_target_pairs={{0,2},{2,0},{1,3},{3,1},{4,6},{6,4},{5,7},{7,5},{8,10},{10,8},{9,1... | collective-permute-start | bytes 454664 | tf_op jit(solution)/shard_map/ppermute | solution.py:589
  9.2 15.7 %collective-permute-start.4 = (bf16[37,16,128]{2,1,0:T(8,128)(2,1)S(1)}, bf16[37,16,128]{2,1,0:T(8,128)(2,1)S(1)}, u32[]{:S(2)}, u32[]{:S(2)}) collective-permute-start(bf16[37,16,128]{2,1,0:T(8,128)(2,1)S(1)} %collective-permute-done.refs_1_.refs_10_), channel_id=1, source_target_pairs={{0,2},{2,0},{1,3},{3,1},{4,6},{6,4},{5,7},{7,5},{8,10},{10,8},{9,1... | collective-permute-start | bytes 454664 | tf_op jit(solution)/shard_map/ppermute | solution.py:589
  17.0 18.3 %collective-permute-start.11 = (bf16[64,16,128]{2,1,0:T(8,128)(2,1)S(1)}, bf16[64,16,128]{2,1,0:T(8,128)(2,1)S(1)}, u32[]{:S(2)}, u32[]{:S(2)}) collective-permute-start(bf16[64,16,128]{2,1,0:T(8,128)(2,1)S(1)} %bitcast.13), channel_id=1, source_target_pairs={{0,4},{4,8},{8,12},{1,5},{5,9},{9,13},{2,6},{6,10},{10,14},{3,7},{... | collective-permute-start | bytes 786440 | tf_op jit(solution)/shard_map/ppermute | solution.py:592
  20.2 19.1 %collective-permute-start.9 = (bf16[8,16,16,128]{3,2,1,0:T(8,128)(2,1)}, bf16[8,16,16,128]{3,2,1,0:T(8,128)(2,1)S(1)}, u32[]{:S(2)}, u32[]{:S(2)}) collective-permute-start(bf16[8,16,16,128]{3,2,1,0:T(8,128)(2,1)} %video.1), channel_id=1, source_target_pairs={{0,1},{1,0},{2,3},{3,2},{4,5},{5,4},{6,7},{7,6},{8,9},{9,8},{10,11... | collective-permute-start | bytes 1572872 | tf_op jit(solution)/shard_map/ppermute | solution.py:56
  24.6 14.8 %collective-permute-start.10 = (bf16[8,16,16,128]{3,2,1,0:T(8,128)(2,1)S(1)}, bf16[8,16,16,128]{3,2,1,0:T(8,128)(2,1)S(1)}, u32[]{:S(2)}, u32[]{:S(2)}) collective-permute-start(bf16[8,16,16,128]{3,2,1,0:T(8,128)(2,1)S(1)} %collective-permute-done.8.refs_4_.refs_2_), channel_id=1, source_target_pairs={{0,1},{1,0},{2,3},{3,2},{4,5},{5,4},{6,7},{7,6},{8,9},{9,8},{10,11... | collective-permute-start | bytes 1572872 | tf_op jit(solution)/shard_map/ppermute | solution.py:56
  24.7 5.1 %collective-permute-start.5 = (bf16[37,16,128]{2,1,0:T(8,128)(2,1)S(1)}, bf16[37,16,128]{2,1,0:T(8,128)(2,1)S(1)}, u32[]{:S(2)}, u32[]{:S(2)}) collective-permute-start(bf16[37,16,128]{2,1,0:T(8,128)(2,1)S(1)} %collective-permute-done.1.refs_2_.refs_11_), channel_id=1, source_target_pairs={{0,2},{2,0},{1,3},{3,1},{4,6},{6,4},{5,7},{7,5},{8,10},{10,8},{9,1... | collective-permute-start | bytes 454664 | tf_op jit(solution)/shard_map/ppermute | solution.py:589
  24.9 8.1 %collective-permute-start.6 = (bf16[37,16,128]{2,1,0:T(8,128)(2,1)S(1)}, bf16[37,16,128]{2,1,0:T(8,128)(2,1)S(1)}, u32[]{:S(2)}, u32[]{:S(2)}) collective-permute-start(bf16[37,16,128]{2,1,0:T(8,128)(2,1)S(1)} %collective-permute-done.2.refs_3_.refs_12_), channel_id=1, source_target_pairs={{0,2},{2,0},{1,3},{3,1},{4,6},{6,4},{5,7},{7,5},{8,10},{10,8},{9,1... | collective-permute-start | bytes 454664 | tf_op jit(solution)/shard_map/ppermute | solution.py:589
  34.0 30.2 %copy-start.6 = (bf16[8,18,16,128]{3,2,1,0:T(8,128)(2,1)}, bf16[8,18,16,128]{3,2,1,0:T(8,128)(2,1)S(1)}, u32[]{:S(2)}) copy-start(bf16[8,18,16,128]{3,2,1,0:T(8,128)(2,1)S(1)} %get-tuple-element.40.up) | copy-start | bytes 1769476
  34.0 23.3 %collective-permute-start.13 = (bf16[8,18,16,128]{3,2,1,0:T(8,128)(2,1)S(1)}, bf16[8,18,16,128]{3,2,1,0:T(8,128)(2,1)S(1)}, u32[]{:S(2)}, u32[]{:S(2)}) collective-permute-start(bf16[8,18,16,128]{3,2,1,0:T(8,128)(2,1)S(1)} %get-tuple-element.40.up), channel_id=1, source_target_pairs={{0,1},{1,0},{2,3},{3,2},{4,5},{5,4},{6,7},{7,6},{8,9},{9,8},{10,11... | collective-permute-start | bytes 1769480 | tf_op jit(solution)/shard_map/ppermute | solution.py:56
  35.4 28.9 %copy-start.8 = (bf16[64,16,128]{2,1,0:T(8,128)(2,1)}, bf16[64,16,128]{2,1,0:T(8,128)(2,1)S(1)}, u32[]{:S(2)}) copy-start(bf16[64,16,128]{2,1,0:T(8,128)(2,1)S(1)} %collective-permute-done.11.refs_7_.refs_6_) | copy-start | bytes 786436
  35.4 4.0 %collective-permute-start.12 = (bf16[64,16,128]{2,1,0:T(8,128)(2,1)S(1)}, bf16[64,16,128]{2,1,0:T(8,128)(2,1)S(1)}, u32[]{:S(2)}, u32[]{:S(2)}) collective-permute-start(bf16[64,16,128]{2,1,0:T(8,128)(2,1)S(1)} %collective-permute-done.11.refs_7_.refs_6_), channel_id=1, source_target_pairs={{0,1},{1,0},{2,3},{3,2},{4,5},{5,4},{6,7},{7,6},{8,9},{9,8},{10,11... | collective-permute-start | bytes 786440 | tf_op jit(solution)/shard_map/ppermute | solution.py:56
  35.5 1.9 %collective-permute-start.7 = (f32[40,128]{1,0:T(8,128)S(1)}, f32[40,128]{1,0:T(8,128)S(1)}, u32[]{:S(2)}, u32[]{:S(2)}) collective-permute-start(f32[40,128]{1,0:T(8,128)S(1)} %get-tuple-element.36.refs_1_.table), channel_id=1, source_target_pairs={{0,1},{1,0},{2,3},{3,2},{4,5},{5,4},{6,7},{7,6},{8,9},{9,8},{10,11... | collective-permute-start | bytes 61448 | tf_op jit(solution)/shard_map/ppermute | solution.py:56
  37.4 17.5 %collective-permute-start.14 = (bf16[2,18,16,128]{3,2,1,0:T(8,128)(2,1)S(1)}, bf16[2,18,16,128]{3,2,1,0:T(8,128)(2,1)S(1)}, u32[]{:S(2)}, u32[]{:S(2)}) collective-permute-start(bf16[2,18,16,128]{3,2,1,0:T(8,128)(2,1)S(1)} %get-tuple-element.41), channel_id=1, source_target_pairs={{4,0},{8,4},{12,8},{5,1},{9,5},{13,9},{6,2},{10,6},{14,10},{7,3},{... | collective-permute-start | bytes 442376 | tf_op jit(solution)/shard_map/ppermute | solution.py:630
  50.4 27.0 %collective-permute-start.18 = (bf16[27,32,128]{2,1,0:T(8,128)(2,1)S(1)}, bf16[27,32,128]{2,1,0:T(8,128)(2,1)S(1)}, u32[]{:S(2)}, u32[]{:S(2)}) collective-permute-start(bf16[27,32,128]{2,1,0:T(8,128)(2,1)S(1)} %get-tuple-element.48), channel_id=1, source_target_pairs={{0,12},{4,0},{8,4},{12,8},{1,13},{5,1},{9,5},{13,9},{2,14},{6,2},{... | collective-permute-start | bytes 663560 | tf_op jit(solution)/shard_map/ppermute | solution.py:664
  50.4 27.0 %collective-permute-start.16 = (bf16[27,32,128]{2,1,0:T(8,128)(2,1)S(1)}, bf16[27,32,128]{2,1,0:T(8,128)(2,1)S(1)}, u32[]{:S(2)}, u32[]{:S(2)}) collective-permute-start(bf16[27,32,128]{2,1,0:T(8,128)(2,1)S(1)} %get-tuple-element.46), channel_id=1, source_target_pairs={{0,4},{4,8},{8,12},{12,0},{1,5},{5,9},{9,13},{13,1},{2,6},{6,10},{... | collective-permute-start | bytes 663560 | tf_op jit(solution)/shard_map/ppermute | solution.py:664
  52.1 26.0 %collective-permute-start.17 = (bf16[27,32,128]{2,1,0:T(8,128)(2,1)S(1)}, bf16[27,32,128]{2,1,0:T(8,128)(2,1)}, u32[]{:S(2)}, u32[]{:S(2)}) collective-permute-start(bf16[27,32,128]{2,1,0:T(8,128)(2,1)S(1)} %get-tuple-element.47), channel_id=1, source_target_pairs={{0,8},{4,12},{8,0},{12,4},{1,9},{5,13},{9,1},{13,5},{2,10},{6,14},... | collective-permute-start | bytes 663560 | tf_op jit(solution)/shard_map/ppermute | solution.py:664
  54.9 2.5 %collective-permute-start.15 = (bf16[2,18,16,128]{3,2,1,0:T(8,128)(2,1)S(1)}, bf16[2,18,16,128]{3,2,1,0:T(8,128)(2,1)S(1)}, u32[]{:S(2)}, u32[]{:S(2)}) collective-permute-start(bf16[2,18,16,128]{3,2,1,0:T(8,128)(2,1)S(1)} %collective-permute-done.14.next_own), channel_id=1, source_target_pairs={{0,1},{1,0},{2,3},{3,2},{4,5},{5,4},{6,7},{7,6},{8,9},{9,8},{10,11... | collective-permute-start | bytes 442376 | tf_op jit(solution)/shard_map/ppermute | solution.py:56
  65.1 15.3 %all-to-all-start = ((f32[16,16,128]{2,1,0:T(8,128)}), f32[16,16,128]{2,1,0:T(8,128)}, u32[]{:S(2)}, u32[]{:S(2)}) async-start(f32[16,16,128]{2,1,0:T(8,128)} %get-tuple-element.42), calls=%async_computation | async-start | bytes 262144 | tf_op jit(solution)/shard_map/all_to_all | solution.py:643
  76.9 3.5 %collective-permute-start.19 = (f32[8,128,128]{2,1,0:T(8,128)}, f32[8,128,128]{2,1,0:T(8,128)}, u32[]{:S(2)}, u32[]{:S(2)}) collective-permute-start(f32[8,128,128]{2,1,0:T(8,128)} %get-tuple-element.51), channel_id=1, source_target_pairs={{0,1},{1,0},{2,3},{3,2},{4,5},{5,4},{6,7},{7,6},{8,9},{9,8},{10,11... | collective-permute-start | bytes 1572872 | tf_op jit(solution)/shard_map/ppermute | solution.py:56
  77.3 3.1 %collective-permute-start.20 = (bf16[8,8,16,128]{3,2,1,0:T(8,128)(2,1)}, bf16[8,8,16,128]{3,2,1,0:T(8,128)(2,1)}, u32[]{:S(2)}, u32[]{:S(2)}) collective-permute-start(bf16[8,8,16,128]{3,2,1,0:T(8,128)(2,1)} %get-tuple-element.53), channel_id=1, source_target_pairs={{0,1},{1,0},{2,3},{3,2},{4,5},{5,4},{6,7},{7,6},{8,9},{9,8},{10,11... | collective-permute-start | bytes 786440 | tf_op jit(solution)/shard_map/ppermute | solution.py:56
  (16 other events, 146.5 us)
